TPU v7x, 32 devices: a whole 2x2x4 slice. The times are simulated.
32 devices in a mesh: ctx: 8 (over z, y), ch: 4 (over x, core).
Axes of the slice: x: 2, y: 2, z: 4, core: 2. Of those that a mesh axis runs over, the one named last changes fastest.
Arguments:
- tokens: bfloat16 [8192, 4096], P('ctx', 'ch'), may hold values from -6 to 6
- w_input: bfloat16 [2, 4096, 4096], P(None, None, 'ch'), may hold values from -0.09375 to 0.09375
- w_output: bfloat16 [4096, 4096], P('ctx', 'ch'), may hold values from -0.09375 to 0.09375
- bias_update: float32 [4096], P('ch'), may hold values from -14 to 1
- bias_cand: float32 [4096], P('ch'), may hold values from -1 to 1
- recur_gain: float32 [4096], P('ch'), may hold values from -0.95 to 0.95
- start_state: float32 [4096], P('ch'), may hold values from -1 to 1
Outputs:
- mixed: bfloat16 [8192, 4096], P('ctx', 'ch')
All inputs are finite; a program needn't handle non-finite values.
Results may differ from a plain program's by a relative error of at most 0.005.
Values may be sent and summed in bfloat16 or wider, within the bound.
No kernel may reach another device: no remote copies, remote signals or barrier semaphores. Data moves between devices by JAX's collectives and lax.ppermute only.
A program may use at most 128 MiB of HBM per device.

v0:
```python
import functools
import math

import jax
import jax.numpy as jnp
from jax import lax
from jax.experimental import pallas as pl
from jax.experimental.pallas import tpu as pltpu
from jax.sharding import PartitionSpec as P


SEGS = 8
LANES = 128
F32 = jnp.float32
BF16 = jnp.bfloat16
VMEM_LIMIT = 60 * 1024 * 1024


def swap(block, axis, bits):
    return lax.ppermute(block, axis, [(i, i ^ bits) for i in range(lax.axis_size(axis))])


def tile_of(width, most):
    return math.gcd(width, most)


def params(limit=VMEM_LIMIT):
    return pltpu.CompilerParams(vmem_limit_bytes=limit)


def cost(flops, nbytes, trans=0):
    return pl.CostEstimate(flops=int(flops), bytes_accessed=int(nbytes), transcendentals=int(trans))


def near_kernel(half, place, *refs):
    blocks = refs[:half]
    w_ref, out_ref = refs[half:]
    depth = blocks[0].shape[1]
    rows = out_ref.shape[1]
    step = tile_of(rows, 256)
    slot = lax.rem(place[0], half)

    def body(m, carry):
        lines = pl.ds(pl.multiple_of(m * step, step), step)
        total = None
        for d in range(half):
            deep = pl.ds(pl.multiple_of((slot ^ d) * depth, depth), depth)
            part = jnp.dot(blocks[d][lines, :], w_ref[0, deep, :], preferred_element_type=F32)
            total = part if total is None else total + part
        out_ref[0, lines, :] = total
        return carry

    lax.fori_loop(0, rows // step, body, 0)


def near_product(place, blocks, weights):
    half = len(blocks)
    rows, depth = blocks[0].shape
    gates, _, width = weights.shape
    tn = tile_of(width, 512)
    spec = pl.BlockSpec((rows, depth), lambda g, n, p: (0, 0))
    return pl.pallas_call(
        functools.partial(near_kernel, half),
        out_shape=jax.ShapeDtypeStruct((gates, rows, width), F32),
        grid_spec=pltpu.PrefetchScalarGridSpec(
            num_scalar_prefetch=1,
            grid=(gates, width // tn),
            in_specs=[spec] * half
            + [pl.BlockSpec((1, half * depth, tn), lambda g, n, p: (g, p[0] // half, n))],
            out_specs=pl.BlockSpec((1, rows, tn), lambda g, n, p: (g, 0, n)),
        ),
        compiler_params=params(),
        cost_estimate=cost(
            2 * gates * rows * half * depth * width,
            gates * width * (half * depth * 2 + rows * 4) + half * rows * depth * 2,
        ),
    )(place, *blocks, weights)


def compose_rows(maps, count, a, b):
    for k in range(count):
        slope = maps[0, k : k + 1, :]
        shift = maps[1, k : k + 1, :]
        b = slope * b + shift
        a = slope * a
    return a, b


def spread_rows(flat, g, j, seg):
    parts = [flat[g, l, pl.ds(j, SEGS, stride=seg), :] for l in range(flat.shape[1])]
    return jnp.concatenate(parts, axis=1)


def gate_kernel(half, chunk, before, last, place, *refs):
    blocks = refs[:half]
    part_ref, w_ref, bias_ref, gain_ref, start_ref = refs[half : half + 5]
    earlier = refs[half + 5 : half + 5 + before]
    outs = refs[half + 5 + before :]
    gates_ref, maps_ref = outs[:2]
    flat = outs[-1]
    depth = blocks[0].shape[1]
    rows = part_ref.shape[1]
    seg = rows // SEGS
    width = part_ref.shape[2]
    slot = lax.rem(place[0], half)
    for g in range(2):
        total = part_ref[g]
        for d in range(half):
            deep = pl.ds(pl.multiple_of((slot ^ d) * depth, depth), depth)
            total = total + jnp.dot(blocks[d][...], w_ref[g, deep, :], preferred_element_type=F32)
        total = (total + bias_ref[g : g + 1, :]).astype(BF16).astype(F32)
        for l in range(width // LANES):
            flat[g, l] = total[:, l * LANES : (l + 1) * LANES]
    gain = jnp.broadcast_to(gain_ref[...], (SEGS, width))

    def pair(jj, carry, first):
        a, b = carry
        held = ([], [])
        for k in range(2):
            j = 2 * jj + k
            pre = spread_rows(flat, 0, j, seg)
            cand = spread_rows(flat, 1, j, seg)
            held[0].append(pre)
            held[1].append(cand)
            update = jax.nn.sigmoid(pre)
            if first and k == 0:
                lead = lax.broadcasted_iota(jnp.int32, (SEGS, width), 0) == 0
                prev = jnp.where(lead & (place[1] == 0), start_ref[...], 0.0)
                squashed = jnp.tanh(cand + gain * prev)
                bend = gain * (1.0 - squashed * squashed)
                offset = update * (squashed - bend * prev)
            else:
                squashed = jnp.tanh(cand)
                bend = gain * (1.0 - squashed * squashed)
                offset = update * squashed
            slope = (1.0 - update) + update * bend
            b = slope * b + offset
            a = slope * a
        lines = pl.ds(pl.multiple_of(jj * 2 * SEGS, 2 * SEGS), 2 * SEGS)
        for g in range(2):
            gates_ref[g, lines, :] = jnp.concatenate(held[g], axis=0).astype(BF16)
        return a, b

    carry = (jnp.ones((SEGS, width), F32), jnp.zeros((SEGS, width), F32))
    if chunk == 0:
        carry = pair(0, carry, True)
        begin = 1
    else:
        begin = 0
    a, b = lax.fori_loop(begin, seg // 2, lambda jj, c: pair(jj, c, False), carry)
    maps_ref[0] = a
    maps_ref[1] = b
    if last:
        total_ref = outs[2]
        ta, tb = jnp.ones((1, width), F32), jnp.zeros((1, width), F32)
        for maps in list(earlier) + [maps_ref]:
            ta, tb = compose_rows(maps, SEGS, ta, tb)
        for i in range(total_ref.shape[0]):
            total_ref[i, 0:1, :] = ta
            total_ref[i, 1:2, :] = tb


def gate_chunk(place, blocks, partial, weights, biases, gain, start, earlier, chunk, last, peers):
    half = len(blocks)
    rows, depth = blocks[0].shape
    gates, _, width = weights.shape
    tn = tile_of(width, 256)
    row_spec = pl.BlockSpec((1, tn), lambda n, p: (0, n))
    map_spec = pl.BlockSpec((2, SEGS, tn), lambda n, p: (0, 0, n))
    out_shape = [
        jax.ShapeDtypeStruct((2, rows, width), BF16),
        jax.ShapeDtypeStruct((2, SEGS, width), F32),
    ]
    out_specs = [pl.BlockSpec((2, rows, tn), lambda n, p: (0, 0, n)), map_spec]
    if last:
        out_shape.append(jax.ShapeDtypeStruct((peers, 2, width), F32))
        out_specs.append(pl.BlockSpec((peers, 2, tn), lambda n, p: (0, 0, n)))
    return pl.pallas_call(
        functools.partial(gate_kernel, half, chunk, len(earlier), last),
        out_shape=out_shape,
        grid_spec=pltpu.PrefetchScalarGridSpec(
            num_scalar_prefetch=1,
            grid=(width // tn,),
            in_specs=[pl.BlockSpec((rows, depth), lambda n, p: (0, 0))] * half
            + [
                pl.BlockSpec((2, rows, tn), lambda n, p: (0, chunk, n)),
                pl.BlockSpec((2, half * depth, tn), lambda n, p: (0, (p[0] // half) ^ 1, n)),
                pl.BlockSpec((2, tn), lambda n, p: (0, n)),
                row_spec,
                row_spec,
            ]
            + [map_spec] * len(earlier),
            out_specs=out_specs,
            scratch_shapes=[pltpu.VMEM((2, tn // LANES, rows, LANES), F32)],
        ),
        compiler_params=params(),
        cost_estimate=cost(
            2 * gates * rows * half * depth * width,
            gates * width * (half * depth * 2 + rows * 6) + half * rows * depth * 2,
            4 * rows * width,
        ),
    )(place, *blocks, partial, weights, biases, gain, start, *earlier)


def entering_state(place, peer_maps, start, peers):
    state = start
    for k in range(peers):
        moved = peer_maps[k, 0:1, :] * state + peer_maps[k, 1:2, :]
        state = jnp.where(place[1] > k, moved, state)
    return state


def enter_segments(maps_list, state, enter):
    for c, maps in enumerate(maps_list):
        for k in range(SEGS):
            enter[c * SEGS + k : c * SEGS + k + 1, :] = state
            state = maps[0, k : k + 1, :] * state + maps[1, k : k + 1, :]


def bend_kernel(chunks, peers, place, *refs):
    gates = refs[:chunks]
    maps = refs[chunks : 2 * chunks]
    peer_ref, gain_ref, start_ref, run_ref, maps_ref, total_ref, enter = refs[2 * chunks :]
    rows, width = gates[0].shape[1:]
    seg = rows // SEGS
    start = start_ref[...]
    enter_segments(maps, entering_state(place, peer_ref, start, peers), enter)
    gain = jnp.broadcast_to(gain_ref[...], (SEGS, width))

    def pair(jj, carry, first):
        lines = pl.ds(pl.multiple_of(jj * 2 * SEGS, 2 * SEGS), 2 * SEGS)
        out = []
        for c in range(chunks):
            state, a, b = carry[c]
            pre2 = gates[c][0, lines, :].astype(F32)
            cand2 = gates[c][1, lines, :].astype(F32)
            for k in range(2):
                pre = pre2[k * SEGS : (k + 1) * SEGS]
                cand = cand2[k * SEGS : (k + 1) * SEGS]
                update = jax.nn.sigmoid(pre)
                keep = 1.0 - update
                if first and k == 0 and c == 0:
                    lead = lax.broadcasted_iota(jnp.int32, (SEGS, width), 0) == 0
                    prev = jnp.where(lead & (place[1] == 0), start, 0.0)
                    squashed = jnp.tanh(cand + gain * prev)
                    bend = gain * (1.0 - squashed * squashed)
                    offset = update * (squashed - bend * prev)
                else:
                    squashed = jnp.tanh(cand)
                    bend = gain * (1.0 - squashed * squashed)
                    offset = update * squashed
                slope = keep + update * bend
                squashed = jnp.tanh(cand + gain * state)
                bend = gain * (1.0 - squashed * squashed)
                slope2 = keep + update * bend
                offset2 = update * (squashed - bend * state)
                state = slope * state + offset
                b = slope2 * b + offset2
                a = slope2 * a
                row = pl.ds(pl.multiple_of(c * rows + (2 * jj + k) * SEGS, SEGS), SEGS)
                run_ref[0, row, :] = a
                run_ref[1, row, :] = b
            out.append((state, a, b))
        return tuple(out)

    one, zero = jnp.ones((SEGS, width), F32), jnp.zeros((SEGS, width), F32)
    carry = tuple((enter[c * SEGS : (c + 1) * SEGS, :], one, zero) for c in range(chunks))
    carry = pair(0, carry, True)
    carry = lax.fori_loop(1, seg // 2, lambda jj, c: pair(jj, c, False), carry)
    for c in range(chunks):
        maps_ref[0, c * SEGS : (c + 1) * SEGS, :] = carry[c][1]
        maps_ref[1, c * SEGS : (c + 1) * SEGS, :] = carry[c][2]
    ta, tb = compose_rows(maps_ref, chunks * SEGS, jnp.ones((1, width), F32), jnp.zeros((1, width), F32))
    for i in range(peers):
        total_ref[i, 0:1, :] = ta
        total_ref[i, 1:2, :] = tb


def bend_all(place, gates, maps, peer_maps, gain, start):
    chunks = len(gates)
    peers = peer_maps.shape[0]
    _, rows, width = gates[0].shape
    tn = tile_of(width, 256)
    row_spec = pl.BlockSpec((1, tn), lambda n, p: (0, n))
    return pl.pallas_call(
        functools.partial(bend_kernel, chunks, peers),
        out_shape=[
            jax.ShapeDtypeStruct((2, chunks * rows, width), F32),
            jax.ShapeDtypeStruct((2, chunks * SEGS, width), F32),
            jax.ShapeDtypeStruct((peers, 2, width), F32),
        ],
        grid_spec=pltpu.PrefetchScalarGridSpec(
            num_scalar_prefetch=1,
            grid=(width // tn,),
            in_specs=[pl.BlockSpec((2, rows, tn), lambda n, p: (0, 0, n))] * chunks
            + [pl.BlockSpec((2, SEGS, tn), lambda n, p: (0, 0, n))] * chunks
            + [pl.BlockSpec((peers, 2, tn), lambda n, p: (0, 0, n)), row_spec, row_spec],
            out_specs=[
                pl.BlockSpec((2, chunks * rows, tn), lambda n, p: (0, 0, n)),
                pl.BlockSpec((2, chunks * SEGS, tn), lambda n, p: (0, 0, n)),
                pl.BlockSpec((peers, 2, tn), lambda n, p: (0, 0, n)),
            ],
            scratch_shapes=[pltpu.VMEM((chunks * SEGS, tn), F32)],
        ),
        compiler_params=params(),
        cost_estimate=cost(
            40 * chunks * rows * width, 12 * chunks * rows * width, 5 * chunks * rows * width
        ),
        name="bend",
    )(place, *gates, *maps, peer_maps, gain, start)


def state_kernel(chunk, peers, place, run_ref, maps_ref, peer_ref, start_ref, out_ref, enter, flat):
    rows, width = out_ref.shape
    seg = rows // SEGS
    state = entering_state(place, peer_ref, start_ref[...], peers)
    for k in range((chunk + 1) * SEGS):
        if k >= chunk * SEGS:
            enter[k - chunk * SEGS : k - chunk * SEGS + 1, :] = state
        state = maps_ref[0, k : k + 1, :] * state + maps_ref[1, k : k + 1, :]
    entered = enter[...]

    def step(j, carry):
        row = pl.ds(pl.multiple_of(j * SEGS, SEGS), SEGS)
        now = run_ref[0, row, :] * entered + run_ref[1, row, :]
        for l in range(width // LANES):
            flat[l, pl.ds(j, SEGS, stride=seg), :] = now[:, l * LANES : (l + 1) * LANES]
        return carry

    lax.fori_loop(0, seg, step, 0, unroll=4)
    for l in range(width // LANES):
        out_ref[:, l * LANES : (l + 1) * LANES] = flat[l].astype(BF16)


def state_chunk(place, run, maps, peer_maps, start, rows, chunk):
    width = run.shape[2]
    peers = peer_maps.shape[0]
    segs = maps.shape[1]
    tn = tile_of(width, 256)
    return pl.pallas_call(
        functools.partial(state_kernel, chunk, peers),
        out_shape=jax.ShapeDtypeStruct((rows, width), BF16),
        grid_spec=pltpu.PrefetchScalarGridSpec(
            num_scalar_prefetch=1,
            grid=(width // tn,),
            in_specs=[
                pl.BlockSpec((2, rows, tn), lambda n, p: (0, chunk, n)),
                pl.BlockSpec((2, segs, tn), lambda n, p: (0, 0, n)),
                pl.BlockSpec((peers, 2, tn), lambda n, p: (0, 0, n)),
                pl.BlockSpec((1, tn), lambda n, p: (0, n)),
            ],
            out_specs=pl.BlockSpec((rows, tn), lambda n, p: (0, n)),
            scratch_shapes=[pltpu.VMEM((SEGS, tn), F32), pltpu.VMEM((tn // LANES, rows, LANES), F32)],
        ),
        compiler_params=params(),
        cost_estimate=cost(2 * rows * width, 10 * rows * width),
    )(place, run, maps, peer_maps, start)


def mix_kernel(groups, group, pieces, peers, place, *refs):
    count = groups * group
    blocks = refs[:count]
    weights = refs[count : count + peers * pieces]
    out_ref, states = refs[-2:]
    rows, depth = blocks[0].shape
    lines_of = weights[0].shape[0]

    @pl.when(pl.program_id(0) == 0)
    def _():
        for c in range(groups):
            for d in range(group):
                deep = pl.ds(pl.multiple_of((place[0] ^ d) * depth, depth), depth)
                states[c * rows : (c + 1) * rows, deep] = blocks[c * group + d][...]

    outer = peers // 2
    total = None
    for s in range(outer):
        source = lax.rem(place[1] // 2 + outer - s, outer)
        for i in range(2):
            owner = source * 2 + (lax.rem(place[1], 2) ^ i)
            for p in range(pieces):
                deep = pl.ds(pl.multiple_of((owner * pieces + p) * lines_of, lines_of), lines_of)
                w_ref = weights[(s * 2 + i) * pieces + p]
                part = jnp.dot(states[:, deep], w_ref[...], preferred_element_type=F32)
                total = part if total is None else total + part
    out_ref[...] = total.astype(BF16)


def mix_rows(place, blocks, weights, whole, first, total_rows, pieces):
    groups, group = len(blocks), len(blocks[0])
    rows, depth = blocks[0][0].shape
    lines_of, width = weights[0].shape
    peers = len(weights) // pieces
    tn = tile_of(width, 256)
    here = groups * rows
    args = [place] + [b for g in blocks for b in g] + list(weights)
    in_specs = [pl.BlockSpec((rows, depth), lambda n, p: (0, 0))] * (groups * group)
    in_specs += [pl.BlockSpec((lines_of, tn), lambda n, p: (0, n))] * len(weights)
    aliases = {}
    if whole is not None:
        aliases = {len(args): 0}
        args.append(whole)
        in_specs.append(pl.BlockSpec(memory_space=pl.ANY))
    return pl.pallas_call(
        functools.partial(mix_kernel, groups, group, pieces, peers),
        out_shape=jax.ShapeDtypeStruct((total_rows, width), BF16),
        grid_spec=pltpu.PrefetchScalarGridSpec(
            num_scalar_prefetch=1,
            grid=(width // tn,),
            in_specs=in_specs,
            out_specs=pl.BlockSpec((here, tn), lambda n, p: (first // here, n)),
            scratch_shapes=[pltpu.VMEM((here, group * depth), BF16)],
        ),
        input_output_aliases=aliases,
        compiler_params=params(),
        cost_estimate=cost(
            2 * here * group * depth * width, 2 * group * depth * (width + here) + 2 * here * width
        ),
    )(*args)


EARLY = 5
CHUNKS = 4


def pieces_of(lines_of):
    return 2 if lines_of % (4 * LANES) == 0 else 1


class Ring:
    def __init__(self, w_output):
        self.peers = lax.axis_size("ctx")
        self.outer = self.peers // 2
        self.pieces = pieces_of(w_output.shape[0])
        lines_of = w_output.shape[0] // self.pieces
        self.held = {}
        for p in range(self.pieces):
            self.held[0, 0, p] = w_output[p * lines_of : (p + 1) * lines_of]

    def ring_step(self, n, gate=None):
        s, p = n // self.pieces + 1, n % self.pieces
        block = self.held[s - 1, 0, p]
        if gate is not None:
            block, _ = lax.optimization_barrier((block, gate))
        route = [(i, (i + 2) % self.peers) for i in range(self.peers)]
        self.held[s, 0, p] = lax.ppermute(block, "ctx", route)

    def swap_step(self, n, gate=None):
        s, p = n // self.pieces, n % self.pieces
        block = self.held[s, 0, p]
        if gate is not None:
            block, _ = lax.optimization_barrier((block, gate))
        self.held[s, 1, p] = swap(block, "ctx", 1)

    def run(self, gate):
        rings, swaps = (self.outer - 1) * self.pieces, self.outer * self.pieces
        for n in range(max(rings, swaps)):
            g = gate if n >= EARLY else None
            if n < rings:
                self.ring_step(n, g)
            if n < swaps:
                self.swap_step(n, g)

    def blocks(self):
        steps = [(s, i) for s in range(self.outer) for i in range(2)]
        return [self.held[s, i, p] for s, i in steps for p in range(self.pieces)]


def layer(tokens, w_input, w_output, bias_update, bias_cand, recur_gain, start_state):
    peers = lax.axis_size("ctx")
    group = lax.axis_size("ch")
    half = group // 2
    total_rows = tokens.shape[0]
    chunks = CHUNKS
    rows = total_rows // chunks
    place = jnp.stack([lax.axis_index("ch"), lax.axis_index("ctx")]).astype(jnp.int32)
    biases = jnp.stack([bias_update, bias_cand], axis=0)
    gain = recur_gain[None, :]
    start = start_state[None, :]

    far = []
    rest = tokens
    for c in range(chunks):
        piece = rest[c * rows : (c + 1) * rows]
        rest, piece = lax.optimization_barrier((rest, piece))
        far.append([swap(piece, "ch", half)])
    near = [tokens]
    for d in range(1, half):
        near.append(swap(tokens, "ch", d))
    for c in range(chunks):
        for d in range(1, half):
            far[c].append(swap(far[c][0], "ch", d))

    partial = near_product(place, near, w_input)
    gates, maps = [], []
    for c in range(chunks):
        last = c == chunks - 1
        out = gate_chunk(
            place, far[c], partial, w_input, biases, gain, start, maps if last else [], c, last, peers
        )
        gates.append(out[0])
        maps.append(out[1])
    peer_maps = lax.all_to_all(out[2], "ctx", 0, 0, tiled=True)
    run, run_maps, totals = bend_all(place, gates, maps, peer_maps, gain, start)
    peer_maps = lax.all_to_all(totals, "ctx", 0, 0, tiled=True)
    ring = Ring(w_output)
    ring.run(peer_maps)

    blocks = []
    for c in range(chunks):
        own = state_chunk(place, run, run_maps, peer_maps, start, rows, c)
        across = swap(own, "ch", half)
        blocks.append([own, across])
    for c in range(chunks):
        own, across = blocks[c]
        lows, highs = [own], [across]
        for d in range(1, half):
            lows.append(swap(own, "ch", d))
            highs.append(swap(across, "ch", d))
        blocks[c] = lows + highs
    weights = ring.blocks()
    mixed = None
    split = chunks - 1 if chunks > 1 else chunks
    mixed = mix_rows(place, blocks[:split], weights, None, 0, total_rows, ring.pieces)
    if split < chunks:
        mixed = mix_rows(
            place, blocks[split:], weights, mixed, split * rows, total_rows, ring.pieces
        )
    return mixed


def solution(mesh):
    return jax.shard_map(
        layer,
        mesh=mesh,
        in_specs=(
            P("ctx", "ch"),
            P(None, None, "ch"),
            P("ctx", "ch"),
            P("ch"),
            P("ch"),
            P("ch"),
            P("ch"),
        ),
        out_specs=P("ctx", "ch"),
        check_vma=False,
    )
```

profile of v0, /device:TPU:0, one launch (start us, length us, event | category | flops | bytes accessed | tf_op | source)
XLA Modules:
  0.0 251.0 jit_solution(16333004339830692670)
XLA Ops:
  0.5 1.9 slice.18
  2.4 1.1 slice.19
  3.5 1.1 slice.20
  4.6 1.1 slice.21
  5.6 2.6 %collective-permute-start.7 = (bf16[256,1024]{1,0:T(8,128)(2,1)S(1)}, bf16[256,1024]{1,0:T(8,128)(2,1)}, u32[]{:S(2)}, u32[]{:S(2)}) collective-permute-start(bf16[256,1024]{1,0:T(8,128)(2,1)S(1)} %slice.21), channel_id=1, source_target_pairs={{0,2},{1,3},{2,0},{3,1},{4,6},{5,7},{6,4},{7,5},{8,10},{9,11},{10,... | collective-permute-start | bytes 1572872 | tf_op jit(solution)/shard_map/ppermute | solution.py:20
  8.3 1.9 collective-permute-start.3
  10.5 10.7 %collective-permute-done.7.refs_0_ = bf16[256,1024]{1,0:T(8,128)(2,1)} collective-permute-done((bf16[256,1024]{1,0:T(8,128)(2,1)S(1)}, bf16[256,1024]{1,0:T(8,128)(2,1)}, u32[]{:S(2)}, u32[]{:S(2)}) %collective-permute-start.7) | collective-permute-done | bytes 524320 | tf_op jit(solution)/shard_map/ppermute | solution.py:20
  21.2 2.1 collective-permute-start.15
  23.3 9.1 %collective-permute-done.5.refs_0_ = bf16[256,1024]{1,0:T(8,128)(2,1)} collective-permute-done((bf16[256,1024]{1,0:T(8,128)(2,1)S(1)}, bf16[256,1024]{1,0:T(8,128)(2,1)}, u32[]{:S(2)}, u32[]{:S(2)}) %collective-permute-start.5) | collective-permute-done | bytes 524320 | tf_op jit(solution)/shard_map/ppermute | solution.py:20
  32.4 2.1 collective-permute-start.14
  34.5 9.0 %collective-permute-done.3.refs_0_ = bf16[256,1024]{1,0:T(8,128)(2,1)S(1)} collective-permute-done((bf16[256,1024]{1,0:T(8,128)(2,1)S(1)}, bf16[256,1024]{1,0:T(8,128)(2,1)S(1)}, u32[]{:S(2)}, u32[]{:S(2)}) %collective-permute-start.3) | collective-permute-done | bytes 524320 | tf_op jit(solution)/shard_map/ppermute | solution.py:20
  43.5 0.7 pad_add_fusion.place
  44.9 9.7 %collective-permute-done.refs_0_ = bf16[256,1024]{1,0:T(8,128)(2,1)} collective-permute-done((bf16[256,1024]{1,0:T(8,128)(2,1)}, bf16[256,1024]{1,0:T(8,128)(2,1)}, u32[]{:S(2)}, u32[]{:S(2)}) %collective-permute-start) | collective-permute-done | bytes 524320 | tf_op jit(solution)/shard_map/ppermute | solution.py:20
  55.2 1.8 collective-permute-start.19
  57.0 1.6 collective-permute-start.18
  58.6 16.4 %shard_map.73.refs_2_ = f32[2,1024,1024]{2,1,0:T(8,128)} custom-call(s32[2]{0:T(128)} %pad_add_fusion.place, bf16[1024,1024]{1,0:T(8,128)(2,1)} %refs_0_.1, bf16[1024,1024]{1,0:T(8,128)(2,1)} %collective-permute-done.2.refs_1_, bf16[2,4096,1024]{2,1,0:T(8,128)(2,1)} %refs_3_.7), custom_call_target="tpu_custom_call" | custom-call | flops 8589934592 | bytes 20971520 | tf_op jit(solution)/shard_map/pallas_call | solution.py:62
  75.0 9.6 %shard_map.76 = (bf16[2,256,1024]{2,1,0:T(8,128)(2,1)}, f32[2,8,1024]{2,1,0:T(8,128)}) custom-call(s32[2]{0:T(128)} %pad_add_fusion.place, bf16[256,1024]{1,0:T(8,128)(2,1)} %collective-permute-done.5.refs_0_, bf16[256,1024]{1,0:T(8,128)(2,1)} %collective-permute-done.6.refs_1_, f32[2,1024,1024]{2,1,0:T(8,128)} %shard_map.73.refs_2_, ...), custom_call_target="tpu_custom_call" | custom-call | flops 2147483648 | bytes 12582912 | tf_op jit(solution)/shard_map/pallas_call | solution.py:178
  84.6 1.6 collective-permute-start.13
  86.2 9.6 %shard_map.75 = (bf16[2,256,1024]{2,1,0:T(8,128)(2,1)}, f32[2,8,1024]{2,1,0:T(8,128)}) custom-call(s32[2]{0:T(128)} %pad_add_fusion.place, bf16[256,1024]{1,0:T(8,128)(2,1)} %copy-done.12, bf16[256,1024]{1,0:T(8,128)(2,1)} %collective-permute-done.4.refs_1_, f32[2,1024,1024]{2,1,0:T(8,128)} %shard_map.73.refs_2_, bf16[2,4096,1024]{2,1,0:T(8,128)(2,1)} %refs_3_.7, ...), custom_call_target="tpu_custom_call" | custom-call | flops 2147483648 | bytes 12582912 | tf_op jit(solution)/shard_map/pallas_call | solution.py:178
  96.3 1.5 collective-permute-start.17
  98.4 1.6 collective-permute-start.22
  100.0 9.4 %shard_map.74 = (bf16[2,256,1024]{2,1,0:T(8,128)(2,1)}, f32[2,8,1024]{2,1,0:T(8,128)}) custom-call(s32[2]{0:T(128)} %pad_add_fusion.place, bf16[256,1024]{1,0:T(8,128)(2,1)} %collective-permute-done.refs_0_, bf16[256,1024]{1,0:T(8,128)(2,1)} %collective-permute-done.1.refs_1_, f32[2,1024,1024]{2,1,0:T(8,128)} %shard_map.73.refs_2_, ...), custom_call_target="tpu_custom_call" | custom-call | flops 2147483648 | bytes 12582912 | tf_op jit(solution)/shard_map/pallas_call | solution.py:178
  109.4 9.7 %shard_map.77 = (bf16[2,256,1024]{2,1,0:T(8,128)(2,1)}, f32[2,8,1024]{2,1,0:T(8,128)}, f32[8,2,1024]{2,1,0:T(2,128)}) custom-call(s32[2]{0:T(128)} %pad_add_fusion.place, bf16[256,1024]{1,0:T(8,128)(2,1)} %collective-permute-done.7.refs_0_, bf16[256,1024]{1,0:T(8,128)(2,1)} %collective-permute-done.8.refs_1_, f32[2,1024,1024]{2,1,0:T(8,128)} %shard_map.73.refs_2_, ...), custom_call_target="tpu_custom_call" | custom-call | flops 2147483648 | bytes 12582912 | tf_op jit(solution)/shard_map/pallas_call | solution.py:178
  119.1 13.8 %all_to_all.10.refs_8_ = f32[8,2,1024]{2,1,0:T(2,128)} all-to-all(f32[8,2,1024]{2,1,0:T(2,128)} %get-tuple-element.42), channel_id=1, replica_groups=mesh['ctx'=8,'ch'=4] {'ctx'}, dimensions={0} | all-to-all | bytes 131072 | tf_op jit(solution)/shard_map/all_to_all | solution.py:503
  132.8 9.6 %bend.1 = (f32[2,1024,1024]{2,1,0:T(8,128)}, f32[2,32,1024]{2,1,0:T(8,128)}, f32[8,2,1024]{2,1,0:T(2,128)}) custom-call(s32[2]{0:T(128)} %pad_add_fusion.place, bf16[2,256,1024]{2,1,0:T(8,128)(2,1)} %get-tuple-element.28.refs_0_, bf16[2,256,1024]{2,1,0:T(8,128)(2,1)} %get-tuple-element.31.refs_1_, bf16[2,256,1024]{2,1,0:T(8,128)(2,1)} %get-tuple-element.34.refs_2_, ...), custom_call_target="tpu_custom_call" | custom-call | flops 41943040 | bytes 12582912 | tf_op jit(solution)/shard_map/bend/pallas_call | solution.py:285
  142.5 11.5 %all_to_all.11.peer_ref = f32[8,2,1024]{2,1,0:T(2,128)} all-to-all(f32[8,2,1024]{2,1,0:T(2,128)} %get-tuple-element.45), channel_id=1, replica_groups=mesh['ctx'=8,'ch'=4] {'ctx'}, dimensions={0} | all-to-all | bytes 131072 | tf_op jit(solution)/shard_map/all_to_all | solution.py:505
  154.0 4.7 %shard_map.79.refs_0_ = bf16[256,1024]{1,0:T(8,128)(2,1)} custom-call(s32[2]{0:T(128)} %pad_add_fusion.place, f32[2,1024,1024]{2,1,0:T(8,128)} %get-tuple-element.43.run_ref, f32[2,32,1024]{2,1,0:T(8,128)} %get-tuple-element.44.maps_ref, f32[8,2,1024]{2,1,0:T(2,128)} %all_to_all.11.peer_ref, f32[1,1024]{1,0:T(1,128)} %bitcast.11), custom_call_target="tpu_custom_call" | custom-call | flops 524288 | bytes 2621440 | tf_op jit(solution)/shard_map/pallas_call | solution.py:340
  158.7 4.8 %shard_map.78.refs_0_ = bf16[256,1024]{1,0:T(8,128)(2,1)} custom-call(s32[2]{0:T(128)} %pad_add_fusion.place, f32[2,1024,1024]{2,1,0:T(8,128)} %get-tuple-element.43.run_ref, f32[2,32,1024]{2,1,0:T(8,128)} %get-tuple-element.44.maps_ref, f32[8,2,1024]{2,1,0:T(2,128)} %all_to_all.11.peer_ref, f32[1,1024]{1,0:T(1,128)} %bitcast.12), custom_call_target="tpu_custom_call" | custom-call | flops 524288 | bytes 2621440 | tf_op jit(solution)/shard_map/pallas_call | solution.py:340
  164.0 1.5 collective-permute-start.10
  166.0 0.9 collective-permute-start.23
  166.9 4.8 %shard_map.80.refs_4_ = bf16[256,1024]{1,0:T(8,128)(2,1)} custom-call(s32[2]{0:T(128)} %pad_add_fusion.place, f32[2,1024,1024]{2,1,0:T(8,128)} %get-tuple-element.43.run_ref, f32[2,32,1024]{2,1,0:T(8,128)} %get-tuple-element.44.maps_ref, f32[8,2,1024]{2,1,0:T(2,128)} %all_to_all.11.peer_ref, f32[1,1024]{1,0:T(1,128)} %bitcast.13), custom_call_target="tpu_custom_call" | custom-call | flops 524288 | bytes 2621440 | tf_op jit(solution)/shard_map/pallas_call | solution.py:340
  171.7 3.3 %collective-permute-done.20.refs_22_.refs_14_ = bf16[256,1024]{1,0:T(8,128)(2,1)S(1)} collective-permute-done((bf16[256,1024]{1,0:T(8,128)(2,1)S(1)}, bf16[256,1024]{1,0:T(8,128)(2,1)S(1)}, u32[]{:S(2)}, u32[]{:S(2)}) %collective-permute-start.20) | collective-permute-done | bytes 524320 | tf_op jit(solution)/shard_map/ppermute | solution.py:20
  175.0 1.5 collective-permute-start.30
  176.5 4.8 %shard_map.81.refs_8_ = bf16[256,1024]{1,0:T(8,128)(2,1)} custom-call(s32[2]{0:T(128)} %pad_add_fusion.place, f32[2,1024,1024]{2,1,0:T(8,128)} %get-tuple-element.43.run_ref, f32[2,32,1024]{2,1,0:T(8,128)} %get-tuple-element.44.maps_ref, f32[8,2,1024]{2,1,0:T(2,128)} %all_to_all.11.peer_ref, f32[1,1024]{1,0:T(1,128)} %bitcast.14), custom_call_target="tpu_custom_call" | custom-call | flops 524288 | bytes 2621440 | tf_op jit(solution)/shard_map/pallas_call | solution.py:340
  181.4 8.9 %collective-permute-done.27.refs_2_ = bf16[256,1024]{1,0:T(8,128)(2,1)} collective-permute-done((bf16[256,1024]{1,0:T(8,128)(2,1)}, bf16[256,1024]{1,0:T(8,128)(2,1)}, u32[]{:S(2)}, u32[]{:S(2)}) %collective-permute-start.27) | collective-permute-done | bytes 524320 | tf_op jit(solution)/shard_map/ppermute | solution.py:20
  190.4 1.5 collective-permute-start.33
  191.9 1.7 collective-permute-start.21
  193.6 8.0 %collective-permute-done.30.refs_6_ = bf16[256,1024]{1,0:T(8,128)(2,1)} collective-permute-done((bf16[256,1024]{1,0:T(8,128)(2,1)}, bf16[256,1024]{1,0:T(8,128)(2,1)}, u32[]{:S(2)}, u32[]{:S(2)}) %collective-permute-start.30) | collective-permute-done | bytes 524320 | tf_op jit(solution)/shard_map/ppermute | solution.py:20
  201.6 1.6 collective-permute-start.24
  203.2 5.8 %collective-permute-done.33.refs_10_ = bf16[256,1024]{1,0:T(8,128)(2,1)S(1)} collective-permute-done((bf16[256,1024]{1,0:T(8,128)(2,1)}, bf16[256,1024]{1,0:T(8,128)(2,1)S(1)}, u32[]{:S(2)}, u32[]{:S(2)}) %collective-permute-start.33) | collective-permute-done | bytes 524320 | tf_op jit(solution)/shard_map/ppermute | solution.py:20
  209.6 1.6 collective-permute-start.25
  211.2 6.8 %collective-permute-done.24.refs_26_.refs_18_ = bf16[256,1024]{1,0:T(8,128)(2,1)S(1)} collective-permute-done((bf16[256,1024]{1,0:T(8,128)(2,1)}, bf16[256,1024]{1,0:T(8,128)(2,1)S(1)}, u32[]{:S(2)}, u32[]{:S(2)}) %collective-permute-start.24) | collective-permute-done | bytes 524320 | tf_op jit(solution)/shard_map/ppermute | solution.py:20
  219.3 0.8 copy-done.25
  220.1 8.6 %collective-permute-done.25.refs_27_.refs_19_ = bf16[256,1024]{1,0:T(8,128)(2,1)S(1)} collective-permute-done((bf16[256,1024]{1,0:T(8,128)(2,1)S(1)}, bf16[256,1024]{1,0:T(8,128)(2,1)S(1)}, u32[]{:S(2)}, u32[]{:S(2)}) %collective-permute-start.25) | collective-permute-done | bytes 524320 | tf_op jit(solution)/shard_map/ppermute | solution.py:20
  228.7 0.8 copy-done.16
  229.5 12.9 %shard_map.82.refs_20_ = bf16[1024,1024]{1,0:T(8,128)(2,1)} custom-call(s32[2]{0:T(128)} %pad_add_fusion.place, bf16[256,1024]{1,0:T(8,128)(2,1)} %shard_map.79.refs_0_, bf16[256,1024]{1,0:T(8,128)(2,1)} %collective-permute-done.26.refs_1_, bf16[256,1024]{1,0:T(8,128)(2,1)} %collective-permute-done.27.refs_2_, bf16[256,1024]{1,0:T(8,128)(2,1)} %copy-done.23, ...), custom_call_target="tpu_custom_call" | custom-call | flops 6442450944 | bytes 16252928 | tf_op jit(solution)/shard_map/pallas_call | solution.py:404
  242.4 0.8 copy-done.17
  243.2 7.8 %shard_map.83 = bf16[1024,1024]{1,0:T(8,128)(2,1)} custom-call(s32[2]{0:T(128)} %pad_add_fusion.place, bf16[256,1024]{1,0:T(8,128)(2,1)} %shard_map.78.refs_0_, bf16[256,1024]{1,0:T(8,128)(2,1)} %copy-done.17, bf16[256,1024]{1,0:T(8,128)(2,1)} %copy-done.10, bf16[256,1024]{1,0:T(8,128)(2,1)} %collective-permute-done.11.refs_3_, ...), custom_call_target="tpu_custom_call", output_to_operand_aliasing={{}: (21, {})} | custom-call | flops 2147483648 | bytes 11010048 | tf_op jit(solution)/shard_map/pallas_call | solution.py:404
  (95 shorter events, 6.1 us)
Async XLA Ops:
  0.0 57.0 %collective-permute-start.2 = (bf16[1024,1024]{1,0:T(8,128)(2,1)}, bf16[1024,1024]{1,0:T(8,128)(2,1)}, u32[]{:S(2)}, u32[]{:S(2)}) collective-permute-start(bf16[1024,1024]{1,0:T(8,128)(2,1)} %refs_0_.1), channel_id=1, source_target_pairs={{0,1},{1,0},{2,3},{3,2},{4,5},{5,4},{6,7},{7,6},{8,9},{9,8},{10,11... | collective-permute-start | bytes 6291464 | tf_op jit(solution)/shard_map/ppermute | solution.py:20
  3.4 40.8 %copy-start.18 = (f32[1024]{0:T(1024)S(1)}, f32[1024]{0:T(1024)}, u32[]{:S(2)}) copy-start(f32[1024]{0:T(1024)} %param.11) | copy-start | bytes 12292
  3.5 40.8 %copy-start.19 = (f32[1024]{0:T(1024)S(1)}, f32[1024]{0:T(1024)}, u32[]{:S(2)}) copy-start(f32[1024]{0:T(1024)} %param.10) | copy-start | bytes 12292
  5.6 15.5 %collective-permute-start.7 = (bf16[256,1024]{1,0:T(8,128)(2,1)S(1)}, bf16[256,1024]{1,0:T(8,128)(2,1)}, u32[]{:S(2)}, u32[]{:S(2)}) collective-permute-start(bf16[256,1024]{1,0:T(8,128)(2,1)S(1)} %slice.21), channel_id=1, source_target_pairs={{0,2},{1,3},{2,0},{3,1},{4,6},{5,7},{6,4},{7,5},{8,10},{9,11},{10,... | collective-permute-start | bytes 1572872 | tf_op jit(solution)/shard_map/ppermute | solution.py:20
  8.3 24.1 %collective-permute-start.5 = (bf16[256,1024]{1,0:T(8,128)(2,1)S(1)}, bf16[256,1024]{1,0:T(8,128)(2,1)}, u32[]{:S(2)}, u32[]{:S(2)}) collective-permute-start(bf16[256,1024]{1,0:T(8,128)(2,1)S(1)} %slice.20), channel_id=1, source_target_pairs={{0,2},{1,3},{2,0},{3,1},{4,6},{5,7},{6,4},{7,5},{8,10},{9,11},{10,... | collective-permute-start | bytes 1572872 | tf_op jit(solution)/shard_map/ppermute | solution.py:20
  8.3 35.2 %collective-permute-start.3 = (bf16[256,1024]{1,0:T(8,128)(2,1)S(1)}, bf16[256,1024]{1,0:T(8,128)(2,1)S(1)}, u32[]{:S(2)}, u32[]{:S(2)}) collective-permute-start(bf16[256,1024]{1,0:T(8,128)(2,1)S(1)} %slice.19), channel_id=1, source_target_pairs={{0,2},{1,3},{2,0},{3,1},{4,6},{5,7},{6,4},{7,5},{8,10},{9,11},{10,... | collective-permute-start | bytes 1572872 | tf_op jit(solution)/shard_map/ppermute | solution.py:20
  10.3 44.3 %collective-permute-start = (bf16[256,1024]{1,0:T(8,128)(2,1)}, bf16[256,1024]{1,0:T(8,128)(2,1)}, u32[]{:S(2)}, u32[]{:S(2)}) collective-permute-start(bf16[256,1024]{1,0:T(8,128)(2,1)} %slice.18), channel_id=1, source_target_pairs={{0,2},{1,3},{2,0},{3,1},{4,6},{5,7},{6,4},{7,5},{8,10},{9,11},{10,... | collective-permute-start | bytes 1572872 | tf_op jit(solution)/shard_map/ppermute | solution.py:20
  10.5 74.1 %copy-start.1 = (bf16[256,1024]{1,0:T(8,128)(2,1)}, bf16[256,1024]{1,0:T(8,128)(2,1)S(1)}, u32[]{:S(2)}) copy-start(bf16[256,1024]{1,0:T(8,128)(2,1)S(1)} %get-tuple-element.49.refs_13_.refs_5_) | copy-start | bytes 1572868
  10.5 85.3 %copy-start.2 = (bf16[256,1024]{1,0:T(8,128)(2,1)}, bf16[256,1024]{1,0:T(8,128)(2,1)S(1)}, u32[]{:S(2)}) copy-start(bf16[256,1024]{1,0:T(8,128)(2,1)S(1)} %get-tuple-element.50.refs_12_.refs_4_) | copy-start | bytes 1572868
  21.2 33.4 %collective-permute-start.15 = (bf16[256,1024]{1,0:T(8,128)(2,1)S(1)}, bf16[256,1024]{1,0:T(8,128)(2,1)S(1)}, u32[]{:S(2)}, u32[]{:S(2)}) collective-permute-start(bf16[256,1024]{1,0:T(8,128)(2,1)S(1)} %get-tuple-element.49.refs_13_.refs_5_), channel_id=1, source_target_pairs={{0,8},{4,12},{8,16},{12,20},{16,24},{20,28},{24,0},{28,4},{1,9},{5... | collective-permute-start | bytes 1572872 | tf_op jit(solution)/shard_map/ppermute | solution.py:446
  32.4 22.7 %collective-permute-start.14 = (bf16[256,1024]{1,0:T(8,128)(2,1)S(1)}, bf16[256,1024]{1,0:T(8,128)(2,1)S(1)}, u32[]{:S(2)}, u32[]{:S(2)}) collective-permute-start(bf16[256,1024]{1,0:T(8,128)(2,1)S(1)} %get-tuple-element.50.refs_12_.refs_4_), channel_id=1, source_target_pairs={{0,8},{4,12},{8,16},{12,20},{16,24},{20,28},{24,0},{28,4},{1,9},{5... | collective-permute-start | bytes 1572872 | tf_op jit(solution)/shard_map/ppermute | solution.py:446
  43.5 31.5 %copy-start.12 = (bf16[256,1024]{1,0:T(8,128)(2,1)}, bf16[256,1024]{1,0:T(8,128)(2,1)S(1)}, u32[]{:S(2)}) copy-start(bf16[256,1024]{1,0:T(8,128)(2,1)S(1)} %collective-permute-done.3.refs_0_) | copy-start | bytes 1572868
  43.5 11.7 %collective-permute-start.6 = (bf16[256,1024]{1,0:T(8,128)(2,1)}, bf16[256,1024]{1,0:T(8,128)(2,1)}, u32[]{:S(2)}, u32[]{:S(2)}) collective-permute-start(bf16[256,1024]{1,0:T(8,128)(2,1)} %collective-permute-done.5.refs_0_), channel_id=1, source_target_pairs={{0,1},{1,0},{2,3},{3,2},{4,5},{5,4},{6,7},{7,6},{8,9},{9,8},{10,11... | collective-permute-start | bytes 1572872 | tf_op jit(solution)/shard_map/ppermute | solution.py:20
  54.6 41.1 %collective-permute-start.8 = (bf16[256,1024]{1,0:T(8,128)(2,1)}, bf16[256,1024]{1,0:T(8,128)(2,1)}, u32[]{:S(2)}, u32[]{:S(2)}) collective-permute-start(bf16[256,1024]{1,0:T(8,128)(2,1)} %collective-permute-done.7.refs_0_), channel_id=1, source_target_pairs={{0,1},{1,0},{2,3},{3,2},{4,5},{5,4},{6,7},{7,6},{8,9},{9,8},{10,11... | collective-permute-start | bytes 1572872 | tf_op jit(solution)/shard_map/ppermute | solution.py:20
  54.6 41.7 %copy-start.4 = (bf16[256,1024]{1,0:T(8,128)(2,1)}, bf16[256,1024]{1,0:T(8,128)(2,1)S(1)}, u32[]{:S(2)}) copy-start(bf16[256,1024]{1,0:T(8,128)(2,1)S(1)} %collective-permute-done.15.refs_17_.refs_9_) | copy-start | bytes 1572868
  54.6 30.0 %collective-permute-start.4 = (bf16[256,1024]{1,0:T(8,128)(2,1)S(1)}, bf16[256,1024]{1,0:T(8,128)(2,1)}, u32[]{:S(2)}, u32[]{:S(2)}) collective-permute-start(bf16[256,1024]{1,0:T(8,128)(2,1)S(1)} %collective-permute-done.3.refs_0_), channel_id=1, source_target_pairs={{0,1},{1,0},{2,3},{3,2},{4,5},{5,4},{6,7},{7,6},{8,9},{9,8},{10,11... | collective-permute-start | bytes 1572872 | tf_op jit(solution)/shard_map/ppermute | solution.py:20
  55.1 42.7 %copy-start.5 = (bf16[256,1024]{1,0:T(8,128)(2,1)}, bf16[256,1024]{1,0:T(8,128)(2,1)S(1)}, u32[]{:S(2)}) copy-start(bf16[256,1024]{1,0:T(8,128)(2,1)S(1)} %collective-permute-done.14.refs_16_.refs_8_) | copy-start | bytes 1572868
  55.1 41.2 %collective-permute-start.1 = (bf16[256,1024]{1,0:T(8,128)(2,1)}, bf16[256,1024]{1,0:T(8,128)(2,1)}, u32[]{:S(2)}, u32[]{:S(2)}) collective-permute-start(bf16[256,1024]{1,0:T(8,128)(2,1)} %collective-permute-done.refs_0_), channel_id=1, source_target_pairs={{0,1},{1,0},{2,3},{3,2},{4,5},{5,4},{6,7},{7,6},{8,9},{9,8},{10,11... | collective-permute-start | bytes 1572872 | tf_op jit(solution)/shard_map/ppermute | solution.py:20
  55.2 42.7 %collective-permute-start.19 = (bf16[256,1024]{1,0:T(8,128)(2,1)S(1)}, bf16[256,1024]{1,0:T(8,128)(2,1)S(1)}, u32[]{:S(2)}, u32[]{:S(2)}) collective-permute-start(bf16[256,1024]{1,0:T(8,128)(2,1)S(1)} %collective-permute-done.15.refs_17_.refs_9_), channel_id=1, source_target_pairs={{0,8},{4,12},{8,16},{12,20},{16,24},{20,28},{24,0},{28,4},{1,9},{5... | collective-permute-start | bytes 1572872 | tf_op jit(solution)/shard_map/ppermute | solution.py:446
  57.0 41.4 %collective-permute-start.18 = (bf16[256,1024]{1,0:T(8,128)(2,1)S(1)}, bf16[256,1024]{1,0:T(8,128)(2,1)S(1)}, u32[]{:S(2)}, u32[]{:S(2)}) collective-permute-start(bf16[256,1024]{1,0:T(8,128)(2,1)S(1)} %collective-permute-done.14.refs_16_.refs_8_), channel_id=1, source_target_pairs={{0,8},{4,12},{8,16},{12,20},{16,24},{20,28},{24,0},{28,4},{1,9},{5... | collective-permute-start | bytes 1572872 | tf_op jit(solution)/shard_map/ppermute | solution.py:446
  84.6 79.0 %collective-permute-start.13 = (bf16[256,1024]{1,0:T(8,128)(2,1)S(1)}, bf16[256,1024]{1,0:T(8,128)(2,1)S(1)}, u32[]{:S(2)}, u32[]{:S(2)}) collective-permute-start(bf16[256,1024]{1,0:T(8,128)(2,1)S(1)} %get-tuple-element.49.refs_13_.refs_5_), channel_id=1, source_target_pairs={{0,4},{4,0},{8,12},{12,8},{16,20},{20,16},{24,28},{28,24},{1,5},{5... | collective-permute-start | bytes 1572872 | tf_op jit(solution)/shard_map/ppermute | solution.py:20
  95.8 68.3 %collective-permute-start.12 = (bf16[256,1024]{1,0:T(8,128)(2,1)S(1)}, bf16[256,1024]{1,0:T(8,128)(2,1)}, u32[]{:S(2)}, u32[]{:S(2)}) collective-permute-start(bf16[256,1024]{1,0:T(8,128)(2,1)S(1)} %get-tuple-element.50.refs_12_.refs_4_), channel_id=1, source_target_pairs={{0,4},{4,0},{8,12},{12,8},{16,20},{20,16},{24,28},{28,24},{1,5},{5... | collective-permute-start | bytes 1572872 | tf_op jit(solution)/shard_map/ppermute | solution.py:20
  96.3 69.2 %collective-permute-start.17 = (bf16[256,1024]{1,0:T(8,128)(2,1)S(1)}, bf16[256,1024]{1,0:T(8,128)(2,1)}, u32[]{:S(2)}, u32[]{:S(2)}) collective-permute-start(bf16[256,1024]{1,0:T(8,128)(2,1)S(1)} %collective-permute-done.15.refs_17_.refs_9_), channel_id=1, source_target_pairs={{0,4},{4,0},{8,12},{12,8},{16,20},{20,16},{24,28},{28,24},{1,5},{5... | collective-permute-start | bytes 1572872 | tf_op jit(solution)/shard_map/ppermute | solution.py:20
  97.9 94.0 %copy-start.6 = (bf16[256,1024]{1,0:T(8,128)(2,1)}, bf16[256,1024]{1,0:T(8,128)(2,1)S(1)}, u32[]{:S(2)}) copy-start(bf16[256,1024]{1,0:T(8,128)(2,1)S(1)} %collective-permute-done.19.refs_21_.refs_13_) | copy-start | bytes 1572868
  97.9 68.2 %collective-permute-start.16 = (bf16[256,1024]{1,0:T(8,128)(2,1)S(1)}, bf16[256,1024]{1,0:T(8,128)(2,1)}, u32[]{:S(2)}, u32[]{:S(2)}) collective-permute-start(bf16[256,1024]{1,0:T(8,128)(2,1)S(1)} %collective-permute-done.14.refs_16_.refs_8_), channel_id=1, source_target_pairs={{0,4},{4,0},{8,12},{12,8},{16,20},{20,16},{24,28},{28,24},{1,5},{5... | collective-permute-start | bytes 1572872 | tf_op jit(solution)/shard_map/ppermute | solution.py:20
  98.4 65.1 %copy-start.7 = (bf16[256,1024]{1,0:T(8,128)(2,1)}, bf16[256,1024]{1,0:T(8,128)(2,1)S(1)}, u32[]{:S(2)}) copy-start(bf16[256,1024]{1,0:T(8,128)(2,1)S(1)} %collective-permute-done.18.refs_20_.refs_12_) | copy-start | bytes 1572868
  98.4 67.6 %collective-permute-start.22 = (bf16[256,1024]{1,0:T(8,128)(2,1)S(1)}, bf16[256,1024]{1,0:T(8,128)(2,1)}, u32[]{:S(2)}, u32[]{:S(2)}) collective-permute-start(bf16[256,1024]{1,0:T(8,128)(2,1)S(1)} %collective-permute-done.18.refs_20_.refs_12_), channel_id=1, source_target_pairs={{0,8},{4,12},{8,16},{12,20},{16,24},{20,28},{24,0},{28,4},{1,9},{5... | collective-permute-start | bytes 1572872 | tf_op jit(solution)/shard_map/ppermute | solution.py:446
  163.5 11.5 %collective-permute-start.20 = (bf16[256,1024]{1,0:T(8,128)(2,1)S(1)}, bf16[256,1024]{1,0:T(8,128)(2,1)S(1)}, u32[]{:S(2)}, u32[]{:S(2)}) collective-permute-start(bf16[256,1024]{1,0:T(8,128)(2,1)S(1)} %collective-permute-done.18.refs_20_.refs_12_), channel_id=1, source_target_pairs={{0,4},{4,0},{8,12},{12,8},{16,20},{20,16},{24,28},{28,24},{1,5},{5... | collective-permute-start | bytes 1572872 | tf_op jit(solution)/shard_map/ppermute | solution.py:20
  164.0 17.3 %collective-permute-start.10 = (bf16[256,1024]{1,0:T(8,128)(2,1)}, bf16[256,1024]{1,0:T(8,128)(2,1)S(1)}, u32[]{:S(2)}, u32[]{:S(2)}) collective-permute-start(bf16[256,1024]{1,0:T(8,128)(2,1)} %shard_map.78.refs_0_), channel_id=1, source_target_pairs={{0,2},{1,3},{2,0},{3,1},{4,6},{5,7},{6,4},{7,5},{8,10},{9,11},{10,... | collective-permute-start | bytes 1572872 | tf_op jit(solution)/shard_map/ppermute | solution.py:20
  165.5 24.9 %collective-permute-start.27 = (bf16[256,1024]{1,0:T(8,128)(2,1)}, bf16[256,1024]{1,0:T(8,128)(2,1)}, u32[]{:S(2)}, u32[]{:S(2)}) collective-permute-start(bf16[256,1024]{1,0:T(8,128)(2,1)} %shard_map.79.refs_0_), channel_id=1, source_target_pairs={{0,2},{1,3},{2,0},{3,1},{4,6},{5,7},{6,4},{7,5},{8,10},{9,11},{10,... | collective-permute-start | bytes 1572872 | tf_op jit(solution)/shard_map/ppermute | solution.py:20
  166.0 25.8 %collective-permute-start.26 = (bf16[256,1024]{1,0:T(8,128)(2,1)}, bf16[256,1024]{1,0:T(8,128)(2,1)}, u32[]{:S(2)}, u32[]{:S(2)}) collective-permute-start(bf16[256,1024]{1,0:T(8,128)(2,1)} %shard_map.79.refs_0_), channel_id=1, source_target_pairs={{0,1},{1,0},{2,3},{3,2},{4,5},{5,4},{6,7},{7,6},{8,9},{9,8},{10,11... | collective-permute-start | bytes 1572872 | tf_op jit(solution)/shard_map/ppermute | solution.py:20
  166.0 25.8 %collective-permute-start.23 = (bf16[256,1024]{1,0:T(8,128)(2,1)S(1)}, bf16[256,1024]{1,0:T(8,128)(2,1)S(1)}, u32[]{:S(2)}, u32[]{:S(2)}) collective-permute-start(bf16[256,1024]{1,0:T(8,128)(2,1)S(1)} %collective-permute-done.19.refs_21_.refs_13_), channel_id=1, source_target_pairs={{0,8},{4,12},{8,16},{12,20},{16,24},{20,28},{24,0},{28,4},{1,9},{5... | collective-permute-start | bytes 1572872 | tf_op jit(solution)/shard_map/ppermute | solution.py:446
  171.7 46.3 %copy-start = (bf16[256,1024]{1,0:T(8,128)(2,1)S(1)}, bf16[256,1024]{1,0:T(8,128)(2,1)}, u32[]{:S(2)}) copy-start(bf16[256,1024]{1,0:T(8,128)(2,1)} %shard_map.78.refs_0_) | copy-start | bytes 1572868
  175.0 26.6 %collective-permute-start.30 = (bf16[256,1024]{1,0:T(8,128)(2,1)}, bf16[256,1024]{1,0:T(8,128)(2,1)}, u32[]{:S(2)}, u32[]{:S(2)}) collective-permute-start(bf16[256,1024]{1,0:T(8,128)(2,1)} %shard_map.80.refs_4_), channel_id=1, source_target_pairs={{0,2},{1,3},{2,0},{3,1},{4,6},{5,7},{6,4},{7,5},{8,10},{9,11},{10,... | collective-permute-start | bytes 1572872 | tf_op jit(solution)/shard_map/ppermute | solution.py:20
  181.3 61.1 %copy-start.10 = (bf16[256,1024]{1,0:T(8,128)(2,1)}, bf16[256,1024]{1,0:T(8,128)(2,1)S(1)}, u32[]{:S(2)}) copy-start(bf16[256,1024]{1,0:T(8,128)(2,1)S(1)} %collective-permute-done.10.refs_2_) | copy-start | bytes 1572868
  181.3 21.9 %collective-permute-start.29 = (bf16[256,1024]{1,0:T(8,128)(2,1)S(1)}, bf16[256,1024]{1,0:T(8,128)(2,1)S(1)}, u32[]{:S(2)}, u32[]{:S(2)}) collective-permute-start(bf16[256,1024]{1,0:T(8,128)(2,1)S(1)} %copy-done.13), channel_id=1, source_target_pairs={{0,1},{1,0},{2,3},{3,2},{4,5},{5,4},{6,7},{7,6},{8,9},{9,8},{10,11... | collective-permute-start | bytes 1572872 | tf_op jit(solution)/shard_map/ppermute | solution.py:20
  190.4 18.7 %collective-permute-start.33 = (bf16[256,1024]{1,0:T(8,128)(2,1)}, bf16[256,1024]{1,0:T(8,128)(2,1)S(1)}, u32[]{:S(2)}, u32[]{:S(2)}) collective-permute-start(bf16[256,1024]{1,0:T(8,128)(2,1)} %shard_map.81.refs_8_), channel_id=1, source_target_pairs={{0,2},{1,3},{2,0},{3,1},{4,6},{5,7},{6,4},{7,5},{8,10},{9,11},{10,... | collective-permute-start | bytes 1572872 | tf_op jit(solution)/shard_map/ppermute | solution.py:20
  191.8 17.2 %collective-permute-start.32 = (bf16[256,1024]{1,0:T(8,128)(2,1)}, bf16[256,1024]{1,0:T(8,128)(2,1)S(1)}, u32[]{:S(2)}, u32[]{:S(2)}) collective-permute-start(bf16[256,1024]{1,0:T(8,128)(2,1)} %shard_map.81.refs_8_), channel_id=1, source_target_pairs={{0,1},{1,0},{2,3},{3,2},{4,5},{5,4},{6,7},{7,6},{8,9},{9,8},{10,11... | collective-permute-start | bytes 1572872 | tf_op jit(solution)/shard_map/ppermute | solution.py:20
  191.9 36.9 %copy-start.11 = (bf16[256,1024]{1,0:T(8,128)(2,1)}, bf16[256,1024]{1,0:T(8,128)(2,1)S(1)}, u32[]{:S(2)}) copy-start(bf16[256,1024]{1,0:T(8,128)(2,1)S(1)} %collective-permute-done.23.refs_25_.refs_17_) | copy-start | bytes 1572868
  191.9 17.7 %collective-permute-start.21 = (bf16[256,1024]{1,0:T(8,128)(2,1)S(1)}, bf16[256,1024]{1,0:T(8,128)(2,1)S(1)}, u32[]{:S(2)}, u32[]{:S(2)}) collective-permute-start(bf16[256,1024]{1,0:T(8,128)(2,1)S(1)} %collective-permute-done.19.refs_21_.refs_13_), channel_id=1, source_target_pairs={{0,4},{4,0},{8,12},{12,8},{16,20},{20,16},{24,28},{28,24},{1,5},{5... | collective-permute-start | bytes 1572872 | tf_op jit(solution)/shard_map/ppermute | solution.py:20
  201.6 16.4 %collective-permute-start.24 = (bf16[256,1024]{1,0:T(8,128)(2,1)}, bf16[256,1024]{1,0:T(8,128)(2,1)S(1)}, u32[]{:S(2)}, u32[]{:S(2)}) collective-permute-start(bf16[256,1024]{1,0:T(8,128)(2,1)} %collective-permute-done.22.refs_24_.refs_16_), channel_id=1, source_target_pairs={{0,4},{4,0},{8,12},{12,8},{16,20},{20,16},{24,28},{28,24},{1,5},{5... | collective-permute-start | bytes 1572872 | tf_op jit(solution)/shard_map/ppermute | solution.py:20
  203.2 14.8 %collective-permute-start.28 = (bf16[256,1024]{1,0:T(8,128)(2,1)}, bf16[256,1024]{1,0:T(8,128)(2,1)S(1)}, u32[]{:S(2)}, u32[]{:S(2)}) collective-permute-start(bf16[256,1024]{1,0:T(8,128)(2,1)} %collective-permute-done.27.refs_2_), channel_id=1, source_target_pairs={{0,1},{1,0},{2,3},{3,2},{4,5},{5,4},{6,7},{7,6},{8,9},{9,8},{10,11... | collective-permute-start | bytes 1572872 | tf_op jit(solution)/shard_map/ppermute | solution.py:20
  209.0 9.4 %collective-permute-start.31 = (bf16[256,1024]{1,0:T(8,128)(2,1)}, bf16[256,1024]{1,0:T(8,128)(2,1)S(1)}, u32[]{:S(2)}, u32[]{:S(2)}) collective-permute-start(bf16[256,1024]{1,0:T(8,128)(2,1)} %collective-permute-done.30.refs_6_), channel_id=1, source_target_pairs={{0,1},{1,0},{2,3},{3,2},{4,5},{5,4},{6,7},{7,6},{8,9},{9,8},{10,11... | collective-permute-start | bytes 1572872 | tf_op jit(solution)/shard_map/ppermute | solution.py:20
  209.1 9.4 %collective-permute-start.34 = (bf16[256,1024]{1,0:T(8,128)(2,1)S(1)}, bf16[256,1024]{1,0:T(8,128)(2,1)S(1)}, u32[]{:S(2)}, u32[]{:S(2)}) collective-permute-start(bf16[256,1024]{1,0:T(8,128)(2,1)S(1)} %collective-permute-done.33.refs_10_), channel_id=1, source_target_pairs={{0,1},{1,0},{2,3},{3,2},{4,5},{5,4},{6,7},{7,6},{8,9},{9,8},{10,11... | collective-permute-start | bytes 1572872 | tf_op jit(solution)/shard_map/ppermute | solution.py:20
  209.6 19.2 %copy-start.14 = (bf16[256,1024]{1,0:T(8,128)(2,1)}, bf16[256,1024]{1,0:T(8,128)(2,1)S(1)}, u32[]{:S(2)}) copy-start(bf16[256,1024]{1,0:T(8,128)(2,1)S(1)} %collective-permute-done.21.refs_23_.refs_15_) | copy-start | bytes 1572868
  209.6 19.2 %collective-permute-start.25 = (bf16[256,1024]{1,0:T(8,128)(2,1)S(1)}, bf16[256,1024]{1,0:T(8,128)(2,1)S(1)}, u32[]{:S(2)}, u32[]{:S(2)}) collective-permute-start(bf16[256,1024]{1,0:T(8,128)(2,1)S(1)} %collective-permute-done.23.refs_25_.refs_17_), channel_id=1, source_target_pairs={{0,4},{4,0},{8,12},{12,8},{16,20},{20,16},{24,28},{28,24},{1,5},{5... | collective-permute-start | bytes 1572872 | tf_op jit(solution)/shard_map/ppermute | solution.py:20
  218.0 24.4 %collective-permute-start.9 = (bf16[256,1024]{1,0:T(8,128)(2,1)S(1)}, bf16[256,1024]{1,0:T(8,128)(2,1)S(1)}, u32[]{:S(2)}, u32[]{:S(2)}) collective-permute-start(bf16[256,1024]{1,0:T(8,128)(2,1)S(1)} %copy-done), channel_id=1, source_target_pairs={{0,1},{1,0},{2,3},{3,2},{4,5},{5,4},{6,7},{7,6},{8,9},{9,8},{10,11... | collective-permute-start | bytes 1572872 | tf_op jit(solution)/shard_map/ppermute | solution.py:20
  218.0 24.4 %collective-permute-start.11 = (bf16[256,1024]{1,0:T(8,128)(2,1)S(1)}, bf16[256,1024]{1,0:T(8,128)(2,1)}, u32[]{:S(2)}, u32[]{:S(2)}) collective-permute-start(bf16[256,1024]{1,0:T(8,128)(2,1)S(1)} %collective-permute-done.10.refs_2_), channel_id=1, source_target_pairs={{0,1},{1,0},{2,3},{3,2},{4,5},{5,4},{6,7},{7,6},{8,9},{9,8},{10,11... | collective-permute-start | bytes 1572872 | tf_op jit(solution)/shard_map/ppermute | solution.py:20
  (13 other events, 78.7 us)
where the time goes:
time: 252 us; the launch traced here: 251 us
  Pallas kernels  104 us (41%)
  waiting for transfers between devices  80 us (32%)
  starting transfers between devices  31.6 us (13%)
  blocking collectives  25.3 us (10%)
  local copies, waits for them, and re-layouts  8.44 us (3%)
    ppermute x29, waiting for transfers between devices, swap(): lax.ppermute(block, axis, [(i, i ^ bits) for i in range(lax.axis_size(axi...  80 us
    pallas_call x4, Pallas kernels, gate_chunk(): pl.pallas_call(functools.partial(gate_kernel, half, chunk, len(earlier),...  38.2 us
    ppermute x29, starting transfers between devices, swap(): lax.ppermute(block, axis, [(i, i ^ bits) for i in range(lax.axis_size(axi...  21.6 us
    pallas_call x2, Pallas kernels, mix_rows(): pl.pallas_call(functools.partial(mix_kernel, groups, group, pieces, peers...  20.7 us
    pallas_call x4, Pallas kernels, state_chunk(): pl.pallas_call(functools.partial(state_kernel, chunk, peers), out_shape=j...  19.1 us
    pallas_call x1, Pallas kernels, near_product(): pl.pallas_call(functools.partial(near_kernel, half), out_shape=jax.ShapeD...  16.4 us
    all_to_all x1, blocking collectives, layer(): peer_maps = lax.all_to_all(out[2], 'ctx', 0, 0, tiled=True)  13.8 us
    all_to_all x1, blocking collectives, layer(): peer_maps = lax.all_to_all(totals, 'ctx', 0, 0, tiled=True)  11.5 us
  transfers between devices with their start and end apart: 35, of which 10 were waited for; matrix products, arithmetic and copies ran while one was open for 3% of the time, Pallas kernels for 38%

commit v1 on v0

--- a/solution.py
+++ b/solution.py
@@ -13,7 +13,7 @@
 LANES = 128
 F32 = jnp.float32
 BF16 = jnp.bfloat16
-VMEM_LIMIT = 60 * 1024 * 1024
+MIB = 1024 * 1024
 
 
 def swap(block, axis, bits):
@@ -24,8 +24,8 @@
     return math.gcd(width, most)
 
 
-def params(limit=VMEM_LIMIT):
-    return pltpu.CompilerParams(vmem_limit_bytes=limit)
+def params(mib):
+    return pltpu.CompilerParams(vmem_limit_bytes=mib * MIB)
 
 
 def cost(flops, nbytes, trans=0):
@@ -36,21 +36,13 @@
     blocks = refs[:half]
     w_ref, out_ref = refs[half:]
     depth = blocks[0].shape[1]
-    rows = out_ref.shape[1]
-    step = tile_of(rows, 256)
     slot = lax.rem(place[0], half)
-
-    def body(m, carry):
-        lines = pl.ds(pl.multiple_of(m * step, step), step)
-        total = None
-        for d in range(half):
-            deep = pl.ds(pl.multiple_of((slot ^ d) * depth, depth), depth)
-            part = jnp.dot(blocks[d][lines, :], w_ref[0, deep, :], preferred_element_type=F32)
-            total = part if total is None else total + part
-        out_ref[0, lines, :] = total
-        return carry
-
-    lax.fori_loop(0, rows // step, body, 0)
+    total = None
+    for d in range(half):
+        deep = pl.ds(pl.multiple_of((slot ^ d) * depth, depth), depth)
+        part = jnp.dot(blocks[d][...], w_ref[0, deep, :], preferred_element_type=F32)
+        total = part if total is None else total + part
+    out_ref[0] = total
 
 
 def near_product(place, blocks, weights):
@@ -69,7 +61,7 @@
             + [pl.BlockSpec((1, half * depth, tn), lambda g, n, p: (g, p[0] // half, n))],
             out_specs=pl.BlockSpec((1, rows, tn), lambda g, n, p: (g, 0, n)),
         ),
-        compiler_params=params(),
+        compiler_params=params(24),
         cost_estimate=cost(
             2 * gates * rows * half * depth * width,
             gates * width * (half * depth * 2 + rows * 4) + half * rows * depth * 2,
@@ -86,72 +78,126 @@
     return a, b
 
 
-def spread_rows(flat, g, j, seg):
-    parts = [flat[g, l, pl.ds(j, SEGS, stride=seg), :] for l in range(flat.shape[1])]
+def spread_rows(flat, g, lane, tiles, j, seg):
+    parts = [flat[g, lane + l, pl.ds(j, SEGS, stride=seg), :] for l in range(tiles)]
     return jnp.concatenate(parts, axis=1)
 
 
-def gate_kernel(half, chunk, before, last, place, *refs):
+def first_slopes(pre, cand, gain):
+    update = jax.nn.sigmoid(pre)
+    keep = 1.0 - update
+    scaled = update * gain
+    squashed = jnp.tanh(cand)
+    slope = keep + (scaled - scaled * squashed * squashed)
+    return update, keep, scaled, slope, update * squashed
+
+
+def lead_row(place, start, shape):
+    lead = lax.broadcasted_iota(jnp.int32, shape, 0) == 0
+    return jnp.where(lead & (place[1] == 0), start, 0.0)
+
+
+def around(update, keep, scaled, cand, gain, prev):
+    squashed = jnp.tanh(cand + gain * prev)
+    bend = scaled - scaled * squashed * squashed
+    return keep + bend, update * squashed - bend * prev
+
+
+def gate_kernel(half, chunk, rows, before, last, place, *refs):
     blocks = refs[:half]
     part_ref, w_ref, bias_ref, gain_ref, start_ref = refs[half : half + 5]
     earlier = refs[half + 5 : half + 5 + before]
-    outs = refs[half + 5 + before :]
-    gates_ref, maps_ref = outs[:2]
-    flat = outs[-1]
+    rest = refs[half + 5 + before :]
+    if last:
+        gates_ref, maps_ref, total_ref = rest[:3]
+    else:
+        gates_ref, maps_ref = rest[:2]
+    lhs, wbuf, pbuf, acc, flat, lsem, wsem, psem = rest[-8:]
     depth = blocks[0].shape[1]
-    rows = part_ref.shape[1]
+    width = gain_ref.shape[1]
     seg = rows // SEGS
-    width = part_ref.shape[2]
+    steps, lines_of = wbuf.shape[0], wbuf.shape[2]
     slot = lax.rem(place[0], half)
+    base = ((place[0] // half) ^ 1) * (half * depth)
+
+    def w_copy(k):
+        lines = pl.ds(pl.multiple_of(base + k * lines_of, lines_of), lines_of)
+        return pltpu.make_async_copy(w_ref.at[:, lines, :], wbuf.at[k], wsem.at[k])
+
+    def l_copy(d):
+        deep = pl.ds(pl.multiple_of((slot ^ d) * depth, depth), depth)
+        return pltpu.make_async_copy(blocks[d], lhs.at[:, deep], lsem.at[d])
+
+    p_copy = pltpu.make_async_copy(part_ref.at[:, chunk * rows : (chunk + 1) * rows, :], pbuf, psem)
+    for d in range(half):
+        l_copy(d).start()
+    for k in range(steps):
+        w_copy(k).start()
+    p_copy.start()
+    for d in range(half):
+        l_copy(d).wait()
+
+    def product(k, g):
+        deep = pl.ds(pl.multiple_of(k * lines_of, lines_of), lines_of)
+        return jnp.dot(lhs[:, deep], wbuf[k, g], preferred_element_type=F32)
+
+    w_copy(0).wait()
     for g in range(2):
-        total = part_ref[g]
-        for d in range(half):
-            deep = pl.ds(pl.multiple_of((slot ^ d) * depth, depth), depth)
-            total = total + jnp.dot(blocks[d][...], w_ref[g, deep, :], preferred_element_type=F32)
-        total = (total + bias_ref[g : g + 1, :]).astype(BF16).astype(F32)
+        acc[g] = product(0, g)
+
+    def more(k, carry):
+        w_copy(k).wait()
+        for g in range(2):
+            acc[g] += product(k, g)
+        return carry
+
+    lax.fori_loop(1, steps, more, 0)
+    p_copy.wait()
+    for g in range(2):
         for l in range(width // LANES):
-            flat[g, l] = total[:, l * LANES : (l + 1) * LANES]
-    gain = jnp.broadcast_to(gain_ref[...], (SEGS, width))
-
-    def pair(jj, carry, first):
-        a, b = carry
-        held = ([], [])
-        for k in range(2):
-            j = 2 * jj + k
-            pre = spread_rows(flat, 0, j, seg)
-            cand = spread_rows(flat, 1, j, seg)
-            held[0].append(pre)
-            held[1].append(cand)
-            update = jax.nn.sigmoid(pre)
-            if first and k == 0:
-                lead = lax.broadcasted_iota(jnp.int32, (SEGS, width), 0) == 0
-                prev = jnp.where(lead & (place[1] == 0), start_ref[...], 0.0)
-                squashed = jnp.tanh(cand + gain * prev)
-                bend = gain * (1.0 - squashed * squashed)
-                offset = update * (squashed - bend * prev)
-            else:
-                squashed = jnp.tanh(cand)
-                bend = gain * (1.0 - squashed * squashed)
-                offset = update * squashed
-            slope = (1.0 - update) + update * bend
-            b = slope * b + offset
-            a = slope * a
-        lines = pl.ds(pl.multiple_of(jj * 2 * SEGS, 2 * SEGS), 2 * SEGS)
-        for g in range(2):
-            gates_ref[g, lines, :] = jnp.concatenate(held[g], axis=0).astype(BF16)
-        return a, b
-
-    carry = (jnp.ones((SEGS, width), F32), jnp.zeros((SEGS, width), F32))
-    if chunk == 0:
-        carry = pair(0, carry, True)
-        begin = 1
-    else:
+            lanes = slice(l * LANES, (l + 1) * LANES)
+            total = acc[g, :, lanes] + pbuf[g, :, lanes] + bias_ref[g : g + 1, lanes]
+            flat[g, l] = total.astype(BF16).astype(F32)
+
+    tiles = tile_of(width // LANES, 2)
+    span = tiles * LANES
+
+    def columns(n, carry_out):
+        wide = pl.ds(pl.multiple_of(n * span, span), span)
+        gain = jnp.broadcast_to(gain_ref[:, wide], (SEGS, span))
+
+        def pair(jj, carry, first):
+            a, b = carry
+            held = ([], [])
+            for k in range(2):
+                j = 2 * jj + k
+                pre = spread_rows(flat, 0, n * tiles, tiles, j, seg)
+                cand = spread_rows(flat, 1, n * tiles, tiles, j, seg)
+                held[0].append(pre)
+                held[1].append(cand)
+                update, keep, scaled, slope, offset = first_slopes(pre, cand, gain)
+                if first and k == 0:
+                    prev = lead_row(place, start_ref[:, wide], (SEGS, span))
+                    slope, offset = around(update, keep, scaled, cand, gain, prev)
+                b = slope * b + offset
+                a = slope * a
+            lines = pl.ds(pl.multiple_of(jj * 2 * SEGS, 2 * SEGS), 2 * SEGS)
+            for g in range(2):
+                gates_ref[g, lines, wide] = jnp.concatenate(held[g], axis=0).astype(BF16)
+            return a, b
+
+        carry = (jnp.ones((SEGS, span), F32), jnp.zeros((SEGS, span), F32))
         begin = 0
-    a, b = lax.fori_loop(begin, seg // 2, lambda jj, c: pair(jj, c, False), carry)
-    maps_ref[0] = a
-    maps_ref[1] = b
+        if chunk == 0:
+            carry = pair(0, carry, True)
+            begin = 1
+        a, b = lax.fori_loop(begin, seg // 2, lambda jj, c: pair(jj, c, False), carry)
+        maps_ref[0, :, wide] = a
+        maps_ref[1, :, wide] = b
+        return carry_out
+
+    lax.fori_loop(0, width // span, columns, 0)
     if last:
-        total_ref = outs[2]
         ta, tb = jnp.ones((1, width), F32), jnp.zeros((1, width), F32)
         for maps in list(earlier) + [maps_ref]:
             ta, tb = compose_rows(maps, SEGS, ta, tb)
@@ -164,36 +210,34 @@
     half = len(blocks)
     rows, depth = blocks[0].shape
     gates, _, width = weights.shape
-    tn = tile_of(width, 256)
-    row_spec = pl.BlockSpec((1, tn), lambda n, p: (0, n))
-    map_spec = pl.BlockSpec((2, SEGS, tn), lambda n, p: (0, 0, n))
+    lines_of = tile_of(half * depth, 512)
+    steps = half * depth // lines_of
+    anywhere = pl.BlockSpec(memory_space=pl.ANY)
+    vmem = pl.BlockSpec(memory_space=pltpu.VMEM)
     out_shape = [
         jax.ShapeDtypeStruct((2, rows, width), BF16),
         jax.ShapeDtypeStruct((2, SEGS, width), F32),
     ]
-    out_specs = [pl.BlockSpec((2, rows, tn), lambda n, p: (0, 0, n)), map_spec]
     if last:
         out_shape.append(jax.ShapeDtypeStruct((peers, 2, width), F32))
-        out_specs.append(pl.BlockSpec((peers, 2, tn), lambda n, p: (0, 0, n)))
     return pl.pallas_call(
-        functools.partial(gate_kernel, half, chunk, len(earlier), last),
+        functools.partial(gate_kernel, half, chunk, rows, len(earlier), last),
         out_shape=out_shape,
-        grid_spec=pltpu.PrefetchScalarGridSpec(
-            num_scalar_prefetch=1,
-            grid=(width // tn,),
-            in_specs=[pl.BlockSpec((rows, depth), lambda n, p: (0, 0))] * half
-            + [
-                pl.BlockSpec((2, rows, tn), lambda n, p: (0, chunk, n)),
-                pl.BlockSpec((2, half * depth, tn), lambda n, p: (0, (p[0] // half) ^ 1, n)),
-                pl.BlockSpec((2, tn), lambda n, p: (0, n)),
-                row_spec,
-                row_spec,
-            ]
-            + [map_spec] * len(earlier),
-            out_specs=out_specs,
-            scratch_shapes=[pltpu.VMEM((2, tn // LANES, rows, LANES), F32)],
-        ),
-        compiler_params=params(),
+        in_specs=[pl.BlockSpec(memory_space=pltpu.SMEM)]
+        + [anywhere] * (half + 2)
+        + [vmem] * (3 + len(earlier)),
+        out_specs=[vmem] * len(out_shape),
+        scratch_shapes=[
+            pltpu.VMEM((rows, half * depth), BF16),
+            pltpu.VMEM((steps, gates, lines_of, width), BF16),
+            pltpu.VMEM((gates, rows, width), F32),
+            pltpu.VMEM((gates, rows, width), F32),
+            pltpu.VMEM((gates, width // LANES, rows, LANES), F32),
+            pltpu.SemaphoreType.DMA((half,)),
+            pltpu.SemaphoreType.DMA((steps,)),
+            pltpu.SemaphoreType.DMA,
+        ],
+        compiler_params=params(24),
         cost_estimate=cost(
             2 * gates * rows * half * depth * width,
             gates * width * (half * depth * 2 + rows * 6) + half * rows * depth * 2,
@@ -221,11 +265,17 @@
     gates = refs[:chunks]
     maps = refs[chunks : 2 * chunks]
     peer_ref, gain_ref, start_ref, run_ref, maps_ref, total_ref, enter = refs[2 * chunks :]
-    rows, width = gates[0].shape[1:]
+    rows, span = gates[0].shape[1:]
+    width = gain_ref.shape[1]
     seg = rows // SEGS
-    start = start_ref[...]
-    enter_segments(maps, entering_state(place, peer_ref, start, peers), enter)
-    gain = jnp.broadcast_to(gain_ref[...], (SEGS, width))
+    n = pl.program_id(0)
+
+    @pl.when(n == 0)
+    def _():
+        enter_segments(maps, entering_state(place, peer_ref, start_ref[...], peers), enter)
+
+    wide = pl.ds(pl.multiple_of(n * span, span), span)
+    gain = jnp.broadcast_to(gain_ref[:, wide], (SEGS, span))
 
     def pair(jj, carry, first):
         lines = pl.ds(pl.multiple_of(jj * 2 * SEGS, 2 * SEGS), 2 * SEGS)
@@ -237,23 +287,11 @@
             for k in range(2):
                 pre = pre2[k * SEGS : (k + 1) * SEGS]
                 cand = cand2[k * SEGS : (k + 1) * SEGS]
-                update = jax.nn.sigmoid(pre)
-                keep = 1.0 - update
+                update, keep, scaled, slope, offset = first_slopes(pre, cand, gain)
                 if first and k == 0 and c == 0:
-                    lead = lax.broadcasted_iota(jnp.int32, (SEGS, width), 0) == 0
-                    prev = jnp.where(lead & (place[1] == 0), start, 0.0)
-                    squashed = jnp.tanh(cand + gain * prev)
-                    bend = gain * (1.0 - squashed * squashed)
-                    offset = update * (squashed - bend * prev)
-                else:
-                    squashed = jnp.tanh(cand)
-                    bend = gain * (1.0 - squashed * squashed)
-                    offset = update * squashed
-                slope = keep + update * bend
-                squashed = jnp.tanh(cand + gain * state)
-                bend = gain * (1.0 - squashed * squashed)
-                slope2 = keep + update * bend
-                offset2 = update * (squashed - bend * state)
+                    prev = lead_row(place, start_ref[:, wide], (SEGS, span))
+                    slope, offset = around(update, keep, scaled, cand, gain, prev)
+                slope2, offset2 = around(update, keep, scaled, cand, gain, state)
                 state = slope * state + offset
                 b = slope2 * b + offset2
                 a = slope2 * a
@@ -263,17 +301,21 @@
             out.append((state, a, b))
         return tuple(out)
 
-    one, zero = jnp.ones((SEGS, width), F32), jnp.zeros((SEGS, width), F32)
-    carry = tuple((enter[c * SEGS : (c + 1) * SEGS, :], one, zero) for c in range(chunks))
+    one, zero = jnp.ones((SEGS, span), F32), jnp.zeros((SEGS, span), F32)
+    carry = tuple((enter[c * SEGS : (c + 1) * SEGS, wide], one, zero) for c in range(chunks))
     carry = pair(0, carry, True)
     carry = lax.fori_loop(1, seg // 2, lambda jj, c: pair(jj, c, False), carry)
     for c in range(chunks):
-        maps_ref[0, c * SEGS : (c + 1) * SEGS, :] = carry[c][1]
-        maps_ref[1, c * SEGS : (c + 1) * SEGS, :] = carry[c][2]
-    ta, tb = compose_rows(maps_ref, chunks * SEGS, jnp.ones((1, width), F32), jnp.zeros((1, width), F32))
-    for i in range(peers):
-        total_ref[i, 0:1, :] = ta
-        total_ref[i, 1:2, :] = tb
+        maps_ref[0, c * SEGS : (c + 1) * SEGS, wide] = carry[c][1]
+        maps_ref[1, c * SEGS : (c + 1) * SEGS, wide] = carry[c][2]
+
+    @pl.when(n == pl.num_programs(0) - 1)
+    def _():
+        ta, tb = jnp.ones((1, width), F32), jnp.zeros((1, width), F32)
+        ta, tb = compose_rows(maps_ref, chunks * SEGS, ta, tb)
+        for i in range(peers):
+            total_ref[i, 0:1, :] = ta
+            total_ref[i, 1:2, :] = tb
 
 
 def bend_all(place, gates, maps, peer_maps, gain, start):
@@ -281,7 +323,8 @@
     peers = peer_maps.shape[0]
     _, rows, width = gates[0].shape
     tn = tile_of(width, 256)
-    row_spec = pl.BlockSpec((1, tn), lambda n, p: (0, n))
+    row_spec = pl.BlockSpec((1, width), lambda n, p: (0, 0))
+    total_spec = pl.BlockSpec((peers, 2, width), lambda n, p: (0, 0, 0))
     return pl.pallas_call(
         functools.partial(bend_kernel, chunks, peers),
         out_shape=[
@@ -293,16 +336,16 @@
             num_scalar_prefetch=1,
             grid=(width // tn,),
             in_specs=[pl.BlockSpec((2, rows, tn), lambda n, p: (0, 0, n))] * chunks
-            + [pl.BlockSpec((2, SEGS, tn), lambda n, p: (0, 0, n))] * chunks
-            + [pl.BlockSpec((peers, 2, tn), lambda n, p: (0, 0, n)), row_spec, row_spec],
+            + [pl.BlockSpec((2, SEGS, width), lambda n, p: (0, 0, 0))] * chunks
+            + [total_spec, row_spec, row_spec],
             out_specs=[
                 pl.BlockSpec((2, chunks * rows, tn), lambda n, p: (0, 0, n)),
-                pl.BlockSpec((2, chunks * SEGS, tn), lambda n, p: (0, 0, n)),
-                pl.BlockSpec((peers, 2, tn), lambda n, p: (0, 0, n)),
+                pl.BlockSpec((2, chunks * SEGS, width), lambda n, p: (0, 0, 0)),
+                total_spec,
             ],
-            scratch_shapes=[pltpu.VMEM((chunks * SEGS, tn), F32)],
-        ),
-        compiler_params=params(),
+            scratch_shapes=[pltpu.VMEM((chunks * SEGS, width), F32)],
+        ),
+        compiler_params=params(16),
         cost_estimate=cost(
             40 * chunks * rows * width, 12 * chunks * rows * width, 5 * chunks * rows * width
         ),
@@ -336,7 +379,7 @@
     width = run.shape[2]
     peers = peer_maps.shape[0]
     segs = maps.shape[1]
-    tn = tile_of(width, 256)
+    tn = tile_of(width, 1024)
     return pl.pallas_call(
         functools.partial(state_kernel, chunk, peers),
         out_shape=jax.ShapeDtypeStruct((rows, width), BF16),
@@ -352,7 +395,7 @@
             out_specs=pl.BlockSpec((rows, tn), lambda n, p: (0, n)),
             scratch_shapes=[pltpu.VMEM((SEGS, tn), F32), pltpu.VMEM((tn // LANES, rows, LANES), F32)],
         ),
-        compiler_params=params(),
+        compiler_params=params(12),
         cost_estimate=cost(2 * rows * width, 10 * rows * width),
     )(place, run, maps, peer_maps, start)
 
@@ -361,29 +404,44 @@
     count = groups * group
     blocks = refs[:count]
     weights = refs[count : count + peers * pieces]
-    out_ref, states = refs[-2:]
+    out_ref, lhs, wbuf, acc, lsem, wsem = refs[-6:]
     rows, depth = blocks[0].shape
     lines_of = weights[0].shape[0]
-
-    @pl.when(pl.program_id(0) == 0)
-    def _():
-        for c in range(groups):
-            for d in range(group):
-                deep = pl.ds(pl.multiple_of((place[0] ^ d) * depth, depth), depth)
-                states[c * rows : (c + 1) * rows, deep] = blocks[c * group + d][...]
-
     outer = peers // 2
-    total = None
-    for s in range(outer):
-        source = lax.rem(place[1] // 2 + outer - s, outer)
-        for i in range(2):
-            owner = source * 2 + (lax.rem(place[1], 2) ^ i)
-            for p in range(pieces):
-                deep = pl.ds(pl.multiple_of((owner * pieces + p) * lines_of, lines_of), lines_of)
-                w_ref = weights[(s * 2 + i) * pieces + p]
-                part = jnp.dot(states[:, deep], w_ref[...], preferred_element_type=F32)
-                total = part if total is None else total + part
-    out_ref[...] = total.astype(BF16)
+
+    def w_copy(n, p):
+        w_ref = weights[n * pieces + p]
+        dst = wbuf.at[n, p * lines_of : (p + 1) * lines_of, :]
+        return pltpu.make_async_copy(w_ref, dst, wsem.at[n, p])
+
+    def l_copy(c, d):
+        deep = pl.ds(pl.multiple_of((place[0] ^ d) * depth, depth), depth)
+        dst = lhs.at[c * rows : (c + 1) * rows, deep]
+        return pltpu.make_async_copy(blocks[c * group + d], dst, lsem.at[c, d])
+
+    for c in range(groups):
+        for d in range(group):
+            l_copy(c, d).start()
+    for n in range(peers):
+        for p in range(pieces):
+            w_copy(n, p).start()
+    for c in range(groups):
+        for d in range(group):
+            l_copy(c, d).wait()
+    span = lines_of * pieces
+    for n in range(peers):
+        source = lax.rem(place[1] // 2 + outer - n // 2, outer)
+        owner = source * 2 + (lax.rem(place[1], 2) ^ (n % 2))
+        deep = pl.ds(pl.multiple_of(owner * span, span), span)
+        for p in range(pieces):
+            w_copy(n, p).wait()
+        part = jnp.dot(lhs[:, deep], wbuf[n], preferred_element_type=F32)
+        if n == 0:
+            acc[...] = part
+        elif n < peers - 1:
+            acc[...] += part
+        else:
+            out_ref[...] = (acc[...] + part).astype(BF16)
 
 
 def mix_rows(place, blocks, weights, whole, first, total_rows, pieces):
@@ -391,28 +449,33 @@
     rows, depth = blocks[0][0].shape
     lines_of, width = weights[0].shape
     peers = len(weights) // pieces
-    tn = tile_of(width, 256)
     here = groups * rows
+    anywhere = pl.BlockSpec(memory_space=pl.ANY)
     args = [place] + [b for g in blocks for b in g] + list(weights)
-    in_specs = [pl.BlockSpec((rows, depth), lambda n, p: (0, 0))] * (groups * group)
-    in_specs += [pl.BlockSpec((lines_of, tn), lambda n, p: (0, n))] * len(weights)
+    in_specs = [anywhere] * (groups * group + len(weights))
     aliases = {}
     if whole is not None:
         aliases = {len(args): 0}
         args.append(whole)
-        in_specs.append(pl.BlockSpec(memory_space=pl.ANY))
+        in_specs.append(anywhere)
     return pl.pallas_call(
         functools.partial(mix_kernel, groups, group, pieces, peers),
         out_shape=jax.ShapeDtypeStruct((total_rows, width), BF16),
         grid_spec=pltpu.PrefetchScalarGridSpec(
             num_scalar_prefetch=1,
-            grid=(width // tn,),
+            grid=(1,),
             in_specs=in_specs,
-            out_specs=pl.BlockSpec((here, tn), lambda n, p: (first // here, n)),
-            scratch_shapes=[pltpu.VMEM((here, group * depth), BF16)],
+            out_specs=pl.BlockSpec((here, width), lambda n, p: (first // here, 0)),
+            scratch_shapes=[
+                pltpu.VMEM((here, group * depth), BF16),
+                pltpu.VMEM((peers, lines_of * pieces, width), BF16),
+                pltpu.VMEM((here, width), F32),
+                pltpu.SemaphoreType.DMA((groups, group)),
+                pltpu.SemaphoreType.DMA((peers, pieces)),
+            ],
         ),
         input_output_aliases=aliases,
-        compiler_params=params(),
+        compiler_params=params(40 if peers <= 8 else 62),
         cost_estimate=cost(
             2 * here * group * depth * width, 2 * group * depth * (width + here) + 2 * here * width
         ),

time: 252 us -> 243 us (0.964)
  Pallas kernels: 104 us -> 72.3 us
  local copies, waits for them, and re-layouts: 8.44 us -> 17.8 us
  waiting for transfers between devices: 80 us -> 88.4 us
  blocking collectives: 25.3 us -> 32.1 us
    pallas_call x4, Pallas kernels: 19.1 us -> 7.8 us  [state_chunk(): pl.pallas_call(functools.partial(state_kernel, chunk, peers), out_shape=j...]
    unnamed x52 -> x20, local copies, waits for them, and re-layouts: 3.27 us -> 13.4 us
    pallas_call x4, Pallas kernels: 38.2 us -> 28.8 us  [gate_chunk(): pl.pallas_call(functools.partial(gate_kernel, half, chunk, rows, len(earl...]
    ppermute x29, waiting for transfers between devices: 80 us -> 88.4 us  [swap(): lax.ppermute(block, axis, [(i, i ^ bits) for i in range(lax.axis_size(axi...]
    all_to_all x1, blocking collectives: 13.8 us -> 20.9 us  [layer(): peer_maps = lax.all_to_all(out[2], 'ctx', 0, 0, tiled=True)]
    pallas_call x2, Pallas kernels: 20.7 us -> 16.2 us  [mix_rows(): pl.pallas_call(functools.partial(mix_kernel, groups, group, pieces, peers...]
    pallas_call x1, Pallas kernels: 16.4 us -> 12.5 us  [near_product(): pl.pallas_call(functools.partial(near_kernel, half), out_shape=jax.ShapeD...]
    pallas_call x1, Pallas kernels: 9.63 us -> 7.06 us  [bend_all(): pl.pallas_call(functools.partial(bend_kernel, chunks, peers), out_shape=[...]
  transfers between devices with their start and end apart: 35 -> 35, of which waited for: 10 -> 11; matrix products, arithmetic and copies ran while one was open for 3% -> 2% of each run, Pallas kernels for 38% -> 28%
where the time goes in v1:
time: 243 us
  waiting for transfers between devices  88.4 us (36%)
  Pallas kernels  72.3 us (30%)
  blocking collectives  32.1 us (13%)
  starting transfers between devices  31.5 us (13%)
  local copies, waits for them, and re-layouts  17.8 us (7%)
    ppermute x29, waiting for transfers between devices, swap(): lax.ppermute(block, axis, [(i, i ^ bits) for i in range(lax.axis_size(axi...  88.4 us
    pallas_call x4, Pallas kernels, gate_chunk(): pl.pallas_call(functools.partial(gate_kernel, half, chunk, rows, len(earl...  28.8 us
    ppermute x29, starting transfers between devices, swap(): lax.ppermute(block, axis, [(i, i ^ bits) for i in range(lax.axis_size(axi...  21.3 us
    all_to_all x1, blocking collectives, layer(): peer_maps = lax.all_to_all(out[2], 'ctx', 0, 0, tiled=True)  20.9 us
    pallas_call x2, Pallas kernels, mix_rows(): pl.pallas_call(functools.partial(mix_kernel, groups, group, pieces, peers...  16.2 us
    unnamed x20, local copies, waits for them, and re-layouts  13.4 us
    pallas_call x1, Pallas kernels, near_product(): pl.pallas_call(functools.partial(near_kernel, half), out_shape=jax.ShapeD...  12.5 us
    all_to_all x1, blocking collectives, layer(): peer_maps = lax.all_to_all(totals, 'ctx', 0, 0, tiled=True)  11.2 us
  transfers between devices with their start and end apart: 35, of which 11 were waited for; matrix products, arithmetic and copies ran while one was open for 2% of the time, Pallas kernels for 28%

profile of v1, /device:TPU:0, one launch (start us, length us, event | category | flops | bytes accessed | tf_op | source)
XLA Modules:
  0.0 242.6 jit_solution(3177389392494622046)
XLA Ops:
  0.5 2.1 slice.18
  2.6 1.1 slice.19
  3.7 1.1 slice.20
  4.9 2.5 %collective-permute-start.7 = (bf16[256,1024]{1,0:T(8,128)(2,1)S(1)}, bf16[256,1024]{1,0:T(8,128)(2,1)}, u32[]{:S(2)}, u32[]{:S(2)}) collective-permute-start(bf16[256,1024]{1,0:T(8,128)(2,1)S(1)} %slice.21), channel_id=1, source_target_pairs={{0,2},{1,3},{2,0},{3,1},{4,6},{5,7},{6,4},{7,5},{8,10},{9,11},{10,... | collective-permute-start | bytes 1572872 | tf_op jit(solution)/shard_map/ppermute | solution.py:20
  7.4 1.9 collective-permute-start.3
  9.5 10.7 %collective-permute-done.7.refs_0_ = bf16[256,1024]{1,0:T(8,128)(2,1)} collective-permute-done((bf16[256,1024]{1,0:T(8,128)(2,1)S(1)}, bf16[256,1024]{1,0:T(8,128)(2,1)}, u32[]{:S(2)}, u32[]{:S(2)}) %collective-permute-start.7) | collective-permute-done | bytes 524320 | tf_op jit(solution)/shard_map/ppermute | solution.py:20
  20.2 2.1 collective-permute-start.15
  22.3 9.1 %collective-permute-done.5.refs_0_ = bf16[256,1024]{1,0:T(8,128)(2,1)} collective-permute-done((bf16[256,1024]{1,0:T(8,128)(2,1)S(1)}, bf16[256,1024]{1,0:T(8,128)(2,1)}, u32[]{:S(2)}, u32[]{:S(2)}) %collective-permute-start.5) | collective-permute-done | bytes 524320 | tf_op jit(solution)/shard_map/ppermute | solution.py:20
  31.4 2.1 collective-permute-start.14
  33.5 9.1 %collective-permute-done.3.refs_0_ = bf16[256,1024]{1,0:T(8,128)(2,1)} collective-permute-done((bf16[256,1024]{1,0:T(8,128)(2,1)S(1)}, bf16[256,1024]{1,0:T(8,128)(2,1)}, u32[]{:S(2)}, u32[]{:S(2)}) %collective-permute-start.3) | collective-permute-done | bytes 524320 | tf_op jit(solution)/shard_map/ppermute | solution.py:20
  42.8 11.0 %collective-permute-done.refs_0_ = bf16[256,1024]{1,0:T(8,128)(2,1)} collective-permute-done((bf16[256,1024]{1,0:T(8,128)(2,1)}, bf16[256,1024]{1,0:T(8,128)(2,1)}, u32[]{:S(2)}, u32[]{:S(2)}) %collective-permute-start) | collective-permute-done | bytes 524320 | tf_op jit(solution)/shard_map/ppermute | solution.py:20
  54.4 1.8 collective-permute-start.19
  56.2 1.6 collective-permute-start.18
  57.8 5.8 %copy-done = bf16[2,4096,1024]{2,1,0:T(8,128)(2,1)S(1)} copy-done((bf16[2,4096,1024]{2,1,0:T(8,128)(2,1)S(1)}, bf16[2,4096,1024]{2,1,0:T(8,128)(2,1)}, u32[]{:S(2)}) %copy-start) | copy-done | bytes 16777240
  63.6 12.5 %shard_map.73.refs_2_ = f32[2,1024,1024]{2,1,0:T(8,128)S(1)} custom-call(s32[2]{0:T(128)S(1)} %pad_add_fusion.place, bf16[1024,1024]{1,0:T(8,128)(2,1)S(1)} %copy-done.2, bf16[1024,1024]{1,0:T(8,128)(2,1)} %collective-permute-done.2.refs_1_, bf16[2,4096,1024]{2,1,0:T(8,128)(2,1)S(1)} %copy-done), custom_call_target="tpu_custom_call" | custom-call | flops 8589934592 | bytes 20971520 | tf_op jit(solution)/shard_map/pallas_call | solution.py:54
  76.1 5.8 %copy-done.1 = bf16[2,4096,1024]{2,1,0:T(8,128)(2,1)S(1)} copy-done((bf16[2,4096,1024]{2,1,0:T(8,128)(2,1)S(1)}, bf16[2,4096,1024]{2,1,0:T(8,128)(2,1)}, u32[]{:S(2)}) %copy-start.1) | copy-done | bytes 16777240
  81.9 7.3 %shard_map.76 = (bf16[2,256,1024]{2,1,0:T(8,128)(2,1)S(1)}, f32[2,8,1024]{2,1,0:T(8,128)S(1)}) custom-call(s32[2]{0:T(128)S(1)} %pad_add_fusion.place, bf16[256,1024]{1,0:T(8,128)(2,1)} %collective-permute-done.5.refs_0_, bf16[256,1024]{1,0:T(8,128)(2,1)} %collective-permute-done.6.refs_1_, f32[2,1024,1024]{2,1,0:T(8,128)S(1)} %shard_map.73.refs_2_, ...), custom_call_target="tpu_custom_call" | custom-call | flops 2147483648 | bytes 12582912 | tf_op jit(solution)/shard_map/pallas_call | solution.py:223
  89.2 1.6 collective-permute-start.13
  90.8 7.1 %shard_map.75 = (bf16[2,256,1024]{2,1,0:T(8,128)(2,1)S(1)}, f32[2,8,1024]{2,1,0:T(8,128)S(1)}) custom-call(s32[2]{0:T(128)S(1)} %pad_add_fusion.place, bf16[256,1024]{1,0:T(8,128)(2,1)} %collective-permute-done.3.refs_0_, bf16[256,1024]{1,0:T(8,128)(2,1)S(1)} %collective-permute-done.4.refs_1_, f32[2,1024,1024]{2,1,0:T(8,128)S(1)} %shard_map.73.refs_2_, ...), custom_call_target="tpu_custom_call" | custom-call | flops 2147483648 | bytes 12582912 | tf_op jit(solution)/shard_map/pallas_call | solution.py:223
  98.0 0.6 collective-permute-start.12
  98.5 1.5 collective-permute-start.17
  100.6 1.6 collective-permute-start.22
  102.1 7.1 %shard_map.74 = (bf16[2,256,1024]{2,1,0:T(8,128)(2,1)S(1)}, f32[2,8,1024]{2,1,0:T(8,128)S(1)}) custom-call(s32[2]{0:T(128)S(1)} %pad_add_fusion.place, bf16[256,1024]{1,0:T(8,128)(2,1)} %collective-permute-done.refs_0_, bf16[256,1024]{1,0:T(8,128)(2,1)S(1)} %collective-permute-done.1.refs_1_, f32[2,1024,1024]{2,1,0:T(8,128)S(1)} %shard_map.73.refs_2_, ...), custom_call_target="tpu_custom_call" | custom-call | flops 2147483648 | bytes 12582912 | tf_op jit(solution)/shard_map/pallas_call | solution.py:223
  109.3 7.2 %shard_map.77 = (bf16[2,256,1024]{2,1,0:T(8,128)(2,1)S(1)}, f32[2,8,1024]{2,1,0:T(8,128)S(1)}, f32[8,2,1024]{2,1,0:T(2,128)S(1)}) custom-call(s32[2]{0:T(128)S(1)} %pad_add_fusion.place, bf16[256,1024]{1,0:T(8,128)(2,1)} %collective-permute-done.7.refs_0_, bf16[256,1024]{1,0:T(8,128)(2,1)S(1)} %collective-permute-done.8.refs_1_, ...), custom_call_target="tpu_custom_call" | custom-call | flops 2147483648 | bytes 12582912 | tf_op jit(solution)/shard_map/pallas_call | solution.py:223
  116.5 20.9 %all_to_all.10.refs_8_ = f32[8,2,1024]{2,1,0:T(2,128)S(1)} all-to-all(f32[8,2,1024]{2,1,0:T(2,128)S(1)} %get-tuple-element.42), channel_id=1, replica_groups=mesh['ctx'=8,'ch'=4] {'ctx'}, dimensions={0} | all-to-all | bytes 131072 | tf_op jit(solution)/shard_map/all_to_all | solution.py:566
  137.4 7.1 %bend.1 = (f32[2,1024,1024]{2,1,0:T(8,128)S(1)}, f32[2,32,1024]{2,1,0:T(8,128)S(1)}, f32[8,2,1024]{2,1,0:T(2,128)S(1)}) custom-call(s32[2]{0:T(128)S(1)} %pad_add_fusion.place, bf16[2,256,1024]{2,1,0:T(8,128)(2,1)S(1)} %get-tuple-element.28.refs_0_, bf16[2,256,1024]{2,1,0:T(8,128)(2,1)S(1)} %get-tuple-element.31.refs_1_, ...), custom_call_target="tpu_custom_call" | custom-call | flops 41943040 | bytes 12582912 | tf_op jit(solution)/shard_map/bend/pallas_call | solution.py:328
  144.5 11.2 %all_to_all.11.peer_ref = f32[8,2,1024]{2,1,0:T(2,128)S(1)} all-to-all(f32[8,2,1024]{2,1,0:T(2,128)S(1)} %get-tuple-element.45), channel_id=1, replica_groups=mesh['ctx'=8,'ch'=4] {'ctx'}, dimensions={0} | all-to-all | bytes 131072 | tf_op jit(solution)/shard_map/all_to_all | solution.py:568
  155.6 1.9 shard_map.79.refs_0_
  157.6 2.0 shard_map.78.refs_0_
  160.0 1.5 collective-permute-start.10
  162.1 1.1 collective-permute-start.23
  163.1 1.9 shard_map.80.refs_4_
  165.1 6.0 %collective-permute-done.20.refs_22_.refs_14_ = bf16[256,1024]{1,0:T(8,128)(2,1)S(1)} collective-permute-done((bf16[256,1024]{1,0:T(8,128)(2,1)S(1)}, bf16[256,1024]{1,0:T(8,128)(2,1)S(1)}, u32[]{:S(2)}, u32[]{:S(2)}) %collective-permute-start.20) | collective-permute-done | bytes 524320 | tf_op jit(solution)/shard_map/ppermute | solution.py:20
  171.1 1.5 collective-permute-start.30
  172.5 2.0 shard_map.81.refs_8_
  174.8 11.2 %collective-permute-done.27.refs_2_ = bf16[256,1024]{1,0:T(8,128)(2,1)S(1)} collective-permute-done((bf16[256,1024]{1,0:T(8,128)(2,1)S(1)}, bf16[256,1024]{1,0:T(8,128)(2,1)S(1)}, u32[]{:S(2)}, u32[]{:S(2)}) %collective-permute-start.27) | collective-permute-done | bytes 524320 | tf_op jit(solution)/shard_map/ppermute | solution.py:20
  186.1 1.5 collective-permute-start.33
  187.6 1.7 collective-permute-start.21
  189.3 8.0 %collective-permute-done.30.refs_6_ = bf16[256,1024]{1,0:T(8,128)(2,1)S(1)} collective-permute-done((bf16[256,1024]{1,0:T(8,128)(2,1)S(1)}, bf16[256,1024]{1,0:T(8,128)(2,1)S(1)}, u32[]{:S(2)}, u32[]{:S(2)}) %collective-permute-start.30) | collective-permute-done | bytes 524320 | tf_op jit(solution)/shard_map/ppermute | solution.py:20
  197.3 1.6 collective-permute-start.24
  198.9 5.9 %collective-permute-done.33.refs_10_ = bf16[256,1024]{1,0:T(8,128)(2,1)S(1)} collective-permute-done((bf16[256,1024]{1,0:T(8,128)(2,1)S(1)}, bf16[256,1024]{1,0:T(8,128)(2,1)S(1)}, u32[]{:S(2)}, u32[]{:S(2)}) %collective-permute-start.33) | collective-permute-done | bytes 524320 | tf_op jit(solution)/shard_map/ppermute | solution.py:20
  205.4 1.6 collective-permute-start.25
  207.0 6.6 %collective-permute-done.24.refs_26_.refs_18_ = bf16[256,1024]{1,0:T(8,128)(2,1)S(1)} collective-permute-done((bf16[256,1024]{1,0:T(8,128)(2,1)S(1)}, bf16[256,1024]{1,0:T(8,128)(2,1)S(1)}, u32[]{:S(2)}, u32[]{:S(2)}) %collective-permute-start.24) | collective-permute-done | bytes 524320 | tf_op jit(solution)/shard_map/ppermute | solution.py:20
  214.2 10.2 %collective-permute-done.25.refs_27_.refs_19_ = bf16[256,1024]{1,0:T(8,128)(2,1)S(1)} collective-permute-done((bf16[256,1024]{1,0:T(8,128)(2,1)S(1)}, bf16[256,1024]{1,0:T(8,128)(2,1)S(1)}, u32[]{:S(2)}, u32[]{:S(2)}) %collective-permute-start.25) | collective-permute-done | bytes 524320 | tf_op jit(solution)/shard_map/ppermute | solution.py:20
  224.4 0.8 copy-done.3
  225.2 11.1 %shard_map.82.refs_20_ = bf16[1024,1024]{1,0:T(8,128)(2,1)} custom-call(s32[2]{0:T(128)S(1)} %pad_add_fusion.place, bf16[256,1024]{1,0:T(8,128)(2,1)S(1)} %shard_map.79.refs_0_, bf16[256,1024]{1,0:T(8,128)(2,1)S(1)} %collective-permute-done.26.refs_1_, bf16[256,1024]{1,0:T(8,128)(2,1)S(1)} %collective-permute-done.27.refs_2_, ...), custom_call_target="tpu_custom_call" | custom-call | flops 6442450944 | bytes 16252928 | tf_op jit(solution)/shard_map/pallas_call | solution.py:461
  236.3 1.0 copy-done.4
  237.3 5.1 %shard_map.83 = bf16[1024,1024]{1,0:T(8,128)(2,1)} custom-call(s32[2]{0:T(128)S(1)} %pad_add_fusion.place, bf16[256,1024]{1,0:T(8,128)(2,1)S(1)} %shard_map.78.refs_0_, bf16[256,1024]{1,0:T(8,128)(2,1)S(1)} %collective-permute-done.9.refs_1_, bf16[256,1024]{1,0:T(8,128)(2,1)S(1)} %collective-permute-done.10.refs_2_, ...), custom_call_target="tpu_custom_call", output_to_operand_aliasing={{}: (21, {})} | custom-call | flops 2147483648 | bytes 11010048 | tf_op jit(solution)/shard_map/pallas_call | solution.py:461
  (63 shorter events, 4.4 us)
Async XLA Ops:
  0.0 4.8 %copy-start.2 = (bf16[1024,1024]{1,0:T(8,128)(2,1)S(1)}, bf16[1024,1024]{1,0:T(8,128)(2,1)}, u32[]{:S(2)}) copy-start(bf16[1024,1024]{1,0:T(8,128)(2,1)} %refs_0_.1) | copy-start | bytes 6291460
  0.0 9.4 %copy-start.7 = (bf16[512,1024]{1,0:T(8,128)(2,1)S(1)}, bf16[512,1024]{1,0:T(8,128)(2,1)}, u32[]{:S(2)}) copy-start(bf16[512,1024]{1,0:T(8,128)(2,1)} %param.9) | copy-start | bytes 3145732
  0.0 56.2 %collective-permute-start.2 = (bf16[1024,1024]{1,0:T(8,128)(2,1)}, bf16[1024,1024]{1,0:T(8,128)(2,1)}, u32[]{:S(2)}, u32[]{:S(2)}) collective-permute-start(bf16[1024,1024]{1,0:T(8,128)(2,1)} %refs_0_.1), channel_id=1, source_target_pairs={{0,1},{1,0},{2,3},{3,2},{4,5},{5,4},{6,7},{7,6},{8,9},{9,8},{10,11... | collective-permute-start | bytes 6291464 | tf_op jit(solution)/shard_map/ppermute | solution.py:20
  3.7 39.1 %copy-start.8 = (f32[1024]{0:T(1024)S(1)}, f32[1024]{0:T(1024)}, u32[]{:S(2)}) copy-start(f32[1024]{0:T(1024)} %param.11) | copy-start | bytes 12292
  3.7 39.1 %copy-start.9 = (f32[1024]{0:T(1024)S(1)}, f32[1024]{0:T(1024)}, u32[]{:S(2)}) copy-start(f32[1024]{0:T(1024)} %param.10) | copy-start | bytes 12292
  4.9 15.3 %collective-permute-start.7 = (bf16[256,1024]{1,0:T(8,128)(2,1)S(1)}, bf16[256,1024]{1,0:T(8,128)(2,1)}, u32[]{:S(2)}, u32[]{:S(2)}) collective-permute-start(bf16[256,1024]{1,0:T(8,128)(2,1)S(1)} %slice.21), channel_id=1, source_target_pairs={{0,2},{1,3},{2,0},{3,1},{4,6},{5,7},{6,4},{7,5},{8,10},{9,11},{10,... | collective-permute-start | bytes 1572872 | tf_op jit(solution)/shard_map/ppermute | solution.py:20
  7.3 24.1 %collective-permute-start.5 = (bf16[256,1024]{1,0:T(8,128)(2,1)S(1)}, bf16[256,1024]{1,0:T(8,128)(2,1)}, u32[]{:S(2)}, u32[]{:S(2)}) collective-permute-start(bf16[256,1024]{1,0:T(8,128)(2,1)S(1)} %slice.20), channel_id=1, source_target_pairs={{0,2},{1,3},{2,0},{3,1},{4,6},{5,7},{6,4},{7,5},{8,10},{9,11},{10,... | collective-permute-start | bytes 1572872 | tf_op jit(solution)/shard_map/ppermute | solution.py:20
  7.4 35.3 %collective-permute-start.3 = (bf16[256,1024]{1,0:T(8,128)(2,1)S(1)}, bf16[256,1024]{1,0:T(8,128)(2,1)}, u32[]{:S(2)}, u32[]{:S(2)}) collective-permute-start(bf16[256,1024]{1,0:T(8,128)(2,1)S(1)} %slice.19), channel_id=1, source_target_pairs={{0,2},{1,3},{2,0},{3,1},{4,6},{5,7},{6,4},{7,5},{8,10},{9,11},{10,... | collective-permute-start | bytes 1572872 | tf_op jit(solution)/shard_map/ppermute | solution.py:20
  9.3 44.5 %collective-permute-start = (bf16[256,1024]{1,0:T(8,128)(2,1)}, bf16[256,1024]{1,0:T(8,128)(2,1)}, u32[]{:S(2)}, u32[]{:S(2)}) collective-permute-start(bf16[256,1024]{1,0:T(8,128)(2,1)} %slice.18), channel_id=1, source_target_pairs={{0,2},{1,3},{2,0},{3,1},{4,6},{5,7},{6,4},{7,5},{8,10},{9,11},{10,... | collective-permute-start | bytes 1572872 | tf_op jit(solution)/shard_map/ppermute | solution.py:20
  20.2 33.7 %collective-permute-start.15 = (bf16[256,1024]{1,0:T(8,128)(2,1)S(1)}, bf16[256,1024]{1,0:T(8,128)(2,1)}, u32[]{:S(2)}, u32[]{:S(2)}) collective-permute-start(bf16[256,1024]{1,0:T(8,128)(2,1)S(1)} %get-tuple-element.49.refs_13_.refs_5_), channel_id=1, source_target_pairs={{0,8},{4,12},{8,16},{12,20},{16,24},{20,28},{24,0},{28,4},{1,9},{5... | collective-permute-start | bytes 1572872 | tf_op jit(solution)/shard_map/ppermute | solution.py:509
  31.4 22.9 %collective-permute-start.14 = (bf16[256,1024]{1,0:T(8,128)(2,1)S(1)}, bf16[256,1024]{1,0:T(8,128)(2,1)}, u32[]{:S(2)}, u32[]{:S(2)}) collective-permute-start(bf16[256,1024]{1,0:T(8,128)(2,1)S(1)} %get-tuple-element.50.refs_12_.refs_4_), channel_id=1, source_target_pairs={{0,8},{4,12},{8,16},{12,20},{16,24},{20,28},{24,0},{28,4},{1,9},{5... | collective-permute-start | bytes 1572872 | tf_op jit(solution)/shard_map/ppermute | solution.py:509
  42.7 11.7 %collective-permute-start.6 = (bf16[256,1024]{1,0:T(8,128)(2,1)}, bf16[256,1024]{1,0:T(8,128)(2,1)}, u32[]{:S(2)}, u32[]{:S(2)}) collective-permute-start(bf16[256,1024]{1,0:T(8,128)(2,1)} %collective-permute-done.5.refs_0_), channel_id=1, source_target_pairs={{0,1},{1,0},{2,3},{3,2},{4,5},{5,4},{6,7},{7,6},{8,9},{9,8},{10,11... | collective-permute-start | bytes 1572872 | tf_op jit(solution)/shard_map/ppermute | solution.py:20
  42.8 33.3 %copy-start.5 = (f32[1024]{0:T(1024)S(1)}, f32[1024]{0:T(1024)}, u32[]{:S(2)}) copy-start(f32[1024]{0:T(1024)} %param.13) | copy-start | bytes 12292
  42.8 33.3 %copy-start.6 = (f32[1024]{0:T(1024)S(1)}, f32[1024]{0:T(1024)}, u32[]{:S(2)}) copy-start(f32[1024]{0:T(1024)} %param.12) | copy-start | bytes 12292
  53.8 44.1 %collective-permute-start.8 = (bf16[256,1024]{1,0:T(8,128)(2,1)}, bf16[256,1024]{1,0:T(8,128)(2,1)S(1)}, u32[]{:S(2)}, u32[]{:S(2)}) collective-permute-start(bf16[256,1024]{1,0:T(8,128)(2,1)} %collective-permute-done.7.refs_0_), channel_id=1, source_target_pairs={{0,1},{1,0},{2,3},{3,2},{4,5},{5,4},{6,7},{7,6},{8,9},{9,8},{10,11... | collective-permute-start | bytes 1572872 | tf_op jit(solution)/shard_map/ppermute | solution.py:20
  53.9 35.3 %collective-permute-start.4 = (bf16[256,1024]{1,0:T(8,128)(2,1)}, bf16[256,1024]{1,0:T(8,128)(2,1)S(1)}, u32[]{:S(2)}, u32[]{:S(2)}) collective-permute-start(bf16[256,1024]{1,0:T(8,128)(2,1)} %collective-permute-done.3.refs_0_), channel_id=1, source_target_pairs={{0,1},{1,0},{2,3},{3,2},{4,5},{5,4},{6,7},{7,6},{8,9},{9,8},{10,11... | collective-permute-start | bytes 1572872 | tf_op jit(solution)/shard_map/ppermute | solution.py:20
  54.3 44.2 %collective-permute-start.1 = (bf16[256,1024]{1,0:T(8,128)(2,1)}, bf16[256,1024]{1,0:T(8,128)(2,1)S(1)}, u32[]{:S(2)}, u32[]{:S(2)}) collective-permute-start(bf16[256,1024]{1,0:T(8,128)(2,1)} %collective-permute-done.refs_0_), channel_id=1, source_target_pairs={{0,1},{1,0},{2,3},{3,2},{4,5},{5,4},{6,7},{7,6},{8,9},{9,8},{10,11... | collective-permute-start | bytes 1572872 | tf_op jit(solution)/shard_map/ppermute | solution.py:20
  54.4 45.6 %collective-permute-start.19 = (bf16[256,1024]{1,0:T(8,128)(2,1)}, bf16[256,1024]{1,0:T(8,128)(2,1)S(1)}, u32[]{:S(2)}, u32[]{:S(2)}) collective-permute-start(bf16[256,1024]{1,0:T(8,128)(2,1)} %collective-permute-done.15.refs_17_.refs_9_), channel_id=1, source_target_pairs={{0,8},{4,12},{8,16},{12,20},{16,24},{20,28},{24,0},{28,4},{1,9},{5... | collective-permute-start | bytes 1572872 | tf_op jit(solution)/shard_map/ppermute | solution.py:509
  56.2 44.3 %collective-permute-start.18 = (bf16[256,1024]{1,0:T(8,128)(2,1)}, bf16[256,1024]{1,0:T(8,128)(2,1)S(1)}, u32[]{:S(2)}, u32[]{:S(2)}) collective-permute-start(bf16[256,1024]{1,0:T(8,128)(2,1)} %collective-permute-done.14.refs_16_.refs_8_), channel_id=1, source_target_pairs={{0,8},{4,12},{8,16},{12,20},{16,24},{20,28},{24,0},{28,4},{1,9},{5... | collective-permute-start | bytes 1572872 | tf_op jit(solution)/shard_map/ppermute | solution.py:509
  57.8 5.8 %copy-start = (bf16[2,4096,1024]{2,1,0:T(8,128)(2,1)S(1)}, bf16[2,4096,1024]{2,1,0:T(8,128)(2,1)}, u32[]{:S(2)}) copy-start(bf16[2,4096,1024]{2,1,0:T(8,128)(2,1)} %refs_3_.7) | copy-start | bytes 50331652
  76.1 5.8 %copy-start.1 = (bf16[2,4096,1024]{2,1,0:T(8,128)(2,1)S(1)}, bf16[2,4096,1024]{2,1,0:T(8,128)(2,1)}, u32[]{:S(2)}) copy-start(bf16[2,4096,1024]{2,1,0:T(8,128)(2,1)} %refs_3_.7) | copy-start | bytes 50331652
  89.2 70.4 %collective-permute-start.13 = (bf16[256,1024]{1,0:T(8,128)(2,1)S(1)}, bf16[256,1024]{1,0:T(8,128)(2,1)S(1)}, u32[]{:S(2)}, u32[]{:S(2)}) collective-permute-start(bf16[256,1024]{1,0:T(8,128)(2,1)S(1)} %get-tuple-element.49.refs_13_.refs_5_), channel_id=1, source_target_pairs={{0,4},{4,0},{8,12},{12,8},{16,20},{20,16},{24,28},{28,24},{1,5},{5... | collective-permute-start | bytes 1572872 | tf_op jit(solution)/shard_map/ppermute | solution.py:20
  98.0 62.1 %collective-permute-start.12 = (bf16[256,1024]{1,0:T(8,128)(2,1)S(1)}, bf16[256,1024]{1,0:T(8,128)(2,1)S(1)}, u32[]{:S(2)}, u32[]{:S(2)}) collective-permute-start(bf16[256,1024]{1,0:T(8,128)(2,1)S(1)} %get-tuple-element.50.refs_12_.refs_4_), channel_id=1, source_target_pairs={{0,4},{4,0},{8,12},{12,8},{16,20},{20,16},{24,28},{28,24},{1,5},{5... | collective-permute-start | bytes 1572872 | tf_op jit(solution)/shard_map/ppermute | solution.py:20
  98.5 63.0 %collective-permute-start.17 = (bf16[256,1024]{1,0:T(8,128)(2,1)}, bf16[256,1024]{1,0:T(8,128)(2,1)S(1)}, u32[]{:S(2)}, u32[]{:S(2)}) collective-permute-start(bf16[256,1024]{1,0:T(8,128)(2,1)} %collective-permute-done.15.refs_17_.refs_9_), channel_id=1, source_target_pairs={{0,4},{4,0},{8,12},{12,8},{16,20},{20,16},{24,28},{28,24},{1,5},{5... | collective-permute-start | bytes 1572872 | tf_op jit(solution)/shard_map/ppermute | solution.py:20
  100.1 62.0 %collective-permute-start.16 = (bf16[256,1024]{1,0:T(8,128)(2,1)}, bf16[256,1024]{1,0:T(8,128)(2,1)S(1)}, u32[]{:S(2)}, u32[]{:S(2)}) collective-permute-start(bf16[256,1024]{1,0:T(8,128)(2,1)} %collective-permute-done.14.refs_16_.refs_8_), channel_id=1, source_target_pairs={{0,4},{4,0},{8,12},{12,8},{16,20},{20,16},{24,28},{28,24},{1,5},{5... | collective-permute-start | bytes 1572872 | tf_op jit(solution)/shard_map/ppermute | solution.py:20
  100.6 61.5 %collective-permute-start.22 = (bf16[256,1024]{1,0:T(8,128)(2,1)S(1)}, bf16[256,1024]{1,0:T(8,128)(2,1)S(1)}, u32[]{:S(2)}, u32[]{:S(2)}) collective-permute-start(bf16[256,1024]{1,0:T(8,128)(2,1)S(1)} %collective-permute-done.18.refs_20_.refs_12_), channel_id=1, source_target_pairs={{0,8},{4,12},{8,16},{12,20},{16,24},{20,28},{24,0},{28,4},{1,9},{5... | collective-permute-start | bytes 1572872 | tf_op jit(solution)/shard_map/ppermute | solution.py:509
  159.6 11.5 %collective-permute-start.20 = (bf16[256,1024]{1,0:T(8,128)(2,1)S(1)}, bf16[256,1024]{1,0:T(8,128)(2,1)S(1)}, u32[]{:S(2)}, u32[]{:S(2)}) collective-permute-start(bf16[256,1024]{1,0:T(8,128)(2,1)S(1)} %collective-permute-done.18.refs_20_.refs_12_), channel_id=1, source_target_pairs={{0,4},{4,0},{8,12},{12,8},{16,20},{20,16},{24,28},{28,24},{1,5},{5... | collective-permute-start | bytes 1572872 | tf_op jit(solution)/shard_map/ppermute | solution.py:20
  160.0 14.8 %collective-permute-start.10 = (bf16[256,1024]{1,0:T(8,128)(2,1)S(1)}, bf16[256,1024]{1,0:T(8,128)(2,1)S(1)}, u32[]{:S(2)}, u32[]{:S(2)}) collective-permute-start(bf16[256,1024]{1,0:T(8,128)(2,1)S(1)} %shard_map.78.refs_0_), channel_id=1, source_target_pairs={{0,2},{1,3},{2,0},{3,1},{4,6},{5,7},{6,4},{7,5},{8,10},{9,11},{10,... | collective-permute-start | bytes 1572872 | tf_op jit(solution)/shard_map/ppermute | solution.py:20
  161.5 24.5 %collective-permute-start.27 = (bf16[256,1024]{1,0:T(8,128)(2,1)S(1)}, bf16[256,1024]{1,0:T(8,128)(2,1)S(1)}, u32[]{:S(2)}, u32[]{:S(2)}) collective-permute-start(bf16[256,1024]{1,0:T(8,128)(2,1)S(1)} %shard_map.79.refs_0_), channel_id=1, source_target_pairs={{0,2},{1,3},{2,0},{3,1},{4,6},{5,7},{6,4},{7,5},{8,10},{9,11},{10,... | collective-permute-start | bytes 1572872 | tf_op jit(solution)/shard_map/ppermute | solution.py:20
  162.1 25.5 %collective-permute-start.26 = (bf16[256,1024]{1,0:T(8,128)(2,1)S(1)}, bf16[256,1024]{1,0:T(8,128)(2,1)S(1)}, u32[]{:S(2)}, u32[]{:S(2)}) collective-permute-start(bf16[256,1024]{1,0:T(8,128)(2,1)S(1)} %shard_map.79.refs_0_), channel_id=1, source_target_pairs={{0,1},{1,0},{2,3},{3,2},{4,5},{5,4},{6,7},{7,6},{8,9},{9,8},{10,11... | collective-permute-start | bytes 1572872 | tf_op jit(solution)/shard_map/ppermute | solution.py:20
  162.1 25.5 %collective-permute-start.23 = (bf16[256,1024]{1,0:T(8,128)(2,1)S(1)}, bf16[256,1024]{1,0:T(8,128)(2,1)S(1)}, u32[]{:S(2)}, u32[]{:S(2)}) collective-permute-start(bf16[256,1024]{1,0:T(8,128)(2,1)S(1)} %collective-permute-done.19.refs_21_.refs_13_), channel_id=1, source_target_pairs={{0,8},{4,12},{8,16},{12,20},{16,24},{20,28},{24,0},{28,4},{1,9},{5... | collective-permute-start | bytes 1572872 | tf_op jit(solution)/shard_map/ppermute | solution.py:509
  171.1 26.2 %collective-permute-start.30 = (bf16[256,1024]{1,0:T(8,128)(2,1)S(1)}, bf16[256,1024]{1,0:T(8,128)(2,1)S(1)}, u32[]{:S(2)}, u32[]{:S(2)}) collective-permute-start(bf16[256,1024]{1,0:T(8,128)(2,1)S(1)} %shard_map.80.refs_4_), channel_id=1, source_target_pairs={{0,2},{1,3},{2,0},{3,1},{4,6},{5,7},{6,4},{7,5},{8,10},{9,11},{10,... | collective-permute-start | bytes 1572872 | tf_op jit(solution)/shard_map/ppermute | solution.py:20
  174.8 24.1 %collective-permute-start.29 = (bf16[256,1024]{1,0:T(8,128)(2,1)S(1)}, bf16[256,1024]{1,0:T(8,128)(2,1)S(1)}, u32[]{:S(2)}, u32[]{:S(2)}) collective-permute-start(bf16[256,1024]{1,0:T(8,128)(2,1)S(1)} %shard_map.80.refs_4_), channel_id=1, source_target_pairs={{0,1},{1,0},{2,3},{3,2},{4,5},{5,4},{6,7},{7,6},{8,9},{9,8},{10,11... | collective-permute-start | bytes 1572872 | tf_op jit(solution)/shard_map/ppermute | solution.py:20
  186.1 18.8 %collective-permute-start.33 = (bf16[256,1024]{1,0:T(8,128)(2,1)S(1)}, bf16[256,1024]{1,0:T(8,128)(2,1)S(1)}, u32[]{:S(2)}, u32[]{:S(2)}) collective-permute-start(bf16[256,1024]{1,0:T(8,128)(2,1)S(1)} %shard_map.81.refs_8_), channel_id=1, source_target_pairs={{0,2},{1,3},{2,0},{3,1},{4,6},{5,7},{6,4},{7,5},{8,10},{9,11},{10,... | collective-permute-start | bytes 1572872 | tf_op jit(solution)/shard_map/ppermute | solution.py:20
  187.5 17.3 %collective-permute-start.32 = (bf16[256,1024]{1,0:T(8,128)(2,1)S(1)}, bf16[256,1024]{1,0:T(8,128)(2,1)S(1)}, u32[]{:S(2)}, u32[]{:S(2)}) collective-permute-start(bf16[256,1024]{1,0:T(8,128)(2,1)S(1)} %shard_map.81.refs_8_), channel_id=1, source_target_pairs={{0,1},{1,0},{2,3},{3,2},{4,5},{5,4},{6,7},{7,6},{8,9},{9,8},{10,11... | collective-permute-start | bytes 1572872 | tf_op jit(solution)/shard_map/ppermute | solution.py:20
  187.6 17.8 %collective-permute-start.21 = (bf16[256,1024]{1,0:T(8,128)(2,1)S(1)}, bf16[256,1024]{1,0:T(8,128)(2,1)S(1)}, u32[]{:S(2)}, u32[]{:S(2)}) collective-permute-start(bf16[256,1024]{1,0:T(8,128)(2,1)S(1)} %collective-permute-done.19.refs_21_.refs_13_), channel_id=1, source_target_pairs={{0,4},{4,0},{8,12},{12,8},{16,20},{20,16},{24,28},{28,24},{1,5},{5... | collective-permute-start | bytes 1572872 | tf_op jit(solution)/shard_map/ppermute | solution.py:20
  197.3 16.4 %collective-permute-start.24 = (bf16[256,1024]{1,0:T(8,128)(2,1)S(1)}, bf16[256,1024]{1,0:T(8,128)(2,1)S(1)}, u32[]{:S(2)}, u32[]{:S(2)}) collective-permute-start(bf16[256,1024]{1,0:T(8,128)(2,1)S(1)} %collective-permute-done.22.refs_24_.refs_16_), channel_id=1, source_target_pairs={{0,4},{4,0},{8,12},{12,8},{16,20},{20,16},{24,28},{28,24},{1,5},{5... | collective-permute-start | bytes 1572872 | tf_op jit(solution)/shard_map/ppermute | solution.py:20
  198.9 14.7 %collective-permute-start.28 = (bf16[256,1024]{1,0:T(8,128)(2,1)S(1)}, bf16[256,1024]{1,0:T(8,128)(2,1)S(1)}, u32[]{:S(2)}, u32[]{:S(2)}) collective-permute-start(bf16[256,1024]{1,0:T(8,128)(2,1)S(1)} %collective-permute-done.27.refs_2_), channel_id=1, source_target_pairs={{0,1},{1,0},{2,3},{3,2},{4,5},{5,4},{6,7},{7,6},{8,9},{9,8},{10,11... | collective-permute-start | bytes 1572872 | tf_op jit(solution)/shard_map/ppermute | solution.py:20
  204.9 9.3 %collective-permute-start.31 = (bf16[256,1024]{1,0:T(8,128)(2,1)S(1)}, bf16[256,1024]{1,0:T(8,128)(2,1)S(1)}, u32[]{:S(2)}, u32[]{:S(2)}) collective-permute-start(bf16[256,1024]{1,0:T(8,128)(2,1)S(1)} %collective-permute-done.30.refs_6_), channel_id=1, source_target_pairs={{0,1},{1,0},{2,3},{3,2},{4,5},{5,4},{6,7},{7,6},{8,9},{9,8},{10,11... | collective-permute-start | bytes 1572872 | tf_op jit(solution)/shard_map/ppermute | solution.py:20
  204.9 9.3 %collective-permute-start.34 = (bf16[256,1024]{1,0:T(8,128)(2,1)S(1)}, bf16[256,1024]{1,0:T(8,128)(2,1)S(1)}, u32[]{:S(2)}, u32[]{:S(2)}) collective-permute-start(bf16[256,1024]{1,0:T(8,128)(2,1)S(1)} %collective-permute-done.33.refs_10_), channel_id=1, source_target_pairs={{0,1},{1,0},{2,3},{3,2},{4,5},{5,4},{6,7},{7,6},{8,9},{9,8},{10,11... | collective-permute-start | bytes 1572872 | tf_op jit(solution)/shard_map/ppermute | solution.py:20
  205.4 19.0 %collective-permute-start.25 = (bf16[256,1024]{1,0:T(8,128)(2,1)S(1)}, bf16[256,1024]{1,0:T(8,128)(2,1)S(1)}, u32[]{:S(2)}, u32[]{:S(2)}) collective-permute-start(bf16[256,1024]{1,0:T(8,128)(2,1)S(1)} %collective-permute-done.23.refs_25_.refs_17_), channel_id=1, source_target_pairs={{0,4},{4,0},{8,12},{12,8},{16,20},{20,16},{24,28},{28,24},{1,5},{5... | collective-permute-start | bytes 1572872 | tf_op jit(solution)/shard_map/ppermute | solution.py:20
  213.7 22.6 %collective-permute-start.9 = (bf16[256,1024]{1,0:T(8,128)(2,1)S(1)}, bf16[256,1024]{1,0:T(8,128)(2,1)S(1)}, u32[]{:S(2)}, u32[]{:S(2)}) collective-permute-start(bf16[256,1024]{1,0:T(8,128)(2,1)S(1)} %shard_map.78.refs_0_), channel_id=1, source_target_pairs={{0,1},{1,0},{2,3},{3,2},{4,5},{5,4},{6,7},{7,6},{8,9},{9,8},{10,11... | collective-permute-start | bytes 1572872 | tf_op jit(solution)/shard_map/ppermute | solution.py:20
  213.7 22.6 %collective-permute-start.11 = (bf16[256,1024]{1,0:T(8,128)(2,1)S(1)}, bf16[256,1024]{1,0:T(8,128)(2,1)S(1)}, u32[]{:S(2)}, u32[]{:S(2)}) collective-permute-start(bf16[256,1024]{1,0:T(8,128)(2,1)S(1)} %collective-permute-done.10.refs_2_), channel_id=1, source_target_pairs={{0,1},{1,0},{2,3},{3,2},{4,5},{5,4},{6,7},{7,6},{8,9},{9,8},{10,11... | collective-permute-start | bytes 1572872 | tf_op jit(solution)/shard_map/ppermute | solution.py:20
  224.4 0.8 copy-start.3
  236.3 1.0 copy-start.4

commit v2 on v1

--- a/solution.py
+++ b/solution.py
@@ -32,41 +32,98 @@
     return pl.CostEstimate(flops=int(flops), bytes_accessed=int(nbytes), transcendentals=int(trans))
 
 
-def near_kernel(half, place, *refs):
+def near_kernel(half, tiles, place, *refs):
     blocks = refs[:half]
-    w_ref, out_ref = refs[half:]
+    w_ref, out_ref, lhs, wbuf, lsem, wsem = refs[half:]
     depth = blocks[0].shape[1]
+    span = wbuf.shape[2]
     slot = lax.rem(place[0], half)
-    total = None
+    base = (place[0] // half) * (half * depth)
+
+    def w_copy(n):
+        lines = pl.ds(pl.multiple_of(base, half * depth), half * depth)
+        wide = pl.ds(pl.multiple_of(lax.rem(n, tiles) * span, span), span)
+        return pltpu.make_async_copy(w_ref.at[n // tiles, lines, wide], wbuf.at[n], wsem.at[n])
+
+    def l_copy(d):
+        deep = pl.ds(pl.multiple_of((slot ^ d) * depth, depth), depth)
+        return pltpu.make_async_copy(blocks[d], lhs.at[:, deep], lsem.at[d])
+
+    count = wbuf.shape[0]
+    w_copy(0).start()
     for d in range(half):
-        deep = pl.ds(pl.multiple_of((slot ^ d) * depth, depth), depth)
-        part = jnp.dot(blocks[d][...], w_ref[0, deep, :], preferred_element_type=F32)
-        total = part if total is None else total + part
-    out_ref[0] = total
+        l_copy(d).start()
+    for n in range(1, count):
+        w_copy(n).start()
+    for d in range(half):
+        l_copy(d).wait()
+
+    def body(n, carry):
+        w_copy(n).wait()
+        wide = pl.ds(pl.multiple_of(lax.rem(n, tiles) * span, span), span)
+        total = None
+        for d in range(half):
+            deep = slice(d * depth, (d + 1) * depth)
+            part = jnp.dot(lhs[:, deep], wbuf[n, deep, :], preferred_element_type=F32)
+            total = part if total is None else total + part
+        out_ref[n // tiles, :, wide] = total
+        return carry
+
+    lax.fori_loop(0, count, body, 0)
 
 
 def near_product(place, blocks, weights):
     half = len(blocks)
     rows, depth = blocks[0].shape
     gates, _, width = weights.shape
-    tn = tile_of(width, 512)
-    spec = pl.BlockSpec((rows, depth), lambda g, n, p: (0, 0))
+    span = tile_of(width, 512)
+    tiles = width // span
+    anywhere = pl.BlockSpec(memory_space=pl.ANY)
     return pl.pallas_call(
-        functools.partial(near_kernel, half),
+        functools.partial(near_kernel, half, tiles),
         out_shape=jax.ShapeDtypeStruct((gates, rows, width), F32),
-        grid_spec=pltpu.PrefetchScalarGridSpec(
-            num_scalar_prefetch=1,
-            grid=(gates, width // tn),
-            in_specs=[spec] * half
-            + [pl.BlockSpec((1, half * depth, tn), lambda g, n, p: (g, p[0] // half, n))],
-            out_specs=pl.BlockSpec((1, rows, tn), lambda g, n, p: (g, 0, n)),
-        ),
-        compiler_params=params(24),
+        in_specs=[pl.BlockSpec(memory_space=pltpu.SMEM)]
+        + [anywhere] * half
+        + [pl.BlockSpec(memory_space=pltpu.HBM)],
+        out_specs=pl.BlockSpec(memory_space=pltpu.VMEM),
+        scratch_shapes=[
+            pltpu.VMEM((rows, half * depth), BF16),
+            pltpu.VMEM((gates * tiles, half * depth, span), BF16),
+            pltpu.SemaphoreType.DMA((half,)),
+            pltpu.SemaphoreType.DMA((gates * tiles,)),
+        ],
+        compiler_params=params(28),
         cost_estimate=cost(
             2 * gates * rows * half * depth * width,
             gates * width * (half * depth * 2 + rows * 4) + half * rows * depth * 2,
         ),
     )(place, *blocks, weights)
+
+
+def split_kernel(sizes, src, *refs):
+    outs, sem = refs[:-1], refs[-1]
+    copies, first = [], 0
+    for k, rows in enumerate(sizes):
+        copies.append(pltpu.make_async_copy(src.at[first : first + rows, :], outs[k], sem.at[k]))
+        first += rows
+    for copy in copies:
+        copy.start()
+    for copy in copies:
+        copy.wait()
+
+
+def split_rows(array, sizes):
+    vmem = pl.BlockSpec(memory_space=pltpu.VMEM)
+    return pl.pallas_call(
+        functools.partial(split_kernel, sizes),
+        out_shape=[jax.ShapeDtypeStruct((rows, array.shape[1]), array.dtype) for rows in sizes],
+        in_specs=[pl.BlockSpec(memory_space=pltpu.HBM)],
+        out_specs=[vmem] * len(sizes),
+        scratch_shapes=[pltpu.SemaphoreType.DMA((len(sizes),))],
+        compiler_params=params(12),
+        cost_estimate=cost(0, 4 * array.shape[0] * array.shape[1]),
+        name="split",
+    )(array)
 
 
 def compose_rows(maps, count, a, b):
@@ -103,7 +160,7 @@
     return keep + bend, update * squashed - bend * prev
 
 
-def gate_kernel(half, chunk, rows, before, last, place, *refs):
+def gate_kernel(half, chunk, first_row, rows, before, last, place, *refs):
     blocks = refs[:half]
     part_ref, w_ref, bias_ref, gain_ref, start_ref = refs[half : half + 5]
     earlier = refs[half + 5 : half + 5 + before]
@@ -128,7 +185,7 @@
         deep = pl.ds(pl.multiple_of((slot ^ d) * depth, depth), depth)
         return pltpu.make_async_copy(blocks[d], lhs.at[:, deep], lsem.at[d])
 
-    p_copy = pltpu.make_async_copy(part_ref.at[:, chunk * rows : (chunk + 1) * rows, :], pbuf, psem)
+    p_copy = pltpu.make_async_copy(part_ref.at[:, first_row : first_row + rows, :], pbuf, psem)
     for d in range(half):
         l_copy(d).start()
     for k in range(steps):
@@ -206,7 +263,9 @@
             total_ref[i, 1:2, :] = tb
 
 
-def gate_chunk(place, blocks, partial, weights, biases, gain, start, earlier, chunk, last, peers):
+def gate_chunk(
+    place, blocks, partial, weights, biases, gain, start, earlier, chunk, first_row, last, peers
+):
     half = len(blocks)
     rows, depth = blocks[0].shape
     gates, _, width = weights.shape
@@ -221,10 +280,11 @@
     if last:
         out_shape.append(jax.ShapeDtypeStruct((peers, 2, width), F32))
     return pl.pallas_call(
-        functools.partial(gate_kernel, half, chunk, rows, len(earlier), last),
+        functools.partial(gate_kernel, half, chunk, first_row, rows, len(earlier), last),
         out_shape=out_shape,
         in_specs=[pl.BlockSpec(memory_space=pltpu.SMEM)]
-        + [anywhere] * (half + 2)
+        + [anywhere] * (half + 1)
+        + [pl.BlockSpec(memory_space=pltpu.HBM)]
         + [vmem] * (3 + len(earlier)),
         out_specs=[vmem] * len(out_shape),
         scratch_shapes=[
@@ -237,7 +297,7 @@
             pltpu.SemaphoreType.DMA((steps,)),
             pltpu.SemaphoreType.DMA,
         ],
-        compiler_params=params(24),
+        compiler_params=params(32),
         cost_estimate=cost(
             2 * gates * rows * half * depth * width,
             gates * width * (half * depth * 2 + rows * 6) + half * rows * depth * 2,
@@ -265,9 +325,12 @@
     gates = refs[:chunks]
     maps = refs[chunks : 2 * chunks]
     peer_ref, gain_ref, start_ref, run_ref, maps_ref, total_ref, enter = refs[2 * chunks :]
-    rows, span = gates[0].shape[1:]
+    span = gates[0].shape[2]
     width = gain_ref.shape[1]
-    seg = rows // SEGS
+    heights = [g.shape[1] for g in gates]
+    firsts = [sum(heights[:c]) for c in range(chunks)]
+    least = min(heights)
+    turns = least // SEGS // 2
     n = pl.program_id(0)
 
     @pl.when(n == 0)
@@ -277,34 +340,41 @@
     wide = pl.ds(pl.multiple_of(n * span, span), span)
     gain = jnp.broadcast_to(gain_ref[:, wide], (SEGS, span))
 
-    def pair(jj, carry, first):
+    def advance(c, jj, held, first):
+        state, a, b = held
         lines = pl.ds(pl.multiple_of(jj * 2 * SEGS, 2 * SEGS), 2 * SEGS)
+        pre2 = gates[c][0, lines, :].astype(F32)
+        cand2 = gates[c][1, lines, :].astype(F32)
+        for k in range(2):
+            pre = pre2[k * SEGS : (k + 1) * SEGS]
+            cand = cand2[k * SEGS : (k + 1) * SEGS]
+            update, keep, scaled, slope, offset = first_slopes(pre, cand, gain)
+            if first and k == 0:
+                prev = lead_row(place, start_ref[:, wide], (SEGS, span))
+                slope, offset = around(update, keep, scaled, cand, gain, prev)
+            slope2, offset2 = around(update, keep, scaled, cand, gain, state)
+            state = slope * state + offset
+            b = slope2 * b + offset2
+            a = slope2 * a
+            row = pl.ds(pl.multiple_of(firsts[c] + (2 * jj + k) * SEGS, SEGS), SEGS)
+            run_ref[0, row, :] = a
+            run_ref[1, row, :] = b
+        return state, a, b
+
+    def pair(turn, carry, first):
         out = []
         for c in range(chunks):
-            state, a, b = carry[c]
-            pre2 = gates[c][0, lines, :].astype(F32)
-            cand2 = gates[c][1, lines, :].astype(F32)
-            for k in range(2):
-                pre = pre2[k * SEGS : (k + 1) * SEGS]
-                cand = cand2[k * SEGS : (k + 1) * SEGS]
-                update, keep, scaled, slope, offset = first_slopes(pre, cand, gain)
-                if first and k == 0 and c == 0:
-                    prev = lead_row(place, start_ref[:, wide], (SEGS, span))
-                    slope, offset = around(update, keep, scaled, cand, gain, prev)
-                slope2, offset2 = around(update, keep, scaled, cand, gain, state)
-                state = slope * state + offset
-                b = slope2 * b + offset2
-                a = slope2 * a
-                row = pl.ds(pl.multiple_of(c * rows + (2 * jj + k) * SEGS, SEGS), SEGS)
-                run_ref[0, row, :] = a
-                run_ref[1, row, :] = b
-            out.append((state, a, b))
+            held = carry[c]
+            times = heights[c] // least
+            for r in range(times):
+                held = advance(c, turn * times + r, held, first and c == 0 and r == 0)
+            out.append(held)
         return tuple(out)
 
     one, zero = jnp.ones((SEGS, span), F32), jnp.zeros((SEGS, span), F32)
     carry = tuple((enter[c * SEGS : (c + 1) * SEGS, wide], one, zero) for c in range(chunks))
     carry = pair(0, carry, True)
-    carry = lax.fori_loop(1, seg // 2, lambda jj, c: pair(jj, c, False), carry)
+    carry = lax.fori_loop(1, turns, lambda turn, c: pair(turn, c, False), carry)
     for c in range(chunks):
         maps_ref[0, c * SEGS : (c + 1) * SEGS, wide] = carry[c][1]
         maps_ref[1, c * SEGS : (c + 1) * SEGS, wide] = carry[c][2]
@@ -321,25 +391,26 @@
 def bend_all(place, gates, maps, peer_maps, gain, start):
     chunks = len(gates)
     peers = peer_maps.shape[0]
-    _, rows, width = gates[0].shape
+    width = gates[0].shape[2]
+    total_rows = sum(g.shape[1] for g in gates)
     tn = tile_of(width, 256)
     row_spec = pl.BlockSpec((1, width), lambda n, p: (0, 0))
     total_spec = pl.BlockSpec((peers, 2, width), lambda n, p: (0, 0, 0))
     return pl.pallas_call(
         functools.partial(bend_kernel, chunks, peers),
         out_shape=[
-            jax.ShapeDtypeStruct((2, chunks * rows, width), F32),
+            jax.ShapeDtypeStruct((2, total_rows, width), F32),
             jax.ShapeDtypeStruct((2, chunks * SEGS, width), F32),
             jax.ShapeDtypeStruct((peers, 2, width), F32),
         ],
         grid_spec=pltpu.PrefetchScalarGridSpec(
             num_scalar_prefetch=1,
             grid=(width // tn,),
-            in_specs=[pl.BlockSpec((2, rows, tn), lambda n, p: (0, 0, n))] * chunks
+            in_specs=[pl.BlockSpec((2, g.shape[1], tn), lambda n, p: (0, 0, n)) for g in gates]
             + [pl.BlockSpec((2, SEGS, width), lambda n, p: (0, 0, 0))] * chunks
             + [total_spec, row_spec, row_spec],
             out_specs=[
-                pl.BlockSpec((2, chunks * rows, tn), lambda n, p: (0, 0, n)),
+                pl.BlockSpec((2, total_rows, tn), lambda n, p: (0, 0, n)),
                 pl.BlockSpec((2, chunks * SEGS, width), lambda n, p: (0, 0, 0)),
                 total_spec,
             ],
@@ -347,7 +418,7 @@
         ),
         compiler_params=params(16),
         cost_estimate=cost(
-            40 * chunks * rows * width, 12 * chunks * rows * width, 5 * chunks * rows * width
+            40 * total_rows * width, 12 * total_rows * width, 5 * total_rows * width
         ),
         name="bend",
     )(place, *gates, *maps, peer_maps, gain, start)
@@ -375,7 +446,7 @@
         out_ref[:, l * LANES : (l + 1) * LANES] = flat[l].astype(BF16)
 
 
-def state_chunk(place, run, maps, peer_maps, start, rows, chunk):
+def state_chunk(place, run, maps, peer_maps, start, first_row, rows, chunk):
     width = run.shape[2]
     peers = peer_maps.shape[0]
     segs = maps.shape[1]
@@ -387,7 +458,7 @@
             num_scalar_prefetch=1,
             grid=(width // tn,),
             in_specs=[
-                pl.BlockSpec((2, rows, tn), lambda n, p: (0, chunk, n)),
+                pl.BlockSpec((2, rows, tn), lambda n, p: (0, first_row // rows, n)),
                 pl.BlockSpec((2, segs, tn), lambda n, p: (0, 0, n)),
                 pl.BlockSpec((peers, 2, tn), lambda n, p: (0, 0, n)),
                 pl.BlockSpec((1, tn), lambda n, p: (0, n)),
@@ -405,7 +476,8 @@
     blocks = refs[:count]
     weights = refs[count : count + peers * pieces]
     out_ref, lhs, wbuf, acc, lsem, wsem = refs[-6:]
-    rows, depth = blocks[0].shape
+    depth = blocks[0].shape[1]
+    heights = [blocks[c * group].shape[0] for c in range(groups)]
     lines_of = weights[0].shape[0]
     outer = peers // 2
 
@@ -416,7 +488,8 @@
 
     def l_copy(c, d):
         deep = pl.ds(pl.multiple_of((place[0] ^ d) * depth, depth), depth)
-        dst = lhs.at[c * rows : (c + 1) * rows, deep]
+        top = sum(heights[:c])
+        dst = lhs.at[top : top + heights[c], deep]
         return pltpu.make_async_copy(blocks[c * group + d], dst, lsem.at[c, d])
 
     for c in range(groups):
@@ -446,10 +519,10 @@
 
 def mix_rows(place, blocks, weights, whole, first, total_rows, pieces):
     groups, group = len(blocks), len(blocks[0])
-    rows, depth = blocks[0][0].shape
+    depth = blocks[0][0].shape[1]
     lines_of, width = weights[0].shape
     peers = len(weights) // pieces
-    here = groups * rows
+    here = sum(g[0].shape[0] for g in blocks)
     anywhere = pl.BlockSpec(memory_space=pl.ANY)
     args = [place] + [b for g in blocks for b in g] + list(weights)
     in_specs = [anywhere] * (groups * group + len(weights))
@@ -483,7 +556,7 @@
 
 
 EARLY = 5
-CHUNKS = 4
+SHARES = (2, 1, 1)
 
 
 def pieces_of(lines_of):
@@ -534,18 +607,16 @@
     group = lax.axis_size("ch")
     half = group // 2
     total_rows = tokens.shape[0]
-    chunks = CHUNKS
-    rows = total_rows // chunks
+    chunks = len(SHARES)
+    sizes = [total_rows * share // sum(SHARES) for share in SHARES]
+    firsts = [sum(sizes[:c]) for c in range(chunks)]
     place = jnp.stack([lax.axis_index("ch"), lax.axis_index("ctx")]).astype(jnp.int32)
     biases = jnp.stack([bias_update, bias_cand], axis=0)
     gain = recur_gain[None, :]
     start = start_state[None, :]
 
     far = []
-    rest = tokens
-    for c in range(chunks):
-        piece = rest[c * rows : (c + 1) * rows]
-        rest, piece = lax.optimization_barrier((rest, piece))
+    for piece in split_rows(tokens, sizes):
         far.append([swap(piece, "ch", half)])
     near = [tokens]
     for d in range(1, half):
@@ -559,7 +630,18 @@
     for c in range(chunks):
         last = c == chunks - 1
         out = gate_chunk(
-            place, far[c], partial, w_input, biases, gain, start, maps if last else [], c, last, peers
+            place,
+            far[c],
+            partial,
+            w_input,
+            biases,
+            gain,
+            start,
+            maps if last else [],
+            c,
+            firsts[c],
+            last,
+            peers,
         )
         gates.append(out[0])
         maps.append(out[1])
@@ -571,7 +653,7 @@
 
     blocks = []
     for c in range(chunks):
-        own = state_chunk(place, run, run_maps, peer_maps, start, rows, c)
+        own = state_chunk(place, run, run_maps, peer_maps, start, firsts[c], sizes[c], c)
         across = swap(own, "ch", half)
         blocks.append([own, across])
     for c in range(chunks):
@@ -587,7 +669,7 @@
     mixed = mix_rows(place, blocks[:split], weights, None, 0, total_rows, ring.pieces)
     if split < chunks:
         mixed = mix_rows(
-            place, blocks[split:], weights, mixed, split * rows, total_rows, ring.pieces
+            place, blocks[split:], weights, mixed, firsts[split], total_rows, ring.pieces
         )
     return mixed
 

time: 243 us -> 219 us (0.901)
  blocking collectives: 32.1 us -> 11.2 us
  waiting for transfers between devices: 88.4 us -> 75 us
  starting transfers between devices: 31.5 us -> 44.5 us
  local copies, waits for them, and re-layouts: 17.8 us -> 10.6 us
  Pallas kernels: 72.3 us -> 76.4 us
    ppermute x29 -> x24, waiting for transfers between devices: 88.4 us -> 73 us  [swap(): lax.ppermute(block, axis, [(i, i ^ bits) for i in range(lax.axis_size(axi...]
    all_to_all x1 -> x0, blocking collectives: 11.2 us -> none  [layer(): peer_maps = lax.all_to_all(totals, 'ctx', 0, 0, tiled=True)]
    all_to_all x1, blocking collectives: 20.9 us -> 11.2 us  [layer(): peer_maps = lax.all_to_all(out[2], 'ctx', 0, 0, tiled=True)]
    ppermute x6, starting transfers between devices: 10.3 us -> 18.5 us  [ring_step(): self.held[s, 0, p] = lax.ppermute(block, 'ctx', route)]
    slice x4 -> x0, local copies, waits for them, and re-layouts: 4.31 us -> none  [layer(): piece = rest[c * rows:(c + 1) * rows]]
    unnamed x20, local copies, waits for them, and re-layouts: 13.4 us -> 9.28 us
    pallas_call x5, Pallas kernels: 41.2 us -> 44.6 us  [the longest x3 30.2 us: gate_chunk(): pl.pallas_call(functools.partial(gate_kernel, half, chunk, first_row, row...]
    all_to_all x0 -> x1, starting transfers between devices: none -> 3.35 us  [layer(): peer_maps = lax.all_to_all(totals, 'ctx', 0, 0, tiled=True)]
  transfers between devices with their start and end apart: 35 -> 31, of which waited for: 11 -> 11; matrix products, arithmetic and copies ran while one was open for 2% -> 1% of each run, Pallas kernels for 28% -> 33%
where the time goes in v2:
time: 219 us; the launch traced here: 218 us
  Pallas kernels  76.4 us (35%)
  waiting for transfers between devices  75 us (34%)
  starting transfers between devices  44.5 us (20%)
  blocking collectives  11.2 us (5%)
  local copies, waits for them, and re-layouts  10.6 us (5%)
    ppermute x24, waiting for transfers between devices, swap(): lax.ppermute(block, axis, [(i, i ^ bits) for i in range(lax.axis_size(axi...  73 us
    pallas_call x3, Pallas kernels, gate_chunk(): pl.pallas_call(functools.partial(gate_kernel, half, chunk, first_row, row...  30.2 us
    ppermute x24, starting transfers between devices, swap(): lax.ppermute(block, axis, [(i, i ^ bits) for i in range(lax.axis_size(axi...  22.6 us
    ppermute x6, starting transfers between devices, ring_step(): self.held[s, 0, p] = lax.ppermute(block, 'ctx', route)  18.5 us
    pallas_call x2, Pallas kernels, mix_rows(): pl.pallas_call(functools.partial(mix_kernel, groups, group, pieces, peers...  17 us
    pallas_call x1, Pallas kernels, near_product(): pl.pallas_call(functools.partial(near_kernel, half, tiles), out_shape=jax...  13.5 us
    all_to_all x1, blocking collectives, layer(): peer_maps = lax.all_to_all(out[2], 'ctx', 0, 0, tiled=True)  11.2 us
    unnamed x20, local copies, waits for them, and re-layouts  9.28 us
  transfers between devices with their start and end apart: 31, of which 11 were waited for; matrix products, arithmetic and copies ran while one was open for 1% of the time, Pallas kernels for 33%

profile of v2, /device:TPU:0, one launch (start us, length us, event | category | flops | bytes accessed | tf_op | source)
XLA Modules:
  0.0 218.2 jit_solution(3286148098884528224)
XLA Ops:
  0.5 1.6 copy-done.2
  2.1 1.0 split.1
  3.1 2.5 %collective-permute-start = (bf16[512,1024]{1,0:T(8,128)(2,1)S(1)}, bf16[512,1024]{1,0:T(8,128)(2,1)}, u32[]{:S(2)}, u32[]{:S(2)}) collective-permute-start(bf16[512,1024]{1,0:T(8,128)(2,1)S(1)} %get-tuple-element.21), channel_id=1, source_target_pairs={{0,2},{1,3},{2,0},{3,1},{4,6},{5,7},{6,4},{7,5},{8,10},{9,11},{10,... | collective-permute-start | bytes 3145736 | tf_op jit(solution)/shard_map/ppermute | solution.py:20
  5.7 24.0 %collective-permute-done.refs_0_ = bf16[512,1024]{1,0:T(8,128)(2,1)} collective-permute-done((bf16[512,1024]{1,0:T(8,128)(2,1)S(1)}, bf16[512,1024]{1,0:T(8,128)(2,1)}, u32[]{:S(2)}, u32[]{:S(2)}) %collective-permute-start) | collective-permute-done | bytes 1048608 | tf_op jit(solution)/shard_map/ppermute | solution.py:20
  29.7 1.3 fusion
  31.0 2.2 collective-permute-start.13
  33.2 1.5 collective-permute-start.11
  34.8 6.0 %collective-permute-done.3.refs_0_ = bf16[256,1024]{1,0:T(8,128)(2,1)} collective-permute-done((bf16[256,1024]{1,0:T(8,128)(2,1)}, bf16[256,1024]{1,0:T(8,128)(2,1)}, u32[]{:S(2)}, u32[]{:S(2)}) %collective-permute-start.3) | collective-permute-done | bytes 524320 | tf_op jit(solution)/shard_map/ppermute | solution.py:20
  40.8 1.7 collective-permute-start.5
  42.5 13.5 %shard_map.73.refs_2_ = f32[2,1024,1024]{2,1,0:T(8,128)S(1)} custom-call(s32[2]{0:T(128)S(1)} %pad_add_fusion.place, bf16[1024,1024]{1,0:T(8,128)(2,1)S(1)} %copy-done.3, bf16[1024,1024]{1,0:T(8,128)(2,1)} %collective-permute-done.2.refs_1_, bf16[2,4096,1024]{2,1,0:T(8,128)(2,1)} %refs_3_.5), custom_call_target="tpu_custom_call" | custom-call | flops 8589934592 | bytes 20971520 | tf_op jit(solution)/shard_map/pallas_call | solution.py:82
  56.0 1.6 collective-permute-start.12
  57.7 1.6 collective-permute-start.17
  59.3 14.5 %shard_map.74 = (bf16[2,512,1024]{2,1,0:T(8,128)(2,1)S(1)}, f32[2,8,1024]{2,1,0:T(8,128)S(1)}) custom-call(s32[2]{0:T(128)S(1)} %pad_add_fusion.place, bf16[512,1024]{1,0:T(8,128)(2,1)} %collective-permute-done.refs_0_, bf16[512,1024]{1,0:T(8,128)(2,1)} %collective-permute-done.1.refs_1_, f32[2,1024,1024]{2,1,0:T(8,128)S(1)} %shard_map.73.refs_2_, ...), custom_call_target="tpu_custom_call" | custom-call | flops 4294967296 | bytes 16777216 | tf_op jit(solution)/shard_map/pallas_call | solution.py:282
  73.8 7.9 %shard_map.75 = (bf16[2,256,1024]{2,1,0:T(8,128)(2,1)S(1)}, f32[2,8,1024]{2,1,0:T(8,128)S(1)}) custom-call(s32[2]{0:T(128)S(1)} %pad_add_fusion.place, bf16[256,1024]{1,0:T(8,128)(2,1)} %collective-permute-done.3.refs_0_, bf16[256,1024]{1,0:T(8,128)(2,1)S(1)} %collective-permute-done.4.refs_1_, f32[2,1024,1024]{2,1,0:T(8,128)S(1)} %shard_map.73.refs_2_, ...), custom_call_target="tpu_custom_call" | custom-call | flops 2147483648 | bytes 12582912 | tf_op jit(solution)/shard_map/pallas_call | solution.py:282
  81.7 7.8 %shard_map.76 = (bf16[2,256,1024]{2,1,0:T(8,128)(2,1)S(1)}, f32[2,8,1024]{2,1,0:T(8,128)S(1)}, f32[8,2,1024]{2,1,0:T(2,128)S(1)}) custom-call(s32[2]{0:T(128)S(1)} %pad_add_fusion.place, bf16[256,1024]{1,0:T(8,128)(2,1)S(1)} %collective-permute-done.5.refs_0_, bf16[256,1024]{1,0:T(8,128)(2,1)S(1)} %collective-permute-done.6.refs_1_, ...), custom_call_target="tpu_custom_call" | custom-call | flops 2147483648 | bytes 12582912 | tf_op jit(solution)/shard_map/pallas_call | solution.py:282
  89.5 11.2 %all_to_all.10.refs_6_ = f32[8,2,1024]{2,1,0:T(2,128)S(1)} all-to-all(f32[8,2,1024]{2,1,0:T(2,128)S(1)} %get-tuple-element.30), channel_id=1, replica_groups=mesh['ctx'=8,'ch'=4] {'ctx'}, dimensions={0} | all-to-all | bytes 131072 | tf_op jit(solution)/shard_map/all_to_all | solution.py:648
  100.7 7.7 %bend.1 = (f32[2,1024,1024]{2,1,0:T(8,128)S(1)}, f32[2,24,1024]{2,1,0:T(8,128)S(1)}, f32[8,2,1024]{2,1,0:T(2,128)}) custom-call(s32[2]{0:T(128)S(1)} %pad_add_fusion.place, bf16[2,512,1024]{2,1,0:T(8,128)(2,1)S(1)} %get-tuple-element.22.refs_0_, bf16[2,256,1024]{2,1,0:T(8,128)(2,1)S(1)} %get-tuple-element.24.refs_1_, ...), custom_call_target="tpu_custom_call" | custom-call | flops 41943040 | bytes 12582912 | tf_op jit(solution)/shard_map/bend/pallas_call | solution.py:399
  108.3 3.3 %copy-done = f32[2,1024,1024]{2,1,0:T(8,128)} copy-done((f32[2,1024,1024]{2,1,0:T(8,128)}, f32[2,1024,1024]{2,1,0:T(8,128)S(1)}, u32[]{:S(2)}) %copy-start) | copy-done | bytes 8388632
  111.6 3.4 %all-to-all-start.1 = ((f32[8,2,1024]{2,1,0:T(2,128)}), f32[8,2,1024]{2,1,0:T(2,128)S(1)}, u32[]{:S(2)}, u32[]{:S(2)}) async-start(f32[8,2,1024]{2,1,0:T(2,128)} %get-tuple-element.33), calls=%async_computation.1 | async-start | bytes 131072 | tf_op jit(solution)/shard_map/all_to_all | solution.py:650
  115.0 1.9 collective-permute-start.10
  116.9 1.5 collective-permute-start.16
  118.4 0.6 collective-permute-start.15
  118.9 1.5 collective-permute-start.14
  120.4 1.9 all-to-all-done.1.peer_ref
  122.3 3.4 %copy-done.1 = f32[2,1024,1024]{2,1,0:T(8,128)S(1)} copy-done((f32[2,1024,1024]{2,1,0:T(8,128)S(1)}, f32[2,1024,1024]{2,1,0:T(8,128)}, u32[]{:S(2)}) %copy-start.1) | copy-done | bytes 8388632
  125.6 3.3 %shard_map.78.refs_0_ = bf16[512,1024]{1,0:T(8,128)(2,1)S(1)} custom-call(s32[2]{0:T(128)S(1)} %pad_add_fusion.place, f32[2,1024,1024]{2,1,0:T(8,128)S(1)} %copy-done.1, f32[2,24,1024]{2,1,0:T(8,128)S(1)} %get-tuple-element.32.maps_ref, f32[8,2,1024]{2,1,0:T(2,128)S(1)} %all-to-all-done.1.peer_ref, f32[1,1024]{1,0:T(1,128)S(1)} %bitcast.10), custom_call_target="tpu_custom_call" | custom-call | flops 1048576 | bytes 5242880 | tf_op jit(solution)/shard_map/pallas_call | solution.py:454
  129.0 0.6 collective-permute-start.25
  129.6 2.0 shard_map.77.refs_0_
  131.7 10.2 %collective-permute-start.20 = (bf16[256,1024]{1,0:T(8,128)(2,1)}, bf16[256,1024]{1,0:T(8,128)(2,1)S(1)}, u32[]{:S(2)}, u32[]{:S(2)}) collective-permute-start(bf16[256,1024]{1,0:T(8,128)(2,1)} %collective-permute-done.16.refs_16_.refs_12_), channel_id=1, source_target_pairs={{0,8},{4,12},{8,16},{12,20},{16,24},{20,28},{24,0},{28,4},{1,9},{5... | collective-permute-start | bytes 1572872 | tf_op jit(solution)/shard_map/ppermute | solution.py:582
  141.9 1.5 collective-permute-start.8
  143.4 9.6 %collective-permute-done.14.refs_14_.refs_10_ = bf16[256,1024]{1,0:T(8,128)(2,1)} collective-permute-done((bf16[256,1024]{1,0:T(8,128)(2,1)S(1)}, bf16[256,1024]{1,0:T(8,128)(2,1)}, u32[]{:S(2)}, u32[]{:S(2)}) %collective-permute-start.14) | collective-permute-done | bytes 524320 | tf_op jit(solution)/shard_map/ppermute | solution.py:20
  153.1 1.5 collective-permute-start.21
  154.5 1.9 shard_map.79.refs_4_
  156.5 0.6 collective-permute-start.28
  157.1 5.3 %collective-permute-done.18.refs_18_.refs_14_ = bf16[256,1024]{1,0:T(8,128)(2,1)S(1)} collective-permute-done((bf16[256,1024]{1,0:T(8,128)(2,1)}, bf16[256,1024]{1,0:T(8,128)(2,1)S(1)}, u32[]{:S(2)}, u32[]{:S(2)}) %collective-permute-start.18) | collective-permute-done | bytes 524320 | tf_op jit(solution)/shard_map/ppermute | solution.py:20
  162.4 3.9 %collective-permute-done.8.refs_2_ = bf16[256,1024]{1,0:T(8,128)(2,1)S(1)} collective-permute-done((bf16[256,1024]{1,0:T(8,128)(2,1)S(1)}, bf16[256,1024]{1,0:T(8,128)(2,1)S(1)}, u32[]{:S(2)}, u32[]{:S(2)}) %collective-permute-start.8) | collective-permute-done | bytes 524320 | tf_op jit(solution)/shard_map/ppermute | solution.py:20
  166.3 4.1 %collective-permute-start.19 = (bf16[256,1024]{1,0:T(8,128)(2,1)S(1)}, bf16[256,1024]{1,0:T(8,128)(2,1)S(1)}, u32[]{:S(2)}, u32[]{:S(2)}) collective-permute-start(bf16[256,1024]{1,0:T(8,128)(2,1)S(1)} %collective-permute-done.17.refs_17_.refs_13_), channel_id=1, source_target_pairs={{0,4},{4,0},{8,12},{12,8},{16,20},{20,16},{24,28},{28,24},{1,5},{5... | collective-permute-start | bytes 1572872 | tf_op jit(solution)/shard_map/ppermute | solution.py:20
  170.4 0.5 collective-permute-start.26
  170.9 3.1 %collective-permute-done.28.refs_6_ = bf16[256,1024]{1,0:T(8,128)(2,1)S(1)} collective-permute-done((bf16[256,1024]{1,0:T(8,128)(2,1)S(1)}, bf16[256,1024]{1,0:T(8,128)(2,1)S(1)}, u32[]{:S(2)}, u32[]{:S(2)}) %collective-permute-start.28) | collective-permute-done | bytes 524320 | tf_op jit(solution)/shard_map/ppermute | solution.py:20
  174.1 2.0 collective-permute-start.22
  176.0 6.7 %collective-permute-done.19.refs_19_.refs_15_ = bf16[256,1024]{1,0:T(8,128)(2,1)S(1)} collective-permute-done((bf16[256,1024]{1,0:T(8,128)(2,1)S(1)}, bf16[256,1024]{1,0:T(8,128)(2,1)S(1)}, u32[]{:S(2)}, u32[]{:S(2)}) %collective-permute-start.19) | collective-permute-done | bytes 524320 | tf_op jit(solution)/shard_map/ppermute | solution.py:20
  182.7 2.5 %collective-permute-start.23 = (bf16[256,1024]{1,0:T(8,128)(2,1)S(1)}, bf16[256,1024]{1,0:T(8,128)(2,1)S(1)}, u32[]{:S(2)}, u32[]{:S(2)}) collective-permute-start(bf16[256,1024]{1,0:T(8,128)(2,1)S(1)} %collective-permute-done.21.refs_21_.refs_17_), channel_id=1, source_target_pairs={{0,4},{4,0},{8,12},{12,8},{16,20},{20,16},{24,28},{28,24},{1,5},{5... | collective-permute-start | bytes 1572872 | tf_op jit(solution)/shard_map/ppermute | solution.py:20
  185.2 8.7 %collective-permute-done.22.refs_22_.refs_18_ = bf16[256,1024]{1,0:T(8,128)(2,1)S(1)} collective-permute-done((bf16[256,1024]{1,0:T(8,128)(2,1)S(1)}, bf16[256,1024]{1,0:T(8,128)(2,1)S(1)}, u32[]{:S(2)}, u32[]{:S(2)}) %collective-permute-start.22) | collective-permute-done | bytes 524320 | tf_op jit(solution)/shard_map/ppermute | solution.py:20
  193.9 0.5 collective-permute-start.9
  194.4 5.7 %collective-permute-done.23.refs_23_.refs_19_ = bf16[256,1024]{1,0:T(8,128)(2,1)S(1)} collective-permute-done((bf16[256,1024]{1,0:T(8,128)(2,1)S(1)}, bf16[256,1024]{1,0:T(8,128)(2,1)S(1)}, u32[]{:S(2)}, u32[]{:S(2)}) %collective-permute-start.23) | collective-permute-done | bytes 524320 | tf_op jit(solution)/shard_map/ppermute | solution.py:20
  200.0 1.0 copy-done.9
  201.0 11.7 %shard_map.80.refs_20_ = bf16[1024,1024]{1,0:T(8,128)(2,1)} custom-call(s32[2]{0:T(128)S(1)} %pad_add_fusion.place, bf16[512,1024]{1,0:T(8,128)(2,1)S(1)} %shard_map.78.refs_0_, bf16[512,1024]{1,0:T(8,128)(2,1)S(1)} %collective-permute-done.24.refs_1_, bf16[512,1024]{1,0:T(8,128)(2,1)S(1)} %collective-permute-done.25.refs_2_, bf16[512,1024]{1,0:T(8,128)(2,1)} %copy-done.9, ...), custom_call_target="tpu_custom_call" | custom-call | flops 6442450944 | bytes 16252928 | tf_op jit(solution)/shard_map/pallas_call | solution.py:534
  212.7 5.3 %shard_map.81 = bf16[1024,1024]{1,0:T(8,128)(2,1)} custom-call(s32[2]{0:T(128)S(1)} %pad_add_fusion.place, bf16[256,1024]{1,0:T(8,128)(2,1)S(1)} %shard_map.77.refs_0_, bf16[256,1024]{1,0:T(8,128)(2,1)S(1)} %collective-permute-done.7.refs_1_, bf16[256,1024]{1,0:T(8,128)(2,1)S(1)} %collective-permute-done.8.refs_2_, ...), custom_call_target="tpu_custom_call", output_to_operand_aliasing={{}: (21, {})} | custom-call | flops 2147483648 | bytes 11010048 | tf_op jit(solution)/shard_map/pallas_call | solution.py:534
  (49 shorter events, 1.0 us)
Async XLA Ops:
  0.0 42.5 %collective-permute-start.2 = (bf16[1024,1024]{1,0:T(8,128)(2,1)}, bf16[1024,1024]{1,0:T(8,128)(2,1)}, u32[]{:S(2)}, u32[]{:S(2)}) collective-permute-start(bf16[1024,1024]{1,0:T(8,128)(2,1)} %refs_0_.1), channel_id=1, source_target_pairs={{0,1},{1,0},{2,3},{3,2},{4,5},{5,4},{6,7},{7,6},{8,9},{9,8},{10,11... | collective-permute-start | bytes 6291464 | tf_op jit(solution)/shard_map/ppermute | solution.py:20
  0.5 1.6 copy-start.2
  2.1 32.7 %copy-start.7 = (f32[1024]{0:T(1024)S(1)}, f32[1024]{0:T(1024)}, u32[]{:S(2)}) copy-start(f32[1024]{0:T(1024)} %param.11) | copy-start | bytes 12292
  2.1 32.7 %copy-start.8 = (f32[1024]{0:T(1024)S(1)}, f32[1024]{0:T(1024)}, u32[]{:S(2)}) copy-start(f32[1024]{0:T(1024)} %param.10) | copy-start | bytes 12292
  2.1 40.5 %copy-start.3 = (bf16[1024,1024]{1,0:T(8,128)(2,1)S(1)}, bf16[1024,1024]{1,0:T(8,128)(2,1)}, u32[]{:S(2)}) copy-start(bf16[1024,1024]{1,0:T(8,128)(2,1)} %refs_0_.1) | copy-start | bytes 6291460
  3.1 27.9 %copy-start.6 = (bf16[256,1024]{1,0:T(8,128)(2,1)}, bf16[256,1024]{1,0:T(8,128)(2,1)S(1)}, u32[]{:S(2)}) copy-start(bf16[256,1024]{1,0:T(8,128)(2,1)S(1)} %get-tuple-element.25) | copy-start | bytes 1572868
  3.1 26.7 %collective-permute-start = (bf16[512,1024]{1,0:T(8,128)(2,1)S(1)}, bf16[512,1024]{1,0:T(8,128)(2,1)}, u32[]{:S(2)}, u32[]{:S(2)}) collective-permute-start(bf16[512,1024]{1,0:T(8,128)(2,1)S(1)} %get-tuple-element.21), channel_id=1, source_target_pairs={{0,2},{1,3},{2,0},{3,1},{4,6},{5,7},{6,4},{7,5},{8,10},{9,11},{10,... | collective-permute-start | bytes 3145736 | tf_op jit(solution)/shard_map/ppermute | solution.py:20
  5.6 35.2 %collective-permute-start.3 = (bf16[256,1024]{1,0:T(8,128)(2,1)}, bf16[256,1024]{1,0:T(8,128)(2,1)}, u32[]{:S(2)}, u32[]{:S(2)}) collective-permute-start(bf16[256,1024]{1,0:T(8,128)(2,1)} %get-tuple-element.23), channel_id=1, source_target_pairs={{0,2},{1,3},{2,0},{3,1},{4,6},{5,7},{6,4},{7,5},{8,10},{9,11},{10,... | collective-permute-start | bytes 1572872 | tf_op jit(solution)/shard_map/ppermute | solution.py:20
  29.7 29.5 %collective-permute-start.1 = (bf16[512,1024]{1,0:T(8,128)(2,1)}, bf16[512,1024]{1,0:T(8,128)(2,1)}, u32[]{:S(2)}, u32[]{:S(2)}) collective-permute-start(bf16[512,1024]{1,0:T(8,128)(2,1)} %collective-permute-done.refs_0_), channel_id=1, source_target_pairs={{0,1},{1,0},{2,3},{3,2},{4,5},{5,4},{6,7},{7,6},{8,9},{9,8},{10,11... | collective-permute-start | bytes 3145736 | tf_op jit(solution)/shard_map/ppermute | solution.py:20
  31.0 25.0 %collective-permute-start.13 = (bf16[256,1024]{1,0:T(8,128)(2,1)S(1)}, bf16[256,1024]{1,0:T(8,128)(2,1)}, u32[]{:S(2)}, u32[]{:S(2)}) collective-permute-start(bf16[256,1024]{1,0:T(8,128)(2,1)S(1)} %get-tuple-element.37.refs_9_.refs_5_), channel_id=1, source_target_pairs={{0,8},{4,12},{8,16},{12,20},{16,24},{20,28},{24,0},{28,4},{1,9},{5... | collective-permute-start | bytes 1572872 | tf_op jit(solution)/shard_map/ppermute | solution.py:582
  33.2 85.8 %collective-permute-start.11 = (bf16[256,1024]{1,0:T(8,128)(2,1)S(1)}, bf16[256,1024]{1,0:T(8,128)(2,1)}, u32[]{:S(2)}, u32[]{:S(2)}) collective-permute-start(bf16[256,1024]{1,0:T(8,128)(2,1)S(1)} %get-tuple-element.37.refs_9_.refs_5_), channel_id=1, source_target_pairs={{0,4},{4,0},{8,12},{12,8},{16,20},{20,16},{24,28},{28,24},{1,5},{5... | collective-permute-start | bytes 1572872 | tf_op jit(solution)/shard_map/ppermute | solution.py:20
  40.8 18.5 %copy-start.4 = (f32[1024]{0:T(1024)S(1)}, f32[1024]{0:T(1024)}, u32[]{:S(2)}) copy-start(f32[1024]{0:T(1024)} %param.13) | copy-start | bytes 12292
  40.8 18.5 %copy-start.5 = (f32[1024]{0:T(1024)S(1)}, f32[1024]{0:T(1024)}, u32[]{:S(2)}) copy-start(f32[1024]{0:T(1024)} %param.12) | copy-start | bytes 12292
  40.8 16.9 %collective-permute-start.5 = (bf16[256,1024]{1,0:T(8,128)(2,1)}, bf16[256,1024]{1,0:T(8,128)(2,1)S(1)}, u32[]{:S(2)}, u32[]{:S(2)}) collective-permute-start(bf16[256,1024]{1,0:T(8,128)(2,1)} %copy-done.6), channel_id=1, source_target_pairs={{0,2},{1,3},{2,0},{3,1},{4,6},{5,7},{6,4},{7,5},{8,10},{9,11},{10,... | collective-permute-start | bytes 1572872 | tf_op jit(solution)/shard_map/ppermute | solution.py:20
  42.5 31.2 %collective-permute-start.4 = (bf16[256,1024]{1,0:T(8,128)(2,1)}, bf16[256,1024]{1,0:T(8,128)(2,1)S(1)}, u32[]{:S(2)}, u32[]{:S(2)}) collective-permute-start(bf16[256,1024]{1,0:T(8,128)(2,1)} %collective-permute-done.3.refs_0_), channel_id=1, source_target_pairs={{0,1},{1,0},{2,3},{3,2},{4,5},{5,4},{6,7},{7,6},{8,9},{9,8},{10,11... | collective-permute-start | bytes 1572872 | tf_op jit(solution)/shard_map/ppermute | solution.py:20
  56.0 60.9 %collective-permute-start.12 = (bf16[256,1024]{1,0:T(8,128)(2,1)S(1)}, bf16[256,1024]{1,0:T(8,128)(2,1)S(1)}, u32[]{:S(2)}, u32[]{:S(2)}) collective-permute-start(bf16[256,1024]{1,0:T(8,128)(2,1)S(1)} %get-tuple-element.38.refs_8_.refs_4_), channel_id=1, source_target_pairs={{0,8},{4,12},{8,16},{12,20},{16,24},{20,28},{24,0},{28,4},{1,9},{5... | collective-permute-start | bytes 1572872 | tf_op jit(solution)/shard_map/ppermute | solution.py:582
  57.7 71.3 %collective-permute-start.17 = (bf16[256,1024]{1,0:T(8,128)(2,1)}, bf16[256,1024]{1,0:T(8,128)(2,1)S(1)}, u32[]{:S(2)}, u32[]{:S(2)}) collective-permute-start(bf16[256,1024]{1,0:T(8,128)(2,1)} %collective-permute-done.13.refs_13_.refs_9_), channel_id=1, source_target_pairs={{0,8},{4,12},{8,16},{12,20},{16,24},{20,28},{24,0},{28,4},{1,9},{5... | collective-permute-start | bytes 1572872 | tf_op jit(solution)/shard_map/ppermute | solution.py:582
  59.2 22.4 %collective-permute-start.6 = (bf16[256,1024]{1,0:T(8,128)(2,1)S(1)}, bf16[256,1024]{1,0:T(8,128)(2,1)S(1)}, u32[]{:S(2)}, u32[]{:S(2)}) collective-permute-start(bf16[256,1024]{1,0:T(8,128)(2,1)S(1)} %collective-permute-done.5.refs_0_), channel_id=1, source_target_pairs={{0,1},{1,0},{2,3},{3,2},{4,5},{5,4},{6,7},{7,6},{8,9},{9,8},{10,11... | collective-permute-start | bytes 1572872 | tf_op jit(solution)/shard_map/ppermute | solution.py:20
  108.3 3.3 %copy-start = (f32[2,1024,1024]{2,1,0:T(8,128)}, f32[2,1024,1024]{2,1,0:T(8,128)S(1)}, u32[]{:S(2)}) copy-start(f32[2,1024,1024]{2,1,0:T(8,128)S(1)} %get-tuple-element.31.run_ref) | copy-start | bytes 25165828
  111.6 10.6 %all-to-all-start.1 = ((f32[8,2,1024]{2,1,0:T(2,128)}), f32[8,2,1024]{2,1,0:T(2,128)S(1)}, u32[]{:S(2)}, u32[]{:S(2)}) async-start(f32[8,2,1024]{2,1,0:T(2,128)} %get-tuple-element.33), calls=%async_computation.1 | async-start | bytes 131072 | tf_op jit(solution)/shard_map/all_to_all | solution.py:650
  115.0 26.9 %collective-permute-start.10 = (bf16[256,1024]{1,0:T(8,128)(2,1)S(1)}, bf16[256,1024]{1,0:T(8,128)(2,1)S(1)}, u32[]{:S(2)}, u32[]{:S(2)}) collective-permute-start(bf16[256,1024]{1,0:T(8,128)(2,1)S(1)} %get-tuple-element.38.refs_8_.refs_4_), channel_id=1, source_target_pairs={{0,4},{4,0},{8,12},{12,8},{16,20},{20,16},{24,28},{28,24},{1,5},{5... | collective-permute-start | bytes 1572872 | tf_op jit(solution)/shard_map/ppermute | solution.py:20
  116.9 14.8 %collective-permute-start.16 = (bf16[256,1024]{1,0:T(8,128)(2,1)S(1)}, bf16[256,1024]{1,0:T(8,128)(2,1)}, u32[]{:S(2)}, u32[]{:S(2)}) collective-permute-start(bf16[256,1024]{1,0:T(8,128)(2,1)S(1)} %collective-permute-done.12.refs_12_.refs_8_), channel_id=1, source_target_pairs={{0,8},{4,12},{8,16},{12,20},{16,24},{20,28},{24,0},{28,4},{1,9},{5... | collective-permute-start | bytes 1572872 | tf_op jit(solution)/shard_map/ppermute | solution.py:582
  118.4 23.6 %collective-permute-start.15 = (bf16[256,1024]{1,0:T(8,128)(2,1)}, bf16[256,1024]{1,0:T(8,128)(2,1)}, u32[]{:S(2)}, u32[]{:S(2)}) collective-permute-start(bf16[256,1024]{1,0:T(8,128)(2,1)} %collective-permute-done.13.refs_13_.refs_9_), channel_id=1, source_target_pairs={{0,4},{4,0},{8,12},{12,8},{16,20},{20,16},{24,28},{28,24},{1,5},{5... | collective-permute-start | bytes 1572872 | tf_op jit(solution)/shard_map/ppermute | solution.py:20
  118.9 34.1 %collective-permute-start.14 = (bf16[256,1024]{1,0:T(8,128)(2,1)S(1)}, bf16[256,1024]{1,0:T(8,128)(2,1)}, u32[]{:S(2)}, u32[]{:S(2)}) collective-permute-start(bf16[256,1024]{1,0:T(8,128)(2,1)S(1)} %collective-permute-done.12.refs_12_.refs_8_), channel_id=1, source_target_pairs={{0,4},{4,0},{8,12},{12,8},{16,20},{20,16},{24,28},{28,24},{1,5},{5... | collective-permute-start | bytes 1572872 | tf_op jit(solution)/shard_map/ppermute | solution.py:20
  122.3 3.4 %copy-start.1 = (f32[2,1024,1024]{2,1,0:T(8,128)S(1)}, f32[2,1024,1024]{2,1,0:T(8,128)}, u32[]{:S(2)}) copy-start(f32[2,1024,1024]{2,1,0:T(8,128)} %copy-done) | copy-start | bytes 25165828
  129.0 41.4 %collective-permute-start.25 = (bf16[512,1024]{1,0:T(8,128)(2,1)S(1)}, bf16[512,1024]{1,0:T(8,128)(2,1)S(1)}, u32[]{:S(2)}, u32[]{:S(2)}) collective-permute-start(bf16[512,1024]{1,0:T(8,128)(2,1)S(1)} %shard_map.78.refs_0_), channel_id=1, source_target_pairs={{0,2},{1,3},{2,0},{3,1},{4,6},{5,7},{6,4},{7,5},{8,10},{9,11},{10,... | collective-permute-start | bytes 3145736 | tf_op jit(solution)/shard_map/ppermute | solution.py:20
  131.7 24.8 %collective-permute-start.20 = (bf16[256,1024]{1,0:T(8,128)(2,1)}, bf16[256,1024]{1,0:T(8,128)(2,1)S(1)}, u32[]{:S(2)}, u32[]{:S(2)}) collective-permute-start(bf16[256,1024]{1,0:T(8,128)(2,1)} %collective-permute-done.16.refs_16_.refs_12_), channel_id=1, source_target_pairs={{0,8},{4,12},{8,16},{12,20},{16,24},{20,28},{24,0},{28,4},{1,9},{5... | collective-permute-start | bytes 1572872 | tf_op jit(solution)/shard_map/ppermute | solution.py:582
  141.9 20.5 %collective-permute-start.18 = (bf16[256,1024]{1,0:T(8,128)(2,1)}, bf16[256,1024]{1,0:T(8,128)(2,1)S(1)}, u32[]{:S(2)}, u32[]{:S(2)}) collective-permute-start(bf16[256,1024]{1,0:T(8,128)(2,1)} %collective-permute-done.16.refs_16_.refs_12_), channel_id=1, source_target_pairs={{0,4},{4,0},{8,12},{12,8},{16,20},{20,16},{24,28},{28,24},{1,5},{5... | collective-permute-start | bytes 1572872 | tf_op jit(solution)/shard_map/ppermute | solution.py:20
  141.9 24.4 %collective-permute-start.8 = (bf16[256,1024]{1,0:T(8,128)(2,1)S(1)}, bf16[256,1024]{1,0:T(8,128)(2,1)S(1)}, u32[]{:S(2)}, u32[]{:S(2)}) collective-permute-start(bf16[256,1024]{1,0:T(8,128)(2,1)S(1)} %shard_map.77.refs_0_), channel_id=1, source_target_pairs={{0,2},{1,3},{2,0},{3,1},{4,6},{5,7},{6,4},{7,5},{8,10},{9,11},{10,... | collective-permute-start | bytes 1572872 | tf_op jit(solution)/shard_map/ppermute | solution.py:20
  153.1 17.3 %collective-permute-start.21 = (bf16[256,1024]{1,0:T(8,128)(2,1)S(1)}, bf16[256,1024]{1,0:T(8,128)(2,1)S(1)}, u32[]{:S(2)}, u32[]{:S(2)}) collective-permute-start(bf16[256,1024]{1,0:T(8,128)(2,1)S(1)} %collective-permute-done.17.refs_17_.refs_13_), channel_id=1, source_target_pairs={{0,8},{4,12},{8,16},{12,20},{16,24},{20,28},{24,0},{28,4},{1,9},{5... | collective-permute-start | bytes 1572872 | tf_op jit(solution)/shard_map/ppermute | solution.py:582
  156.5 17.5 %collective-permute-start.28 = (bf16[256,1024]{1,0:T(8,128)(2,1)S(1)}, bf16[256,1024]{1,0:T(8,128)(2,1)S(1)}, u32[]{:S(2)}, u32[]{:S(2)}) collective-permute-start(bf16[256,1024]{1,0:T(8,128)(2,1)S(1)} %shard_map.79.refs_4_), channel_id=1, source_target_pairs={{0,2},{1,3},{2,0},{3,1},{4,6},{5,7},{6,4},{7,5},{8,10},{9,11},{10,... | collective-permute-start | bytes 1572872 | tf_op jit(solution)/shard_map/ppermute | solution.py:20
  162.4 13.6 %collective-permute-start.27 = (bf16[256,1024]{1,0:T(8,128)(2,1)S(1)}, bf16[256,1024]{1,0:T(8,128)(2,1)S(1)}, u32[]{:S(2)}, u32[]{:S(2)}) collective-permute-start(bf16[256,1024]{1,0:T(8,128)(2,1)S(1)} %shard_map.79.refs_4_), channel_id=1, source_target_pairs={{0,1},{1,0},{2,3},{3,2},{4,5},{5,4},{6,7},{7,6},{8,9},{9,8},{10,11... | collective-permute-start | bytes 1572872 | tf_op jit(solution)/shard_map/ppermute | solution.py:20
  166.3 16.4 %collective-permute-start.19 = (bf16[256,1024]{1,0:T(8,128)(2,1)S(1)}, bf16[256,1024]{1,0:T(8,128)(2,1)S(1)}, u32[]{:S(2)}, u32[]{:S(2)}) collective-permute-start(bf16[256,1024]{1,0:T(8,128)(2,1)S(1)} %collective-permute-done.17.refs_17_.refs_13_), channel_id=1, source_target_pairs={{0,4},{4,0},{8,12},{12,8},{16,20},{20,16},{24,28},{28,24},{1,5},{5... | collective-permute-start | bytes 1572872 | tf_op jit(solution)/shard_map/ppermute | solution.py:20
  170.4 29.6 %collective-permute-start.24 = (bf16[512,1024]{1,0:T(8,128)(2,1)S(1)}, bf16[512,1024]{1,0:T(8,128)(2,1)S(1)}, u32[]{:S(2)}, u32[]{:S(2)}) collective-permute-start(bf16[512,1024]{1,0:T(8,128)(2,1)S(1)} %shard_map.78.refs_0_), channel_id=1, source_target_pairs={{0,1},{1,0},{2,3},{3,2},{4,5},{5,4},{6,7},{7,6},{8,9},{9,8},{10,11... | collective-permute-start | bytes 3145736 | tf_op jit(solution)/shard_map/ppermute | solution.py:20
  170.4 29.6 %collective-permute-start.26 = (bf16[512,1024]{1,0:T(8,128)(2,1)S(1)}, bf16[512,1024]{1,0:T(8,128)(2,1)S(1)}, u32[]{:S(2)}, u32[]{:S(2)}) collective-permute-start(bf16[512,1024]{1,0:T(8,128)(2,1)S(1)} %collective-permute-done.25.refs_2_), channel_id=1, source_target_pairs={{0,1},{1,0},{2,3},{3,2},{4,5},{5,4},{6,7},{7,6},{8,9},{9,8},{10,11... | collective-permute-start | bytes 3145736 | tf_op jit(solution)/shard_map/ppermute | solution.py:20
  174.1 19.8 %collective-permute-start.22 = (bf16[256,1024]{1,0:T(8,128)(2,1)S(1)}, bf16[256,1024]{1,0:T(8,128)(2,1)S(1)}, u32[]{:S(2)}, u32[]{:S(2)}) collective-permute-start(bf16[256,1024]{1,0:T(8,128)(2,1)S(1)} %collective-permute-done.20.refs_20_.refs_16_), channel_id=1, source_target_pairs={{0,4},{4,0},{8,12},{12,8},{16,20},{20,16},{24,28},{28,24},{1,5},{5... | collective-permute-start | bytes 1572872 | tf_op jit(solution)/shard_map/ppermute | solution.py:20
  176.0 17.8 %collective-permute-start.29 = (bf16[256,1024]{1,0:T(8,128)(2,1)S(1)}, bf16[256,1024]{1,0:T(8,128)(2,1)S(1)}, u32[]{:S(2)}, u32[]{:S(2)}) collective-permute-start(bf16[256,1024]{1,0:T(8,128)(2,1)S(1)} %collective-permute-done.28.refs_6_), channel_id=1, source_target_pairs={{0,1},{1,0},{2,3},{3,2},{4,5},{5,4},{6,7},{7,6},{8,9},{9,8},{10,11... | collective-permute-start | bytes 1572872 | tf_op jit(solution)/shard_map/ppermute | solution.py:20
  182.7 17.3 %collective-permute-start.23 = (bf16[256,1024]{1,0:T(8,128)(2,1)S(1)}, bf16[256,1024]{1,0:T(8,128)(2,1)S(1)}, u32[]{:S(2)}, u32[]{:S(2)}) collective-permute-start(bf16[256,1024]{1,0:T(8,128)(2,1)S(1)} %collective-permute-done.21.refs_21_.refs_17_), channel_id=1, source_target_pairs={{0,4},{4,0},{8,12},{12,8},{16,20},{20,16},{24,28},{28,24},{1,5},{5... | collective-permute-start | bytes 1572872 | tf_op jit(solution)/shard_map/ppermute | solution.py:20
  193.8 18.9 %collective-permute-start.7 = (bf16[256,1024]{1,0:T(8,128)(2,1)S(1)}, bf16[256,1024]{1,0:T(8,128)(2,1)S(1)}, u32[]{:S(2)}, u32[]{:S(2)}) collective-permute-start(bf16[256,1024]{1,0:T(8,128)(2,1)S(1)} %shard_map.77.refs_0_), channel_id=1, source_target_pairs={{0,1},{1,0},{2,3},{3,2},{4,5},{5,4},{6,7},{7,6},{8,9},{9,8},{10,11... | collective-permute-start | bytes 1572872 | tf_op jit(solution)/shard_map/ppermute | solution.py:20
  193.9 18.9 %collective-permute-start.9 = (bf16[256,1024]{1,0:T(8,128)(2,1)S(1)}, bf16[256,1024]{1,0:T(8,128)(2,1)S(1)}, u32[]{:S(2)}, u32[]{:S(2)}) collective-permute-start(bf16[256,1024]{1,0:T(8,128)(2,1)S(1)} %collective-permute-done.8.refs_2_), channel_id=1, source_target_pairs={{0,1},{1,0},{2,3},{3,2},{4,5},{5,4},{6,7},{7,6},{8,9},{9,8},{10,11... | collective-permute-start | bytes 1572872 | tf_op jit(solution)/shard_map/ppermute | solution.py:20
  200.0 1.0 copy-start.9

commit v3 on v2

--- a/solution.py
+++ b/solution.py
@@ -213,10 +213,9 @@
     for g in range(2):
         for l in range(width // LANES):
             lanes = slice(l * LANES, (l + 1) * LANES)
-            total = acc[g, :, lanes] + pbuf[g, :, lanes] + bias_ref[g : g + 1, lanes]
-            flat[g, l] = total.astype(BF16).astype(F32)
-
-    tiles = tile_of(width // LANES, 2)
+            flat[g, l] = acc[g, :, lanes] + pbuf[g, :, lanes] + bias_ref[g : g + 1, lanes]
+
+    tiles = tile_of(width // LANES, 8)
     span = tiles * LANES
 
     def columns(n, carry_out):
@@ -225,22 +224,22 @@
 
         def pair(jj, carry, first):
             a, b = carry
-            held = ([], [])
+            lines = pl.ds(pl.multiple_of(jj * 2 * SEGS, 2 * SEGS), 2 * SEGS)
+            held = []
+            for g in range(2):
+                rows2 = [spread_rows(flat, g, n * tiles, tiles, 2 * jj + k, seg) for k in range(2)]
+                rounded = jnp.concatenate(rows2, axis=0).astype(BF16)
+                gates_ref[g, lines, wide] = rounded
+                held.append(rounded.astype(F32))
             for k in range(2):
-                j = 2 * jj + k
-                pre = spread_rows(flat, 0, n * tiles, tiles, j, seg)
-                cand = spread_rows(flat, 1, n * tiles, tiles, j, seg)
-                held[0].append(pre)
-                held[1].append(cand)
+                pre = held[0][k * SEGS : (k + 1) * SEGS]
+                cand = held[1][k * SEGS : (k + 1) * SEGS]
                 update, keep, scaled, slope, offset = first_slopes(pre, cand, gain)
                 if first and k == 0:
                     prev = lead_row(place, start_ref[:, wide], (SEGS, span))
                     slope, offset = around(update, keep, scaled, cand, gain, prev)
                 b = slope * b + offset
                 a = slope * a
-            lines = pl.ds(pl.multiple_of(jj * 2 * SEGS, 2 * SEGS), 2 * SEGS)
-            for g in range(2):
-                gates_ref[g, lines, wide] = jnp.concatenate(held[g], axis=0).astype(BF16)
             return a, b
 
         carry = (jnp.ones((SEGS, span), F32), jnp.zeros((SEGS, span), F32))
@@ -471,15 +470,17 @@
     )(place, run, maps, peer_maps, start)
 
 
-def mix_kernel(groups, group, pieces, peers, place, *refs):
+def mix_kernel(groups, group, pieces, peers, slots, before, place, *refs):
     count = groups * group
     blocks = refs[:count]
-    weights = refs[count : count + peers * pieces]
+    weights = refs[count : count + len(slots) * 2 * pieces]
     out_ref, lhs, wbuf, acc, lsem, wsem = refs[-6:]
+    prev_ref = refs[count + len(weights)] if before else None
     depth = blocks[0].shape[1]
     heights = [blocks[c * group].shape[0] for c in range(groups)]
     lines_of = weights[0].shape[0]
     outer = peers // 2
+    here = len(slots) * 2
 
     def w_copy(n, p):
         w_ref = weights[n * pieces + p]
@@ -492,66 +493,77 @@
         dst = lhs.at[top : top + heights[c], deep]
         return pltpu.make_async_copy(blocks[c * group + d], dst, lsem.at[c, d])
 
-    for c in range(groups):
-        for d in range(group):
-            l_copy(c, d).start()
-    for n in range(peers):
+    for n in range(here):
         for p in range(pieces):
             w_copy(n, p).start()
     for c in range(groups):
         for d in range(group):
+            l_copy(c, d).start()
+    for c in range(groups):
+        for d in range(group):
             l_copy(c, d).wait()
     span = lines_of * pieces
-    for n in range(peers):
-        source = lax.rem(place[1] // 2 + outer - n // 2, outer)
+    for n in range(here):
+        source = lax.rem(place[1] // 2 + outer - slots[n // 2], outer)
         owner = source * 2 + (lax.rem(place[1], 2) ^ (n % 2))
         deep = pl.ds(pl.multiple_of(owner * span, span), span)
         for p in range(pieces):
             w_copy(n, p).wait()
         part = jnp.dot(lhs[:, deep], wbuf[n], preferred_element_type=F32)
-        if n == 0:
+        if n == 0 and before:
+            part = part + prev_ref[...]
+        if n > 0:
+            part = acc[...] + part
+        if n < here - 1:
             acc[...] = part
-        elif n < peers - 1:
-            acc[...] += part
         else:
-            out_ref[...] = (acc[...] + part).astype(BF16)
-
-
-def mix_rows(place, blocks, weights, whole, first, total_rows, pieces):
+            out_ref[...] = part.astype(out_ref.dtype)
+
+
+def mix_rows(place, blocks, weights, slots, prev, final, whole, first, total_rows, pieces):
     groups, group = len(blocks), len(blocks[0])
     depth = blocks[0][0].shape[1]
     lines_of, width = weights[0].shape
     peers = len(weights) // pieces
-    here = sum(g[0].shape[0] for g in blocks)
-    anywhere = pl.BlockSpec(memory_space=pl.ANY)
-    args = [place] + [b for g in blocks for b in g] + list(weights)
-    in_specs = [anywhere] * (groups * group + len(weights))
+    rows = sum(g[0].shape[0] for g in blocks)
+    used = [weights[(s * 2 + i) * pieces + p] for s in slots for i in range(2) for p in range(pieces)]
+    args = [place] + [b for g in blocks for b in g] + used
+    in_specs = [pl.BlockSpec(memory_space=pl.ANY)] * (groups * group)
+    in_specs += [pl.BlockSpec(memory_space=pltpu.HBM)] * len(used)
+    if prev is not None:
+        args.append(prev)
+        in_specs.append(pl.BlockSpec((rows, width), lambda n, p: (0, 0)))
     aliases = {}
     if whole is not None:
         aliases = {len(args): 0}
         args.append(whole)
-        in_specs.append(anywhere)
+        in_specs.append(pl.BlockSpec(memory_space=pl.ANY))
+    deep = len(slots) * 2 * pieces * lines_of
+    if final:
+        out_shape = jax.ShapeDtypeStruct((total_rows, width), BF16)
+        out_spec = pl.BlockSpec((rows, width), lambda n, p: (first // rows, 0))
+    else:
+        out_shape = jax.ShapeDtypeStruct((rows, width), F32)
+        out_spec = pl.BlockSpec((rows, width), lambda n, p: (0, 0))
     return pl.pallas_call(
-        functools.partial(mix_kernel, groups, group, pieces, peers),
-        out_shape=jax.ShapeDtypeStruct((total_rows, width), BF16),
+        functools.partial(mix_kernel, groups, group, pieces, peers, tuple(slots), prev is not None),
+        out_shape=out_shape,
         grid_spec=pltpu.PrefetchScalarGridSpec(
             num_scalar_prefetch=1,
             grid=(1,),
             in_specs=in_specs,
-            out_specs=pl.BlockSpec((here, width), lambda n, p: (first // here, 0)),
+            out_specs=out_spec,
             scratch_shapes=[
-                pltpu.VMEM((here, group * depth), BF16),
-                pltpu.VMEM((peers, lines_of * pieces, width), BF16),
-                pltpu.VMEM((here, width), F32),
+                pltpu.VMEM((rows, group * depth), BF16),
+                pltpu.VMEM((len(slots) * 2, lines_of * pieces, width), BF16),
+                pltpu.VMEM((rows, width), F32),
                 pltpu.SemaphoreType.DMA((groups, group)),
-                pltpu.SemaphoreType.DMA((peers, pieces)),
+                pltpu.SemaphoreType.DMA((len(slots) * 2, pieces)),
             ],
         ),
         input_output_aliases=aliases,
         compiler_params=params(40 if peers <= 8 else 62),
-        cost_estimate=cost(
-            2 * here * group * depth * width, 2 * group * depth * (width + here) + 2 * here * width
-        ),
+        cost_estimate=cost(2 * rows * deep * width, 2 * deep * (width + rows) + 4 * rows * width),
     )(*args)
 
 
@@ -664,14 +676,27 @@
             highs.append(swap(across, "ch", d))
         blocks[c] = lows + highs
     weights = ring.blocks()
-    mixed = None
-    split = chunks - 1 if chunks > 1 else chunks
-    mixed = mix_rows(place, blocks[:split], weights, None, 0, total_rows, ring.pieces)
-    if split < chunks:
-        mixed = mix_rows(
-            place, blocks[split:], weights, mixed, firsts[split], total_rows, ring.pieces
-        )
-    return mixed
+    split = chunks - 1
+    late = max(1, ring.outer // 4)
+    slots = list(range(ring.outer))
+    partial = mix_rows(
+        place, blocks[:split], weights, slots[:-late], None, False, None, 0, total_rows, ring.pieces
+    )
+    mixed = mix_rows(
+        place, blocks[:split], weights, slots[-late:], partial, True, None, 0, total_rows, ring.pieces
+    )
+    return mix_rows(
+        place,
+        blocks[split:],
+        weights,
+        slots,
+        None,
+        True,
+        mixed,
+        firsts[split],
+        total_rows,
+        ring.pieces,
+    )
 
 
 def solution(mesh):

time: 219 us -> 232 us (1.059)
  waiting for transfers between devices: 75 us -> 92.7 us
  starting transfers between devices: 44.5 us -> 34.9 us
  Pallas kernels: 76.4 us -> 79.5 us
    ppermute x24, waiting for transfers between devices: 73 us -> 89 us  [swap(): lax.ppermute(block, axis, [(i, i ^ bits) for i in range(lax.axis_size(axi...]
    ppermute x6, starting transfers between devices: 18.5 us -> 10.5 us  [ring_step(): self.held[s, 0, p] = lax.ppermute(block, 'ctx', route)]
    pallas_call x2 -> x3, Pallas kernels: 17 us -> 19.5 us  [mix_rows(): pl.pallas_call(functools.partial(mix_kernel, groups, group, pieces, peers...]
    unnamed x20 -> x18, local copies, waits for them, and re-layouts: 9.28 us -> 10.2 us
  transfers between devices with their start and end apart: 31 -> 31, of which waited for: 11 -> 12; matrix products, arithmetic and copies ran while one was open for 1% -> 1% of each run, Pallas kernels for 33% -> 32%
where the time goes in v3:
time: 232 us
  waiting for transfers between devices  92.7 us (40%)
  Pallas kernels  79.5 us (34%)
  starting transfers between devices  34.9 us (15%)
  blocking collectives  12.8 us (6%)
  local copies, waits for them, and re-layouts  11.4 us (5%)
    ppermute x24, waiting for transfers between devices, swap(): lax.ppermute(block, axis, [(i, i ^ bits) for i in range(lax.axis_size(axi...  89 us
    pallas_call x3, Pallas kernels, gate_chunk(): pl.pallas_call(functools.partial(gate_kernel, half, chunk, first_row, row...  30.5 us
    ppermute x24, starting transfers between devices, swap(): lax.ppermute(block, axis, [(i, i ^ bits) for i in range(lax.axis_size(axi...  21 us
    pallas_call x3, Pallas kernels, mix_rows(): pl.pallas_call(functools.partial(mix_kernel, groups, group, pieces, peers...  19.5 us
    pallas_call x1, Pallas kernels, near_product(): pl.pallas_call(functools.partial(near_kernel, half, tiles), out_shape=jax...  13.5 us
    all_to_all x1, blocking collectives, layer(): peer_maps = lax.all_to_all(out[2], 'ctx', 0, 0, tiled=True)  12.8 us
    ppermute x6, starting transfers between devices, ring_step(): self.held[s, 0, p] = lax.ppermute(block, 'ctx', route)  10.5 us
    unnamed x18, local copies, waits for them, and re-layouts  10.2 us
  transfers between devices with their start and end apart: 31, of which 12 were waited for; matrix products, arithmetic and copies ran while one was open for 1% of the time, Pallas kernels for 32%

profile of v3, /device:TPU:0, one launch (start us, length us, event | category | flops | bytes accessed | tf_op | source)
XLA Modules:
  0.0 231.7 jit_solution(3584749867179476753)
XLA Ops:
  0.5 1.6 copy-done.3
  2.1 1.2 split.1
  3.3 2.5 %collective-permute-start = (bf16[512,1024]{1,0:T(8,128)(2,1)S(1)}, bf16[512,1024]{1,0:T(8,128)(2,1)}, u32[]{:S(2)}, u32[]{:S(2)}) collective-permute-start(bf16[512,1024]{1,0:T(8,128)(2,1)S(1)} %get-tuple-element.21), channel_id=1, source_target_pairs={{0,2},{1,3},{2,0},{3,1},{4,6},{5,7},{6,4},{7,5},{8,10},{9,11},{10,... | collective-permute-start | bytes 3145736 | tf_op jit(solution)/shard_map/ppermute | solution.py:20
  5.9 1.9 collective-permute-start.5
  7.8 22.1 %collective-permute-done.refs_0_ = bf16[512,1024]{1,0:T(8,128)(2,1)} collective-permute-done((bf16[512,1024]{1,0:T(8,128)(2,1)S(1)}, bf16[512,1024]{1,0:T(8,128)(2,1)}, u32[]{:S(2)}, u32[]{:S(2)}) %collective-permute-start) | collective-permute-done | bytes 1048608 | tf_op jit(solution)/shard_map/ppermute | solution.py:20
  29.9 1.3 fusion
  31.2 2.2 collective-permute-start.13
  33.4 7.7 %collective-permute-done.3.refs_0_ = bf16[256,1024]{1,0:T(8,128)(2,1)} collective-permute-done((bf16[256,1024]{1,0:T(8,128)(2,1)}, bf16[256,1024]{1,0:T(8,128)(2,1)}, u32[]{:S(2)}, u32[]{:S(2)}) %collective-permute-start.3) | collective-permute-done | bytes 524320 | tf_op jit(solution)/shard_map/ppermute | solution.py:20
  41.2 2.1 collective-permute-start.12
  43.3 8.9 %collective-permute-done.5.refs_0_ = bf16[256,1024]{1,0:T(8,128)(2,1)} collective-permute-done((bf16[256,1024]{1,0:T(8,128)(2,1)}, bf16[256,1024]{1,0:T(8,128)(2,1)}, u32[]{:S(2)}, u32[]{:S(2)}) %collective-permute-start.5) | collective-permute-done | bytes 524320 | tf_op jit(solution)/shard_map/ppermute | solution.py:20
  52.7 13.5 %shard_map.73.refs_2_ = f32[2,1024,1024]{2,1,0:T(8,128)S(1)} custom-call(s32[2]{0:T(128)S(1)} %pad_add_fusion.place, bf16[1024,1024]{1,0:T(8,128)(2,1)S(1)} %copy-done.4, bf16[1024,1024]{1,0:T(8,128)(2,1)} %collective-permute-done.2.refs_1_, bf16[2,4096,1024]{2,1,0:T(8,128)(2,1)} %refs_3_.5), custom_call_target="tpu_custom_call" | custom-call | flops 8589934592 | bytes 20971520 | tf_op jit(solution)/shard_map/pallas_call | solution.py:82
  66.2 14.7 %shard_map.74 = (bf16[2,512,1024]{2,1,0:T(8,128)(2,1)S(1)}, f32[2,8,1024]{2,1,0:T(8,128)S(1)}) custom-call(s32[2]{0:T(128)S(1)} %pad_add_fusion.place, bf16[512,1024]{1,0:T(8,128)(2,1)} %collective-permute-done.refs_0_, bf16[512,1024]{1,0:T(8,128)(2,1)} %collective-permute-done.1.refs_1_, f32[2,1024,1024]{2,1,0:T(8,128)S(1)} %shard_map.73.refs_2_, ...), custom_call_target="tpu_custom_call" | custom-call | flops 4294967296 | bytes 16777216 | tf_op jit(solution)/shard_map/pallas_call | solution.py:281
  81.0 7.9 %shard_map.75 = (bf16[2,256,1024]{2,1,0:T(8,128)(2,1)S(1)}, f32[2,8,1024]{2,1,0:T(8,128)S(1)}) custom-call(s32[2]{0:T(128)S(1)} %pad_add_fusion.place, bf16[256,1024]{1,0:T(8,128)(2,1)} %collective-permute-done.3.refs_0_, bf16[256,1024]{1,0:T(8,128)(2,1)S(1)} %collective-permute-done.4.refs_1_, f32[2,1024,1024]{2,1,0:T(8,128)S(1)} %shard_map.73.refs_2_, ...), custom_call_target="tpu_custom_call" | custom-call | flops 2147483648 | bytes 12582912 | tf_op jit(solution)/shard_map/pallas_call | solution.py:281
  88.9 7.9 %shard_map.76 = (bf16[2,256,1024]{2,1,0:T(8,128)(2,1)S(1)}, f32[2,8,1024]{2,1,0:T(8,128)S(1)}, f32[8,2,1024]{2,1,0:T(2,128)S(1)}) custom-call(s32[2]{0:T(128)S(1)} %pad_add_fusion.place, bf16[256,1024]{1,0:T(8,128)(2,1)} %collective-permute-done.5.refs_0_, bf16[256,1024]{1,0:T(8,128)(2,1)S(1)} %collective-permute-done.6.refs_1_, ...), custom_call_target="tpu_custom_call" | custom-call | flops 2147483648 | bytes 12582912 | tf_op jit(solution)/shard_map/pallas_call | solution.py:281
  96.8 12.8 %all_to_all.10.refs_6_ = f32[8,2,1024]{2,1,0:T(2,128)S(1)} all-to-all(f32[8,2,1024]{2,1,0:T(2,128)S(1)} %get-tuple-element.30), channel_id=1, replica_groups=mesh['ctx'=8,'ch'=4] {'ctx'}, dimensions={0} | all-to-all | bytes 131072 | tf_op jit(solution)/shard_map/all_to_all | solution.py:660
  109.6 7.7 %bend.1 = (f32[2,1024,1024]{2,1,0:T(8,128)S(1)}, f32[2,24,1024]{2,1,0:T(8,128)S(1)}, f32[8,2,1024]{2,1,0:T(2,128)}) custom-call(s32[2]{0:T(128)S(1)} %pad_add_fusion.place, bf16[2,512,1024]{2,1,0:T(8,128)(2,1)S(1)} %get-tuple-element.22.refs_0_, bf16[2,256,1024]{2,1,0:T(8,128)(2,1)S(1)} %get-tuple-element.24.refs_1_, ...), custom_call_target="tpu_custom_call" | custom-call | flops 41943040 | bytes 12582912 | tf_op jit(solution)/shard_map/bend/pallas_call | solution.py:398
  117.2 3.3 %copy-done = f32[2,1024,1024]{2,1,0:T(8,128)} copy-done((f32[2,1024,1024]{2,1,0:T(8,128)}, f32[2,1024,1024]{2,1,0:T(8,128)S(1)}, u32[]{:S(2)}) %copy-start) | copy-done | bytes 8388632
  120.5 3.4 %all-to-all-start.1 = ((f32[8,2,1024]{2,1,0:T(2,128)}), f32[8,2,1024]{2,1,0:T(2,128)S(1)}, u32[]{:S(2)}, u32[]{:S(2)}) async-start(f32[8,2,1024]{2,1,0:T(2,128)} %get-tuple-element.33), calls=%async_computation.1 | async-start | bytes 131072 | tf_op jit(solution)/shard_map/all_to_all | solution.py:662
  123.9 1.9 collective-permute-start.11
  126.0 1.9 collective-permute-start.16
  127.8 1.5 collective-permute-start.17
  129.3 1.8 all-to-all-done.1.peer_ref
  131.2 3.4 %copy-done.1 = f32[2,1024,1024]{2,1,0:T(8,128)S(1)} copy-done((f32[2,1024,1024]{2,1,0:T(8,128)S(1)}, f32[2,1024,1024]{2,1,0:T(8,128)}, u32[]{:S(2)}) %copy-start.1) | copy-done | bytes 8388632
  134.5 3.3 %shard_map.78.refs_0_ = bf16[512,1024]{1,0:T(8,128)(2,1)S(1)} custom-call(s32[2]{0:T(128)S(1)} %pad_add_fusion.place, f32[2,1024,1024]{2,1,0:T(8,128)S(1)} %copy-done.1, f32[2,24,1024]{2,1,0:T(8,128)S(1)} %get-tuple-element.32.maps_ref, f32[8,2,1024]{2,1,0:T(2,128)S(1)} %all-to-all-done.1.peer_ref, f32[1,1024]{1,0:T(1,128)S(1)} %bitcast.10), custom_call_target="tpu_custom_call" | custom-call | flops 1048576 | bytes 5242880 | tf_op jit(solution)/shard_map/pallas_call | solution.py:453
  137.9 1.6 collective-permute-start.25
  139.4 1.4 collective-permute-start.15
  140.8 9.9 %collective-permute-done.10.refs_10_.refs_6_ = bf16[256,1024]{1,0:T(8,128)(2,1)} collective-permute-done((bf16[256,1024]{1,0:T(8,128)(2,1)S(1)}, bf16[256,1024]{1,0:T(8,128)(2,1)}, u32[]{:S(2)}, u32[]{:S(2)}) %collective-permute-start.10) | collective-permute-done | bytes 524320 | tf_op jit(solution)/shard_map/ppermute | solution.py:20
  150.7 1.5 collective-permute-start.14
  152.1 1.4 collective-permute-start.20
  154.2 2.0 shard_map.77.refs_0_
  156.2 5.6 %collective-permute-done.15.refs_15_.refs_11_ = bf16[256,1024]{1,0:T(8,128)(2,1)S(1)} collective-permute-done((bf16[256,1024]{1,0:T(8,128)(2,1)}, bf16[256,1024]{1,0:T(8,128)(2,1)S(1)}, u32[]{:S(2)}, u32[]{:S(2)}) %collective-permute-start.15) | collective-permute-done | bytes 524320 | tf_op jit(solution)/shard_map/ppermute | solution.py:20
  161.8 1.5 collective-permute-start.8
  163.3 1.9 shard_map.79.refs_4_
  165.2 7.8 %collective-permute-done.14.refs_14_.refs_10_ = bf16[256,1024]{1,0:T(8,128)(2,1)S(1)} collective-permute-done((bf16[256,1024]{1,0:T(8,128)(2,1)}, bf16[256,1024]{1,0:T(8,128)(2,1)S(1)}, u32[]{:S(2)}, u32[]{:S(2)}) %collective-permute-start.14) | collective-permute-done | bytes 524320 | tf_op jit(solution)/shard_map/ppermute | solution.py:20
  173.0 1.5 collective-permute-start.28
  174.5 1.6 collective-permute-start.21
  176.1 6.1 %collective-permute-done.18.refs_18_.refs_14_ = bf16[256,1024]{1,0:T(8,128)(2,1)S(1)} collective-permute-done((bf16[256,1024]{1,0:T(8,128)(2,1)}, bf16[256,1024]{1,0:T(8,128)(2,1)S(1)}, u32[]{:S(2)}, u32[]{:S(2)}) %collective-permute-start.18) | collective-permute-done | bytes 524320 | tf_op jit(solution)/shard_map/ppermute | solution.py:20
  182.7 1.4 collective-permute-start.19
  184.1 1.8 collective-permute-done.21.refs_9_.refs_17_
  186.0 1.1 collective-permute-done.27.refs_5_
  187.1 1.4 collective-permute-start.22
  188.4 9.3 %collective-permute-done.19.refs_19_.refs_15_ = bf16[256,1024]{1,0:T(8,128)(2,1)S(1)} collective-permute-done((bf16[256,1024]{1,0:T(8,128)(2,1)}, bf16[256,1024]{1,0:T(8,128)(2,1)S(1)}, u32[]{:S(2)}, u32[]{:S(2)}) %collective-permute-start.19) | collective-permute-done | bytes 524320 | tf_op jit(solution)/shard_map/ppermute | solution.py:20
  197.7 1.4 collective-permute-start.23
  199.6 9.5 %shard_map.80.refs_12_ = f32[768,1024]{1,0:T(8,128)} custom-call(s32[2]{0:T(128)S(1)} %pad_add_fusion.place, bf16[512,1024]{1,0:T(8,128)(2,1)S(1)} %shard_map.78.refs_0_, bf16[512,1024]{1,0:T(8,128)(2,1)S(1)} %collective-permute-done.24.refs_1_, bf16[512,1024]{1,0:T(8,128)(2,1)S(1)} %collective-permute-done.25.refs_2_, ...), custom_call_target="tpu_custom_call" | custom-call | flops 4831838208 | bytes 14155776 | tf_op jit(solution)/shard_map/pallas_call | solution.py:548
  209.2 10.5 %collective-permute-done.23.refs_11_.refs_19_ = bf16[256,1024]{1,0:T(8,128)(2,1)S(1)} collective-permute-done((bf16[256,1024]{1,0:T(8,128)(2,1)S(1)}, bf16[256,1024]{1,0:T(8,128)(2,1)S(1)}, u32[]{:S(2)}, u32[]{:S(2)}) %collective-permute-start.23) | collective-permute-done | bytes 524320 | tf_op jit(solution)/shard_map/ppermute | solution.py:20
  219.7 1.9 copy-done.2
  221.6 4.9 %shard_map.81.refs_20_ = bf16[1024,1024]{1,0:T(8,128)(2,1)} custom-call(s32[2]{0:T(128)S(1)} %pad_add_fusion.place, bf16[512,1024]{1,0:T(8,128)(2,1)S(1)} %shard_map.78.refs_0_, bf16[512,1024]{1,0:T(8,128)(2,1)S(1)} %collective-permute-done.24.refs_1_, bf16[512,1024]{1,0:T(8,128)(2,1)S(1)} %collective-permute-done.25.refs_2_, ...), custom_call_target="tpu_custom_call" | custom-call | flops 1610612736 | bytes 6815744 | tf_op jit(solution)/shard_map/pallas_call | solution.py:548
  226.5 5.0 %shard_map.82 = bf16[1024,1024]{1,0:T(8,128)(2,1)} custom-call(s32[2]{0:T(128)S(1)} %pad_add_fusion.place, bf16[256,1024]{1,0:T(8,128)(2,1)S(1)} %shard_map.77.refs_0_, bf16[256,1024]{1,0:T(8,128)(2,1)S(1)} %collective-permute-done.7.refs_1_, bf16[256,1024]{1,0:T(8,128)(2,1)S(1)} %collective-permute-done.8.refs_2_, ...), custom_call_target="tpu_custom_call", output_to_operand_aliasing={{}: (21, {})} | custom-call | flops 2147483648 | bytes 11534336 | tf_op jit(solution)/shard_map/pallas_call | solution.py:548
  (48 shorter events, 3.2 us)
Async XLA Ops:
  0.0 52.2 %collective-permute-start.2 = (bf16[1024,1024]{1,0:T(8,128)(2,1)}, bf16[1024,1024]{1,0:T(8,128)(2,1)}, u32[]{:S(2)}, u32[]{:S(2)}) collective-permute-start(bf16[1024,1024]{1,0:T(8,128)(2,1)} %refs_0_.1), channel_id=1, source_target_pairs={{0,1},{1,0},{2,3},{3,2},{4,5},{5,4},{6,7},{7,6},{8,9},{9,8},{10,11... | collective-permute-start | bytes 6291464 | tf_op jit(solution)/shard_map/ppermute | solution.py:20
  0.5 1.6 copy-start.3
  2.1 31.3 %copy-start.7 = (f32[1024]{0:T(1024)S(1)}, f32[1024]{0:T(1024)}, u32[]{:S(2)}) copy-start(f32[1024]{0:T(1024)} %param.11) | copy-start | bytes 12292
  2.1 31.3 %copy-start.8 = (f32[1024]{0:T(1024)S(1)}, f32[1024]{0:T(1024)}, u32[]{:S(2)}) copy-start(f32[1024]{0:T(1024)} %param.10) | copy-start | bytes 12292
  2.1 50.6 %copy-start.4 = (bf16[1024,1024]{1,0:T(8,128)(2,1)S(1)}, bf16[1024,1024]{1,0:T(8,128)(2,1)}, u32[]{:S(2)}) copy-start(bf16[1024,1024]{1,0:T(8,128)(2,1)} %refs_0_.1) | copy-start | bytes 6291460
  3.3 26.7 %collective-permute-start = (bf16[512,1024]{1,0:T(8,128)(2,1)S(1)}, bf16[512,1024]{1,0:T(8,128)(2,1)}, u32[]{:S(2)}, u32[]{:S(2)}) collective-permute-start(bf16[512,1024]{1,0:T(8,128)(2,1)S(1)} %get-tuple-element.21), channel_id=1, source_target_pairs={{0,2},{1,3},{2,0},{3,1},{4,6},{5,7},{6,4},{7,5},{8,10},{9,11},{10,... | collective-permute-start | bytes 3145736 | tf_op jit(solution)/shard_map/ppermute | solution.py:20
  5.8 35.4 %collective-permute-start.3 = (bf16[256,1024]{1,0:T(8,128)(2,1)}, bf16[256,1024]{1,0:T(8,128)(2,1)}, u32[]{:S(2)}, u32[]{:S(2)}) collective-permute-start(bf16[256,1024]{1,0:T(8,128)(2,1)} %get-tuple-element.23), channel_id=1, source_target_pairs={{0,2},{1,3},{2,0},{3,1},{4,6},{5,7},{6,4},{7,5},{8,10},{9,11},{10,... | collective-permute-start | bytes 1572872 | tf_op jit(solution)/shard_map/ppermute | solution.py:20
  5.9 46.3 %collective-permute-start.5 = (bf16[256,1024]{1,0:T(8,128)(2,1)}, bf16[256,1024]{1,0:T(8,128)(2,1)}, u32[]{:S(2)}, u32[]{:S(2)}) collective-permute-start(bf16[256,1024]{1,0:T(8,128)(2,1)} %get-tuple-element.25), channel_id=1, source_target_pairs={{0,2},{1,3},{2,0},{3,1},{4,6},{5,7},{6,4},{7,5},{8,10},{9,11},{10,... | collective-permute-start | bytes 1572872 | tf_op jit(solution)/shard_map/ppermute | solution.py:20
  29.9 36.3 %collective-permute-start.1 = (bf16[512,1024]{1,0:T(8,128)(2,1)}, bf16[512,1024]{1,0:T(8,128)(2,1)}, u32[]{:S(2)}, u32[]{:S(2)}) collective-permute-start(bf16[512,1024]{1,0:T(8,128)(2,1)} %collective-permute-done.refs_0_), channel_id=1, source_target_pairs={{0,1},{1,0},{2,3},{3,2},{4,5},{5,4},{6,7},{7,6},{8,9},{9,8},{10,11... | collective-permute-start | bytes 3145736 | tf_op jit(solution)/shard_map/ppermute | solution.py:20
  31.2 96.7 %collective-permute-start.13 = (bf16[256,1024]{1,0:T(8,128)(2,1)S(1)}, bf16[256,1024]{1,0:T(8,128)(2,1)}, u32[]{:S(2)}, u32[]{:S(2)}) collective-permute-start(bf16[256,1024]{1,0:T(8,128)(2,1)S(1)} %get-tuple-element.37.refs_9_.refs_5_), channel_id=1, source_target_pairs={{0,8},{4,12},{8,16},{12,20},{16,24},{20,28},{24,0},{28,4},{1,9},{5... | collective-permute-start | bytes 1572872 | tf_op jit(solution)/shard_map/ppermute | solution.py:594
  41.2 25.1 %copy-start.5 = (f32[1024]{0:T(1024)S(1)}, f32[1024]{0:T(1024)}, u32[]{:S(2)}) copy-start(f32[1024]{0:T(1024)} %param.13) | copy-start | bytes 12292
  41.2 25.1 %copy-start.6 = (f32[1024]{0:T(1024)S(1)}, f32[1024]{0:T(1024)}, u32[]{:S(2)}) copy-start(f32[1024]{0:T(1024)} %param.12) | copy-start | bytes 12292
  41.2 84.8 %collective-permute-start.12 = (bf16[256,1024]{1,0:T(8,128)(2,1)S(1)}, bf16[256,1024]{1,0:T(8,128)(2,1)}, u32[]{:S(2)}, u32[]{:S(2)}) collective-permute-start(bf16[256,1024]{1,0:T(8,128)(2,1)S(1)} %get-tuple-element.38.refs_8_.refs_4_), channel_id=1, source_target_pairs={{0,8},{4,12},{8,16},{12,20},{16,24},{20,28},{24,0},{28,4},{1,9},{5... | collective-permute-start | bytes 1572872 | tf_op jit(solution)/shard_map/ppermute | solution.py:594
  52.2 28.7 %collective-permute-start.4 = (bf16[256,1024]{1,0:T(8,128)(2,1)}, bf16[256,1024]{1,0:T(8,128)(2,1)S(1)}, u32[]{:S(2)}, u32[]{:S(2)}) collective-permute-start(bf16[256,1024]{1,0:T(8,128)(2,1)} %collective-permute-done.3.refs_0_), channel_id=1, source_target_pairs={{0,1},{1,0},{2,3},{3,2},{4,5},{5,4},{6,7},{7,6},{8,9},{9,8},{10,11... | collective-permute-start | bytes 1572872 | tf_op jit(solution)/shard_map/ppermute | solution.py:20
  52.2 36.6 %collective-permute-start.6 = (bf16[256,1024]{1,0:T(8,128)(2,1)}, bf16[256,1024]{1,0:T(8,128)(2,1)S(1)}, u32[]{:S(2)}, u32[]{:S(2)}) collective-permute-start(bf16[256,1024]{1,0:T(8,128)(2,1)} %collective-permute-done.5.refs_0_), channel_id=1, source_target_pairs={{0,1},{1,0},{2,3},{3,2},{4,5},{5,4},{6,7},{7,6},{8,9},{9,8},{10,11... | collective-permute-start | bytes 1572872 | tf_op jit(solution)/shard_map/ppermute | solution.py:20
  117.2 3.3 %copy-start = (f32[2,1024,1024]{2,1,0:T(8,128)}, f32[2,1024,1024]{2,1,0:T(8,128)S(1)}, u32[]{:S(2)}) copy-start(f32[2,1024,1024]{2,1,0:T(8,128)S(1)} %get-tuple-element.31.run_ref) | copy-start | bytes 25165828
  120.5 10.6 %all-to-all-start.1 = ((f32[8,2,1024]{2,1,0:T(2,128)}), f32[8,2,1024]{2,1,0:T(2,128)S(1)}, u32[]{:S(2)}, u32[]{:S(2)}) async-start(f32[8,2,1024]{2,1,0:T(2,128)} %get-tuple-element.33), calls=%async_computation.1 | async-start | bytes 131072 | tf_op jit(solution)/shard_map/all_to_all | solution.py:662
  123.9 15.5 %collective-permute-start.11 = (bf16[256,1024]{1,0:T(8,128)(2,1)S(1)}, bf16[256,1024]{1,0:T(8,128)(2,1)S(1)}, u32[]{:S(2)}, u32[]{:S(2)}) collective-permute-start(bf16[256,1024]{1,0:T(8,128)(2,1)S(1)} %get-tuple-element.37.refs_9_.refs_5_), channel_id=1, source_target_pairs={{0,4},{4,0},{8,12},{12,8},{16,20},{20,16},{24,28},{28,24},{1,5},{5... | collective-permute-start | bytes 1572872 | tf_op jit(solution)/shard_map/ppermute | solution.py:20
  125.8 24.8 %collective-permute-start.10 = (bf16[256,1024]{1,0:T(8,128)(2,1)S(1)}, bf16[256,1024]{1,0:T(8,128)(2,1)}, u32[]{:S(2)}, u32[]{:S(2)}) collective-permute-start(bf16[256,1024]{1,0:T(8,128)(2,1)S(1)} %get-tuple-element.38.refs_8_.refs_4_), channel_id=1, source_target_pairs={{0,4},{4,0},{8,12},{12,8},{16,20},{20,16},{24,28},{28,24},{1,5},{5... | collective-permute-start | bytes 1572872 | tf_op jit(solution)/shard_map/ppermute | solution.py:20
  126.0 26.1 %collective-permute-start.16 = (bf16[256,1024]{1,0:T(8,128)(2,1)}, bf16[256,1024]{1,0:T(8,128)(2,1)}, u32[]{:S(2)}, u32[]{:S(2)}) collective-permute-start(bf16[256,1024]{1,0:T(8,128)(2,1)} %collective-permute-done.12.refs_12_.refs_8_), channel_id=1, source_target_pairs={{0,8},{4,12},{8,16},{12,20},{16,24},{20,28},{24,0},{28,4},{1,9},{5... | collective-permute-start | bytes 1572872 | tf_op jit(solution)/shard_map/ppermute | solution.py:594
  127.8 25.7 %collective-permute-start.17 = (bf16[256,1024]{1,0:T(8,128)(2,1)}, bf16[256,1024]{1,0:T(8,128)(2,1)}, u32[]{:S(2)}, u32[]{:S(2)}) collective-permute-start(bf16[256,1024]{1,0:T(8,128)(2,1)} %collective-permute-done.13.refs_13_.refs_9_), channel_id=1, source_target_pairs={{0,8},{4,12},{8,16},{12,20},{16,24},{20,28},{24,0},{28,4},{1,9},{5... | collective-permute-start | bytes 1572872 | tf_op jit(solution)/shard_map/ppermute | solution.py:594
  131.2 3.4 %copy-start.1 = (f32[2,1024,1024]{2,1,0:T(8,128)S(1)}, f32[2,1024,1024]{2,1,0:T(8,128)}, u32[]{:S(2)}) copy-start(f32[2,1024,1024]{2,1,0:T(8,128)} %copy-done) | copy-start | bytes 25165828
  137.9 44.3 %collective-permute-start.25 = (bf16[512,1024]{1,0:T(8,128)(2,1)S(1)}, bf16[512,1024]{1,0:T(8,128)(2,1)S(1)}, u32[]{:S(2)}, u32[]{:S(2)}) collective-permute-start(bf16[512,1024]{1,0:T(8,128)(2,1)S(1)} %shard_map.78.refs_0_), channel_id=1, source_target_pairs={{0,2},{1,3},{2,0},{3,1},{4,6},{5,7},{6,4},{7,5},{8,10},{9,11},{10,... | collective-permute-start | bytes 3145736 | tf_op jit(solution)/shard_map/ppermute | solution.py:20
  139.4 22.4 %collective-permute-start.15 = (bf16[256,1024]{1,0:T(8,128)(2,1)}, bf16[256,1024]{1,0:T(8,128)(2,1)S(1)}, u32[]{:S(2)}, u32[]{:S(2)}) collective-permute-start(bf16[256,1024]{1,0:T(8,128)(2,1)} %collective-permute-done.13.refs_13_.refs_9_), channel_id=1, source_target_pairs={{0,4},{4,0},{8,12},{12,8},{16,20},{20,16},{24,28},{28,24},{1,5},{5... | collective-permute-start | bytes 1572872 | tf_op jit(solution)/shard_map/ppermute | solution.py:20
  150.7 22.4 %collective-permute-start.14 = (bf16[256,1024]{1,0:T(8,128)(2,1)}, bf16[256,1024]{1,0:T(8,128)(2,1)S(1)}, u32[]{:S(2)}, u32[]{:S(2)}) collective-permute-start(bf16[256,1024]{1,0:T(8,128)(2,1)} %collective-permute-done.12.refs_12_.refs_8_), channel_id=1, source_target_pairs={{0,4},{4,0},{8,12},{12,8},{16,20},{20,16},{24,28},{28,24},{1,5},{5... | collective-permute-start | bytes 1572872 | tf_op jit(solution)/shard_map/ppermute | solution.py:20
  152.1 22.4 %collective-permute-start.20 = (bf16[256,1024]{1,0:T(8,128)(2,1)}, bf16[256,1024]{1,0:T(8,128)(2,1)S(1)}, u32[]{:S(2)}, u32[]{:S(2)}) collective-permute-start(bf16[256,1024]{1,0:T(8,128)(2,1)} %collective-permute-done.16.refs_16_.refs_12_), channel_id=1, source_target_pairs={{0,8},{4,12},{8,16},{12,20},{16,24},{20,28},{24,0},{28,4},{1,9},{5... | collective-permute-start | bytes 1572872 | tf_op jit(solution)/shard_map/ppermute | solution.py:594
  153.5 28.6 %collective-permute-start.18 = (bf16[256,1024]{1,0:T(8,128)(2,1)}, bf16[256,1024]{1,0:T(8,128)(2,1)S(1)}, u32[]{:S(2)}, u32[]{:S(2)}) collective-permute-start(bf16[256,1024]{1,0:T(8,128)(2,1)} %collective-permute-done.16.refs_16_.refs_12_), channel_id=1, source_target_pairs={{0,4},{4,0},{8,12},{12,8},{16,20},{20,16},{24,28},{28,24},{1,5},{5... | collective-permute-start | bytes 1572872 | tf_op jit(solution)/shard_map/ppermute | solution.py:20
  161.8 20.9 %collective-permute-start.8 = (bf16[256,1024]{1,0:T(8,128)(2,1)S(1)}, bf16[256,1024]{1,0:T(8,128)(2,1)S(1)}, u32[]{:S(2)}, u32[]{:S(2)}) collective-permute-start(bf16[256,1024]{1,0:T(8,128)(2,1)S(1)} %shard_map.77.refs_0_), channel_id=1, source_target_pairs={{0,2},{1,3},{2,0},{3,1},{4,6},{5,7},{6,4},{7,5},{8,10},{9,11},{10,... | collective-permute-start | bytes 1572872 | tf_op jit(solution)/shard_map/ppermute | solution.py:20
  173.0 9.7 %collective-permute-start.28 = (bf16[256,1024]{1,0:T(8,128)(2,1)S(1)}, bf16[256,1024]{1,0:T(8,128)(2,1)S(1)}, u32[]{:S(2)}, u32[]{:S(2)}) collective-permute-start(bf16[256,1024]{1,0:T(8,128)(2,1)S(1)} %shard_map.79.refs_4_), channel_id=1, source_target_pairs={{0,2},{1,3},{2,0},{3,1},{4,6},{5,7},{6,4},{7,5},{8,10},{9,11},{10,... | collective-permute-start | bytes 1572872 | tf_op jit(solution)/shard_map/ppermute | solution.py:20
  174.5 11.4 %collective-permute-start.21 = (bf16[256,1024]{1,0:T(8,128)(2,1)}, bf16[256,1024]{1,0:T(8,128)(2,1)S(1)}, u32[]{:S(2)}, u32[]{:S(2)}) collective-permute-start(bf16[256,1024]{1,0:T(8,128)(2,1)} %collective-permute-done.17.refs_17_.refs_13_), channel_id=1, source_target_pairs={{0,8},{4,12},{8,16},{12,20},{16,24},{20,28},{24,0},{28,4},{1,9},{5... | collective-permute-start | bytes 1572872 | tf_op jit(solution)/shard_map/ppermute | solution.py:594
  182.1 17.0 %collective-permute-start.24 = (bf16[512,1024]{1,0:T(8,128)(2,1)S(1)}, bf16[512,1024]{1,0:T(8,128)(2,1)S(1)}, u32[]{:S(2)}, u32[]{:S(2)}) collective-permute-start(bf16[512,1024]{1,0:T(8,128)(2,1)S(1)} %shard_map.78.refs_0_), channel_id=1, source_target_pairs={{0,1},{1,0},{2,3},{3,2},{4,5},{5,4},{6,7},{7,6},{8,9},{9,8},{10,11... | collective-permute-start | bytes 3145736 | tf_op jit(solution)/shard_map/ppermute | solution.py:20
  182.1 17.5 %collective-permute-start.26 = (bf16[512,1024]{1,0:T(8,128)(2,1)S(1)}, bf16[512,1024]{1,0:T(8,128)(2,1)S(1)}, u32[]{:S(2)}, u32[]{:S(2)}) collective-permute-start(bf16[512,1024]{1,0:T(8,128)(2,1)S(1)} %collective-permute-done.25.refs_2_), channel_id=1, source_target_pairs={{0,1},{1,0},{2,3},{3,2},{4,5},{5,4},{6,7},{7,6},{8,9},{9,8},{10,11... | collective-permute-start | bytes 3145736 | tf_op jit(solution)/shard_map/ppermute | solution.py:20
  182.7 4.4 %collective-permute-start.27 = (bf16[256,1024]{1,0:T(8,128)(2,1)S(1)}, bf16[256,1024]{1,0:T(8,128)(2,1)S(1)}, u32[]{:S(2)}, u32[]{:S(2)}) collective-permute-start(bf16[256,1024]{1,0:T(8,128)(2,1)S(1)} %shard_map.79.refs_4_), channel_id=1, source_target_pairs={{0,1},{1,0},{2,3},{3,2},{4,5},{5,4},{6,7},{7,6},{8,9},{9,8},{10,11... | collective-permute-start | bytes 1572872 | tf_op jit(solution)/shard_map/ppermute | solution.py:20
  182.7 15.0 %collective-permute-start.19 = (bf16[256,1024]{1,0:T(8,128)(2,1)}, bf16[256,1024]{1,0:T(8,128)(2,1)S(1)}, u32[]{:S(2)}, u32[]{:S(2)}) collective-permute-start(bf16[256,1024]{1,0:T(8,128)(2,1)} %collective-permute-done.17.refs_17_.refs_13_), channel_id=1, source_target_pairs={{0,4},{4,0},{8,12},{12,8},{16,20},{20,16},{24,28},{28,24},{1,5},{5... | collective-permute-start | bytes 1572872 | tf_op jit(solution)/shard_map/ppermute | solution.py:20
  186.0 13.2 %collective-permute-start.29 = (bf16[256,1024]{1,0:T(8,128)(2,1)S(1)}, bf16[256,1024]{1,0:T(8,128)(2,1)S(1)}, u32[]{:S(2)}, u32[]{:S(2)}) collective-permute-start(bf16[256,1024]{1,0:T(8,128)(2,1)S(1)} %collective-permute-done.28.refs_6_), channel_id=1, source_target_pairs={{0,1},{1,0},{2,3},{3,2},{4,5},{5,4},{6,7},{7,6},{8,9},{9,8},{10,11... | collective-permute-start | bytes 1572872 | tf_op jit(solution)/shard_map/ppermute | solution.py:20
  187.1 22.1 %collective-permute-start.22 = (bf16[256,1024]{1,0:T(8,128)(2,1)S(1)}, bf16[256,1024]{1,0:T(8,128)(2,1)S(1)}, u32[]{:S(2)}, u32[]{:S(2)}) collective-permute-start(bf16[256,1024]{1,0:T(8,128)(2,1)S(1)} %collective-permute-done.20.refs_8_.refs_16_), channel_id=1, source_target_pairs={{0,4},{4,0},{8,12},{12,8},{16,20},{20,16},{24,28},{28,24},{1,5},{5... | collective-permute-start | bytes 1572872 | tf_op jit(solution)/shard_map/ppermute | solution.py:20
  197.7 21.9 %collective-permute-start.23 = (bf16[256,1024]{1,0:T(8,128)(2,1)S(1)}, bf16[256,1024]{1,0:T(8,128)(2,1)S(1)}, u32[]{:S(2)}, u32[]{:S(2)}) collective-permute-start(bf16[256,1024]{1,0:T(8,128)(2,1)S(1)} %collective-permute-done.21.refs_9_.refs_17_), channel_id=1, source_target_pairs={{0,4},{4,0},{8,12},{12,8},{16,20},{20,16},{24,28},{28,24},{1,5},{5... | collective-permute-start | bytes 1572872 | tf_op jit(solution)/shard_map/ppermute | solution.py:20
  199.1 27.4 %collective-permute-start.7 = (bf16[256,1024]{1,0:T(8,128)(2,1)S(1)}, bf16[256,1024]{1,0:T(8,128)(2,1)S(1)}, u32[]{:S(2)}, u32[]{:S(2)}) collective-permute-start(bf16[256,1024]{1,0:T(8,128)(2,1)S(1)} %shard_map.77.refs_0_), channel_id=1, source_target_pairs={{0,1},{1,0},{2,3},{3,2},{4,5},{5,4},{6,7},{7,6},{8,9},{9,8},{10,11... | collective-permute-start | bytes 1572872 | tf_op jit(solution)/shard_map/ppermute | solution.py:20
  199.1 27.4 %collective-permute-start.9 = (bf16[256,1024]{1,0:T(8,128)(2,1)S(1)}, bf16[256,1024]{1,0:T(8,128)(2,1)S(1)}, u32[]{:S(2)}, u32[]{:S(2)}) collective-permute-start(bf16[256,1024]{1,0:T(8,128)(2,1)S(1)} %collective-permute-done.8.refs_2_), channel_id=1, source_target_pairs={{0,1},{1,0},{2,3},{3,2},{4,5},{5,4},{6,7},{7,6},{8,9},{9,8},{10,11... | collective-permute-start | bytes 1572872 | tf_op jit(solution)/shard_map/ppermute | solution.py:20
  219.7 1.9 copy-start.2

commit v4 on v3

v4 whole, which is shorter than its diff:
```python
import functools
import math

import jax
import jax.numpy as jnp
from jax import lax
from jax.experimental import pallas as pl
from jax.experimental.pallas import tpu as pltpu
from jax.sharding import PartitionSpec as P


SEGS = 8
LANES = 128
BLOCK = 256
F32 = jnp.float32
BF16 = jnp.bfloat16
MIB = 1024 * 1024


def swap(block, axis, bits):
    return lax.ppermute(block, axis, [(i, i ^ bits) for i in range(lax.axis_size(axis))])


def tile_of(width, most):
    return math.gcd(width, most)


def params(mib):
    return pltpu.CompilerParams(vmem_limit_bytes=mib * MIB)


def cost(flops, nbytes, trans=0):
    return pl.CostEstimate(flops=int(flops), bytes_accessed=int(nbytes), transcendentals=int(trans))


def near_kernel(half, tiles, heights, place, *refs):
    count = len(heights)
    blocks = refs[: half * count]
    w_ref, out_ref, lhs, wbuf, lsem, wsem = refs[half * count :]
    depth = blocks[0].shape[1]
    span = wbuf.shape[2]
    slot = lax.rem(place[0], half)
    base = (place[0] // half) * (half * depth)

    def w_copy(n):
        lines = pl.ds(pl.multiple_of(base, half * depth), half * depth)
        wide = pl.ds(pl.multiple_of(lax.rem(n, tiles) * span, span), span)
        return pltpu.make_async_copy(w_ref.at[n // tiles, lines, wide], wbuf.at[n], wsem.at[n])

    def l_copy(d, k):
        deep = pl.ds(pl.multiple_of((slot ^ d) * depth, depth), depth)
        top = sum(heights[:k])
        dst = lhs.at[top : top + heights[k], deep]
        return pltpu.make_async_copy(blocks[d * count + k], dst, lsem.at[d, k])

    steps = wbuf.shape[0]
    for n in range(steps):
        w_copy(n).start()
    for d in range(half):
        for k in range(count):
            l_copy(d, k).start()
    for d in range(half):
        for k in range(count):
            l_copy(d, k).wait()

    def body(n, carry):
        w_copy(n).wait()
        wide = pl.ds(pl.multiple_of(lax.rem(n, tiles) * span, span), span)
        total = None
        for d in range(half):
            deep = slice(d * depth, (d + 1) * depth)
            part = jnp.dot(lhs[:, deep], wbuf[n, deep, :], preferred_element_type=F32)
            total = part if total is None else total + part
        out_ref[n // tiles, :, wide] = total
        return carry

    lax.fori_loop(0, steps, body, 0)


def near_product(place, blocks, weights):
    half = len(blocks)
    heights = tuple(b.shape[0] for b in blocks[0])
    rows, depth = sum(heights), blocks[0][0].shape[1]
    gates, _, width = weights.shape
    span = tile_of(width, 512)
    tiles = width // span
    return pl.pallas_call(
        functools.partial(near_kernel, half, tiles, heights),
        out_shape=jax.ShapeDtypeStruct((gates, rows, width), F32),
        in_specs=[pl.BlockSpec(memory_space=pltpu.SMEM)]
        + [pl.BlockSpec(memory_space=pl.ANY)] * (half * len(heights))
        + [pl.BlockSpec(memory_space=pltpu.HBM)],
        out_specs=pl.BlockSpec(memory_space=pltpu.VMEM),
        scratch_shapes=[
            pltpu.VMEM((rows, half * depth), BF16),
            pltpu.VMEM((gates * tiles, half * depth, span), BF16),
            pltpu.SemaphoreType.DMA((half, len(heights))),
            pltpu.SemaphoreType.DMA((gates * tiles,)),
        ],
        compiler_params=params(28),
        cost_estimate=cost(
            2 * gates * rows * half * depth * width,
            gates * width * (half * depth * 2 + rows * 4) + half * rows * depth * 2,
        ),
    )(place, *[piece for block in blocks for piece in block], weights)


def row_order(transposed):
    shape = (BLOCK, BLOCK)
    row = lax.broadcasted_iota(jnp.int32, shape, 1 if transposed else 0)
    token = lax.broadcasted_iota(jnp.int32, shape, 0 if transposed else 1)
    chosen = lax.rem(row, SEGS) * (BLOCK // SEGS) + row // SEGS == token
    return jnp.where(chosen, 1.0, 0.0).astype(BF16)


def split_kernel(first, sizes, joined, src, *refs):
    count = len(sizes)
    outs = refs[:count]
    buf, sem = refs[-2:]
    blocks = sum(sizes) // BLOCK
    copies = []
    for k in range(blocks):
        lines = pl.ds(first + k * BLOCK, BLOCK)
        copies.append(pltpu.make_async_copy(src.at[lines, :], buf.at[k], sem.at[k]))
    for copy in copies:
        copy.start()
    order = row_order(False)
    k = 0
    for c in range(count):
        for r in range(sizes[c] // BLOCK):
            copies[k].wait()
            moved = jnp.dot(order, buf[k], preferred_element_type=F32).astype(BF16)
            outs[c][r * BLOCK : (r + 1) * BLOCK, :] = moved
            if joined:
                refs[count][k * BLOCK : (k + 1) * BLOCK, :] = moved
            k += 1


def split_rows(array, first, sizes, joined):
    vmem = pl.BlockSpec(memory_space=pltpu.VMEM)
    rows, width = sum(sizes), array.shape[1]
    shapes = list(sizes) + ([rows] if joined else [])
    return pl.pallas_call(
        functools.partial(split_kernel, first, tuple(sizes), joined),
        out_shape=[jax.ShapeDtypeStruct((r, width), array.dtype) for r in shapes],
        in_specs=[pl.BlockSpec(memory_space=pltpu.HBM)],
        out_specs=[vmem] * len(shapes),
        scratch_shapes=[
            pltpu.VMEM((rows // BLOCK, BLOCK, width), BF16),
            pltpu.SemaphoreType.DMA((rows // BLOCK,)),
        ],
        compiler_params=params(12),
        cost_estimate=cost(2 * rows * BLOCK * width, 4 * rows * width),
    )(array)


def compose_rows(maps, count, a, b):
    for k in range(count):
        slope = maps[0, k : k + 1, :]
        shift = maps[1, k : k + 1, :]
        b = slope * b + shift
        a = slope * a
    return a, b


def first_slopes(pre, cand, gain):
    update = jax.nn.sigmoid(pre)
    keep = 1.0 - update
    scaled = update * gain
    squashed = jnp.tanh(cand)
    slope = keep + (scaled - scaled * squashed * squashed)
    return update, keep, scaled, slope, update * squashed


def lead_row(place, start, shape):
    lead = lax.broadcasted_iota(jnp.int32, shape, 0) == 0
    return jnp.where(lead & (place[1] == 0), start, 0.0)


def around(update, keep, scaled, cand, gain, prev):
    squashed = jnp.tanh(cand + gain * prev)
    bend = scaled - scaled * squashed * squashed
    return keep + bend, update * squashed - bend * prev


def gate_kernel(half, first_row, rows, before, last, place, *refs):
    blocks = refs[:half]
    part_ref, w_ref, bias_ref, gain_ref, start_ref = refs[half : half + 5]
    earlier = refs[half + 5 : half + 5 + before]
    rest = refs[half + 5 + before :]
    if last:
        gates_ref, maps_ref, total_ref = rest[:3]
    else:
        gates_ref, maps_ref = rest[:2]
    wbuf, acc, wsem = rest[-3:]
    depth = blocks[0].shape[1]
    width = gain_ref.shape[1]
    seg = BLOCK // SEGS
    count = rows // BLOCK
    lines_of = wbuf.shape[3]
    parts = depth // lines_of
    slot = lax.rem(place[0], half)
    base = ((place[0] // half) ^ 1) * (half * depth)

    def w_copy(g, d, q):
        top = base + (slot ^ d) * depth + q * lines_of
        lines = pl.ds(pl.multiple_of(top, lines_of), lines_of)
        return pltpu.make_async_copy(w_ref.at[g, lines, :], wbuf.at[g, d, q], wsem.at[g, d, q])

    every = [(d, q) for d in range(half) for q in range(parts)]
    for g in range(2):
        for d, q in every:
            w_copy(g, d, q).start()
    for g in range(2):
        for d, q in every:
            w_copy(g, d, q).wait()
            deep = slice(q * lines_of, (q + 1) * lines_of)
            part = jnp.dot(blocks[d][:, deep], wbuf[g, d, q], preferred_element_type=F32)
            if (d, q) == (0, 0):
                acc[g] = part
            else:
                acc[g] += part

    span = tile_of(width, 512)

    def columns(n, carry_out):
        wide = pl.ds(pl.multiple_of(n * span, span), span)
        gain = jnp.broadcast_to(gain_ref[:, wide], (SEGS, span))
        bias = [jnp.broadcast_to(bias_ref[g : g + 1, wide], (2 * SEGS, span)) for g in range(2)]

        def pair(jj, carry, first):
            out = []
            for c in range(count):
                a, b = carry[c]
                lines = pl.ds(pl.multiple_of(c * BLOCK + jj * 2 * SEGS, 2 * SEGS), 2 * SEGS)
                deep = pl.ds(
                    pl.multiple_of(first_row + c * BLOCK + jj * 2 * SEGS, 2 * SEGS), 2 * SEGS
                )
                held = []
                for g in range(2):
                    total = acc[g, lines, wide] + part_ref[g, deep, wide] + bias[g]
                    rounded = total.astype(BF16)
                    gates_ref[g, lines, wide] = rounded
                    held.append(rounded.astype(F32))
                for k in range(2):
                    pre = held[0][k * SEGS : (k + 1) * SEGS]
                    cand = held[1][k * SEGS : (k + 1) * SEGS]
                    update, keep, scaled, slope, offset = first_slopes(pre, cand, gain)
                    if first and k == 0 and c == 0:
                        prev = lead_row(place, start_ref[:, wide], (SEGS, span))
                        slope, offset = around(update, keep, scaled, cand, gain, prev)
                    b = slope * b + offset
                    a = slope * a
                out.append((a, b))
            return tuple(out)

        carry = ((jnp.ones((SEGS, span), F32), jnp.zeros((SEGS, span), F32)),) * count
        begin = 0
        if first_row == 0:
            carry = pair(0, carry, True)
            begin = 1
        carry = lax.fori_loop(begin, seg // 2, lambda jj, c: pair(jj, c, False), carry)
        for c in range(count):
            maps_ref[0, c * SEGS : (c + 1) * SEGS, wide] = carry[c][0]
            maps_ref[1, c * SEGS : (c + 1) * SEGS, wide] = carry[c][1]
        return carry_out

    lax.fori_loop(0, width // span, columns, 0)
    if last:
        ta, tb = jnp.ones((1, width), F32), jnp.zeros((1, width), F32)
        for maps in list(earlier) + [maps_ref]:
            ta, tb = compose_rows(maps, maps.shape[1], ta, tb)
        for i in range(total_ref.shape[0]):
            total_ref[i, 0:1, :] = ta
            total_ref[i, 1:2, :] = tb


def gate_chunk(place, blocks, partial, weights, biases, gain, start, earlier, first_row, last, peers):
    half = len(blocks)
    rows, depth = blocks[0].shape
    gates, _, width = weights.shape
    lines_of = tile_of(depth, 512)
    vmem = pl.BlockSpec(memory_space=pltpu.VMEM)
    out_shape = [
        jax.ShapeDtypeStruct((2, rows, width), BF16),
        jax.ShapeDtypeStruct((2, rows // BLOCK * SEGS, width), F32),
    ]
    if last:
        out_shape.append(jax.ShapeDtypeStruct((peers, 2, width), F32))
    return pl.pallas_call(
        functools.partial(gate_kernel, half, first_row, rows, len(earlier), last),
        out_shape=out_shape,
        in_specs=[pl.BlockSpec(memory_space=pltpu.SMEM)]
        + [vmem] * (half + 1)
        + [pl.BlockSpec(memory_space=pltpu.HBM)]
        + [vmem] * (3 + len(earlier)),
        out_specs=[vmem] * len(out_shape),
        scratch_shapes=[
            pltpu.VMEM((gates, half, depth // lines_of, lines_of, width), BF16),
            pltpu.VMEM((gates, rows, width), F32),
            pltpu.SemaphoreType.DMA((gates, half, depth // lines_of)),
        ],
        compiler_params=params(32),
        cost_estimate=cost(
            2 * gates * rows * half * depth * width,
            gates * width * (half * depth * 2 + rows * 6) + half * rows * depth * 2,
            4 * rows * width,
        ),
    )(place, *blocks, partial, weights, biases, gain, start, *earlier)


def entering_state(place, peer_maps, start, peers):
    state = start
    for k in range(peers):
        moved = peer_maps[k, 0:1, :] * state + peer_maps[k, 1:2, :]
        state = jnp.where(place[1] > k, moved, state)
    return state


def enter_segments(maps_list, state, enter):
    row = 0
    for maps in maps_list:
        for k in range(maps.shape[1]):
            enter[row : row + 1, :] = state
            state = maps[0, k : k + 1, :] * state + maps[1, k : k + 1, :]
            row += 1


def bend_kernel(chunks, peers, place, *refs):
    gates = refs[:chunks]
    maps = refs[chunks : 2 * chunks]
    peer_ref, gain_ref, start_ref, run_ref, maps_ref, total_ref, enter = refs[2 * chunks :]
    span = gates[0].shape[2]
    width = gain_ref.shape[1]
    where = [(c, r * BLOCK) for c in range(chunks) for r in range(gates[c].shape[1] // BLOCK)]
    n = pl.program_id(0)

    @pl.when(n == 0)
    def _():
        enter_segments(maps, entering_state(place, peer_ref, start_ref[...], peers), enter)

    wide = pl.ds(pl.multiple_of(n * span, span), span)
    gain = jnp.broadcast_to(gain_ref[:, wide], (SEGS, span))

    def advance(block, jj, held, first):
        state, a, b = held
        c, top = where[block]
        lines = pl.ds(pl.multiple_of(top + jj * 2 * SEGS, 2 * SEGS), 2 * SEGS)
        pre2 = gates[c][0, lines, :].astype(F32)
        cand2 = gates[c][1, lines, :].astype(F32)
        for k in range(2):
            pre = pre2[k * SEGS : (k + 1) * SEGS]
            cand = cand2[k * SEGS : (k + 1) * SEGS]
            update, keep, scaled, slope, offset = first_slopes(pre, cand, gain)
            if first and k == 0 and block == 0:
                prev = lead_row(place, start_ref[:, wide], (SEGS, span))
                slope, offset = around(update, keep, scaled, cand, gain, prev)
            slope2, offset2 = around(update, keep, scaled, cand, gain, state)
            state = slope * state + offset
            b = slope2 * b + offset2
            a = slope2 * a
            row = pl.ds(pl.multiple_of(block * BLOCK + (2 * jj + k) * SEGS, SEGS), SEGS)
            run_ref[0, row, :] = a
            run_ref[1, row, :] = b
        return state, a, b

    def pair(jj, carry, first):
        return tuple(advance(m, jj, carry[m], first) for m in range(len(where)))

    one, zero = jnp.ones((SEGS, span), F32), jnp.zeros((SEGS, span), F32)
    carry = tuple((enter[m * SEGS : (m + 1) * SEGS, wide], one, zero) for m in range(len(where)))
    carry = pair(0, carry, True)
    carry = lax.fori_loop(1, BLOCK // SEGS // 2, lambda jj, c: pair(jj, c, False), carry)
    for m in range(len(where)):
        maps_ref[0, m * SEGS : (m + 1) * SEGS, wide] = carry[m][1]
        maps_ref[1, m * SEGS : (m + 1) * SEGS, wide] = carry[m][2]

    @pl.when(n == pl.num_programs(0) - 1)
    def _():
        ta, tb = jnp.ones((1, width), F32), jnp.zeros((1, width), F32)
        ta, tb = compose_rows(maps_ref, maps_ref.shape[1], ta, tb)
        for i in range(peers):
            total_ref[i, 0:1, :] = ta
            total_ref[i, 1:2, :] = tb


def bend_all(place, gates, maps, peer_maps, gain, start):
    chunks = len(gates)
    peers = peer_maps.shape[0]
    width = gates[0].shape[2]
    total_rows = sum(g.shape[1] for g in gates)
    segs = total_rows // BLOCK * SEGS
    tn = tile_of(width, 256)
    row_spec = pl.BlockSpec((1, width), lambda n, p: (0, 0))
    total_spec = pl.BlockSpec((peers, 2, width), lambda n, p: (0, 0, 0))
    return pl.pallas_call(
        functools.partial(bend_kernel, chunks, peers),
        out_shape=[
            jax.ShapeDtypeStruct((2, total_rows, width), F32),
            jax.ShapeDtypeStruct((2, segs, width), F32),
            jax.ShapeDtypeStruct((peers, 2, width), F32),
        ],
        grid_spec=pltpu.PrefetchScalarGridSpec(
            num_scalar_prefetch=1,
            grid=(width // tn,),
            in_specs=[pl.BlockSpec((2, g.shape[1], tn), lambda n, p: (0, 0, n)) for g in gates]
            + [pl.BlockSpec((2, m.shape[1], width), lambda n, p: (0, 0, 0)) for m in maps]
            + [total_spec, row_spec, row_spec],
            out_specs=[
                pl.BlockSpec((2, total_rows, tn), lambda n, p: (0, 0, n)),
                pl.BlockSpec((2, segs, width), lambda n, p: (0, 0, 0)),
                total_spec,
            ],
            scratch_shapes=[pltpu.VMEM((segs, width), F32)],
        ),
        compiler_params=params(16),
        cost_estimate=cost(
            40 * total_rows * width, 12 * total_rows * width, 5 * total_rows * width
        ),
        name="bend",
    )(place, *gates, *maps, peer_maps, gain, start)


def state_kernel(first_row, peers, place, run_ref, maps_ref, peer_ref, start_ref, out_ref, enter):
    rows = out_ref.shape[0]
    begin = first_row // BLOCK * SEGS
    state = entering_state(place, peer_ref, start_ref[...], peers)
    for k in range(begin + rows // BLOCK * SEGS):
        if k >= begin:
            enter[k - begin : k - begin + 1, :] = state
        state = maps_ref[0, k : k + 1, :] * state + maps_ref[1, k : k + 1, :]
    for c in range(rows // BLOCK):
        once = enter[c * SEGS : (c + 1) * SEGS, :]
        entered = jnp.concatenate([once, once], axis=0)

        def step(jj, carry):
            at = pl.multiple_of(c * BLOCK + jj * 2 * SEGS, 2 * SEGS)
            lines = pl.ds(at, 2 * SEGS)
            deep = pl.ds(pl.multiple_of(first_row + at, 2 * SEGS), 2 * SEGS)
            out_ref[lines, :] = (run_ref[0, deep, :] * entered + run_ref[1, deep, :]).astype(BF16)
            return carry

        lax.fori_loop(0, BLOCK // SEGS // 2, step, 0)


def state_chunk(place, run, maps, peer_maps, start, first_row, rows):
    width = run.shape[2]
    peers = peer_maps.shape[0]
    vmem = pl.BlockSpec(memory_space=pltpu.VMEM)
    return pl.pallas_call(
        functools.partial(state_kernel, first_row, peers),
        out_shape=jax.ShapeDtypeStruct((rows, width), BF16),
        in_specs=[pl.BlockSpec(memory_space=pltpu.SMEM)] + [vmem] * 4,
        out_specs=vmem,
        scratch_shapes=[pltpu.VMEM((rows // BLOCK * SEGS, width), F32)],
        compiler_params=params(16),
        cost_estimate=cost(2 * rows * width, 10 * rows * width),
    )(place, run, maps, peer_maps, start)


def mix_kernel(groups, group, pieces, peers, slots, final, before, place, *refs):
    count = groups * group
    blocks = refs[:count]
    weights = refs[count : count + len(slots) * 2 * pieces]
    out_ref, lhs, wbuf, acc, lsem, wsem = refs[-6:]
    prev_ref = refs[count + len(weights)] if before else None
    depth = blocks[0].shape[1]
    heights = [blocks[c * group].shape[0] for c in range(groups)]
    lines_of = weights[0].shape[0]
    outer = peers // 2
    here = len(slots) * 2

    def w_copy(n, p):
        w_ref = weights[n * pieces + p]
        dst = wbuf.at[n, p * lines_of : (p + 1) * lines_of, :]
        return pltpu.make_async_copy(w_ref, dst, wsem.at[n, p])

    def l_copy(c, d):
        deep = pl.ds(pl.multiple_of((place[0] ^ d) * depth, depth), depth)
        top = sum(heights[:c])
        dst = lhs.at[top : top + heights[c], deep]
        return pltpu.make_async_copy(blocks[c * group + d], dst, lsem.at[c, d])

    for n in range(here):
        for p in range(pieces):
            w_copy(n, p).start()
    for c in range(groups):
        for d in range(group):
            l_copy(c, d).start()
    for c in range(groups):
        for d in range(group):
            l_copy(c, d).wait()
    span = lines_of * pieces
    for n in range(here):
        source = lax.rem(place[1] // 2 + outer - slots[n // 2], outer)
        owner = source * 2 + (lax.rem(place[1], 2) ^ (n % 2))
        deep = pl.ds(pl.multiple_of(owner * span, span), span)
        for p in range(pieces):
            w_copy(n, p).wait()
        part = jnp.dot(lhs[:, deep], wbuf[n], preferred_element_type=F32)
        if n == 0 and before:
            part = part + prev_ref[...]
        if n > 0:
            part = acc[...] + part
        if n < here - 1:
            acc[...] = part
        elif not final:
            out_ref[...] = part
        else:
            acc[...] = part
            order = row_order(True)
            for m in range(acc.shape[0] // BLOCK):
                lines = slice(m * BLOCK, (m + 1) * BLOCK)
                rounded = acc[lines, :].astype(BF16)
                moved = jnp.dot(order, rounded, preferred_element_type=F32)
                out_ref[lines, :] = moved.astype(BF16)


def mix_rows(place, blocks, weights, slots, prev, final, whole, first, total_rows, pieces):
    groups, group = len(blocks), len(blocks[0])
    depth = blocks[0][0].shape[1]
    lines_of, width = weights[0].shape
    peers = len(weights) // pieces
    rows = sum(g[0].shape[0] for g in blocks)
    used = [weights[(s * 2 + i) * pieces + p] for s in slots for i in range(2) for p in range(pieces)]
    args = [place] + [b for g in blocks for b in g] + used
    in_specs = [pl.BlockSpec(memory_space=pl.ANY)] * (groups * group)
    in_specs += [pl.BlockSpec(memory_space=pltpu.HBM)] * len(used)
    if prev is not None:
        args.append(prev)
        in_specs.append(pl.BlockSpec((rows, width), lambda n, p: (0, 0)))
    aliases = {}
    if whole is not None:
        aliases = {len(args): 0}
        args.append(whole)
        in_specs.append(pl.BlockSpec(memory_space=pl.ANY))
    deep = len(slots) * 2 * pieces * lines_of
    if final:
        out_shape = jax.ShapeDtypeStruct((total_rows, width), BF16)
        out_spec = pl.BlockSpec((rows, width), lambda n, p: (first // rows, 0))
    else:
        out_shape = jax.ShapeDtypeStruct((rows, width), F32)
        out_spec = pl.BlockSpec((rows, width), lambda n, p: (0, 0))
    return pl.pallas_call(
        functools.partial(
            mix_kernel, groups, group, pieces, peers, tuple(slots), final, prev is not None
        ),
        out_shape=out_shape,
        grid_spec=pltpu.PrefetchScalarGridSpec(
            num_scalar_prefetch=1,
            grid=(1,),
            in_specs=in_specs,
            out_specs=out_spec,
            scratch_shapes=[
                pltpu.VMEM((rows, group * depth), BF16),
                pltpu.VMEM((len(slots) * 2, lines_of * pieces, width), BF16),
                pltpu.VMEM((rows, width), F32),
                pltpu.SemaphoreType.DMA((groups, group)),
                pltpu.SemaphoreType.DMA((len(slots) * 2, pieces)),
            ],
        ),
        input_output_aliases=aliases,
        compiler_params=params(40 if peers <= 8 else 62),
        cost_estimate=cost(2 * rows * deep * width, 2 * deep * (width + rows) + 4 * rows * width),
    )(*args)


EARLY = 5
SHARES = (2, 1, 1)


def pieces_of(lines_of):
    return 2 if lines_of % (4 * LANES) == 0 else 1


class Ring:
    def __init__(self, w_output):
        self.peers = lax.axis_size("ctx")
        self.outer = self.peers // 2
        self.pieces = pieces_of(w_output.shape[0])
        lines_of = w_output.shape[0] // self.pieces
        self.held = {}
        for p in range(self.pieces):
            self.held[0, 0, p] = w_output[p * lines_of : (p + 1) * lines_of]

    def ring_step(self, n, gate=None):
        s, p = n // self.pieces + 1, n % self.pieces
        block = self.held[s - 1, 0, p]
        if gate is not None:
            block, _ = lax.optimization_barrier((block, gate))
        route = [(i, (i + 2) % self.peers) for i in range(self.peers)]
        self.held[s, 0, p] = lax.ppermute(block, "ctx", route)

    def swap_step(self, n, gate=None):
        s, p = n // self.pieces, n % self.pieces
        block = self.held[s, 0, p]
        if gate is not None:
            block, _ = lax.optimization_barrier((block, gate))
        self.held[s, 1, p] = swap(block, "ctx", 1)

    def run(self, gate):
        rings, swaps = (self.outer - 1) * self.pieces, self.outer * self.pieces
        for n in range(max(rings, swaps)):
            g = gate if n >= EARLY else None
            if n < rings:
                self.ring_step(n, g)
            if n < swaps:
                self.swap_step(n, g)

    def blocks(self):
        steps = [(s, i) for s in range(self.outer) for i in range(2)]
        return [self.held[s, i, p] for s, i in steps for p in range(self.pieces)]


def layer(tokens, w_input, w_output, bias_update, bias_cand, recur_gain, start_state):
    peers = lax.axis_size("ctx")
    group = lax.axis_size("ch")
    half = group // 2
    total_rows = tokens.shape[0]
    chunks = len(SHARES)
    sizes = [total_rows * share // sum(SHARES) for share in SHARES]
    firsts = [sum(sizes[:c]) for c in range(chunks)]
    place = jnp.stack([lax.axis_index("ch"), lax.axis_index("ctx")]).astype(jnp.int32)
    biases = jnp.stack([bias_update, bias_cand], axis=0)
    gain = recur_gain[None, :]
    start = start_state[None, :]

    (head,) = split_rows(tokens, 0, sizes[:1], False)
    *others, tail = split_rows(tokens, sizes[0], sizes[1:], True)
    far = []
    for piece in [head, *others]:
        far.append([swap(piece, "ch", half)])
    near = [[head, tail]]
    for d in range(1, half):
        near.append([swap(head, "ch", d)])
        near[d].append(swap(tail, "ch", d))
    for c in range(chunks):
        for d in range(1, half):
            far[c].append(swap(far[c][0], "ch", d))

    partial = near_product(place, near, w_input)
    gates, maps = [], []
    for c in range(chunks):
        last = c == chunks - 1
        out = gate_chunk(
            place,
            far[c],
            partial,
            w_input,
            biases,
            gain,
            start,
            maps if last else [],
            firsts[c],
            last,
            peers,
        )
        gates.append(out[0])
        maps.append(out[1])
    peer_maps = lax.all_to_all(out[2], "ctx", 0, 0, tiled=True)
    run, run_maps, totals = bend_all(place, gates, maps, peer_maps, gain, start)
    peer_maps = lax.all_to_all(totals, "ctx", 0, 0, tiled=True)
    ring = Ring(w_output)
    ring.run(peer_maps)

    blocks = []
    for c in range(chunks):
        own = state_chunk(place, run, run_maps, peer_maps, start, firsts[c], sizes[c])
        across = swap(own, "ch", half)
        blocks.append([own, across])
    for c in range(chunks):
        own, across = blocks[c]
        lows, highs = [own], [across]
        for d in range(1, half):
            lows.append(swap(own, "ch", d))
            highs.append(swap(across, "ch", d))
        blocks[c] = lows + highs
    weights = ring.blocks()
    late = max(1, ring.outer // 4)
    slots = list(range(ring.outer))

    def mix(c, used, prev, final, whole):
        return mix_rows(
            place,
            blocks[c : c + 1],
            weights,
            used,
            prev,
            final,
            whole,
            firsts[c],
            total_rows,
            ring.pieces,
        )

    partial = mix(0, slots[:-late], None, False, None)
    mixed = mix(0, slots[-late:], partial, True, None)
    for c in range(1, chunks):
        mixed = mix(c, slots, None, True, mixed)
    return mixed


def solution(mesh):
    return jax.shard_map(
        layer,
        mesh=mesh,
        in_specs=(
            P("ctx", "ch"),
            P(None, None, "ch"),
            P("ctx", "ch"),
            P("ch"),
            P("ch"),
            P("ch"),
            P("ch"),
        ),
        out_specs=P("ctx", "ch"),
        check_vma=False,
    )
```

time: 232 us -> 228 us (0.983)
  waiting for transfers between devices: 92.7 us -> 108 us
  blocking collectives: 12.8 us -> 0 us
  Pallas kernels: 79.5 us -> 68.5 us
  local copies, waits for them, and re-layouts: 11.4 us -> 18.8 us
  starting transfers between devices: 34.9 us -> 31.8 us
    ppermute x24 -> x25, waiting for transfers between devices: 89 us -> 61.6 us  [swap(): lax.ppermute(block, axis, [(i, i ^ bits) for i in range(lax.axis_size(axi...]
    ppermute x6, waiting for transfers between devices: 1.85 us -> 19.2 us  [ring_step(): self.held[s, 0, p] = lax.ppermute(block, 'ctx', route)]
    all_to_all x1 -> x0, blocking collectives: 12.8 us -> none  [layer(): peer_maps = lax.all_to_all(out[2], 'ctx', 0, 0, tiled=True)]
    all_to_all x1, waiting for transfers between devices: 1.84 us -> 14.6 us  [layer(): peer_maps = lax.all_to_all(totals, 'ctx', 0, 0, tiled=True)]
    all_to_all x0 -> x1, waiting for transfers between devices: none -> 12.7 us  [layer(): peer_maps = lax.all_to_all(out[2], 'ctx', 0, 0, tiled=True)]
    pallas_call x8 -> x9, Pallas kernels: 52.4 us -> 41.5 us  [the longest x3 22 us: gate_chunk(): pl.pallas_call(functools.partial(gate_kernel, half, first_row, rows, len(...]
    unnamed x18 -> x40, local copies, waits for them, and re-layouts: 10.2 us -> 17.5 us
    all_to_all x0 -> x1, starting transfers between devices: none -> 6.08 us  [layer(): peer_maps = lax.all_to_all(out[2], 'ctx', 0, 0, tiled=True)]
  transfers between devices with their start and end apart: 31 -> 33, of which waited for: 12 -> 11; matrix products, arithmetic and copies ran while one was open for 1% -> 1% of each run, Pallas kernels for 32% -> 27%
where the time goes in v4:
time: 228 us
  waiting for transfers between devices  108 us (47%)
  Pallas kernels  68.5 us (30%)
  starting transfers between devices  31.8 us (14%)
  local copies, waits for them, and re-layouts  18.8 us (8%)
    ppermute x25, waiting for transfers between devices, swap(): lax.ppermute(block, axis, [(i, i ^ bits) for i in range(lax.axis_size(axi...  61.6 us
    pallas_call x3, Pallas kernels, gate_chunk(): pl.pallas_call(functools.partial(gate_kernel, half, first_row, rows, len(...  22 us
    pallas_call x4, Pallas kernels, mix_rows(): pl.pallas_call(functools.partial(mix_kernel, groups, group, pieces, peers...  20.2 us
    ppermute x6, waiting for transfers between devices, ring_step(): self.held[s, 0, p] = lax.ppermute(block, 'ctx', route)  19.2 us
    unnamed x40, local copies, waits for them, and re-layouts  17.5 us
    ppermute x25, starting transfers between devices, swap(): lax.ppermute(block, axis, [(i, i ^ bits) for i in range(lax.axis_size(axi...  15.6 us
    all_to_all x1, waiting for transfers between devices, layer(): peer_maps = lax.all_to_all(totals, 'ctx', 0, 0, tiled=True)  14.6 us
    pallas_call x1, Pallas kernels, near_product(): pl.pallas_call(functools.partial(near_kernel, half, tiles, heights), out_...  14.2 us
  transfers between devices with their start and end apart: 33, of which 11 were waited for; matrix products, arithmetic and copies ran while one was open for 1% of the time, Pallas kernels for 27%

profile of v4, /device:TPU:0, one launch (start us, length us, event | category | flops | bytes accessed | tf_op | source)
XLA Modules:
  0.0 227.8 jit_solution(12243810808656806260)
XLA Ops:
  0.0 1.6 copy-done.2
  2.3 3.0 %collective-permute-start = (bf16[512,1024]{1,0:T(8,128)(2,1)S(1)}, bf16[512,1024]{1,0:T(8,128)(2,1)}, u32[]{:S(2)}, u32[]{:S(2)}) collective-permute-start(bf16[512,1024]{1,0:T(8,128)(2,1)S(1)} %shard_map.73.refs_0_), channel_id=1, source_target_pairs={{0,2},{1,3},{2,0},{3,1},{4,6},{5,7},{6,4},{7,5},{8,10},{9,11},{10,... | collective-permute-start | bytes 3145736 | tf_op jit(solution)/shard_map/ppermute | solution.py:21
  5.4 1.9 shard_map.74
  7.9 1.9 collective-permute-start.6
  9.9 1.3 fusion
  11.2 18.3 %collective-permute-done.refs_0_ = bf16[512,1024]{1,0:T(8,128)(2,1)} collective-permute-done((bf16[512,1024]{1,0:T(8,128)(2,1)S(1)}, bf16[512,1024]{1,0:T(8,128)(2,1)}, u32[]{:S(2)}, u32[]{:S(2)}) %collective-permute-start) | collective-permute-done | bytes 1048608 | tf_op jit(solution)/shard_map/ppermute | solution.py:21
  29.6 11.1 %collective-permute-done.4.refs_0_ = bf16[256,1024]{1,0:T(8,128)(2,1)S(1)} collective-permute-done((bf16[256,1024]{1,0:T(8,128)(2,1)}, bf16[256,1024]{1,0:T(8,128)(2,1)S(1)}, u32[]{:S(2)}, u32[]{:S(2)}) %collective-permute-start.4) | collective-permute-done | bytes 524320 | tf_op jit(solution)/shard_map/ppermute | solution.py:21
  40.6 0.8 copy-done.3
  41.4 2.1 collective-permute-start.13
  43.6 7.5 %collective-permute-done.6.refs_0_ = bf16[256,1024]{1,0:T(8,128)(2,1)S(1)} collective-permute-done((bf16[256,1024]{1,0:T(8,128)(2,1)}, bf16[256,1024]{1,0:T(8,128)(2,1)S(1)}, u32[]{:S(2)}, u32[]{:S(2)}) %collective-permute-start.6) | collective-permute-done | bytes 524320 | tf_op jit(solution)/shard_map/ppermute | solution.py:21
  51.5 14.2 %shard_map.75.refs_2_ = f32[2,1024,1024]{2,1,0:T(8,128)S(1)} custom-call(s32[2]{0:T(128)S(1)} %pad_add_fusion.place, bf16[512,1024]{1,0:T(8,128)(2,1)S(1)} %shard_map.73.refs_0_, bf16[512,1024]{1,0:T(8,128)(2,1)} %get-tuple-element.21.refs_1_, bf16[512,1024]{1,0:T(8,128)(2,1)} %collective-permute-done.2.refs_2_, ...), custom_call_target="tpu_custom_call" | custom-call | flops 8589934592 | bytes 20971520 | tf_op jit(solution)/shard_map/pallas_call | solution.py:87
  65.8 5.8 %shard_map.77 = (bf16[2,256,1024]{2,1,0:T(8,128)(2,1)S(1)}, f32[2,8,1024]{2,1,0:T(8,128)S(1)}) custom-call(s32[2]{0:T(128)S(1)} %pad_add_fusion.place, bf16[256,1024]{1,0:T(8,128)(2,1)S(1)} %copy-done.4, bf16[256,1024]{1,0:T(8,128)(2,1)S(1)} %collective-permute-done.5.refs_1_, f32[2,1024,1024]{2,1,0:T(8,128)S(1)} %shard_map.75.refs_2_, ...), custom_call_target="tpu_custom_call" | custom-call | flops 2147483648 | bytes 12582912 | tf_op jit(solution)/shard_map/pallas_call | solution.py:290
  71.6 1.0 copy-done.12
  72.6 9.5 %shard_map.76 = (bf16[2,512,1024]{2,1,0:T(8,128)(2,1)S(1)}, f32[2,16,1024]{2,1,0:T(8,128)S(1)}) custom-call(s32[2]{0:T(128)S(1)} %pad_add_fusion.place, bf16[512,1024]{1,0:T(8,128)(2,1)} %collective-permute-done.refs_0_, bf16[512,1024]{1,0:T(8,128)(2,1)S(1)} %collective-permute-done.1.refs_1_, f32[2,1024,1024]{2,1,0:T(8,128)S(1)} %shard_map.75.refs_2_, ...), custom_call_target="tpu_custom_call" | custom-call | flops 4294967296 | bytes 16777216 | tf_op jit(solution)/shard_map/pallas_call | solution.py:290
  82.2 6.7 %shard_map.78 = (bf16[2,256,1024]{2,1,0:T(8,128)(2,1)S(1)}, f32[2,8,1024]{2,1,0:T(8,128)S(1)}, f32[8,2,1024]{2,1,0:T(2,128)}) custom-call(s32[2]{0:T(128)S(1)} %pad_add_fusion.place, bf16[256,1024]{1,0:T(8,128)(2,1)S(1)} %collective-permute-done.6.refs_0_, bf16[256,1024]{1,0:T(8,128)(2,1)S(1)} %collective-permute-done.7.refs_1_, ...), custom_call_target="tpu_custom_call" | custom-call | flops 2147483648 | bytes 12582912 | tf_op jit(solution)/shard_map/pallas_call | solution.py:290
  88.9 1.0 copy-done.14
  89.9 6.1 %all-to-all-start = ((f32[8,2,1024]{2,1,0:T(2,128)}), f32[8,2,1024]{2,1,0:T(2,128)S(1)}, u32[]{:S(2)}, u32[]{:S(2)}) async-start(f32[8,2,1024]{2,1,0:T(2,128)} %get-tuple-element.30), calls=%async_computation | async-start | bytes 131072 | tf_op jit(solution)/shard_map/all_to_all | solution.py:660
  96.0 2.0 collective-permute-start.14
  98.0 1.5 collective-permute-start.11
  100.0 12.7 %all-to-all-done.refs_6_ = f32[8,2,1024]{2,1,0:T(2,128)S(1)} async-done(((f32[8,2,1024]{2,1,0:T(2,128)}), f32[8,2,1024]{2,1,0:T(2,128)S(1)}, u32[]{:S(2)}, u32[]{:S(2)}) %all-to-all-start) | async-done | bytes 65568 | tf_op jit(solution)/shard_map/all_to_all | solution.py:660
  112.8 0.9 copy-done.7
  113.7 1.6 copy-done.11
  115.3 1.2 copy-done.13
  116.5 1.2 copy-done.15
  117.7 0.8 copy-done.17
  118.6 6.9 %bend.1 = (f32[2,1024,1024]{2,1,0:T(8,128)S(1)}, f32[2,32,1024]{2,1,0:T(8,128)S(1)}, f32[8,2,1024]{2,1,0:T(2,128)S(1)}) custom-call(s32[2]{0:T(128)S(1)} %pad_add_fusion.place, bf16[2,512,1024]{2,1,0:T(8,128)(2,1)S(1)} %copy-done.11, bf16[2,256,1024]{2,1,0:T(8,128)(2,1)S(1)} %copy-done.13, bf16[2,256,1024]{2,1,0:T(8,128)(2,1)S(1)} %copy-done.15, ...), custom_call_target="tpu_custom_call" | custom-call | flops 41943040 | bytes 12582912 | tf_op jit(solution)/shard_map/bend/pallas_call | solution.py:396
  125.5 3.3 %copy-done = f32[2,1024,1024]{2,1,0:T(8,128)} copy-done((f32[2,1024,1024]{2,1,0:T(8,128)}, f32[2,1024,1024]{2,1,0:T(8,128)S(1)}, u32[]{:S(2)}) %copy-start) | copy-done | bytes 8388632
  129.4 3.4 %all-to-all-start.1 = ((f32[8,2,1024]{2,1,0:T(2,128)}), f32[8,2,1024]{2,1,0:T(2,128)S(1)}, u32[]{:S(2)}, u32[]{:S(2)}) async-start(f32[8,2,1024]{2,1,0:T(2,128)} %copy-done.8), calls=%async_computation.1 | async-start | bytes 131072 | tf_op jit(solution)/shard_map/all_to_all | solution.py:662
  132.8 1.9 collective-permute-start.17
  134.7 14.6 %all-to-all-done.1.peer_ref = f32[8,2,1024]{2,1,0:T(2,128)S(1)} async-done(((f32[8,2,1024]{2,1,0:T(2,128)}), f32[8,2,1024]{2,1,0:T(2,128)S(1)}, u32[]{:S(2)}, u32[]{:S(2)}) %all-to-all-start.1) | async-done | bytes 65568 | tf_op jit(solution)/shard_map/all_to_all | solution.py:662
  149.3 3.4 %copy-done.1 = f32[2,1024,1024]{2,1,0:T(8,128)S(1)} copy-done((f32[2,1024,1024]{2,1,0:T(8,128)S(1)}, f32[2,1024,1024]{2,1,0:T(8,128)}, u32[]{:S(2)}) %copy-start.1) | copy-done | bytes 8388632
  152.7 1.0 shard_map.81.refs_0_
  154.7 1.1 collective-permute-start.15
  155.8 0.9 collective-permute-start.16
  156.7 1.1 collective-permute-start.19
  157.8 11.5 %collective-permute-done.18.refs_13_ = bf16[256,1024]{1,0:T(8,128)(2,1)S(1)} collective-permute-done((bf16[256,1024]{1,0:T(8,128)(2,1)S(1)}, bf16[256,1024]{1,0:T(8,128)(2,1)S(1)}, u32[]{:S(2)}, u32[]{:S(2)}) %collective-permute-start.18) | collective-permute-done | bytes 524320 | tf_op jit(solution)/shard_map/ppermute | solution.py:592
  169.3 0.8 shard_map.79.refs_0_
  170.5 4.6 %collective-permute-done.19.refs_14_ = bf16[256,1024]{1,0:T(8,128)(2,1)S(1)} collective-permute-done((bf16[256,1024]{1,0:T(8,128)(2,1)}, bf16[256,1024]{1,0:T(8,128)(2,1)S(1)}, u32[]{:S(2)}, u32[]{:S(2)}) %collective-permute-start.19) | collective-permute-done | bytes 524320 | tf_op jit(solution)/shard_map/ppermute | solution.py:21
  175.6 4.9 %collective-permute-done.21.refs_4_.refs_16_ = bf16[256,1024]{1,0:T(8,128)(2,1)S(1)} collective-permute-done((bf16[256,1024]{1,0:T(8,128)(2,1)}, bf16[256,1024]{1,0:T(8,128)(2,1)S(1)}, u32[]{:S(2)}, u32[]{:S(2)}) %collective-permute-start.21) | collective-permute-done | bytes 524320 | tf_op jit(solution)/shard_map/ppermute | solution.py:592
  180.5 0.8 shard_map.80.refs_0_
  181.3 2.1 collective-permute-start.23
  183.4 2.7 %collective-permute-done.22.refs_5_.refs_17_ = bf16[256,1024]{1,0:T(8,128)(2,1)S(1)} collective-permute-done((bf16[256,1024]{1,0:T(8,128)(2,1)S(1)}, bf16[256,1024]{1,0:T(8,128)(2,1)S(1)}, u32[]{:S(2)}, u32[]{:S(2)}) %collective-permute-start.22) | collective-permute-done | bytes 524320 | tf_op jit(solution)/shard_map/ppermute | solution.py:592
  186.1 9.2 %collective-permute-done.20.refs_15_ = bf16[256,1024]{1,0:T(8,128)(2,1)S(1)} collective-permute-done((bf16[256,1024]{1,0:T(8,128)(2,1)S(1)}, bf16[256,1024]{1,0:T(8,128)(2,1)S(1)}, u32[]{:S(2)}, u32[]{:S(2)}) %collective-permute-start.20) | collective-permute-done | bytes 524320 | tf_op jit(solution)/shard_map/ppermute | solution.py:21
  195.3 11.0 %collective-permute-done.23.refs_6_.refs_18_ = bf16[256,1024]{1,0:T(8,128)(2,1)S(1)} collective-permute-done((bf16[256,1024]{1,0:T(8,128)(2,1)S(1)}, bf16[256,1024]{1,0:T(8,128)(2,1)S(1)}, u32[]{:S(2)}, u32[]{:S(2)}) %collective-permute-start.23) | collective-permute-done | bytes 524320 | tf_op jit(solution)/shard_map/ppermute | solution.py:21
  207.4 5.6 %shard_map.82.refs_8_ = f32[512,1024]{1,0:T(8,128)S(1)} custom-call(s32[2]{0:T(128)S(1)} %pad_add_fusion.place, bf16[512,1024]{1,0:T(8,128)(2,1)S(1)} %shard_map.81.refs_0_, bf16[512,1024]{1,0:T(8,128)(2,1)S(1)} %collective-permute-done.28.refs_1_, bf16[512,1024]{1,0:T(8,128)(2,1)S(1)} %collective-permute-done.29.refs_2_, ...), custom_call_target="tpu_custom_call" | custom-call | flops 3221225472 | bytes 11534336 | tf_op jit(solution)/shard_map/pallas_call | solution.py:544
  213.0 4.2 %shard_map.83.refs_20_ = bf16[1024,1024]{1,0:T(8,128)(2,1)} custom-call(s32[2]{0:T(128)S(1)} %pad_add_fusion.place, bf16[512,1024]{1,0:T(8,128)(2,1)S(1)} %shard_map.81.refs_0_, bf16[512,1024]{1,0:T(8,128)(2,1)S(1)} %collective-permute-done.28.refs_1_, bf16[512,1024]{1,0:T(8,128)(2,1)S(1)} %collective-permute-done.29.refs_2_, ...), custom_call_target="tpu_custom_call" | custom-call | flops 1073741824 | bytes 5242880 | tf_op jit(solution)/shard_map/pallas_call | solution.py:544
  217.2 5.2 %shard_map.84.refs_20_ = bf16[1024,1024]{1,0:T(8,128)(2,1)} custom-call(s32[2]{0:T(128)S(1)} %pad_add_fusion.place, bf16[256,1024]{1,0:T(8,128)(2,1)S(1)} %shard_map.80.refs_0_, bf16[256,1024]{1,0:T(8,128)(2,1)S(1)} %collective-permute-done.25.refs_1_, bf16[256,1024]{1,0:T(8,128)(2,1)S(1)} %collective-permute-done.26.refs_2_, ...), custom_call_target="tpu_custom_call", output_to_operand_aliasing={{}: (21, {})} | custom-call | flops 2147483648 | bytes 11534336 | tf_op jit(solution)/shard_map/pallas_call | solution.py:544
  222.5 5.2 %shard_map.85 = bf16[1024,1024]{1,0:T(8,128)(2,1)} custom-call(s32[2]{0:T(128)S(1)} %pad_add_fusion.place, bf16[256,1024]{1,0:T(8,128)(2,1)S(1)} %shard_map.79.refs_0_, bf16[256,1024]{1,0:T(8,128)(2,1)S(1)} %collective-permute-done.8.refs_1_, bf16[256,1024]{1,0:T(8,128)(2,1)S(1)} %collective-permute-done.9.refs_2_, ...), custom_call_target="tpu_custom_call", output_to_operand_aliasing={{}: (21, {})} | custom-call | flops 2147483648 | bytes 11534336 | tf_op jit(solution)/shard_map/pallas_call | solution.py:544
  (75 shorter events, 6.2 us)
Async XLA Ops:
  0.0 1.6 copy-start.2
  1.6 8.3 %copy-start.18 = (f32[1024]{0:T(1024)S(1)}, f32[1024]{0:T(1024)}, u32[]{:S(2)}) copy-start(f32[1024]{0:T(1024)} %param.11) | copy-start | bytes 12292
  1.6 8.3 %copy-start.19 = (f32[1024]{0:T(1024)S(1)}, f32[1024]{0:T(1024)}, u32[]{:S(2)}) copy-start(f32[1024]{0:T(1024)} %param.10) | copy-start | bytes 12292
  2.3 27.1 %collective-permute-start = (bf16[512,1024]{1,0:T(8,128)(2,1)S(1)}, bf16[512,1024]{1,0:T(8,128)(2,1)}, u32[]{:S(2)}, u32[]{:S(2)}) collective-permute-start(bf16[512,1024]{1,0:T(8,128)(2,1)S(1)} %shard_map.73.refs_0_), channel_id=1, source_target_pairs={{0,2},{1,3},{2,0},{3,1},{4,6},{5,7},{6,4},{7,5},{8,10},{9,11},{10,... | collective-permute-start | bytes 3145736 | tf_op jit(solution)/shard_map/ppermute | solution.py:21
  5.4 45.6 %collective-permute-start.2 = (bf16[512,1024]{1,0:T(8,128)(2,1)S(1)}, bf16[512,1024]{1,0:T(8,128)(2,1)}, u32[]{:S(2)}, u32[]{:S(2)}) collective-permute-start(bf16[512,1024]{1,0:T(8,128)(2,1)S(1)} %shard_map.73.refs_0_), channel_id=1, source_target_pairs={{0,1},{1,0},{2,3},{3,2},{4,5},{5,4},{6,7},{7,6},{8,9},{9,8},{10,11... | collective-permute-start | bytes 3145736 | tf_op jit(solution)/shard_map/ppermute | solution.py:21
  7.3 44.3 %collective-permute-start.3 = (bf16[512,1024]{1,0:T(8,128)(2,1)}, bf16[512,1024]{1,0:T(8,128)(2,1)}, u32[]{:S(2)}, u32[]{:S(2)}) collective-permute-start(bf16[512,1024]{1,0:T(8,128)(2,1)} %get-tuple-element.21.refs_1_), channel_id=1, source_target_pairs={{0,1},{1,0},{2,3},{3,2},{4,5},{5,4},{6,7},{7,6},{8,9},{9,8},{10,11... | collective-permute-start | bytes 3145736 | tf_op jit(solution)/shard_map/ppermute | solution.py:21
  7.8 32.8 %collective-permute-start.4 = (bf16[256,1024]{1,0:T(8,128)(2,1)}, bf16[256,1024]{1,0:T(8,128)(2,1)S(1)}, u32[]{:S(2)}, u32[]{:S(2)}) collective-permute-start(bf16[256,1024]{1,0:T(8,128)(2,1)} %get-tuple-element.23), channel_id=1, source_target_pairs={{0,2},{1,3},{2,0},{3,1},{4,6},{5,7},{6,4},{7,5},{8,10},{9,11},{10,... | collective-permute-start | bytes 1572872 | tf_op jit(solution)/shard_map/ppermute | solution.py:21
  7.9 43.1 %collective-permute-start.6 = (bf16[256,1024]{1,0:T(8,128)(2,1)}, bf16[256,1024]{1,0:T(8,128)(2,1)S(1)}, u32[]{:S(2)}, u32[]{:S(2)}) collective-permute-start(bf16[256,1024]{1,0:T(8,128)(2,1)} %get-tuple-element.25), channel_id=1, source_target_pairs={{0,2},{1,3},{2,0},{3,1},{4,6},{5,7},{6,4},{7,5},{8,10},{9,11},{10,... | collective-permute-start | bytes 1572872 | tf_op jit(solution)/shard_map/ppermute | solution.py:21
  29.5 43.1 %collective-permute-start.1 = (bf16[512,1024]{1,0:T(8,128)(2,1)}, bf16[512,1024]{1,0:T(8,128)(2,1)S(1)}, u32[]{:S(2)}, u32[]{:S(2)}) collective-permute-start(bf16[512,1024]{1,0:T(8,128)(2,1)} %collective-permute-done.refs_0_), channel_id=1, source_target_pairs={{0,1},{1,0},{2,3},{3,2},{4,5},{5,4},{6,7},{7,6},{8,9},{9,8},{10,11... | collective-permute-start | bytes 3145736 | tf_op jit(solution)/shard_map/ppermute | solution.py:21
  41.4 24.3 %copy-start.4 = (bf16[256,1024]{1,0:T(8,128)(2,1)S(1)}, bf16[256,1024]{1,0:T(8,128)(2,1)}, u32[]{:S(2)}) copy-start(bf16[256,1024]{1,0:T(8,128)(2,1)} %copy-done.3) | copy-start | bytes 1572868
  41.4 24.3 %copy-start.5 = (f32[1024]{0:T(1024)S(1)}, f32[1024]{0:T(1024)}, u32[]{:S(2)}) copy-start(f32[1024]{0:T(1024)} %param.13) | copy-start | bytes 12292
  41.4 24.4 %copy-start.9 = (f32[1024]{0:T(1024)S(1)}, f32[1024]{0:T(1024)}, u32[]{:S(2)}) copy-start(f32[1024]{0:T(1024)} %param.12) | copy-start | bytes 12292
  41.4 91.3 %collective-permute-start.13 = (bf16[256,1024]{1,0:T(8,128)(2,1)S(1)}, bf16[256,1024]{1,0:T(8,128)(2,1)S(1)}, u32[]{:S(2)}, u32[]{:S(2)}) collective-permute-start(bf16[256,1024]{1,0:T(8,128)(2,1)S(1)} %get-tuple-element.38.refs_4_), channel_id=1, source_target_pairs={{0,8},{4,12},{8,16},{12,20},{16,24},{20,28},{24,0},{28,4},{1,9},{5... | collective-permute-start | bytes 1572872 | tf_op jit(solution)/shard_map/ppermute | solution.py:592
  51.0 14.8 %collective-permute-start.5 = (bf16[256,1024]{1,0:T(8,128)(2,1)}, bf16[256,1024]{1,0:T(8,128)(2,1)S(1)}, u32[]{:S(2)}, u32[]{:S(2)}) collective-permute-start(bf16[256,1024]{1,0:T(8,128)(2,1)} %copy-done.3), channel_id=1, source_target_pairs={{0,1},{1,0},{2,3},{3,2},{4,5},{5,4},{6,7},{7,6},{8,9},{9,8},{10,11... | collective-permute-start | bytes 1572872 | tf_op jit(solution)/shard_map/ppermute | solution.py:21
  51.0 31.1 %collective-permute-start.7 = (bf16[256,1024]{1,0:T(8,128)(2,1)S(1)}, bf16[256,1024]{1,0:T(8,128)(2,1)S(1)}, u32[]{:S(2)}, u32[]{:S(2)}) collective-permute-start(bf16[256,1024]{1,0:T(8,128)(2,1)S(1)} %collective-permute-done.6.refs_0_), channel_id=1, source_target_pairs={{0,1},{1,0},{2,3},{3,2},{4,5},{5,4},{6,7},{7,6},{8,9},{9,8},{10,11... | collective-permute-start | bytes 1572872 | tf_op jit(solution)/shard_map/ppermute | solution.py:21
  82.1 6.8 %copy-start.6 = (f32[2,16,1024]{2,1,0:T(8,128)}, f32[2,16,1024]{2,1,0:T(8,128)S(1)}, u32[]{:S(2)}) copy-start(f32[2,16,1024]{2,1,0:T(8,128)S(1)} %get-tuple-element.26.refs_7_.refs_3_) | copy-start | bytes 393220
  82.1 6.8 %copy-start.10 = (bf16[2,512,1024]{2,1,0:T(8,128)(2,1)}, bf16[2,512,1024]{2,1,0:T(8,128)(2,1)S(1)}, u32[]{:S(2)}) copy-start(bf16[2,512,1024]{2,1,0:T(8,128)(2,1)S(1)} %get-tuple-element.22.refs_0_) | copy-start | bytes 6291460
  88.9 1.0 copy-start.14
  89.9 6.1 %copy-start.16 = (f32[2,8,1024]{2,1,0:T(8,128)}, f32[2,8,1024]{2,1,0:T(8,128)S(1)}, u32[]{:S(2)}) copy-start(f32[2,8,1024]{2,1,0:T(8,128)S(1)} %get-tuple-element.29.refs_5_) | copy-start | bytes 196612
  89.9 22.9 %all-to-all-start = ((f32[8,2,1024]{2,1,0:T(2,128)}), f32[8,2,1024]{2,1,0:T(2,128)S(1)}, u32[]{:S(2)}, u32[]{:S(2)}) async-start(f32[8,2,1024]{2,1,0:T(2,128)} %get-tuple-element.30), calls=%async_computation | async-start | bytes 131072 | tf_op jit(solution)/shard_map/all_to_all | solution.py:660
  96.0 58.2 %collective-permute-start.14 = (bf16[256,1024]{1,0:T(8,128)(2,1)S(1)}, bf16[256,1024]{1,0:T(8,128)(2,1)S(1)}, u32[]{:S(2)}, u32[]{:S(2)}) collective-permute-start(bf16[256,1024]{1,0:T(8,128)(2,1)S(1)} %get-tuple-element.37.refs_5_), channel_id=1, source_target_pairs={{0,8},{4,12},{8,16},{12,20},{16,24},{20,28},{24,0},{28,4},{1,9},{5... | collective-permute-start | bytes 1572872 | tf_op jit(solution)/shard_map/ppermute | solution.py:592
  98.0 56.6 %collective-permute-start.11 = (bf16[256,1024]{1,0:T(8,128)(2,1)S(1)}, bf16[256,1024]{1,0:T(8,128)(2,1)S(1)}, u32[]{:S(2)}, u32[]{:S(2)}) collective-permute-start(bf16[256,1024]{1,0:T(8,128)(2,1)S(1)} %get-tuple-element.38.refs_4_), channel_id=1, source_target_pairs={{0,4},{4,0},{8,12},{12,8},{16,20},{20,16},{24,28},{28,24},{1,5},{5... | collective-permute-start | bytes 1572872 | tf_op jit(solution)/shard_map/ppermute | solution.py:21
  99.5 56.3 %collective-permute-start.12 = (bf16[256,1024]{1,0:T(8,128)(2,1)S(1)}, bf16[256,1024]{1,0:T(8,128)(2,1)S(1)}, u32[]{:S(2)}, u32[]{:S(2)}) collective-permute-start(bf16[256,1024]{1,0:T(8,128)(2,1)S(1)} %get-tuple-element.37.refs_5_), channel_id=1, source_target_pairs={{0,4},{4,0},{8,12},{12,8},{16,20},{20,16},{24,28},{28,24},{1,5},{5... | collective-permute-start | bytes 1572872 | tf_op jit(solution)/shard_map/ppermute | solution.py:21
  113.7 1.6 copy-start.11
  115.3 1.2 copy-start.13
  116.5 1.2 copy-start.15
  125.4 3.3 %copy-start = (f32[2,1024,1024]{2,1,0:T(8,128)}, f32[2,1024,1024]{2,1,0:T(8,128)S(1)}, u32[]{:S(2)}) copy-start(f32[2,1024,1024]{2,1,0:T(8,128)S(1)} %get-tuple-element.31.run_ref) | copy-start | bytes 25165828
  129.4 19.9 %all-to-all-start.1 = ((f32[8,2,1024]{2,1,0:T(2,128)}), f32[8,2,1024]{2,1,0:T(2,128)S(1)}, u32[]{:S(2)}, u32[]{:S(2)}) async-start(f32[8,2,1024]{2,1,0:T(2,128)} %copy-done.8), calls=%async_computation.1 | async-start | bytes 131072 | tf_op jit(solution)/shard_map/all_to_all | solution.py:662
  132.8 23.9 %collective-permute-start.17 = (bf16[256,1024]{1,0:T(8,128)(2,1)S(1)}, bf16[256,1024]{1,0:T(8,128)(2,1)}, u32[]{:S(2)}, u32[]{:S(2)}) collective-permute-start(bf16[256,1024]{1,0:T(8,128)(2,1)S(1)} %collective-permute-done.13.refs_8_), channel_id=1, source_target_pairs={{0,8},{4,12},{8,16},{12,20},{16,24},{20,28},{24,0},{28,4},{1,9},{5... | collective-permute-start | bytes 1572872 | tf_op jit(solution)/shard_map/ppermute | solution.py:592
  149.3 3.4 %copy-start.1 = (f32[2,1024,1024]{2,1,0:T(8,128)S(1)}, f32[2,1024,1024]{2,1,0:T(8,128)}, u32[]{:S(2)}) copy-start(f32[2,1024,1024]{2,1,0:T(8,128)} %copy-done) | copy-start | bytes 25165828
  153.6 21.5 %collective-permute-start.29 = (bf16[512,1024]{1,0:T(8,128)(2,1)S(1)}, bf16[512,1024]{1,0:T(8,128)(2,1)S(1)}, u32[]{:S(2)}, u32[]{:S(2)}) collective-permute-start(bf16[512,1024]{1,0:T(8,128)(2,1)S(1)} %shard_map.81.refs_0_), channel_id=1, source_target_pairs={{0,2},{1,3},{2,0},{3,1},{4,6},{5,7},{6,4},{7,5},{8,10},{9,11},{10,... | collective-permute-start | bytes 3145736 | tf_op jit(solution)/shard_map/ppermute | solution.py:21
  154.2 15.1 %collective-permute-start.18 = (bf16[256,1024]{1,0:T(8,128)(2,1)S(1)}, bf16[256,1024]{1,0:T(8,128)(2,1)S(1)}, u32[]{:S(2)}, u32[]{:S(2)}) collective-permute-start(bf16[256,1024]{1,0:T(8,128)(2,1)S(1)} %collective-permute-done.14.refs_9_), channel_id=1, source_target_pairs={{0,8},{4,12},{8,16},{12,20},{16,24},{20,28},{24,0},{28,4},{1,9},{5... | collective-permute-start | bytes 1572872 | tf_op jit(solution)/shard_map/ppermute | solution.py:592
  154.7 15.5 %collective-permute-start.15 = (bf16[256,1024]{1,0:T(8,128)(2,1)S(1)}, bf16[256,1024]{1,0:T(8,128)(2,1)S(1)}, u32[]{:S(2)}, u32[]{:S(2)}) collective-permute-start(bf16[256,1024]{1,0:T(8,128)(2,1)S(1)} %collective-permute-done.13.refs_8_), channel_id=1, source_target_pairs={{0,4},{4,0},{8,12},{12,8},{16,20},{20,16},{24,28},{28,24},{1,5},{5... | collective-permute-start | bytes 1572872 | tf_op jit(solution)/shard_map/ppermute | solution.py:21
  155.8 14.5 %collective-permute-start.16 = (bf16[256,1024]{1,0:T(8,128)(2,1)S(1)}, bf16[256,1024]{1,0:T(8,128)(2,1)S(1)}, u32[]{:S(2)}, u32[]{:S(2)}) collective-permute-start(bf16[256,1024]{1,0:T(8,128)(2,1)S(1)} %collective-permute-done.14.refs_9_), channel_id=1, source_target_pairs={{0,4},{4,0},{8,12},{12,8},{16,20},{20,16},{24,28},{28,24},{1,5},{5... | collective-permute-start | bytes 1572872 | tf_op jit(solution)/shard_map/ppermute | solution.py:21
  156.7 18.4 %collective-permute-start.19 = (bf16[256,1024]{1,0:T(8,128)(2,1)}, bf16[256,1024]{1,0:T(8,128)(2,1)S(1)}, u32[]{:S(2)}, u32[]{:S(2)}) collective-permute-start(bf16[256,1024]{1,0:T(8,128)(2,1)} %collective-permute-done.17.refs_12_), channel_id=1, source_target_pairs={{0,4},{4,0},{8,12},{12,8},{16,20},{20,16},{24,28},{28,24},{1,5},{5... | collective-permute-start | bytes 1572872 | tf_op jit(solution)/shard_map/ppermute | solution.py:21
  169.3 11.2 %collective-permute-start.21 = (bf16[256,1024]{1,0:T(8,128)(2,1)}, bf16[256,1024]{1,0:T(8,128)(2,1)S(1)}, u32[]{:S(2)}, u32[]{:S(2)}) collective-permute-start(bf16[256,1024]{1,0:T(8,128)(2,1)} %collective-permute-done.17.refs_12_), channel_id=1, source_target_pairs={{0,8},{4,12},{8,16},{12,20},{16,24},{20,28},{24,0},{28,4},{1,9},{5... | collective-permute-start | bytes 1572872 | tf_op jit(solution)/shard_map/ppermute | solution.py:592
  170.2 11.2 %collective-permute-start.9 = (bf16[256,1024]{1,0:T(8,128)(2,1)S(1)}, bf16[256,1024]{1,0:T(8,128)(2,1)S(1)}, u32[]{:S(2)}, u32[]{:S(2)}) collective-permute-start(bf16[256,1024]{1,0:T(8,128)(2,1)S(1)} %shard_map.79.refs_0_), channel_id=1, source_target_pairs={{0,2},{1,3},{2,0},{3,1},{4,6},{5,7},{6,4},{7,5},{8,10},{9,11},{10,... | collective-permute-start | bytes 1572872 | tf_op jit(solution)/shard_map/ppermute | solution.py:21
  170.3 15.9 %collective-permute-start.22 = (bf16[256,1024]{1,0:T(8,128)(2,1)S(1)}, bf16[256,1024]{1,0:T(8,128)(2,1)S(1)}, u32[]{:S(2)}, u32[]{:S(2)}) collective-permute-start(bf16[256,1024]{1,0:T(8,128)(2,1)S(1)} %collective-permute-done.18.refs_13_), channel_id=1, source_target_pairs={{0,8},{4,12},{8,16},{12,20},{16,24},{20,28},{24,0},{28,4},{1,9},{5... | collective-permute-start | bytes 1572872 | tf_op jit(solution)/shard_map/ppermute | solution.py:592
  175.1 31.8 %collective-permute-start.28 = (bf16[512,1024]{1,0:T(8,128)(2,1)S(1)}, bf16[512,1024]{1,0:T(8,128)(2,1)S(1)}, u32[]{:S(2)}, u32[]{:S(2)}) collective-permute-start(bf16[512,1024]{1,0:T(8,128)(2,1)S(1)} %shard_map.81.refs_0_), channel_id=1, source_target_pairs={{0,1},{1,0},{2,3},{3,2},{4,5},{5,4},{6,7},{7,6},{8,9},{9,8},{10,11... | collective-permute-start | bytes 3145736 | tf_op jit(solution)/shard_map/ppermute | solution.py:21
  175.1 31.9 %collective-permute-start.30 = (bf16[512,1024]{1,0:T(8,128)(2,1)S(1)}, bf16[512,1024]{1,0:T(8,128)(2,1)S(1)}, u32[]{:S(2)}, u32[]{:S(2)}) collective-permute-start(bf16[512,1024]{1,0:T(8,128)(2,1)S(1)} %collective-permute-done.29.refs_2_), channel_id=1, source_target_pairs={{0,1},{1,0},{2,3},{3,2},{4,5},{5,4},{6,7},{7,6},{8,9},{9,8},{10,11... | collective-permute-start | bytes 3145736 | tf_op jit(solution)/shard_map/ppermute | solution.py:21
  180.5 14.8 %collective-permute-start.20 = (bf16[256,1024]{1,0:T(8,128)(2,1)S(1)}, bf16[256,1024]{1,0:T(8,128)(2,1)S(1)}, u32[]{:S(2)}, u32[]{:S(2)}) collective-permute-start(bf16[256,1024]{1,0:T(8,128)(2,1)S(1)} %collective-permute-done.18.refs_13_), channel_id=1, source_target_pairs={{0,4},{4,0},{8,12},{12,8},{16,20},{20,16},{24,28},{28,24},{1,5},{5... | collective-permute-start | bytes 1572872 | tf_op jit(solution)/shard_map/ppermute | solution.py:21
  181.3 25.0 %collective-permute-start.23 = (bf16[256,1024]{1,0:T(8,128)(2,1)S(1)}, bf16[256,1024]{1,0:T(8,128)(2,1)S(1)}, u32[]{:S(2)}, u32[]{:S(2)}) collective-permute-start(bf16[256,1024]{1,0:T(8,128)(2,1)S(1)} %collective-permute-done.21.refs_4_.refs_16_), channel_id=1, source_target_pairs={{0,4},{4,0},{8,12},{12,8},{16,20},{20,16},{24,28},{28,24},{1,5},{5... | collective-permute-start | bytes 1572872 | tf_op jit(solution)/shard_map/ppermute | solution.py:21
  186.1 20.2 %collective-permute-start.26 = (bf16[256,1024]{1,0:T(8,128)(2,1)S(1)}, bf16[256,1024]{1,0:T(8,128)(2,1)S(1)}, u32[]{:S(2)}, u32[]{:S(2)}) collective-permute-start(bf16[256,1024]{1,0:T(8,128)(2,1)S(1)} %shard_map.80.refs_0_), channel_id=1, source_target_pairs={{0,2},{1,3},{2,0},{3,1},{4,6},{5,7},{6,4},{7,5},{8,10},{9,11},{10,... | collective-permute-start | bytes 1572872 | tf_op jit(solution)/shard_map/ppermute | solution.py:21
  195.3 17.6 %collective-permute-start.24 = (bf16[256,1024]{1,0:T(8,128)(2,1)S(1)}, bf16[256,1024]{1,0:T(8,128)(2,1)S(1)}, u32[]{:S(2)}, u32[]{:S(2)}) collective-permute-start(bf16[256,1024]{1,0:T(8,128)(2,1)S(1)} %collective-permute-done.22.refs_5_.refs_17_), channel_id=1, source_target_pairs={{0,4},{4,0},{8,12},{12,8},{16,20},{20,16},{24,28},{28,24},{1,5},{5... | collective-permute-start | bytes 1572872 | tf_op jit(solution)/shard_map/ppermute | solution.py:21
  206.3 10.9 %collective-permute-start.25 = (bf16[256,1024]{1,0:T(8,128)(2,1)S(1)}, bf16[256,1024]{1,0:T(8,128)(2,1)S(1)}, u32[]{:S(2)}, u32[]{:S(2)}) collective-permute-start(bf16[256,1024]{1,0:T(8,128)(2,1)S(1)} %shard_map.80.refs_0_), channel_id=1, source_target_pairs={{0,1},{1,0},{2,3},{3,2},{4,5},{5,4},{6,7},{7,6},{8,9},{9,8},{10,11... | collective-permute-start | bytes 1572872 | tf_op jit(solution)/shard_map/ppermute | solution.py:21
  206.4 10.9 %collective-permute-start.27 = (bf16[256,1024]{1,0:T(8,128)(2,1)S(1)}, bf16[256,1024]{1,0:T(8,128)(2,1)S(1)}, u32[]{:S(2)}, u32[]{:S(2)}) collective-permute-start(bf16[256,1024]{1,0:T(8,128)(2,1)S(1)} %collective-permute-done.26.refs_2_), channel_id=1, source_target_pairs={{0,1},{1,0},{2,3},{3,2},{4,5},{5,4},{6,7},{7,6},{8,9},{9,8},{10,11... | collective-permute-start | bytes 1572872 | tf_op jit(solution)/shard_map/ppermute | solution.py:21
  206.9 15.6 %collective-permute-start.8 = (bf16[256,1024]{1,0:T(8,128)(2,1)S(1)}, bf16[256,1024]{1,0:T(8,128)(2,1)S(1)}, u32[]{:S(2)}, u32[]{:S(2)}) collective-permute-start(bf16[256,1024]{1,0:T(8,128)(2,1)S(1)} %shard_map.79.refs_0_), channel_id=1, source_target_pairs={{0,1},{1,0},{2,3},{3,2},{4,5},{5,4},{6,7},{7,6},{8,9},{9,8},{10,11... | collective-permute-start | bytes 1572872 | tf_op jit(solution)/shard_map/ppermute | solution.py:21
  206.9 15.5 %collective-permute-start.10 = (bf16[256,1024]{1,0:T(8,128)(2,1)S(1)}, bf16[256,1024]{1,0:T(8,128)(2,1)S(1)}, u32[]{:S(2)}, u32[]{:S(2)}) collective-permute-start(bf16[256,1024]{1,0:T(8,128)(2,1)S(1)} %collective-permute-done.9.refs_2_), channel_id=1, source_target_pairs={{0,1},{1,0},{2,3},{3,2},{4,5},{5,4},{6,7},{7,6},{8,9},{9,8},{10,11... | collective-permute-start | bytes 1572872 | tf_op jit(solution)/shard_map/ppermute | solution.py:21
  (5 other events, 4.2 us)

commit v5 on v4

--- a/solution.py
+++ b/solution.py
@@ -154,10 +154,10 @@
     )(array)
 
 
-def compose_rows(maps, count, a, b):
-    for k in range(count):
-        slope = maps[0, k : k + 1, :]
-        shift = maps[1, k : k + 1, :]
+def compose_rows(maps, cols, a, b):
+    for k in range(maps.shape[1]):
+        slope = maps[0, k : k + 1, cols]
+        shift = maps[1, k : k + 1, cols]
         b = slope * b + shift
         a = slope * a
     return a, b
@@ -183,7 +183,7 @@
     return keep + bend, update * squashed - bend * prev
 
 
-def gate_kernel(half, first_row, rows, before, last, place, *refs):
+def gate_kernel(half, first_row, rows, first_col, before, last, place, *refs):
     blocks = refs[:half]
     part_ref, w_ref, bias_ref, gain_ref, start_ref = refs[half : half + 5]
     earlier = refs[half + 5 : half + 5 + before]
@@ -194,7 +194,8 @@
         gates_ref, maps_ref = rest[:2]
     wbuf, acc, wsem = rest[-3:]
     depth = blocks[0].shape[1]
-    width = gain_ref.shape[1]
+    width = acc.shape[2]
+    cols = slice(first_col, first_col + width)
     seg = BLOCK // SEGS
     count = rows // BLOCK
     lines_of = wbuf.shape[3]
@@ -205,7 +206,7 @@
     def w_copy(g, d, q):
         top = base + (slot ^ d) * depth + q * lines_of
         lines = pl.ds(pl.multiple_of(top, lines_of), lines_of)
-        return pltpu.make_async_copy(w_ref.at[g, lines, :], wbuf.at[g, d, q], wsem.at[g, d, q])
+        return pltpu.make_async_copy(w_ref.at[g, lines, cols], wbuf.at[g, d, q], wsem.at[g, d, q])
 
     every = [(d, q) for d in range(half) for q in range(parts)]
     for g in range(2):
@@ -225,8 +226,9 @@
 
     def columns(n, carry_out):
         wide = pl.ds(pl.multiple_of(n * span, span), span)
-        gain = jnp.broadcast_to(gain_ref[:, wide], (SEGS, span))
-        bias = [jnp.broadcast_to(bias_ref[g : g + 1, wide], (2 * SEGS, span)) for g in range(2)]
+        there = pl.ds(pl.multiple_of(first_col + n * span, span), span)
+        gain = jnp.broadcast_to(gain_ref[:, there], (SEGS, span))
+        bias = [jnp.broadcast_to(bias_ref[g : g + 1, there], (2 * SEGS, span)) for g in range(2)]
 
         def pair(jj, carry, first):
             out = []
@@ -238,7 +240,7 @@
                 )
                 held = []
                 for g in range(2):
-                    total = acc[g, lines, wide] + part_ref[g, deep, wide] + bias[g]
+                    total = acc[g, lines, wide] + part_ref[g, deep, there] + bias[g]
                     rounded = total.astype(BF16)
                     gates_ref[g, lines, wide] = rounded
                     held.append(rounded.astype(F32))
@@ -247,7 +249,7 @@
                     cand = held[1][k * SEGS : (k + 1) * SEGS]
                     update, keep, scaled, slope, offset = first_slopes(pre, cand, gain)
                     if first and k == 0 and c == 0:
-                        prev = lead_row(place, start_ref[:, wide], (SEGS, span))
+                        prev = lead_row(place, start_ref[:, there], (SEGS, span))
                         slope, offset = around(update, keep, scaled, cand, gain, prev)
                     b = slope * b + offset
                     a = slope * a
@@ -268,17 +270,21 @@
     lax.fori_loop(0, width // span, columns, 0)
     if last:
         ta, tb = jnp.ones((1, width), F32), jnp.zeros((1, width), F32)
-        for maps in list(earlier) + [maps_ref]:
-            ta, tb = compose_rows(maps, maps.shape[1], ta, tb)
+        for maps in earlier:
+            ta, tb = compose_rows(maps, cols, ta, tb)
+        ta, tb = compose_rows(maps_ref, slice(0, width), ta, tb)
         for i in range(total_ref.shape[0]):
             total_ref[i, 0:1, :] = ta
             total_ref[i, 1:2, :] = tb
 
 
-def gate_chunk(place, blocks, partial, weights, biases, gain, start, earlier, first_row, last, peers):
+def gate_chunk(
+    place, blocks, partial, weights, biases, gain, start, earlier, first_row, window, last, peers
+):
     half = len(blocks)
     rows, depth = blocks[0].shape
-    gates, _, width = weights.shape
+    gates = weights.shape[0]
+    first_col, width = window
     lines_of = tile_of(depth, 512)
     vmem = pl.BlockSpec(memory_space=pltpu.VMEM)
     out_shape = [
@@ -288,7 +294,7 @@
     if last:
         out_shape.append(jax.ShapeDtypeStruct((peers, 2, width), F32))
     return pl.pallas_call(
-        functools.partial(gate_kernel, half, first_row, rows, len(earlier), last),
+        functools.partial(gate_kernel, half, first_row, rows, first_col, len(earlier), last),
         out_shape=out_shape,
         in_specs=[pl.BlockSpec(memory_space=pltpu.SMEM)]
         + [vmem] * (half + 1)
@@ -378,20 +384,27 @@
     @pl.when(n == pl.num_programs(0) - 1)
     def _():
         ta, tb = jnp.ones((1, width), F32), jnp.zeros((1, width), F32)
-        ta, tb = compose_rows(maps_ref, maps_ref.shape[1], ta, tb)
+        ta, tb = compose_rows(maps_ref, slice(0, width), ta, tb)
         for i in range(peers):
             total_ref[i, 0:1, :] = ta
             total_ref[i, 1:2, :] = tb
 
 
-def bend_all(place, gates, maps, peer_maps, gain, start):
+def bend_all(place, gates, maps, peer_maps, gain, start, window):
     chunks = len(gates)
     peers = peer_maps.shape[0]
-    width = gates[0].shape[2]
+    first_col, width = window
     total_rows = sum(g.shape[1] for g in gates)
     segs = total_rows // BLOCK * SEGS
     tn = tile_of(width, 256)
-    row_spec = pl.BlockSpec((1, width), lambda n, p: (0, 0))
+    row_spec = pl.BlockSpec((1, width), lambda n, p: (0, first_col // width))
+
+    def columns(array, shape, wide):
+        offset = first_col // wide if array.shape[2] > width else 0
+        if wide == width:
+            return pl.BlockSpec(shape, lambda n, p: (0, 0, offset))
+        return pl.BlockSpec(shape, lambda n, p: (0, 0, n + offset))
+
     total_spec = pl.BlockSpec((peers, 2, width), lambda n, p: (0, 0, 0))
     return pl.pallas_call(
         functools.partial(bend_kernel, chunks, peers),
@@ -403,8 +416,8 @@
         grid_spec=pltpu.PrefetchScalarGridSpec(
             num_scalar_prefetch=1,
             grid=(width // tn,),
-            in_specs=[pl.BlockSpec((2, g.shape[1], tn), lambda n, p: (0, 0, n)) for g in gates]
-            + [pl.BlockSpec((2, m.shape[1], width), lambda n, p: (0, 0, 0)) for m in maps]
+            in_specs=[columns(g, (2, g.shape[1], tn), tn) for g in gates]
+            + [columns(m, (2, m.shape[1], width), width) for m in maps]
             + [total_spec, row_spec, row_spec],
             out_specs=[
                 pl.BlockSpec((2, total_rows, tn), lambda n, p: (0, 0, n)),
@@ -417,55 +430,63 @@
         cost_estimate=cost(
             40 * total_rows * width, 12 * total_rows * width, 5 * total_rows * width
         ),
-        name="bend",
     )(place, *gates, *maps, peer_maps, gain, start)
 
 
-def state_kernel(first_row, peers, place, run_ref, maps_ref, peer_ref, start_ref, out_ref, enter):
+def state_kernel(first_row, first_cols, peers, place, *refs):
+    sides = len(first_cols)
+    start_ref, out_ref, enter = refs[3 * sides :]
     rows = out_ref.shape[0]
     begin = first_row // BLOCK * SEGS
-    state = entering_state(place, peer_ref, start_ref[...], peers)
-    for k in range(begin + rows // BLOCK * SEGS):
-        if k >= begin:
-            enter[k - begin : k - begin + 1, :] = state
-        state = maps_ref[0, k : k + 1, :] * state + maps_ref[1, k : k + 1, :]
-    for c in range(rows // BLOCK):
-        once = enter[c * SEGS : (c + 1) * SEGS, :]
-        entered = jnp.concatenate([once, once], axis=0)
-
-        def step(jj, carry):
-            at = pl.multiple_of(c * BLOCK + jj * 2 * SEGS, 2 * SEGS)
-            lines = pl.ds(at, 2 * SEGS)
-            deep = pl.ds(pl.multiple_of(first_row + at, 2 * SEGS), 2 * SEGS)
-            out_ref[lines, :] = (run_ref[0, deep, :] * entered + run_ref[1, deep, :]).astype(BF16)
-            return carry
-
-        lax.fori_loop(0, BLOCK // SEGS // 2, step, 0)
-
-
-def state_chunk(place, run, maps, peer_maps, start, first_row, rows):
-    width = run.shape[2]
-    peers = peer_maps.shape[0]
+    for m in range(sides):
+        run_ref, maps_ref, peer_ref = refs[3 * m : 3 * m + 3]
+        width = run_ref.shape[2]
+        cols = slice(m * width, (m + 1) * width)
+        start = start_ref[:, first_cols[m] : first_cols[m] + width]
+        state = entering_state(place, peer_ref, start, peers)
+        for k in range(begin + rows // BLOCK * SEGS):
+            if k >= begin:
+                enter[k - begin : k - begin + 1, :] = state
+            state = maps_ref[0, k : k + 1, :] * state + maps_ref[1, k : k + 1, :]
+        for c in range(rows // BLOCK):
+            once = enter[c * SEGS : (c + 1) * SEGS, :]
+            entered = jnp.concatenate([once, once], axis=0)
+
+            def step(jj, carry):
+                at = pl.multiple_of(c * BLOCK + jj * 2 * SEGS, 2 * SEGS)
+                lines = pl.ds(at, 2 * SEGS)
+                deep = pl.ds(pl.multiple_of(first_row + at, 2 * SEGS), 2 * SEGS)
+                now = run_ref[0, deep, :] * entered + run_ref[1, deep, :]
+                out_ref[lines, cols] = now.astype(BF16)
+                return carry
+
+            lax.fori_loop(0, BLOCK // SEGS // 2, step, 0)
+
+
+def state_chunk(place, sides, start, first_row, rows):
+    peers = sides[0][3].shape[0]
+    widths = [side[1].shape[2] for side in sides]
     vmem = pl.BlockSpec(memory_space=pltpu.VMEM)
+    first_cols = tuple(side[0] for side in sides)
     return pl.pallas_call(
-        functools.partial(state_kernel, first_row, peers),
-        out_shape=jax.ShapeDtypeStruct((rows, width), BF16),
-        in_specs=[pl.BlockSpec(memory_space=pltpu.SMEM)] + [vmem] * 4,
+        functools.partial(state_kernel, first_row, first_cols, peers),
+        out_shape=jax.ShapeDtypeStruct((rows, sum(widths)), BF16),
+        in_specs=[pl.BlockSpec(memory_space=pltpu.SMEM)] + [vmem] * (3 * len(sides) + 1),
         out_specs=vmem,
-        scratch_shapes=[pltpu.VMEM((rows // BLOCK * SEGS, width), F32)],
+        scratch_shapes=[pltpu.VMEM((rows // BLOCK * SEGS, widths[0]), F32)],
         compiler_params=params(16),
-        cost_estimate=cost(2 * rows * width, 10 * rows * width),
-    )(place, run, maps, peer_maps, start)
-
-
-def mix_kernel(groups, group, pieces, peers, slots, final, before, place, *refs):
-    count = groups * group
+        cost_estimate=cost(2 * rows * sum(widths), 10 * rows * sum(widths)),
+    )(place, *[part for side in sides for part in side[1:]], start)
+
+
+def mix_kernel(sides, group, pieces, peers, slots, final, before, place, *refs):
+    count = sides * group
     blocks = refs[:count]
     weights = refs[count : count + len(slots) * 2 * pieces]
     out_ref, lhs, wbuf, acc, lsem, wsem = refs[-6:]
     prev_ref = refs[count + len(weights)] if before else None
-    depth = blocks[0].shape[1]
-    heights = [blocks[c * group].shape[0] for c in range(groups)]
+    part_of = blocks[0].shape[1]
+    depth = part_of * sides
     lines_of = weights[0].shape[0]
     outer = peers // 2
     here = len(slots) * 2
@@ -476,18 +497,18 @@
         return pltpu.make_async_copy(w_ref, dst, wsem.at[n, p])
 
     def l_copy(c, d):
-        deep = pl.ds(pl.multiple_of((place[0] ^ d) * depth, depth), depth)
-        top = sum(heights[:c])
-        dst = lhs.at[top : top + heights[c], deep]
-        return pltpu.make_async_copy(blocks[c * group + d], dst, lsem.at[c, d])
+        at = pl.multiple_of((place[0] ^ d) * depth + c * part_of, part_of)
+        return pltpu.make_async_copy(
+            blocks[c * group + d], lhs.at[:, pl.ds(at, part_of)], lsem.at[c, d]
+        )
 
     for n in range(here):
         for p in range(pieces):
             w_copy(n, p).start()
-    for c in range(groups):
+    for c in range(sides):
         for d in range(group):
             l_copy(c, d).start()
-    for c in range(groups):
+    for c in range(sides):
         for d in range(group):
             l_copy(c, d).wait()
     span = lines_of * pieces
@@ -517,14 +538,14 @@
 
 
 def mix_rows(place, blocks, weights, slots, prev, final, whole, first, total_rows, pieces):
-    groups, group = len(blocks), len(blocks[0])
-    depth = blocks[0][0].shape[1]
+    sides, group = len(blocks), len(blocks[0])
+    depth = blocks[0][0].shape[1] * sides
     lines_of, width = weights[0].shape
     peers = len(weights) // pieces
-    rows = sum(g[0].shape[0] for g in blocks)
+    rows = blocks[0][0].shape[0]
     used = [weights[(s * 2 + i) * pieces + p] for s in slots for i in range(2) for p in range(pieces)]
     args = [place] + [b for g in blocks for b in g] + used
-    in_specs = [pl.BlockSpec(memory_space=pl.ANY)] * (groups * group)
+    in_specs = [pl.BlockSpec(memory_space=pl.ANY)] * (sides * group)
     in_specs += [pl.BlockSpec(memory_space=pltpu.HBM)] * len(used)
     if prev is not None:
         args.append(prev)
@@ -543,7 +564,7 @@
         out_spec = pl.BlockSpec((rows, width), lambda n, p: (0, 0))
     return pl.pallas_call(
         functools.partial(
-            mix_kernel, groups, group, pieces, peers, tuple(slots), final, prev is not None
+            mix_kernel, sides, group, pieces, peers, tuple(slots), final, prev is not None
         ),
         out_shape=out_shape,
         grid_spec=pltpu.PrefetchScalarGridSpec(
@@ -555,7 +576,7 @@
                 pltpu.VMEM((rows, group * depth), BF16),
                 pltpu.VMEM((len(slots) * 2, lines_of * pieces, width), BF16),
                 pltpu.VMEM((rows, width), F32),
-                pltpu.SemaphoreType.DMA((groups, group)),
+                pltpu.SemaphoreType.DMA((sides, group)),
                 pltpu.SemaphoreType.DMA((len(slots) * 2, pieces)),
             ],
         ),
@@ -639,9 +660,9 @@
             far[c].append(swap(far[c][0], "ch", d))
 
     partial = near_product(place, near, w_input)
+    width = w_input.shape[2]
     gates, maps = [], []
-    for c in range(chunks):
-        last = c == chunks - 1
+    for c in range(chunks - 1):
         out = gate_chunk(
             place,
             far[c],
@@ -650,31 +671,55 @@
             biases,
             gain,
             start,
-            maps if last else [],
+            [],
             firsts[c],
-            last,
+            (0, width),
+            False,
             peers,
         )
         gates.append(out[0])
         maps.append(out[1])
-    peer_maps = lax.all_to_all(out[2], "ctx", 0, 0, tiled=True)
-    run, run_maps, totals = bend_all(place, gates, maps, peer_maps, gain, start)
-    peer_maps = lax.all_to_all(totals, "ctx", 0, 0, tiled=True)
+    windows = [(0, width // 2), (width // 2, width // 2)]
+    sides = []
+    for window in windows:
+        out = gate_chunk(
+            place,
+            far[-1],
+            partial,
+            w_input,
+            biases,
+            gain,
+            start,
+            maps,
+            firsts[-1],
+            window,
+            True,
+            peers,
+        )
+        peer_maps = lax.all_to_all(out[2], "ctx", 0, 0, tiled=True)
+        sides.append((out[0], out[1], peer_maps))
+    for m, window in enumerate(windows):
+        run, run_maps, totals = bend_all(
+            place, gates + [sides[m][0]], maps + [sides[m][1]], sides[m][2], gain, start, window
+        )
+        peer_maps = lax.all_to_all(totals, "ctx", 0, 0, tiled=True)
+        sides[m] = (window[0], run, run_maps, peer_maps)
     ring = Ring(w_output)
     ring.run(peer_maps)
 
-    blocks = []
-    for c in range(chunks):
-        own = state_chunk(place, run, run_maps, peer_maps, start, firsts[c], sizes[c])
-        across = swap(own, "ch", half)
-        blocks.append([own, across])
-    for c in range(chunks):
-        own, across = blocks[c]
+    plan = [(f"0{m}", 0, [sides[m]]) for m in range(len(sides))]
+    plan += [(f"{c}0", c, sides) for c in range(1, chunks)]
+    sent = []
+    for label, c, used in plan:
+        own = state_chunk(place, used, start, firsts[c], sizes[c])
+        sent.append((label, c, own, swap(own, "ch", half)))
+    blocks = [[] for _ in range(chunks)]
+    for label, c, own, across in sent:
         lows, highs = [own], [across]
         for d in range(1, half):
             lows.append(swap(own, "ch", d))
             highs.append(swap(across, "ch", d))
-        blocks[c] = lows + highs
+        blocks[c].append(lows + highs)
     weights = ring.blocks()
     late = max(1, ring.outer // 4)
     slots = list(range(ring.outer))
@@ -682,7 +727,7 @@
     def mix(c, used, prev, final, whole):
         return mix_rows(
             place,
-            blocks[c : c + 1],
+            blocks[c],
             weights,
             used,
             prev,

time: 228 us -> 231 us (1.013)
  waiting for transfers between devices: 108 us -> 63 us
  local copies, waits for them, and re-layouts: 18.8 us -> 33.5 us
  blocking collectives: 0 us -> 12.7 us
  starting transfers between devices: 31.8 us -> 44.5 us
  Pallas kernels: 68.5 us -> 74.6 us
    ppermute x6, waiting for transfers between devices: 19.2 us -> 0.02 us  [ring_step(): self.held[s, 0, p] = lax.ppermute(block, 'ctx', route)]
    unnamed x40 -> x86, local copies, waits for them, and re-layouts: 17.5 us -> 33.5 us
    all_to_all x1, waiting for transfers between devices: 14.6 us -> 0.01 us  [layer(): peer_maps = lax.all_to_all(totals, 'ctx', 0, 0, tiled=True)]
    all_to_all x1 -> x2, waiting for transfers between devices: 12.7 us -> 0.01 us  [layer(): peer_maps = lax.all_to_all(out[2], 'ctx', 0, 0, tiled=True)]
    all_to_all x0 -> x1, blocking collectives: none -> 12.7 us  [layer(): peer_maps = lax.all_to_all(totals, 'ctx', 0, 0, tiled=True)]
    pallas_call x10 -> x12, Pallas kernels: 44.8 us -> 50.2 us  [the longest x4 25.5 us: gate_chunk(): pl.pallas_call(functools.partial(gate_kernel, half, first_row, rows, firs...]
    all_to_all x1 -> x2, starting transfers between devices: 6.08 us -> 10.9 us  [layer(): peer_maps = lax.all_to_all(out[2], 'ctx', 0, 0, tiled=True)]
    ppermute x25 -> x28, starting transfers between devices: 15.6 us -> 20.3 us  [swap(): lax.ppermute(block, axis, [(i, i ^ bits) for i in range(lax.axis_size(axi...]
  transfers between devices with their start and end apart: 33 -> 37, of which waited for: 11 -> 8; matrix products, arithmetic and copies ran while one was open for 1% -> 0% of each run, Pallas kernels for 27% -> 30%
where the time goes in v5:
time: 231 us; the launch traced here: 229 us
  Pallas kernels  74.6 us (32%)
  waiting for transfers between devices  63 us (27%)
  starting transfers between devices  44.5 us (19%)
  local copies, waits for them, and re-layouts  33.5 us (15%)
  blocking collectives  12.7 us (5%)
    ppermute x28, waiting for transfers between devices, swap(): lax.ppermute(block, axis, [(i, i ^ bits) for i in range(lax.axis_size(axi...  63 us
    unnamed x86, local copies, waits for them, and re-layouts  33.5 us
    pallas_call x4, Pallas kernels, gate_chunk(): pl.pallas_call(functools.partial(gate_kernel, half, first_row, rows, firs...  25.5 us
    pallas_call x4, Pallas kernels, mix_rows(): pl.pallas_call(functools.partial(mix_kernel, sides, group, pieces, peers,...  20.4 us
    ppermute x28, starting transfers between devices, swap(): lax.ppermute(block, axis, [(i, i ^ bits) for i in range(lax.axis_size(axi...  20.3 us
    pallas_call x1, Pallas kernels, near_product(): pl.pallas_call(functools.partial(near_kernel, half, tiles, heights), out_...  14.3 us
    all_to_all x1, blocking collectives, layer(): peer_maps = lax.all_to_all(totals, 'ctx', 0, 0, tiled=True)  12.7 us
    all_to_all x2, starting transfers between devices, layer(): peer_maps = lax.all_to_all(out[2], 'ctx', 0, 0, tiled=True)  10.9 us
  transfers between devices with their start and end apart: 37, of which 8 were waited for; matrix products, arithmetic and copies ran while one was open for 0% of the time, Pallas kernels for 30%

profile of v5, /device:TPU:0, one launch (start us, length us, event | category | flops | bytes accessed | tf_op | source)
XLA Modules:
  0.0 229.1 jit_solution(4176937819232842663)
XLA Ops:
  0.0 1.6 copy-done.8
  2.4 3.0 %collective-permute-start = (bf16[512,1024]{1,0:T(8,128)(2,1)S(1)}, bf16[512,1024]{1,0:T(8,128)(2,1)}, u32[]{:S(2)}, u32[]{:S(2)}) collective-permute-start(bf16[512,1024]{1,0:T(8,128)(2,1)S(1)} %shard_map.73.refs_0_), channel_id=1, source_target_pairs={{0,2},{1,3},{2,0},{3,1},{4,6},{5,7},{6,4},{7,5},{8,10},{9,11},{10,... | collective-permute-start | bytes 3145736 | tf_op jit(solution)/shard_map/ppermute | solution.py:21
  5.4 1.7 shard_map.74
  8.6 2.1 collective-permute-start.13
  10.7 18.8 %collective-permute-done.refs_0_ = bf16[512,1024]{1,0:T(8,128)(2,1)} collective-permute-done((bf16[512,1024]{1,0:T(8,128)(2,1)S(1)}, bf16[512,1024]{1,0:T(8,128)(2,1)}, u32[]{:S(2)}, u32[]{:S(2)}) %collective-permute-start) | collective-permute-done | bytes 1048608 | tf_op jit(solution)/shard_map/ppermute | solution.py:21
  29.6 10.2 %collective-permute-done.4.refs_0_ = bf16[256,1024]{1,0:T(8,128)(2,1)S(1)} collective-permute-done((bf16[256,1024]{1,0:T(8,128)(2,1)}, bf16[256,1024]{1,0:T(8,128)(2,1)S(1)}, u32[]{:S(2)}, u32[]{:S(2)}) %collective-permute-start.4) | collective-permute-done | bytes 524320 | tf_op jit(solution)/shard_map/ppermute | solution.py:21
  39.8 1.7 collective-permute-start.6
  41.6 1.6 collective-permute-start.14
  43.1 1.6 collective-permute-start.17
  44.8 1.2 copy-done.14
  46.0 14.3 %shard_map.75.refs_2_ = f32[2,1024,1024]{2,1,0:T(8,128)S(1)} custom-call(s32[2]{0:T(128)S(1)} %pad_add_fusion.place, bf16[512,1024]{1,0:T(8,128)(2,1)S(1)} %copy-done.14, bf16[512,1024]{1,0:T(8,128)(2,1)} %get-tuple-element.27.refs_1_, bf16[512,1024]{1,0:T(8,128)(2,1)} %collective-permute-done.2.refs_2_, bf16[512,1024]{1,0:T(8,128)(2,1)} %collective-permute-done.3.refs_3_, ...), custom_call_target="tpu_custom_call" | custom-call | flops 8589934592 | bytes 20971520 | tf_op jit(solution)/shard_map/pallas_call | solution.py:87
  60.4 1.6 collective-permute-start.11
  62.0 6.6 %shard_map.77 = (bf16[2,256,1024]{2,1,0:T(8,128)(2,1)S(1)}, f32[2,8,1024]{2,1,0:T(8,128)S(1)}) custom-call(s32[2]{0:T(128)S(1)} %pad_add_fusion.place, bf16[256,1024]{1,0:T(8,128)(2,1)S(1)} %copy-done.16, bf16[256,1024]{1,0:T(8,128)(2,1)S(1)} %collective-permute-done.5.refs_1_, f32[2,1024,1024]{2,1,0:T(8,128)S(1)} %shard_map.75.refs_2_, ...), custom_call_target="tpu_custom_call" | custom-call | flops 2147483648 | bytes 12582912 | tf_op jit(solution)/shard_map/pallas_call | solution.py:296
  69.5 1.6 collective-permute-start.12
  71.1 1.6 collective-permute-start.18
  72.9 9.3 %shard_map.76 = (bf16[2,512,1024]{2,1,0:T(8,128)(2,1)S(1)}, f32[2,16,1024]{2,1,0:T(8,128)S(1)}) custom-call(s32[2]{0:T(128)S(1)} %pad_add_fusion.place, bf16[512,1024]{1,0:T(8,128)(2,1)} %collective-permute-done.refs_0_, bf16[512,1024]{1,0:T(8,128)(2,1)S(1)} %collective-permute-done.1.refs_1_, f32[2,1024,1024]{2,1,0:T(8,128)S(1)} %shard_map.75.refs_2_, ...), custom_call_target="tpu_custom_call" | custom-call | flops 4294967296 | bytes 16777216 | tf_op jit(solution)/shard_map/pallas_call | solution.py:296
  82.3 4.9 %shard_map.78 = (bf16[2,256,512]{2,1,0:T(8,128)(2,1)S(1)}, f32[2,8,512]{2,1,0:T(8,128)S(1)}, f32[8,2,512]{2,1,0:T(2,128)}) custom-call(s32[2]{0:T(128)S(1)} %pad_add_fusion.place, bf16[256,1024]{1,0:T(8,128)(2,1)S(1)} %collective-permute-done.6.refs_0_, bf16[256,1024]{1,0:T(8,128)(2,1)S(1)} %collective-permute-done.7.refs_1_, ...), custom_call_target="tpu_custom_call" | custom-call | flops 1073741824 | bytes 6815744 | tf_op jit(solution)/shard_map/pallas_call | solution.py:296
  88.7 4.9 %all-to-all-start = ((f32[8,2,512]{2,1,0:T(2,128)}), f32[8,2,512]{2,1,0:T(2,128)S(1)}, u32[]{:S(2)}, u32[]{:S(2)}) async-start(f32[8,2,512]{2,1,0:T(2,128)} %get-tuple-element.36), calls=%async_computation | async-start | bytes 65536 | tf_op jit(solution)/shard_map/all_to_all | solution.py:699
  93.6 3.4 %copy-done.1 = f32[2,1024,1024]{2,1,0:T(8,128)S(1)} copy-done((f32[2,1024,1024]{2,1,0:T(8,128)S(1)}, f32[2,1024,1024]{2,1,0:T(8,128)}, u32[]{:S(2)}) %copy-start.1) | copy-done | bytes 8388632
  99.1 4.6 %shard_map.80 = (bf16[2,256,512]{2,1,0:T(8,128)(2,1)S(1)}, f32[2,8,512]{2,1,0:T(8,128)S(1)}, f32[8,2,512]{2,1,0:T(2,128)}) custom-call(s32[2]{0:T(128)S(1)} %pad_add_fusion.place, bf16[256,1024]{1,0:T(8,128)(2,1)S(1)} %copy-done.10, bf16[256,1024]{1,0:T(8,128)(2,1)S(1)} %copy-done.12, f32[2,1024,1024]{2,1,0:T(8,128)S(1)} %copy-done.1, ...), custom_call_target="tpu_custom_call" | custom-call | flops 1073741824 | bytes 6815744 | tf_op jit(solution)/shard_map/pallas_call | solution.py:296
  105.1 6.0 %all-to-all-start.2 = ((f32[8,2,512]{2,1,0:T(2,128)}), f32[8,2,512]{2,1,0:T(2,128)S(1)}, u32[]{:S(2)}, u32[]{:S(2)}) async-start(f32[8,2,512]{2,1,0:T(2,128)} %get-tuple-element.42), calls=%async_computation.2 | async-start | bytes 65536 | tf_op jit(solution)/shard_map/all_to_all | solution.py:699
  111.1 2.0 collective-permute-start.15
  113.2 1.6 copy-done.26
  114.8 1.2 copy-done.29
  117.9 3.8 %shard_map.79 = (f32[2,1024,512]{2,1,0:T(8,128)S(1)}, f32[2,32,512]{2,1,0:T(8,128)S(1)}, f32[8,2,512]{2,1,0:T(2,128)S(1)}) custom-call(s32[2]{0:T(128)S(1)} %pad_add_fusion.place, bf16[2,512,1024]{2,1,0:T(8,128)(2,1)S(1)} %copy-done.26, bf16[2,256,1024]{2,1,0:T(8,128)(2,1)S(1)} %copy-done.29, bf16[2,256,512]{2,1,0:T(8,128)(2,1)S(1)} %copy-done.35, ...), custom_call_target="tpu_custom_call" | custom-call | flops 20971520 | bytes 6291456 | tf_op jit(solution)/shard_map/pallas_call | solution.py:409
  121.7 2.0 copy-done.2
  124.3 5.9 %all-to-all-start.1 = ((f32[8,2,512]{2,1,0:T(2,128)}), f32[8,2,512]{2,1,0:T(2,128)}, u32[]{:S(2)}, u32[]{:S(2)}) async-start(f32[8,2,512]{2,1,0:T(2,128)} %copy-done.23), calls=%async_computation.1 | async-start | bytes 65536 | tf_op jit(solution)/shard_map/all_to_all | solution.py:705
  131.9 1.6 copy-done.27
  133.5 1.2 copy-done.30
  136.5 3.8 %shard_map.81 = (f32[2,1024,512]{2,1,0:T(8,128)S(1)}, f32[2,32,512]{2,1,0:T(8,128)S(1)}, f32[8,2,512]{2,1,0:T(2,128)S(1)}) custom-call(s32[2]{0:T(128)S(1)} %pad_add_fusion.place, bf16[2,512,1024]{2,1,0:T(8,128)(2,1)S(1)} %copy-done.27, bf16[2,256,1024]{2,1,0:T(8,128)(2,1)S(1)} %copy-done.30, bf16[2,256,512]{2,1,0:T(8,128)(2,1)S(1)} %copy-done.33, ...), custom_call_target="tpu_custom_call" | custom-call | flops 20971520 | bytes 6291456 | tf_op jit(solution)/shard_map/pallas_call | solution.py:409
  140.3 2.0 copy-done.5
  143.0 12.7 %all_to_all.20.refs_5_.refs_2_ = f32[8,2,512]{2,1,0:T(2,128)S(1)} all-to-all(f32[8,2,512]{2,1,0:T(2,128)} %copy-done.24), channel_id=1, replica_groups=mesh['ctx'=8,'ch'=4] {'ctx'}, dimensions={0} | all-to-all | bytes 65536 | tf_op jit(solution)/shard_map/all_to_all | solution.py:705
  155.6 2.2 copy-done.3
  157.8 2.2 copy-done.6
  160.0 1.2 shard_map.82.refs_0_
  162.7 1.6 collective-permute-start.20
  167.4 8.8 %collective-permute-done.19.refs_18_.refs_14_ = bf16[256,1024]{1,0:T(8,128)(2,1)S(1)} collective-permute-done((bf16[256,1024]{1,0:T(8,128)(2,1)S(1)}, bf16[256,1024]{1,0:T(8,128)(2,1)S(1)}, u32[]{:S(2)}, u32[]{:S(2)}) %collective-permute-start.19) | collective-permute-done | bytes 524320 | tf_op jit(solution)/shard_map/ppermute | solution.py:21
  177.0 1.2 collective-permute-start.32
  179.4 8.0 %collective-permute-done.20.refs_19_.refs_15_ = bf16[256,1024]{1,0:T(8,128)(2,1)S(1)} collective-permute-done((bf16[256,1024]{1,0:T(8,128)(2,1)}, bf16[256,1024]{1,0:T(8,128)(2,1)S(1)}, u32[]{:S(2)}, u32[]{:S(2)}) %collective-permute-start.20) | collective-permute-done | bytes 524320 | tf_op jit(solution)/shard_map/ppermute | solution.py:21
  188.2 5.1 %collective-permute-done.23.refs_10_.refs_18_ = bf16[256,1024]{1,0:T(8,128)(2,1)S(1)} collective-permute-done((bf16[256,1024]{1,0:T(8,128)(2,1)}, bf16[256,1024]{1,0:T(8,128)(2,1)S(1)}, u32[]{:S(2)}, u32[]{:S(2)}) %collective-permute-start.23) | collective-permute-done | bytes 524320 | tf_op jit(solution)/shard_map/ppermute | solution.py:21
  193.8 5.3 %collective-permute-done.32.refs_6_ = bf16[512,512]{1,0:T(8,128)(2,1)S(1)} collective-permute-done((bf16[512,512]{1,0:T(8,128)(2,1)S(1)}, bf16[512,512]{1,0:T(8,128)(2,1)S(1)}, u32[]{:S(2)}, u32[]{:S(2)}) %collective-permute-start.32) | collective-permute-done | bytes 524320 | tf_op jit(solution)/shard_map/ppermute | solution.py:21
  199.1 5.6 %collective-permute-done.26.refs_2_ = bf16[256,1024]{1,0:T(8,128)(2,1)S(1)} collective-permute-done((bf16[256,1024]{1,0:T(8,128)(2,1)S(1)}, bf16[256,1024]{1,0:T(8,128)(2,1)S(1)}, u32[]{:S(2)}, u32[]{:S(2)}) %collective-permute-start.26) | collective-permute-done | bytes 524320 | tf_op jit(solution)/shard_map/ppermute | solution.py:21
  204.7 1.5 collective-permute-start.24
  207.3 5.4 %shard_map.86.refs_12_ = f32[512,1024]{1,0:T(8,128)S(1)} custom-call(s32[2]{0:T(128)S(1)} %pad_add_fusion.place, bf16[512,512]{1,0:T(8,128)(2,1)S(1)} %shard_map.84.refs_0_, bf16[512,512]{1,0:T(8,128)(2,1)S(1)} %collective-permute-done.28.refs_1_, bf16[512,512]{1,0:T(8,128)(2,1)S(1)} %collective-permute-done.29.refs_2_, ...), custom_call_target="tpu_custom_call" | custom-call | flops 3221225472 | bytes 11534336 | tf_op jit(solution)/shard_map/pallas_call | solution.py:565
  212.7 1.2 collective-permute-done.24.refs_11_.refs_19_
  213.9 4.4 %shard_map.87.refs_20_ = bf16[1024,1024]{1,0:T(8,128)(2,1)} custom-call(s32[2]{0:T(128)S(1)} %pad_add_fusion.place, bf16[512,512]{1,0:T(8,128)(2,1)S(1)} %shard_map.84.refs_0_, bf16[512,512]{1,0:T(8,128)(2,1)S(1)} %collective-permute-done.28.refs_1_, bf16[512,512]{1,0:T(8,128)(2,1)S(1)} %collective-permute-done.29.refs_2_, ...), custom_call_target="tpu_custom_call" | custom-call | flops 1073741824 | bytes 5242880 | tf_op jit(solution)/shard_map/pallas_call | solution.py:565
  218.3 5.3 %shard_map.88.refs_20_ = bf16[1024,1024]{1,0:T(8,128)(2,1)} custom-call(s32[2]{0:T(128)S(1)} %pad_add_fusion.place, bf16[256,1024]{1,0:T(8,128)(2,1)S(1)} %shard_map.83.refs_0_, bf16[256,1024]{1,0:T(8,128)(2,1)S(1)} %collective-permute-done.25.refs_1_, bf16[256,1024]{1,0:T(8,128)(2,1)S(1)} %collective-permute-done.26.refs_2_, ...), custom_call_target="tpu_custom_call", output_to_operand_aliasing={{}: (21, {})} | custom-call | flops 2147483648 | bytes 11534336 | tf_op jit(solution)/shard_map/pallas_call | solution.py:565
  223.7 5.3 %shard_map.89 = bf16[1024,1024]{1,0:T(8,128)(2,1)} custom-call(s32[2]{0:T(128)S(1)} %pad_add_fusion.place, bf16[256,1024]{1,0:T(8,128)(2,1)S(1)} %shard_map.82.refs_0_, bf16[256,1024]{1,0:T(8,128)(2,1)S(1)} %collective-permute-done.8.refs_1_, bf16[256,1024]{1,0:T(8,128)(2,1)S(1)} %collective-permute-done.9.refs_2_, ...), custom_call_target="tpu_custom_call", output_to_operand_aliasing={{}: (21, {})} | custom-call | flops 2147483648 | bytes 11534336 | tf_op jit(solution)/shard_map/pallas_call | solution.py:565
  (133 shorter events, 23.9 us)
Async XLA Ops:
  1.6 6.9 %copy-start.40 = (bf16[512,1024]{1,0:T(8,128)(2,1)S(1)}, bf16[512,1024]{1,0:T(8,128)(2,1)}, u32[]{:S(2)}) copy-start(bf16[512,1024]{1,0:T(8,128)(2,1)} %param.9) | copy-start | bytes 3145732
  2.3 6.3 %copy-start.13 = (bf16[512,1024]{1,0:T(8,128)(2,1)}, bf16[512,1024]{1,0:T(8,128)(2,1)S(1)}, u32[]{:S(2)}) copy-start(bf16[512,1024]{1,0:T(8,128)(2,1)S(1)} %shard_map.73.refs_0_) | copy-start | bytes 3145732
  2.4 8.3 %copy-start.41 = (f32[1024]{0:T(1024)S(1)}, f32[1024]{0:T(1024)}, u32[]{:S(2)}) copy-start(f32[1024]{0:T(1024)} %param.11) | copy-start | bytes 12292
  2.4 8.3 %copy-start.42 = (f32[1024]{0:T(1024)S(1)}, f32[1024]{0:T(1024)}, u32[]{:S(2)}) copy-start(f32[1024]{0:T(1024)} %param.10) | copy-start | bytes 12292
  2.4 27.1 %collective-permute-start = (bf16[512,1024]{1,0:T(8,128)(2,1)S(1)}, bf16[512,1024]{1,0:T(8,128)(2,1)}, u32[]{:S(2)}, u32[]{:S(2)}) collective-permute-start(bf16[512,1024]{1,0:T(8,128)(2,1)S(1)} %shard_map.73.refs_0_), channel_id=1, source_target_pairs={{0,2},{1,3},{2,0},{3,1},{4,6},{5,7},{6,4},{7,5},{8,10},{9,11},{10,... | collective-permute-start | bytes 3145736 | tf_op jit(solution)/shard_map/ppermute | solution.py:21
  5.4 37.7 %collective-permute-start.2 = (bf16[512,1024]{1,0:T(8,128)(2,1)S(1)}, bf16[512,1024]{1,0:T(8,128)(2,1)}, u32[]{:S(2)}, u32[]{:S(2)}) collective-permute-start(bf16[512,1024]{1,0:T(8,128)(2,1)S(1)} %shard_map.73.refs_0_), channel_id=1, source_target_pairs={{0,1},{1,0},{2,3},{3,2},{4,5},{5,4},{6,7},{7,6},{8,9},{9,8},{10,11... | collective-permute-start | bytes 3145736 | tf_op jit(solution)/shard_map/ppermute | solution.py:21
  7.9 35.2 %collective-permute-start.3 = (bf16[512,1024]{1,0:T(8,128)(2,1)}, bf16[512,1024]{1,0:T(8,128)(2,1)}, u32[]{:S(2)}, u32[]{:S(2)}) collective-permute-start(bf16[512,1024]{1,0:T(8,128)(2,1)} %get-tuple-element.27.refs_1_), channel_id=1, source_target_pairs={{0,1},{1,0},{2,3},{3,2},{4,5},{5,4},{6,7},{7,6},{8,9},{9,8},{10,11... | collective-permute-start | bytes 3145736 | tf_op jit(solution)/shard_map/ppermute | solution.py:21
  8.5 31.4 %collective-permute-start.4 = (bf16[256,1024]{1,0:T(8,128)(2,1)}, bf16[256,1024]{1,0:T(8,128)(2,1)S(1)}, u32[]{:S(2)}, u32[]{:S(2)}) collective-permute-start(bf16[256,1024]{1,0:T(8,128)(2,1)} %get-tuple-element.29), channel_id=1, source_target_pairs={{0,2},{1,3},{2,0},{3,1},{4,6},{5,7},{6,4},{7,5},{8,10},{9,11},{10,... | collective-permute-start | bytes 1572872 | tf_op jit(solution)/shard_map/ppermute | solution.py:21
  8.6 32.9 %collective-permute-start.13 = (bf16[256,1024]{1,0:T(8,128)(2,1)S(1)}, bf16[256,1024]{1,0:T(8,128)(2,1)S(1)}, u32[]{:S(2)}, u32[]{:S(2)}) collective-permute-start(bf16[256,1024]{1,0:T(8,128)(2,1)S(1)} %get-tuple-element.50.refs_8_.refs_4_), channel_id=1, source_target_pairs={{0,8},{4,12},{8,16},{12,20},{16,24},{20,28},{24,0},{28,4},{1,9},{5... | collective-permute-start | bytes 1572872 | tf_op jit(solution)/shard_map/ppermute | solution.py:613
  29.5 43.2 %collective-permute-start.1 = (bf16[512,1024]{1,0:T(8,128)(2,1)}, bf16[512,1024]{1,0:T(8,128)(2,1)S(1)}, u32[]{:S(2)}, u32[]{:S(2)}) collective-permute-start(bf16[512,1024]{1,0:T(8,128)(2,1)} %collective-permute-done.refs_0_), channel_id=1, source_target_pairs={{0,1},{1,0},{2,3},{3,2},{4,5},{5,4},{6,7},{7,6},{8,9},{9,8},{10,11... | collective-permute-start | bytes 3145736 | tf_op jit(solution)/shard_map/ppermute | solution.py:21
  39.8 20.5 %collective-permute-start.6 = (bf16[256,1024]{1,0:T(8,128)(2,1)}, bf16[256,1024]{1,0:T(8,128)(2,1)S(1)}, u32[]{:S(2)}, u32[]{:S(2)}) collective-permute-start(bf16[256,1024]{1,0:T(8,128)(2,1)} %copy-done.31), channel_id=1, source_target_pairs={{0,2},{1,3},{2,0},{3,1},{4,6},{5,7},{6,4},{7,5},{8,10},{9,11},{10,... | collective-permute-start | bytes 1572872 | tf_op jit(solution)/shard_map/ppermute | solution.py:21
  41.6 28.0 %collective-permute-start.14 = (bf16[256,1024]{1,0:T(8,128)(2,1)S(1)}, bf16[256,1024]{1,0:T(8,128)(2,1)S(1)}, u32[]{:S(2)}, u32[]{:S(2)}) collective-permute-start(bf16[256,1024]{1,0:T(8,128)(2,1)S(1)} %get-tuple-element.49.refs_9_.refs_5_), channel_id=1, source_target_pairs={{0,8},{4,12},{8,16},{12,20},{16,24},{20,28},{24,0},{28,4},{1,9},{5... | collective-permute-start | bytes 1572872 | tf_op jit(solution)/shard_map/ppermute | solution.py:613
  43.1 18.8 %collective-permute-start.5 = (bf16[256,1024]{1,0:T(8,128)(2,1)}, bf16[256,1024]{1,0:T(8,128)(2,1)S(1)}, u32[]{:S(2)}, u32[]{:S(2)}) collective-permute-start(bf16[256,1024]{1,0:T(8,128)(2,1)} %copy-done.15), channel_id=1, source_target_pairs={{0,1},{1,0},{2,3},{3,2},{4,5},{5,4},{6,7},{7,6},{8,9},{9,8},{10,11... | collective-permute-start | bytes 1572872 | tf_op jit(solution)/shard_map/ppermute | solution.py:21
  43.1 28.0 %collective-permute-start.17 = (bf16[256,1024]{1,0:T(8,128)(2,1)S(1)}, bf16[256,1024]{1,0:T(8,128)(2,1)S(1)}, u32[]{:S(2)}, u32[]{:S(2)}) collective-permute-start(bf16[256,1024]{1,0:T(8,128)(2,1)S(1)} %collective-permute-done.13.refs_12_.refs_8_), channel_id=1, source_target_pairs={{0,8},{4,12},{8,16},{12,20},{16,24},{20,28},{24,0},{28,4},{1,9},{5... | collective-permute-start | bytes 1572872 | tf_op jit(solution)/shard_map/ppermute | solution.py:613
  46.0 15.9 %copy-start.16 = (bf16[256,1024]{1,0:T(8,128)(2,1)S(1)}, bf16[256,1024]{1,0:T(8,128)(2,1)}, u32[]{:S(2)}) copy-start(bf16[256,1024]{1,0:T(8,128)(2,1)} %copy-done.15) | copy-start | bytes 1572868
  46.0 15.9 %copy-start.19 = (f32[1024]{0:T(1024)S(1)}, f32[1024]{0:T(1024)}, u32[]{:S(2)}) copy-start(f32[1024]{0:T(1024)} %param.13) | copy-start | bytes 12292
  46.0 16.0 %copy-start.20 = (f32[1024]{0:T(1024)S(1)}, f32[1024]{0:T(1024)}, u32[]{:S(2)}) copy-start(f32[1024]{0:T(1024)} %param.12) | copy-start | bytes 12292
  60.3 22.0 %copy-start = (f32[2,1024,1024]{2,1,0:T(8,128)}, f32[2,1024,1024]{2,1,0:T(8,128)S(1)}, u32[]{:S(2)}) copy-start(f32[2,1024,1024]{2,1,0:T(8,128)S(1)} %shard_map.75.refs_2_) | copy-start | bytes 25165828
  60.3 22.0 %copy-start.9 = (bf16[256,1024]{1,0:T(8,128)(2,1)}, bf16[256,1024]{1,0:T(8,128)(2,1)S(1)}, u32[]{:S(2)}) copy-start(bf16[256,1024]{1,0:T(8,128)(2,1)S(1)} %collective-permute-done.6.refs_0_) | copy-start | bytes 1572868
  60.4 52.8 %collective-permute-start.11 = (bf16[256,1024]{1,0:T(8,128)(2,1)S(1)}, bf16[256,1024]{1,0:T(8,128)(2,1)S(1)}, u32[]{:S(2)}, u32[]{:S(2)}) collective-permute-start(bf16[256,1024]{1,0:T(8,128)(2,1)S(1)} %get-tuple-element.50.refs_8_.refs_4_), channel_id=1, source_target_pairs={{0,4},{4,0},{8,12},{12,8},{16,20},{20,16},{24,28},{28,24},{1,5},{5... | collective-permute-start | bytes 1572872 | tf_op jit(solution)/shard_map/ppermute | solution.py:21
  61.9 20.4 %collective-permute-start.7 = (bf16[256,1024]{1,0:T(8,128)(2,1)S(1)}, bf16[256,1024]{1,0:T(8,128)(2,1)S(1)}, u32[]{:S(2)}, u32[]{:S(2)}) collective-permute-start(bf16[256,1024]{1,0:T(8,128)(2,1)S(1)} %collective-permute-done.6.refs_0_), channel_id=1, source_target_pairs={{0,1},{1,0},{2,3},{3,2},{4,5},{5,4},{6,7},{7,6},{8,9},{9,8},{10,11... | collective-permute-start | bytes 1572872 | tf_op jit(solution)/shard_map/ppermute | solution.py:21
  69.5 43.7 %copy-start.17 = (f32[2,8,1024]{2,1,0:T(8,128)}, f32[2,8,1024]{2,1,0:T(8,128)S(1)}, u32[]{:S(2)}) copy-start(f32[2,8,1024]{2,1,0:T(8,128)S(1)} %get-tuple-element.33.refs_8_.refs_4_) | copy-start | bytes 196612
  69.5 91.7 %collective-permute-start.12 = (bf16[256,1024]{1,0:T(8,128)(2,1)S(1)}, bf16[256,1024]{1,0:T(8,128)(2,1)}, u32[]{:S(2)}, u32[]{:S(2)}) collective-permute-start(bf16[256,1024]{1,0:T(8,128)(2,1)S(1)} %get-tuple-element.49.refs_9_.refs_5_), channel_id=1, source_target_pairs={{0,4},{4,0},{8,12},{12,8},{16,20},{20,16},{24,28},{28,24},{1,5},{5... | collective-permute-start | bytes 1572872 | tf_op jit(solution)/shard_map/ppermute | solution.py:21
  71.1 90.7 %collective-permute-start.18 = (bf16[256,1024]{1,0:T(8,128)(2,1)S(1)}, bf16[256,1024]{1,0:T(8,128)(2,1)}, u32[]{:S(2)}, u32[]{:S(2)}) collective-permute-start(bf16[256,1024]{1,0:T(8,128)(2,1)S(1)} %collective-permute-done.14.refs_13_.refs_9_), channel_id=1, source_target_pairs={{0,8},{4,12},{8,16},{12,20},{16,24},{20,28},{24,0},{28,4},{1,9},{5... | collective-permute-start | bytes 1572872 | tf_op jit(solution)/shard_map/ppermute | solution.py:613
  72.7 89.9 %collective-permute-start.21 = (bf16[256,1024]{1,0:T(8,128)(2,1)S(1)}, bf16[256,1024]{1,0:T(8,128)(2,1)}, u32[]{:S(2)}, u32[]{:S(2)}) collective-permute-start(bf16[256,1024]{1,0:T(8,128)(2,1)S(1)} %collective-permute-done.17.refs_16_.refs_12_), channel_id=1, source_target_pairs={{0,8},{4,12},{8,16},{12,20},{16,24},{20,28},{24,0},{28,4},{1,9},{5... | collective-permute-start | bytes 1572872 | tf_op jit(solution)/shard_map/ppermute | solution.py:613
  88.7 16.4 %all-to-all-start = ((f32[8,2,512]{2,1,0:T(2,128)}), f32[8,2,512]{2,1,0:T(2,128)S(1)}, u32[]{:S(2)}, u32[]{:S(2)}) async-start(f32[8,2,512]{2,1,0:T(2,128)} %get-tuple-element.36), calls=%async_computation | async-start | bytes 65536 | tf_op jit(solution)/shard_map/all_to_all | solution.py:699
  105.1 19.2 %all-to-all-start.2 = ((f32[8,2,512]{2,1,0:T(2,128)}), f32[8,2,512]{2,1,0:T(2,128)S(1)}, u32[]{:S(2)}, u32[]{:S(2)}) async-start(f32[8,2,512]{2,1,0:T(2,128)} %get-tuple-element.42), calls=%async_computation.2 | async-start | bytes 65536 | tf_op jit(solution)/shard_map/all_to_all | solution.py:699
  111.1 53.1 %collective-permute-start.15 = (bf16[256,1024]{1,0:T(8,128)(2,1)S(1)}, bf16[256,1024]{1,0:T(8,128)(2,1)}, u32[]{:S(2)}, u32[]{:S(2)}) collective-permute-start(bf16[256,1024]{1,0:T(8,128)(2,1)S(1)} %collective-permute-done.13.refs_12_.refs_8_), channel_id=1, source_target_pairs={{0,4},{4,0},{8,12},{12,8},{16,20},{20,16},{24,28},{28,24},{1,5},{5... | collective-permute-start | bytes 1572872 | tf_op jit(solution)/shard_map/ppermute | solution.py:21
  113.2 51.4 %collective-permute-start.16 = (bf16[256,1024]{1,0:T(8,128)(2,1)S(1)}, bf16[256,1024]{1,0:T(8,128)(2,1)}, u32[]{:S(2)}, u32[]{:S(2)}) collective-permute-start(bf16[256,1024]{1,0:T(8,128)(2,1)S(1)} %collective-permute-done.14.refs_13_.refs_9_), channel_id=1, source_target_pairs={{0,4},{4,0},{8,12},{12,8},{16,20},{20,16},{24,28},{28,24},{1,5},{5... | collective-permute-start | bytes 1572872 | tf_op jit(solution)/shard_map/ppermute | solution.py:21
  124.3 18.6 %all-to-all-start.1 = ((f32[8,2,512]{2,1,0:T(2,128)}), f32[8,2,512]{2,1,0:T(2,128)}, u32[]{:S(2)}, u32[]{:S(2)}) async-start(f32[8,2,512]{2,1,0:T(2,128)} %copy-done.23), calls=%async_computation.1 | async-start | bytes 65536 | tf_op jit(solution)/shard_map/all_to_all | solution.py:705
  161.3 14.9 %collective-permute-start.19 = (bf16[256,1024]{1,0:T(8,128)(2,1)S(1)}, bf16[256,1024]{1,0:T(8,128)(2,1)S(1)}, u32[]{:S(2)}, u32[]{:S(2)}) collective-permute-start(bf16[256,1024]{1,0:T(8,128)(2,1)S(1)} %collective-permute-done.17.refs_16_.refs_12_), channel_id=1, source_target_pairs={{0,4},{4,0},{8,12},{12,8},{16,20},{20,16},{24,28},{28,24},{1,5},{5... | collective-permute-start | bytes 1572872 | tf_op jit(solution)/shard_map/ppermute | solution.py:21
  161.8 15.1 %collective-permute-start.9 = (bf16[256,1024]{1,0:T(8,128)(2,1)S(1)}, bf16[256,1024]{1,0:T(8,128)(2,1)S(1)}, u32[]{:S(2)}, u32[]{:S(2)}) collective-permute-start(bf16[256,1024]{1,0:T(8,128)(2,1)S(1)} %shard_map.82.refs_0_), channel_id=1, source_target_pairs={{0,2},{1,3},{2,0},{3,1},{4,6},{5,7},{6,4},{7,5},{8,10},{9,11},{10,... | collective-permute-start | bytes 1572872 | tf_op jit(solution)/shard_map/ppermute | solution.py:21
  162.7 24.7 %collective-permute-start.20 = (bf16[256,1024]{1,0:T(8,128)(2,1)}, bf16[256,1024]{1,0:T(8,128)(2,1)S(1)}, u32[]{:S(2)}, u32[]{:S(2)}) collective-permute-start(bf16[256,1024]{1,0:T(8,128)(2,1)} %collective-permute-done.18.refs_17_.refs_13_), channel_id=1, source_target_pairs={{0,4},{4,0},{8,12},{12,8},{16,20},{20,16},{24,28},{28,24},{1,5},{5... | collective-permute-start | bytes 1572872 | tf_op jit(solution)/shard_map/ppermute | solution.py:21
  164.2 24.0 %collective-permute-start.22 = (bf16[256,1024]{1,0:T(8,128)(2,1)}, bf16[256,1024]{1,0:T(8,128)(2,1)S(1)}, u32[]{:S(2)}, u32[]{:S(2)}) collective-permute-start(bf16[256,1024]{1,0:T(8,128)(2,1)} %collective-permute-done.18.refs_17_.refs_13_), channel_id=1, source_target_pairs={{0,8},{4,12},{8,16},{12,20},{16,24},{20,28},{24,0},{28,4},{1,9},{5... | collective-permute-start | bytes 1572872 | tf_op jit(solution)/shard_map/ppermute | solution.py:613
  164.6 28.7 %collective-permute-start.23 = (bf16[256,1024]{1,0:T(8,128)(2,1)}, bf16[256,1024]{1,0:T(8,128)(2,1)S(1)}, u32[]{:S(2)}, u32[]{:S(2)}) collective-permute-start(bf16[256,1024]{1,0:T(8,128)(2,1)} %collective-permute-done.21.refs_8_.refs_16_), channel_id=1, source_target_pairs={{0,4},{4,0},{8,12},{12,8},{16,20},{20,16},{24,28},{28,24},{1,5},{5... | collective-permute-start | bytes 1572872 | tf_op jit(solution)/shard_map/ppermute | solution.py:21
  166.5 11.7 %copy-start.4 = (f32[2,1024,512]{2,1,0:T(8,128)S(1)}, f32[2,1024,512]{2,1,0:T(8,128)}, u32[]{:S(2)}) copy-start(f32[2,1024,512]{2,1,0:T(8,128)} %copy-done.2) | copy-start | bytes 12582916
  176.1 17.2 %collective-permute-start.29 = (bf16[512,512]{1,0:T(8,128)(2,1)S(1)}, bf16[512,512]{1,0:T(8,128)(2,1)S(1)}, u32[]{:S(2)}, u32[]{:S(2)}) collective-permute-start(bf16[512,512]{1,0:T(8,128)(2,1)S(1)} %shard_map.84.refs_0_), channel_id=1, source_target_pairs={{0,2},{1,3},{2,0},{3,1},{4,6},{5,7},{6,4},{7,5},{8,10},{9,11},{10,... | collective-permute-start | bytes 1572872 | tf_op jit(solution)/shard_map/ppermute | solution.py:21
  177.0 22.1 %collective-permute-start.32 = (bf16[512,512]{1,0:T(8,128)(2,1)S(1)}, bf16[512,512]{1,0:T(8,128)(2,1)S(1)}, u32[]{:S(2)}, u32[]{:S(2)}) collective-permute-start(bf16[512,512]{1,0:T(8,128)(2,1)S(1)} %shard_map.85.refs_4_), channel_id=1, source_target_pairs={{0,2},{1,3},{2,0},{3,1},{4,6},{5,7},{6,4},{7,5},{8,10},{9,11},{10,... | collective-permute-start | bytes 1572872 | tf_op jit(solution)/shard_map/ppermute | solution.py:21
  187.4 17.3 %collective-permute-start.26 = (bf16[256,1024]{1,0:T(8,128)(2,1)S(1)}, bf16[256,1024]{1,0:T(8,128)(2,1)S(1)}, u32[]{:S(2)}, u32[]{:S(2)}) collective-permute-start(bf16[256,1024]{1,0:T(8,128)(2,1)S(1)} %shard_map.83.refs_0_), channel_id=1, source_target_pairs={{0,2},{1,3},{2,0},{3,1},{4,6},{5,7},{6,4},{7,5},{8,10},{9,11},{10,... | collective-permute-start | bytes 1572872 | tf_op jit(solution)/shard_map/ppermute | solution.py:21
  188.2 18.1 %collective-permute-start.28 = (bf16[512,512]{1,0:T(8,128)(2,1)S(1)}, bf16[512,512]{1,0:T(8,128)(2,1)S(1)}, u32[]{:S(2)}, u32[]{:S(2)}) collective-permute-start(bf16[512,512]{1,0:T(8,128)(2,1)S(1)} %shard_map.84.refs_0_), channel_id=1, source_target_pairs={{0,1},{1,0},{2,3},{3,2},{4,5},{5,4},{6,7},{7,6},{8,9},{9,8},{10,11... | collective-permute-start | bytes 1572872 | tf_op jit(solution)/shard_map/ppermute | solution.py:21
  193.3 13.0 %collective-permute-start.31 = (bf16[512,512]{1,0:T(8,128)(2,1)S(1)}, bf16[512,512]{1,0:T(8,128)(2,1)S(1)}, u32[]{:S(2)}, u32[]{:S(2)}) collective-permute-start(bf16[512,512]{1,0:T(8,128)(2,1)S(1)} %shard_map.85.refs_4_), channel_id=1, source_target_pairs={{0,1},{1,0},{2,3},{3,2},{4,5},{5,4},{6,7},{7,6},{8,9},{9,8},{10,11... | collective-permute-start | bytes 1572872 | tf_op jit(solution)/shard_map/ppermute | solution.py:21
  193.3 13.5 %collective-permute-start.30 = (bf16[512,512]{1,0:T(8,128)(2,1)S(1)}, bf16[512,512]{1,0:T(8,128)(2,1)S(1)}, u32[]{:S(2)}, u32[]{:S(2)}) collective-permute-start(bf16[512,512]{1,0:T(8,128)(2,1)S(1)} %collective-permute-done.29.refs_2_), channel_id=1, source_target_pairs={{0,1},{1,0},{2,3},{3,2},{4,5},{5,4},{6,7},{7,6},{8,9},{9,8},{10,11... | collective-permute-start | bytes 1572872 | tf_op jit(solution)/shard_map/ppermute | solution.py:21
  199.1 7.8 %collective-permute-start.33 = (bf16[512,512]{1,0:T(8,128)(2,1)S(1)}, bf16[512,512]{1,0:T(8,128)(2,1)S(1)}, u32[]{:S(2)}, u32[]{:S(2)}) collective-permute-start(bf16[512,512]{1,0:T(8,128)(2,1)S(1)} %collective-permute-done.32.refs_6_), channel_id=1, source_target_pairs={{0,1},{1,0},{2,3},{3,2},{4,5},{5,4},{6,7},{7,6},{8,9},{9,8},{10,11... | collective-permute-start | bytes 1572872 | tf_op jit(solution)/shard_map/ppermute | solution.py:21
  204.7 9.2 %collective-permute-start.24 = (bf16[256,1024]{1,0:T(8,128)(2,1)S(1)}, bf16[256,1024]{1,0:T(8,128)(2,1)S(1)}, u32[]{:S(2)}, u32[]{:S(2)}) collective-permute-start(bf16[256,1024]{1,0:T(8,128)(2,1)S(1)} %collective-permute-done.22.refs_9_.refs_17_), channel_id=1, source_target_pairs={{0,4},{4,0},{8,12},{12,8},{16,20},{20,16},{24,28},{28,24},{1,5},{5... | collective-permute-start | bytes 1572872 | tf_op jit(solution)/shard_map/ppermute | solution.py:21
  206.3 12.0 %collective-permute-start.25 = (bf16[256,1024]{1,0:T(8,128)(2,1)S(1)}, bf16[256,1024]{1,0:T(8,128)(2,1)S(1)}, u32[]{:S(2)}, u32[]{:S(2)}) collective-permute-start(bf16[256,1024]{1,0:T(8,128)(2,1)S(1)} %shard_map.83.refs_0_), channel_id=1, source_target_pairs={{0,1},{1,0},{2,3},{3,2},{4,5},{5,4},{6,7},{7,6},{8,9},{9,8},{10,11... | collective-permute-start | bytes 1572872 | tf_op jit(solution)/shard_map/ppermute | solution.py:21
  206.3 12.0 %collective-permute-start.27 = (bf16[256,1024]{1,0:T(8,128)(2,1)S(1)}, bf16[256,1024]{1,0:T(8,128)(2,1)S(1)}, u32[]{:S(2)}, u32[]{:S(2)}) collective-permute-start(bf16[256,1024]{1,0:T(8,128)(2,1)S(1)} %collective-permute-done.26.refs_2_), channel_id=1, source_target_pairs={{0,1},{1,0},{2,3},{3,2},{4,5},{5,4},{6,7},{7,6},{8,9},{9,8},{10,11... | collective-permute-start | bytes 1572872 | tf_op jit(solution)/shard_map/ppermute | solution.py:21
  206.8 16.8 %collective-permute-start.8 = (bf16[256,1024]{1,0:T(8,128)(2,1)S(1)}, bf16[256,1024]{1,0:T(8,128)(2,1)S(1)}, u32[]{:S(2)}, u32[]{:S(2)}) collective-permute-start(bf16[256,1024]{1,0:T(8,128)(2,1)S(1)} %shard_map.82.refs_0_), channel_id=1, source_target_pairs={{0,1},{1,0},{2,3},{3,2},{4,5},{5,4},{6,7},{7,6},{8,9},{9,8},{10,11... | collective-permute-start | bytes 1572872 | tf_op jit(solution)/shard_map/ppermute | solution.py:21
  206.9 16.8 %collective-permute-start.10 = (bf16[256,1024]{1,0:T(8,128)(2,1)S(1)}, bf16[256,1024]{1,0:T(8,128)(2,1)S(1)}, u32[]{:S(2)}, u32[]{:S(2)}) collective-permute-start(bf16[256,1024]{1,0:T(8,128)(2,1)S(1)} %collective-permute-done.9.refs_2_), channel_id=1, source_target_pairs={{0,1},{1,0},{2,3},{3,2},{4,5},{5,4},{6,7},{7,6},{8,9},{9,8},{10,11... | collective-permute-start | bytes 1572872 | tf_op jit(solution)/shard_map/ppermute | solution.py:21
  (32 other events, 56.3 us)

commit v6 on v4

--- a/solution.py
+++ b/solution.py
@@ -149,7 +149,7 @@
             pltpu.VMEM((rows // BLOCK, BLOCK, width), BF16),
             pltpu.SemaphoreType.DMA((rows // BLOCK,)),
         ],
-        compiler_params=params(12),
+        compiler_params=params(60),
         cost_estimate=cost(2 * rows * BLOCK * width, 4 * rows * width),
     )(array)
 
@@ -463,7 +463,7 @@
     blocks = refs[:count]
     weights = refs[count : count + len(slots) * 2 * pieces]
     out_ref, lhs, wbuf, acc, lsem, wsem = refs[-6:]
-    prev_ref = refs[count + len(weights)] if before else None
+    prev_refs = refs[count + len(weights) : count + len(weights) + before]
     depth = blocks[0].shape[1]
     heights = [blocks[c * group].shape[0] for c in range(groups)]
     lines_of = weights[0].shape[0]
@@ -490,6 +490,10 @@
     for c in range(groups):
         for d in range(group):
             l_copy(c, d).wait()
+    top = 0
+    for prev in prev_refs:
+        acc[top : top + prev.shape[0], :] = prev[...]
+        top += prev.shape[0]
     span = lines_of * pieces
     for n in range(here):
         source = lax.rem(place[1] // 2 + outer - slots[n // 2], outer)
@@ -498,9 +502,7 @@
         for p in range(pieces):
             w_copy(n, p).wait()
         part = jnp.dot(lhs[:, deep], wbuf[n], preferred_element_type=F32)
-        if n == 0 and before:
-            part = part + prev_ref[...]
-        if n > 0:
+        if n > 0 or before:
             part = acc[...] + part
         if n < here - 1:
             acc[...] = part
@@ -526,9 +528,8 @@
     args = [place] + [b for g in blocks for b in g] + used
     in_specs = [pl.BlockSpec(memory_space=pl.ANY)] * (groups * group)
     in_specs += [pl.BlockSpec(memory_space=pltpu.HBM)] * len(used)
-    if prev is not None:
-        args.append(prev)
-        in_specs.append(pl.BlockSpec((rows, width), lambda n, p: (0, 0)))
+    args += prev
+    in_specs += [pl.BlockSpec((q.shape[0], width), lambda n, p: (0, 0)) for q in prev]
     aliases = {}
     if whole is not None:
         aliases = {len(args): 0}
@@ -543,7 +544,7 @@
         out_spec = pl.BlockSpec((rows, width), lambda n, p: (0, 0))
     return pl.pallas_call(
         functools.partial(
-            mix_kernel, groups, group, pieces, peers, tuple(slots), final, prev is not None
+            mix_kernel, groups, group, pieces, peers, tuple(slots), final, len(prev)
         ),
         out_shape=out_shape,
         grid_spec=pltpu.PrefetchScalarGridSpec(
@@ -679,24 +680,24 @@
     late = max(1, ring.outer // 4)
     slots = list(range(ring.outer))
 
-    def mix(c, used, prev, final, whole):
+    def mix(part, used, prev, final, whole):
         return mix_rows(
             place,
-            blocks[c : c + 1],
+            blocks[part],
             weights,
             used,
             prev,
             final,
             whole,
-            firsts[c],
+            firsts[part][0],
             total_rows,
             ring.pieces,
         )
 
-    partial = mix(0, slots[:-late], None, False, None)
-    mixed = mix(0, slots[-late:], partial, True, None)
-    for c in range(1, chunks):
-        mixed = mix(c, slots, None, True, mixed)
+    early, late_slots = slots[:-late], slots[-late:]
+    partials = [mix(slice(c, c + 1), early, [], False, None) for c in range(chunks - 1)]
+    mixed = mix(slice(0, chunks - 1), late_slots, partials, True, None)
+    mixed = mix(slice(chunks - 1, chunks), slots, [], True, mixed)
     return mixed
 
 

time: 228 us -> 224 us (0.982)
  blocking collectives: 0 us -> 12.6 us
  waiting for transfers between devices: 108 us -> 98 us
  local copies, waits for them, and re-layouts: 18.8 us -> 10.3 us
    ppermute x25, waiting for transfers between devices: 61.6 us -> 96.5 us  [swap(): lax.ppermute(block, axis, [(i, i ^ bits) for i in range(lax.axis_size(axi...]
    ppermute x6, waiting for transfers between devices: 19.2 us -> 0.02 us  [ring_step(): self.held[s, 0, p] = lax.ppermute(block, 'ctx', route)]
    all_to_all x1 -> x0, waiting for transfers between devices: 14.6 us -> none  [layer(): peer_maps = lax.all_to_all(totals, 'ctx', 0, 0, tiled=True)]
    all_to_all x0 -> x1, blocking collectives: none -> 12.6 us  [layer(): peer_maps = lax.all_to_all(totals, 'ctx', 0, 0, tiled=True)]
    all_to_all x1, waiting for transfers between devices: 12.7 us -> 1.49 us  [layer(): peer_maps = lax.all_to_all(out[2], 'ctx', 0, 0, tiled=True)]
    unnamed x40 -> x32, local copies, waits for them, and re-layouts: 17.5 us -> 8.92 us
    all_to_all x1 -> x0, starting transfers between devices: 3.35 us -> none  [layer(): peer_maps = lax.all_to_all(totals, 'ctx', 0, 0, tiled=True)]
    pallas_call x2, Pallas kernels: 2.63 us -> 5.49 us  [split_rows(): pl.pallas_call(functools.partial(split_kernel, first, tuple(sizes), joine...]
  transfers between devices with their start and end apart: 33 -> 32, of which waited for: 11 -> 11; matrix products, arithmetic and copies ran while one was open for 1% -> 1% of each run, Pallas kernels for 27% -> 28%
where the time goes in v6:
time: 224 us
  waiting for transfers between devices  98 us (44%)
  Pallas kernels  70.4 us (31%)
  starting transfers between devices  31.9 us (14%)
  blocking collectives  12.6 us (6%)
  local copies, waits for them, and re-layouts  10.3 us (5%)
    ppermute x25, waiting for transfers between devices, swap(): lax.ppermute(block, axis, [(i, i ^ bits) for i in range(lax.axis_size(axi...  96.5 us
    pallas_call x3, Pallas kernels, gate_chunk(): pl.pallas_call(functools.partial(gate_kernel, half, first_row, rows, len(...  21.9 us
    pallas_call x4, Pallas kernels, mix_rows(): pl.pallas_call(functools.partial(mix_kernel, groups, group, pieces, peers...  19.6 us
    ppermute x25, starting transfers between devices, swap(): lax.ppermute(block, axis, [(i, i ^ bits) for i in range(lax.axis_size(axi...  17.9 us
    pallas_call x1, Pallas kernels, near_product(): pl.pallas_call(functools.partial(near_kernel, half, tiles, heights), out_...  14.1 us
    all_to_all x1, blocking collectives, layer(): peer_maps = lax.all_to_all(totals, 'ctx', 0, 0, tiled=True)  12.6 us
    ppermute x6, starting transfers between devices, ring_step(): self.held[s, 0, p] = lax.ppermute(block, 'ctx', route)  9.14 us
    unnamed x32, local copies, waits for them, and re-layouts  8.92 us
  transfers between devices with their start and end apart: 32, of which 11 were waited for; matrix products, arithmetic and copies ran while one was open for 1% of the time, Pallas kernels for 28%

profile of v6, /device:TPU:0, one launch (start us, length us, event | category | flops | bytes accessed | tf_op | source)
XLA Modules:
  0.0 223.6 jit_solution(2684427160759528099)
XLA Ops:
  0.0 2.7 %shard_map.73.refs_0_ = bf16[512,1024]{1,0:T(8,128)(2,1)} custom-call(bf16[1024,1024]{1,0:T(8,128)(2,1)} %src.3), custom_call_target="tpu_custom_call" | custom-call | flops 268435456 | bytes 2097152 | tf_op jit(solution)/shard_map/pallas_call | solution.py:143
  2.7 3.0 %collective-permute-start = (bf16[512,1024]{1,0:T(8,128)(2,1)}, bf16[512,1024]{1,0:T(8,128)(2,1)}, u32[]{:S(2)}, u32[]{:S(2)}) collective-permute-start(bf16[512,1024]{1,0:T(8,128)(2,1)} %shard_map.73.refs_0_), channel_id=1, source_target_pairs={{0,2},{1,3},{2,0},{3,1},{4,6},{5,7},{6,4},{7,5},{8,10},{9,11},{10,... | collective-permute-start | bytes 3145736 | tf_op jit(solution)/shard_map/ppermute | solution.py:21
  5.7 2.8 %shard_map.74 = (bf16[256,1024]{1,0:T(8,128)(2,1)}, bf16[256,1024]{1,0:T(8,128)(2,1)}, bf16[512,1024]{1,0:T(8,128)(2,1)}) custom-call(bf16[1024,1024]{1,0:T(8,128)(2,1)} %src.3), custom_call_target="tpu_custom_call" | custom-call | flops 268435456 | bytes 2097152 | tf_op jit(solution)/shard_map/pallas_call | solution.py:143
  9.2 1.9 collective-permute-start.6
  11.2 1.4 fusion
  12.5 17.5 %collective-permute-done.refs_0_ = bf16[512,1024]{1,0:T(8,128)(2,1)} collective-permute-done((bf16[512,1024]{1,0:T(8,128)(2,1)}, bf16[512,1024]{1,0:T(8,128)(2,1)}, u32[]{:S(2)}, u32[]{:S(2)}) %collective-permute-start) | collective-permute-done | bytes 1048608 | tf_op jit(solution)/shard_map/ppermute | solution.py:21
  30.1 11.1 %collective-permute-done.4.refs_0_ = bf16[256,1024]{1,0:T(8,128)(2,1)S(1)} collective-permute-done((bf16[256,1024]{1,0:T(8,128)(2,1)}, bf16[256,1024]{1,0:T(8,128)(2,1)S(1)}, u32[]{:S(2)}, u32[]{:S(2)}) %collective-permute-start.4) | collective-permute-done | bytes 524320 | tf_op jit(solution)/shard_map/ppermute | solution.py:21
  41.2 0.8 copy-done.3
  42.0 2.1 collective-permute-start.14
  44.1 7.5 %collective-permute-done.6.refs_0_ = bf16[256,1024]{1,0:T(8,128)(2,1)S(1)} collective-permute-done((bf16[256,1024]{1,0:T(8,128)(2,1)}, bf16[256,1024]{1,0:T(8,128)(2,1)S(1)}, u32[]{:S(2)}, u32[]{:S(2)}) %collective-permute-start.6) | collective-permute-done | bytes 524320 | tf_op jit(solution)/shard_map/ppermute | solution.py:21
  52.4 1.8 collective-permute-start.13
  54.7 14.1 %shard_map.75.refs_2_ = f32[2,1024,1024]{2,1,0:T(8,128)S(1)} custom-call(s32[2]{0:T(128)S(1)} %pad_add_fusion.place, bf16[512,1024]{1,0:T(8,128)(2,1)S(1)} %copy-done, bf16[512,1024]{1,0:T(8,128)(2,1)S(1)} %copy-done.9, bf16[512,1024]{1,0:T(8,128)(2,1)} %collective-permute-done.2.refs_2_, bf16[512,1024]{1,0:T(8,128)(2,1)} %collective-permute-done.3.refs_3_, ...), custom_call_target="tpu_custom_call" | custom-call | flops 8589934592 | bytes 20971520 | tf_op jit(solution)/shard_map/pallas_call | solution.py:87
  68.8 5.8 %shard_map.77 = (bf16[2,256,1024]{2,1,0:T(8,128)(2,1)S(1)}, f32[2,8,1024]{2,1,0:T(8,128)S(1)}) custom-call(s32[2]{0:T(128)S(1)} %pad_add_fusion.place, bf16[256,1024]{1,0:T(8,128)(2,1)S(1)} %copy-done.4, bf16[256,1024]{1,0:T(8,128)(2,1)S(1)} %collective-permute-done.5.refs_1_, f32[2,1024,1024]{2,1,0:T(8,128)S(1)} %shard_map.75.refs_2_, ...), custom_call_target="tpu_custom_call" | custom-call | flops 2147483648 | bytes 12582912 | tf_op jit(solution)/shard_map/pallas_call | solution.py:290
  74.7 1.0 copy-done.10
  75.6 9.5 %shard_map.76 = (bf16[2,512,1024]{2,1,0:T(8,128)(2,1)S(1)}, f32[2,16,1024]{2,1,0:T(8,128)S(1)}) custom-call(s32[2]{0:T(128)S(1)} %pad_add_fusion.place, bf16[512,1024]{1,0:T(8,128)(2,1)} %collective-permute-done.refs_0_, bf16[512,1024]{1,0:T(8,128)(2,1)S(1)} %collective-permute-done.1.refs_1_, f32[2,1024,1024]{2,1,0:T(8,128)S(1)} %shard_map.75.refs_2_, ...), custom_call_target="tpu_custom_call" | custom-call | flops 4294967296 | bytes 16777216 | tf_op jit(solution)/shard_map/pallas_call | solution.py:290
  85.2 1.3 copy-done.7
  86.5 6.5 %shard_map.78 = (bf16[2,256,1024]{2,1,0:T(8,128)(2,1)S(1)}, f32[2,8,1024]{2,1,0:T(8,128)S(1)}, f32[8,2,1024]{2,1,0:T(2,128)}) custom-call(s32[2]{0:T(128)S(1)} %pad_add_fusion.place, bf16[256,1024]{1,0:T(8,128)(2,1)S(1)} %copy-done.2, bf16[256,1024]{1,0:T(8,128)(2,1)S(1)} %collective-permute-done.7.refs_1_, f32[2,1024,1024]{2,1,0:T(8,128)S(1)} %shard_map.75.refs_2_, ...), custom_call_target="tpu_custom_call" | custom-call | flops 2147483648 | bytes 12582912 | tf_op jit(solution)/shard_map/pallas_call | solution.py:290
  93.0 1.0 copy-done.12
  94.0 4.8 %all-to-all-start = ((f32[8,2,1024]{2,1,0:T(2,128)}), f32[8,2,1024]{2,1,0:T(2,128)S(1)}, u32[]{:S(2)}, u32[]{:S(2)}) async-start(f32[8,2,1024]{2,1,0:T(2,128)} %get-tuple-element.30), calls=%async_computation | async-start | bytes 131072 | tf_op jit(solution)/shard_map/all_to_all | solution.py:661
  98.8 2.0 collective-permute-start.12
  100.9 2.0 collective-permute-start.17
  102.9 1.5 collective-permute-start.18
  104.4 1.5 all-to-all-done.refs_6_
  105.9 1.6 copy-done.8
  107.5 1.2 copy-done.11
  108.7 1.2 copy-done.13
  109.9 6.9 %bend.1 = (f32[2,1024,1024]{2,1,0:T(8,128)S(1)}, f32[2,32,1024]{2,1,0:T(8,128)S(1)}, f32[8,2,1024]{2,1,0:T(2,128)S(1)}) custom-call(s32[2]{0:T(128)S(1)} %pad_add_fusion.place, bf16[2,512,1024]{2,1,0:T(8,128)(2,1)S(1)} %copy-done.8, bf16[2,256,1024]{2,1,0:T(8,128)(2,1)S(1)} %copy-done.11, bf16[2,256,1024]{2,1,0:T(8,128)(2,1)S(1)} %copy-done.13, ...), custom_call_target="tpu_custom_call" | custom-call | flops 41943040 | bytes 12582912 | tf_op jit(solution)/shard_map/bend/pallas_call | solution.py:396
  116.8 12.6 %all_to_all.10.peer_ref = f32[8,2,1024]{2,1,0:T(2,128)S(1)} all-to-all(f32[8,2,1024]{2,1,0:T(2,128)S(1)} %get-tuple-element.33), channel_id=1, replica_groups=mesh['ctx'=8,'ch'=4] {'ctx'}, dimensions={0} | all-to-all | bytes 131072 | tf_op jit(solution)/shard_map/all_to_all | solution.py:663
  129.4 1.0 shard_map.80.refs_0_
  130.3 1.6 collective-permute-start.26
  131.9 1.0 collective-permute-start.16
  132.8 1.1 collective-permute-start.15
  133.9 0.9 collective-permute-start.21
  135.2 0.8 shard_map.79.refs_0_
  136.0 10.7 %collective-permute-done.16.refs_11_ = bf16[256,1024]{1,0:T(8,128)(2,1)S(1)} collective-permute-done((bf16[256,1024]{1,0:T(8,128)(2,1)S(1)}, bf16[256,1024]{1,0:T(8,128)(2,1)S(1)}, u32[]{:S(2)}, u32[]{:S(2)}) %collective-permute-start.16) | collective-permute-done | bytes 524320 | tf_op jit(solution)/shard_map/ppermute | solution.py:21
  147.2 0.8 shard_map.81.refs_0_.refs_4_
  148.0 9.9 %collective-permute-done.15.refs_10_ = bf16[256,1024]{1,0:T(8,128)(2,1)S(1)} collective-permute-done((bf16[256,1024]{1,0:T(8,128)(2,1)S(1)}, bf16[256,1024]{1,0:T(8,128)(2,1)S(1)}, u32[]{:S(2)}, u32[]{:S(2)}) %collective-permute-start.15) | collective-permute-done | bytes 524320 | tf_op jit(solution)/shard_map/ppermute | solution.py:21
  158.4 0.9 collective-permute-start.22
  159.3 8.1 %collective-permute-done.19.refs_14_ = bf16[256,1024]{1,0:T(8,128)(2,1)S(1)} collective-permute-done((bf16[256,1024]{1,0:T(8,128)(2,1)}, bf16[256,1024]{1,0:T(8,128)(2,1)S(1)}, u32[]{:S(2)}, u32[]{:S(2)}) %collective-permute-start.19) | collective-permute-done | bytes 524320 | tf_op jit(solution)/shard_map/ppermute | solution.py:21
  168.0 9.4 %collective-permute-done.29.refs_2_.refs_6_ = bf16[256,1024]{1,0:T(8,128)(2,1)S(1)} collective-permute-done((bf16[256,1024]{1,0:T(8,128)(2,1)S(1)}, bf16[256,1024]{1,0:T(8,128)(2,1)S(1)}, u32[]{:S(2)}, u32[]{:S(2)}) %collective-permute-start.29) | collective-permute-done | bytes 524320 | tf_op jit(solution)/shard_map/ppermute | solution.py:21
  177.4 1.5 collective-permute-start.20
  179.5 12.9 %collective-permute-done.20.refs_15_ = bf16[256,1024]{1,0:T(8,128)(2,1)S(1)} collective-permute-done((bf16[256,1024]{1,0:T(8,128)(2,1)}, bf16[256,1024]{1,0:T(8,128)(2,1)S(1)}, u32[]{:S(2)}, u32[]{:S(2)}) %collective-permute-start.20) | collective-permute-done | bytes 524320 | tf_op jit(solution)/shard_map/ppermute | solution.py:21
  192.4 1.5 collective-permute-start.24
  194.4 3.3 %shard_map.83.refs_13_ = f32[256,1024]{1,0:T(8,128)S(1)} custom-call(s32[2]{0:T(128)S(1)} %pad_add_fusion.place, bf16[256,1024]{1,0:T(8,128)(2,1)S(1)} %shard_map.81.refs_0_.refs_4_, bf16[256,1024]{1,0:T(8,128)(2,1)S(1)} %collective-permute-done.28.refs_1_.refs_5_, bf16[256,1024]{1,0:T(8,128)(2,1)S(1)} %collective-permute-done.29.refs_2_.refs_6_, ...), custom_call_target="tpu_custom_call" | custom-call | flops 1610612736 | bytes 8912896 | tf_op jit(solution)/shard_map/pallas_call | solution.py:545
  197.7 5.5 %shard_map.82.refs_12_ = f32[512,1024]{1,0:T(8,128)S(1)} custom-call(s32[2]{0:T(128)S(1)} %pad_add_fusion.place, bf16[512,1024]{1,0:T(8,128)(2,1)S(1)} %shard_map.80.refs_0_, bf16[512,1024]{1,0:T(8,128)(2,1)S(1)} %collective-permute-done.25.refs_1_, bf16[512,1024]{1,0:T(8,128)(2,1)S(1)} %collective-permute-done.26.refs_2_, ...), custom_call_target="tpu_custom_call" | custom-call | flops 3221225472 | bytes 11534336 | tf_op jit(solution)/shard_map/pallas_call | solution.py:545
  203.6 9.1 %collective-permute-done.24.refs_11_.refs_19_ = bf16[256,1024]{1,0:T(8,128)(2,1)S(1)} collective-permute-done((bf16[256,1024]{1,0:T(8,128)(2,1)S(1)}, bf16[256,1024]{1,0:T(8,128)(2,1)S(1)}, u32[]{:S(2)}, u32[]{:S(2)}) %collective-permute-start.24) | collective-permute-done | bytes 524320 | tf_op jit(solution)/shard_map/ppermute | solution.py:21
  212.8 5.5 %shard_map.84.refs_20_ = bf16[1024,1024]{1,0:T(8,128)(2,1)} custom-call(s32[2]{0:T(128)S(1)} %pad_add_fusion.place, bf16[512,1024]{1,0:T(8,128)(2,1)S(1)} %shard_map.80.refs_0_, bf16[512,1024]{1,0:T(8,128)(2,1)S(1)} %collective-permute-done.25.refs_1_, bf16[512,1024]{1,0:T(8,128)(2,1)S(1)} %collective-permute-done.26.refs_2_, ...), custom_call_target="tpu_custom_call" | custom-call | flops 1610612736 | bytes 6815744 | tf_op jit(solution)/shard_map/pallas_call | solution.py:545
  218.3 5.2 %shard_map.85 = bf16[1024,1024]{1,0:T(8,128)(2,1)} custom-call(s32[2]{0:T(128)S(1)} %pad_add_fusion.place, bf16[256,1024]{1,0:T(8,128)(2,1)S(1)} %shard_map.79.refs_0_, bf16[256,1024]{1,0:T(8,128)(2,1)S(1)} %collective-permute-done.8.refs_1_, bf16[256,1024]{1,0:T(8,128)(2,1)S(1)} %collective-permute-done.9.refs_2_, ...), custom_call_target="tpu_custom_call", output_to_operand_aliasing={{}: (21, {})} | custom-call | flops 2147483648 | bytes 11534336 | tf_op jit(solution)/shard_map/pallas_call | solution.py:545
  (66 shorter events, 5.7 us)
Async XLA Ops:
  0.0 11.2 %copy-start.14 = (f32[1024]{0:T(1024)S(1)}, f32[1024]{0:T(1024)}, u32[]{:S(2)}) copy-start(f32[1024]{0:T(1024)} %param.11) | copy-start | bytes 12292
  0.0 11.2 %copy-start.15 = (f32[1024]{0:T(1024)S(1)}, f32[1024]{0:T(1024)}, u32[]{:S(2)}) copy-start(f32[1024]{0:T(1024)} %param.10) | copy-start | bytes 12292
  2.7 52.0 %copy-start = (bf16[512,1024]{1,0:T(8,128)(2,1)S(1)}, bf16[512,1024]{1,0:T(8,128)(2,1)}, u32[]{:S(2)}) copy-start(bf16[512,1024]{1,0:T(8,128)(2,1)} %shard_map.73.refs_0_) | copy-start | bytes 3145732
  2.7 27.4 %collective-permute-start = (bf16[512,1024]{1,0:T(8,128)(2,1)}, bf16[512,1024]{1,0:T(8,128)(2,1)}, u32[]{:S(2)}, u32[]{:S(2)}) collective-permute-start(bf16[512,1024]{1,0:T(8,128)(2,1)} %shard_map.73.refs_0_), channel_id=1, source_target_pairs={{0,2},{1,3},{2,0},{3,1},{4,6},{5,7},{6,4},{7,5},{8,10},{9,11},{10,... | collective-permute-start | bytes 3145736 | tf_op jit(solution)/shard_map/ppermute | solution.py:21
  5.7 48.5 %collective-permute-start.2 = (bf16[512,1024]{1,0:T(8,128)(2,1)}, bf16[512,1024]{1,0:T(8,128)(2,1)}, u32[]{:S(2)}, u32[]{:S(2)}) collective-permute-start(bf16[512,1024]{1,0:T(8,128)(2,1)} %shard_map.73.refs_0_), channel_id=1, source_target_pairs={{0,1},{1,0},{2,3},{3,2},{4,5},{5,4},{6,7},{7,6},{8,9},{9,8},{10,11... | collective-permute-start | bytes 3145736 | tf_op jit(solution)/shard_map/ppermute | solution.py:21
  8.6 45.6 %collective-permute-start.3 = (bf16[512,1024]{1,0:T(8,128)(2,1)}, bf16[512,1024]{1,0:T(8,128)(2,1)}, u32[]{:S(2)}, u32[]{:S(2)}) collective-permute-start(bf16[512,1024]{1,0:T(8,128)(2,1)} %get-tuple-element.21.refs_1_), channel_id=1, source_target_pairs={{0,1},{1,0},{2,3},{3,2},{4,5},{5,4},{6,7},{7,6},{8,9},{9,8},{10,11... | collective-permute-start | bytes 3145736 | tf_op jit(solution)/shard_map/ppermute | solution.py:21
  9.1 32.0 %collective-permute-start.4 = (bf16[256,1024]{1,0:T(8,128)(2,1)}, bf16[256,1024]{1,0:T(8,128)(2,1)S(1)}, u32[]{:S(2)}, u32[]{:S(2)}) collective-permute-start(bf16[256,1024]{1,0:T(8,128)(2,1)} %get-tuple-element.23), channel_id=1, source_target_pairs={{0,2},{1,3},{2,0},{3,1},{4,6},{5,7},{6,4},{7,5},{8,10},{9,11},{10,... | collective-permute-start | bytes 1572872 | tf_op jit(solution)/shard_map/ppermute | solution.py:21
  9.2 42.3 %collective-permute-start.6 = (bf16[256,1024]{1,0:T(8,128)(2,1)}, bf16[256,1024]{1,0:T(8,128)(2,1)S(1)}, u32[]{:S(2)}, u32[]{:S(2)}) collective-permute-start(bf16[256,1024]{1,0:T(8,128)(2,1)} %get-tuple-element.25), channel_id=1, source_target_pairs={{0,2},{1,3},{2,0},{3,1},{4,6},{5,7},{6,4},{7,5},{8,10},{9,11},{10,... | collective-permute-start | bytes 1572872 | tf_op jit(solution)/shard_map/ppermute | solution.py:21
  11.2 43.5 %copy-start.9 = (bf16[512,1024]{1,0:T(8,128)(2,1)S(1)}, bf16[512,1024]{1,0:T(8,128)(2,1)}, u32[]{:S(2)}) copy-start(bf16[512,1024]{1,0:T(8,128)(2,1)} %get-tuple-element.21.refs_1_) | copy-start | bytes 3145732
  30.0 45.6 %collective-permute-start.1 = (bf16[512,1024]{1,0:T(8,128)(2,1)}, bf16[512,1024]{1,0:T(8,128)(2,1)S(1)}, u32[]{:S(2)}, u32[]{:S(2)}) collective-permute-start(bf16[512,1024]{1,0:T(8,128)(2,1)} %collective-permute-done.refs_0_), channel_id=1, source_target_pairs={{0,1},{1,0},{2,3},{3,2},{4,5},{5,4},{6,7},{7,6},{8,9},{9,8},{10,11... | collective-permute-start | bytes 3145736 | tf_op jit(solution)/shard_map/ppermute | solution.py:21
  41.2 0.8 copy-start.3
  42.0 60.9 %collective-permute-start.14 = (bf16[256,1024]{1,0:T(8,128)(2,1)S(1)}, bf16[256,1024]{1,0:T(8,128)(2,1)S(1)}, u32[]{:S(2)}, u32[]{:S(2)}) collective-permute-start(bf16[256,1024]{1,0:T(8,128)(2,1)S(1)} %get-tuple-element.37.refs_5_), channel_id=1, source_target_pairs={{0,8},{4,12},{8,16},{12,20},{16,24},{20,28},{24,0},{28,4},{1,9},{5... | collective-permute-start | bytes 1572872 | tf_op jit(solution)/shard_map/ppermute | solution.py:593
  51.6 0.8 copy-start.1
  52.4 16.4 %copy-start.4 = (bf16[256,1024]{1,0:T(8,128)(2,1)S(1)}, bf16[256,1024]{1,0:T(8,128)(2,1)}, u32[]{:S(2)}) copy-start(bf16[256,1024]{1,0:T(8,128)(2,1)} %copy-done.3) | copy-start | bytes 1572868
  52.4 16.4 %copy-start.5 = (f32[1024]{0:T(1024)S(1)}, f32[1024]{0:T(1024)}, u32[]{:S(2)}) copy-start(f32[1024]{0:T(1024)} %param.13) | copy-start | bytes 12292
  52.4 16.4 %copy-start.6 = (f32[1024]{0:T(1024)S(1)}, f32[1024]{0:T(1024)}, u32[]{:S(2)}) copy-start(f32[1024]{0:T(1024)} %param.12) | copy-start | bytes 12292
  52.4 48.5 %collective-permute-start.13 = (bf16[256,1024]{1,0:T(8,128)(2,1)S(1)}, bf16[256,1024]{1,0:T(8,128)(2,1)S(1)}, u32[]{:S(2)}, u32[]{:S(2)}) collective-permute-start(bf16[256,1024]{1,0:T(8,128)(2,1)S(1)} %get-tuple-element.38.refs_4_), channel_id=1, source_target_pairs={{0,8},{4,12},{8,16},{12,20},{16,24},{20,28},{24,0},{28,4},{1,9},{5... | collective-permute-start | bytes 1572872 | tf_op jit(solution)/shard_map/ppermute | solution.py:593
  54.2 14.6 %collective-permute-start.5 = (bf16[256,1024]{1,0:T(8,128)(2,1)}, bf16[256,1024]{1,0:T(8,128)(2,1)S(1)}, u32[]{:S(2)}, u32[]{:S(2)}) collective-permute-start(bf16[256,1024]{1,0:T(8,128)(2,1)} %copy-done.3), channel_id=1, source_target_pairs={{0,1},{1,0},{2,3},{3,2},{4,5},{5,4},{6,7},{7,6},{8,9},{9,8},{10,11... | collective-permute-start | bytes 1572872 | tf_op jit(solution)/shard_map/ppermute | solution.py:21
  54.2 32.3 %collective-permute-start.7 = (bf16[256,1024]{1,0:T(8,128)(2,1)}, bf16[256,1024]{1,0:T(8,128)(2,1)S(1)}, u32[]{:S(2)}, u32[]{:S(2)}) collective-permute-start(bf16[256,1024]{1,0:T(8,128)(2,1)} %copy-done.1), channel_id=1, source_target_pairs={{0,1},{1,0},{2,3},{3,2},{4,5},{5,4},{6,7},{7,6},{8,9},{9,8},{10,11... | collective-permute-start | bytes 1572872 | tf_op jit(solution)/shard_map/ppermute | solution.py:21
  74.6 1.0 copy-start.10
  75.6 10.9 %copy-start.2 = (bf16[256,1024]{1,0:T(8,128)(2,1)S(1)}, bf16[256,1024]{1,0:T(8,128)(2,1)}, u32[]{:S(2)}) copy-start(bf16[256,1024]{1,0:T(8,128)(2,1)} %copy-done.1) | copy-start | bytes 1572868
  85.2 1.3 copy-start.7
  93.0 1.0 copy-start.12
  94.0 11.8 %all-to-all-start = ((f32[8,2,1024]{2,1,0:T(2,128)}), f32[8,2,1024]{2,1,0:T(2,128)S(1)}, u32[]{:S(2)}, u32[]{:S(2)}) async-start(f32[8,2,1024]{2,1,0:T(2,128)} %get-tuple-element.30), calls=%async_computation | async-start | bytes 131072 | tf_op jit(solution)/shard_map/all_to_all | solution.py:661
  98.8 33.0 %collective-permute-start.12 = (bf16[256,1024]{1,0:T(8,128)(2,1)S(1)}, bf16[256,1024]{1,0:T(8,128)(2,1)S(1)}, u32[]{:S(2)}, u32[]{:S(2)}) collective-permute-start(bf16[256,1024]{1,0:T(8,128)(2,1)S(1)} %get-tuple-element.37.refs_5_), channel_id=1, source_target_pairs={{0,4},{4,0},{8,12},{12,8},{16,20},{20,16},{24,28},{28,24},{1,5},{5... | collective-permute-start | bytes 1572872 | tf_op jit(solution)/shard_map/ppermute | solution.py:21
  100.9 32.0 %collective-permute-start.11 = (bf16[256,1024]{1,0:T(8,128)(2,1)S(1)}, bf16[256,1024]{1,0:T(8,128)(2,1)S(1)}, u32[]{:S(2)}, u32[]{:S(2)}) collective-permute-start(bf16[256,1024]{1,0:T(8,128)(2,1)S(1)} %get-tuple-element.38.refs_4_), channel_id=1, source_target_pairs={{0,4},{4,0},{8,12},{12,8},{16,20},{20,16},{24,28},{28,24},{1,5},{5... | collective-permute-start | bytes 1572872 | tf_op jit(solution)/shard_map/ppermute | solution.py:21
  100.9 33.0 %collective-permute-start.17 = (bf16[256,1024]{1,0:T(8,128)(2,1)S(1)}, bf16[256,1024]{1,0:T(8,128)(2,1)}, u32[]{:S(2)}, u32[]{:S(2)}) collective-permute-start(bf16[256,1024]{1,0:T(8,128)(2,1)S(1)} %collective-permute-done.13.refs_8_), channel_id=1, source_target_pairs={{0,8},{4,12},{8,16},{12,20},{16,24},{20,28},{24,0},{28,4},{1,9},{5... | collective-permute-start | bytes 1572872 | tf_op jit(solution)/shard_map/ppermute | solution.py:593
  102.9 31.9 %collective-permute-start.18 = (bf16[256,1024]{1,0:T(8,128)(2,1)S(1)}, bf16[256,1024]{1,0:T(8,128)(2,1)}, u32[]{:S(2)}, u32[]{:S(2)}) collective-permute-start(bf16[256,1024]{1,0:T(8,128)(2,1)S(1)} %collective-permute-done.14.refs_9_), channel_id=1, source_target_pairs={{0,8},{4,12},{8,16},{12,20},{16,24},{20,28},{24,0},{28,4},{1,9},{5... | collective-permute-start | bytes 1572872 | tf_op jit(solution)/shard_map/ppermute | solution.py:593
  105.9 1.6 copy-start.8
  107.4 1.2 copy-start.11
  108.7 1.2 copy-start.13
  130.3 37.1 %collective-permute-start.26 = (bf16[512,1024]{1,0:T(8,128)(2,1)S(1)}, bf16[512,1024]{1,0:T(8,128)(2,1)S(1)}, u32[]{:S(2)}, u32[]{:S(2)}) collective-permute-start(bf16[512,1024]{1,0:T(8,128)(2,1)S(1)} %shard_map.80.refs_0_), channel_id=1, source_target_pairs={{0,2},{1,3},{2,0},{3,1},{4,6},{5,7},{6,4},{7,5},{8,10},{9,11},{10,... | collective-permute-start | bytes 3145736 | tf_op jit(solution)/shard_map/ppermute | solution.py:21
  131.9 14.8 %collective-permute-start.16 = (bf16[256,1024]{1,0:T(8,128)(2,1)S(1)}, bf16[256,1024]{1,0:T(8,128)(2,1)S(1)}, u32[]{:S(2)}, u32[]{:S(2)}) collective-permute-start(bf16[256,1024]{1,0:T(8,128)(2,1)S(1)} %collective-permute-done.14.refs_9_), channel_id=1, source_target_pairs={{0,4},{4,0},{8,12},{12,8},{16,20},{20,16},{24,28},{28,24},{1,5},{5... | collective-permute-start | bytes 1572872 | tf_op jit(solution)/shard_map/ppermute | solution.py:21
  132.8 25.1 %collective-permute-start.15 = (bf16[256,1024]{1,0:T(8,128)(2,1)S(1)}, bf16[256,1024]{1,0:T(8,128)(2,1)S(1)}, u32[]{:S(2)}, u32[]{:S(2)}) collective-permute-start(bf16[256,1024]{1,0:T(8,128)(2,1)S(1)} %collective-permute-done.13.refs_8_), channel_id=1, source_target_pairs={{0,4},{4,0},{8,12},{12,8},{16,20},{20,16},{24,28},{28,24},{1,5},{5... | collective-permute-start | bytes 1572872 | tf_op jit(solution)/shard_map/ppermute | solution.py:21
  133.9 24.5 %collective-permute-start.21 = (bf16[256,1024]{1,0:T(8,128)(2,1)}, bf16[256,1024]{1,0:T(8,128)(2,1)S(1)}, u32[]{:S(2)}, u32[]{:S(2)}) collective-permute-start(bf16[256,1024]{1,0:T(8,128)(2,1)} %collective-permute-done.17.refs_12_), channel_id=1, source_target_pairs={{0,8},{4,12},{8,16},{12,20},{16,24},{20,28},{24,0},{28,4},{1,9},{5... | collective-permute-start | bytes 1572872 | tf_op jit(solution)/shard_map/ppermute | solution.py:593
  134.8 32.6 %collective-permute-start.19 = (bf16[256,1024]{1,0:T(8,128)(2,1)}, bf16[256,1024]{1,0:T(8,128)(2,1)S(1)}, u32[]{:S(2)}, u32[]{:S(2)}) collective-permute-start(bf16[256,1024]{1,0:T(8,128)(2,1)} %collective-permute-done.17.refs_12_), channel_id=1, source_target_pairs={{0,4},{4,0},{8,12},{12,8},{16,20},{20,16},{24,28},{28,24},{1,5},{5... | collective-permute-start | bytes 1572872 | tf_op jit(solution)/shard_map/ppermute | solution.py:21
  146.7 21.2 %collective-permute-start.9 = (bf16[256,1024]{1,0:T(8,128)(2,1)S(1)}, bf16[256,1024]{1,0:T(8,128)(2,1)S(1)}, u32[]{:S(2)}, u32[]{:S(2)}) collective-permute-start(bf16[256,1024]{1,0:T(8,128)(2,1)S(1)} %shard_map.79.refs_0_), channel_id=1, source_target_pairs={{0,2},{1,3},{2,0},{3,1},{4,6},{5,7},{6,4},{7,5},{8,10},{9,11},{10,... | collective-permute-start | bytes 1572872 | tf_op jit(solution)/shard_map/ppermute | solution.py:21
  157.9 19.5 %collective-permute-start.29 = (bf16[256,1024]{1,0:T(8,128)(2,1)S(1)}, bf16[256,1024]{1,0:T(8,128)(2,1)S(1)}, u32[]{:S(2)}, u32[]{:S(2)}) collective-permute-start(bf16[256,1024]{1,0:T(8,128)(2,1)S(1)} %shard_map.81.refs_0_.refs_4_), channel_id=1, source_target_pairs={{0,2},{1,3},{2,0},{3,1},{4,6},{5,7},{6,4},{7,5},{8,10},{9,11},{10,... | collective-permute-start | bytes 1572872 | tf_op jit(solution)/shard_map/ppermute | solution.py:21
  158.4 20.4 %collective-permute-start.22 = (bf16[256,1024]{1,0:T(8,128)(2,1)}, bf16[256,1024]{1,0:T(8,128)(2,1)S(1)}, u32[]{:S(2)}, u32[]{:S(2)}) collective-permute-start(bf16[256,1024]{1,0:T(8,128)(2,1)} %collective-permute-done.18.refs_13_), channel_id=1, source_target_pairs={{0,8},{4,12},{8,16},{12,20},{16,24},{20,28},{24,0},{28,4},{1,9},{5... | collective-permute-start | bytes 1572872 | tf_op jit(solution)/shard_map/ppermute | solution.py:593
  167.4 26.5 %collective-permute-start.25 = (bf16[512,1024]{1,0:T(8,128)(2,1)S(1)}, bf16[512,1024]{1,0:T(8,128)(2,1)S(1)}, u32[]{:S(2)}, u32[]{:S(2)}) collective-permute-start(bf16[512,1024]{1,0:T(8,128)(2,1)S(1)} %shard_map.80.refs_0_), channel_id=1, source_target_pairs={{0,1},{1,0},{2,3},{3,2},{4,5},{5,4},{6,7},{7,6},{8,9},{9,8},{10,11... | collective-permute-start | bytes 3145736 | tf_op jit(solution)/shard_map/ppermute | solution.py:21
  167.4 30.3 %collective-permute-start.27 = (bf16[512,1024]{1,0:T(8,128)(2,1)S(1)}, bf16[512,1024]{1,0:T(8,128)(2,1)S(1)}, u32[]{:S(2)}, u32[]{:S(2)}) collective-permute-start(bf16[512,1024]{1,0:T(8,128)(2,1)S(1)} %collective-permute-done.26.refs_2_), channel_id=1, source_target_pairs={{0,1},{1,0},{2,3},{3,2},{4,5},{5,4},{6,7},{7,6},{8,9},{9,8},{10,11... | collective-permute-start | bytes 3145736 | tf_op jit(solution)/shard_map/ppermute | solution.py:21
  167.9 11.0 %collective-permute-start.28 = (bf16[256,1024]{1,0:T(8,128)(2,1)S(1)}, bf16[256,1024]{1,0:T(8,128)(2,1)S(1)}, u32[]{:S(2)}, u32[]{:S(2)}) collective-permute-start(bf16[256,1024]{1,0:T(8,128)(2,1)S(1)} %shard_map.81.refs_0_.refs_4_), channel_id=1, source_target_pairs={{0,1},{1,0},{2,3},{3,2},{4,5},{5,4},{6,7},{7,6},{8,9},{9,8},{10,11... | collective-permute-start | bytes 1572872 | tf_op jit(solution)/shard_map/ppermute | solution.py:21
  177.4 15.0 %collective-permute-start.20 = (bf16[256,1024]{1,0:T(8,128)(2,1)}, bf16[256,1024]{1,0:T(8,128)(2,1)S(1)}, u32[]{:S(2)}, u32[]{:S(2)}) collective-permute-start(bf16[256,1024]{1,0:T(8,128)(2,1)} %collective-permute-done.18.refs_13_), channel_id=1, source_target_pairs={{0,4},{4,0},{8,12},{12,8},{16,20},{20,16},{24,28},{28,24},{1,5},{5... | collective-permute-start | bytes 1572872 | tf_op jit(solution)/shard_map/ppermute | solution.py:21
  178.9 15.0 %collective-permute-start.30 = (bf16[256,1024]{1,0:T(8,128)(2,1)S(1)}, bf16[256,1024]{1,0:T(8,128)(2,1)S(1)}, u32[]{:S(2)}, u32[]{:S(2)}) collective-permute-start(bf16[256,1024]{1,0:T(8,128)(2,1)S(1)} %collective-permute-done.29.refs_2_.refs_6_), channel_id=1, source_target_pairs={{0,1},{1,0},{2,3},{3,2},{4,5},{5,4},{6,7},{7,6},{8,9},{9,8},{10,11... | collective-permute-start | bytes 1572872 | tf_op jit(solution)/shard_map/ppermute | solution.py:21
  178.9 24.8 %collective-permute-start.23 = (bf16[256,1024]{1,0:T(8,128)(2,1)S(1)}, bf16[256,1024]{1,0:T(8,128)(2,1)S(1)}, u32[]{:S(2)}, u32[]{:S(2)}) collective-permute-start(bf16[256,1024]{1,0:T(8,128)(2,1)S(1)} %collective-permute-done.21.refs_8_.refs_16_), channel_id=1, source_target_pairs={{0,4},{4,0},{8,12},{12,8},{16,20},{20,16},{24,28},{28,24},{1,5},{5... | collective-permute-start | bytes 1572872 | tf_op jit(solution)/shard_map/ppermute | solution.py:21
  192.4 20.4 %collective-permute-start.24 = (bf16[256,1024]{1,0:T(8,128)(2,1)S(1)}, bf16[256,1024]{1,0:T(8,128)(2,1)S(1)}, u32[]{:S(2)}, u32[]{:S(2)}) collective-permute-start(bf16[256,1024]{1,0:T(8,128)(2,1)S(1)} %collective-permute-done.22.refs_9_.refs_17_), channel_id=1, source_target_pairs={{0,4},{4,0},{8,12},{12,8},{16,20},{20,16},{24,28},{28,24},{1,5},{5... | collective-permute-start | bytes 1572872 | tf_op jit(solution)/shard_map/ppermute | solution.py:21
  193.9 24.4 %collective-permute-start.8 = (bf16[256,1024]{1,0:T(8,128)(2,1)S(1)}, bf16[256,1024]{1,0:T(8,128)(2,1)S(1)}, u32[]{:S(2)}, u32[]{:S(2)}) collective-permute-start(bf16[256,1024]{1,0:T(8,128)(2,1)S(1)} %shard_map.79.refs_0_), channel_id=1, source_target_pairs={{0,1},{1,0},{2,3},{3,2},{4,5},{5,4},{6,7},{7,6},{8,9},{9,8},{10,11... | collective-permute-start | bytes 1572872 | tf_op jit(solution)/shard_map/ppermute | solution.py:21
  193.9 24.4 %collective-permute-start.10 = (bf16[256,1024]{1,0:T(8,128)(2,1)S(1)}, bf16[256,1024]{1,0:T(8,128)(2,1)S(1)}, u32[]{:S(2)}, u32[]{:S(2)}) collective-permute-start(bf16[256,1024]{1,0:T(8,128)(2,1)S(1)} %collective-permute-done.9.refs_2_), channel_id=1, source_target_pairs={{0,1},{1,0},{2,3},{3,2},{4,5},{5,4},{6,7},{7,6},{8,9},{9,8},{10,11... | collective-permute-start | bytes 1572872 | tf_op jit(solution)/shard_map/ppermute | solution.py:21

commit v7 on v6

--- a/solution.py
+++ b/solution.py
@@ -458,21 +458,22 @@
     )(place, run, maps, peer_maps, start)
 
 
-def mix_kernel(groups, group, pieces, peers, slots, final, before, place, *refs):
+def mix_kernel(groups, group, cuts, peers, slots, final, before, place, *refs):
     count = groups * group
     blocks = refs[:count]
-    weights = refs[count : count + len(slots) * 2 * pieces]
+    starts = [sum(len(cut) for cut in cuts[:n]) for n in range(len(cuts) + 1)]
+    weights = refs[count : count + starts[-1]]
     out_ref, lhs, wbuf, acc, lsem, wsem = refs[-6:]
     prev_refs = refs[count + len(weights) : count + len(weights) + before]
     depth = blocks[0].shape[1]
     heights = [blocks[c * group].shape[0] for c in range(groups)]
-    lines_of = weights[0].shape[0]
     outer = peers // 2
     here = len(slots) * 2
 
     def w_copy(n, p):
-        w_ref = weights[n * pieces + p]
-        dst = wbuf.at[n, p * lines_of : (p + 1) * lines_of, :]
+        w_ref = weights[starts[n] + p]
+        top = sum(cuts[n][:p])
+        dst = wbuf.at[n, top : top + cuts[n][p], :]
         return pltpu.make_async_copy(w_ref, dst, wsem.at[n, p])
 
     def l_copy(c, d):
@@ -482,7 +483,7 @@
         return pltpu.make_async_copy(blocks[c * group + d], dst, lsem.at[c, d])
 
     for n in range(here):
-        for p in range(pieces):
+        for p in range(len(cuts[n])):
             w_copy(n, p).start()
     for c in range(groups):
         for d in range(group):
@@ -494,12 +495,12 @@
     for prev in prev_refs:
         acc[top : top + prev.shape[0], :] = prev[...]
         top += prev.shape[0]
-    span = lines_of * pieces
+    span = wbuf.shape[1]
     for n in range(here):
         source = lax.rem(place[1] // 2 + outer - slots[n // 2], outer)
         owner = source * 2 + (lax.rem(place[1], 2) ^ (n % 2))
         deep = pl.ds(pl.multiple_of(owner * span, span), span)
-        for p in range(pieces):
+        for p in range(len(cuts[n])):
             w_copy(n, p).wait()
         part = jnp.dot(lhs[:, deep], wbuf[n], preferred_element_type=F32)
         if n > 0 or before:
@@ -518,13 +519,17 @@
                 out_ref[lines, :] = moved.astype(BF16)
 
 
-def mix_rows(place, blocks, weights, slots, prev, final, whole, first, total_rows, pieces):
+def mix_rows(place, blocks, weights, slots, prev, final, whole, first, total_rows):
     groups, group = len(blocks), len(blocks[0])
     depth = blocks[0][0].shape[1]
-    lines_of, width = weights[0].shape
-    peers = len(weights) // pieces
+    width = weights[0][0].shape[1]
+    peers = len(weights)
+    span = sum(piece.shape[0] for piece in weights[0])
     rows = sum(g[0].shape[0] for g in blocks)
-    used = [weights[(s * 2 + i) * pieces + p] for s in slots for i in range(2) for p in range(pieces)]
+    chosen = [weights[s * 2 + i] for s in slots for i in range(2)]
+    cuts = tuple(tuple(piece.shape[0] for piece in pieces) for pieces in chosen)
+    used = [piece for pieces in chosen for piece in pieces]
+    most = max(len(cut) for cut in cuts)
     args = [place] + [b for g in blocks for b in g] + used
     in_specs = [pl.BlockSpec(memory_space=pl.ANY)] * (groups * group)
     in_specs += [pl.BlockSpec(memory_space=pltpu.HBM)] * len(used)
@@ -535,7 +540,7 @@
         aliases = {len(args): 0}
         args.append(whole)
         in_specs.append(pl.BlockSpec(memory_space=pl.ANY))
-    deep = len(slots) * 2 * pieces * lines_of
+    deep = len(slots) * 2 * span
     if final:
         out_shape = jax.ShapeDtypeStruct((total_rows, width), BF16)
         out_spec = pl.BlockSpec((rows, width), lambda n, p: (first // rows, 0))
@@ -544,7 +549,7 @@
         out_spec = pl.BlockSpec((rows, width), lambda n, p: (0, 0))
     return pl.pallas_call(
         functools.partial(
-            mix_kernel, groups, group, pieces, peers, tuple(slots), final, len(prev)
+            mix_kernel, groups, group, cuts, peers, tuple(slots), final, len(prev)
         ),
         out_shape=out_shape,
         grid_spec=pltpu.PrefetchScalarGridSpec(
@@ -554,10 +559,10 @@
             out_specs=out_spec,
             scratch_shapes=[
                 pltpu.VMEM((rows, group * depth), BF16),
-                pltpu.VMEM((len(slots) * 2, lines_of * pieces, width), BF16),
+                pltpu.VMEM((len(slots) * 2, span, width), BF16),
                 pltpu.VMEM((rows, width), F32),
                 pltpu.SemaphoreType.DMA((groups, group)),
-                pltpu.SemaphoreType.DMA((len(slots) * 2, pieces)),
+                pltpu.SemaphoreType.DMA((len(slots) * 2, most)),
             ],
         ),
         input_output_aliases=aliases,
@@ -566,51 +571,76 @@
     )(*args)
 
 
-EARLY = 5
 SHARES = (2, 1, 1)
-
-
-def pieces_of(lines_of):
-    return 2 if lines_of % (4 * LANES) == 0 else 1
-
-
-class Ring:
-    def __init__(self, w_output):
-        self.peers = lax.axis_size("ctx")
-        self.outer = self.peers // 2
-        self.pieces = pieces_of(w_output.shape[0])
-        lines_of = w_output.shape[0] // self.pieces
-        self.held = {}
-        for p in range(self.pieces):
-            self.held[0, 0, p] = w_output[p * lines_of : (p + 1) * lines_of]
-
-    def ring_step(self, n, gate=None):
-        s, p = n // self.pieces + 1, n % self.pieces
-        block = self.held[s - 1, 0, p]
-        if gate is not None:
-            block, _ = lax.optimization_barrier((block, gate))
-        route = [(i, (i + 2) % self.peers) for i in range(self.peers)]
-        self.held[s, 0, p] = lax.ppermute(block, "ctx", route)
-
-    def swap_step(self, n, gate=None):
-        s, p = n // self.pieces, n % self.pieces
-        block = self.held[s, 0, p]
-        if gate is not None:
-            block, _ = lax.optimization_barrier((block, gate))
-        self.held[s, 1, p] = swap(block, "ctx", 1)
-
-    def run(self, gate):
-        rings, swaps = (self.outer - 1) * self.pieces, self.outer * self.pieces
-        for n in range(max(rings, swaps)):
-            g = gate if n >= EARLY else None
-            if n < rings:
-                self.ring_step(n, g)
-            if n < swaps:
-                self.swap_step(n, g)
-
-    def blocks(self):
-        steps = [(s, i) for s in range(self.outer) for i in range(2)]
-        return [self.held[s, i, p] for s, i in steps for p in range(self.pieces)]
+RINGS_EARLY = 2
+SWAPS_EARLY = 1
+
+
+def cut_of(rows, shares):
+    parts = [rows * share // sum(shares) for share in shares]
+    return parts if min(parts) >= LANES else [rows]
+
+
+def ring_cut(step, outer, rows):
+    return cut_of(rows, (1, 1) if step == outer - 1 else (1,))
+
+
+def swap_cut(step, outer, rows):
+    if step == SWAPS_EARLY + 1 and step < outer - 1:
+        return cut_of(rows, (1, 3))
+    return ring_cut(step, outer, rows)
+
+
+def recut(blocks, parts):
+    if [b.shape[0] for b in blocks] == parts:
+        return blocks
+    (block,) = blocks
+    tops = [sum(parts[:p]) for p in range(len(parts))]
+    return [block[top : top + part] for top, part in zip(tops, parts)]
+
+
+def behind(block, gate):
+    return block if gate is None else lax.optimization_barrier((block, gate))[0]
+
+
+def gather_early(w_output):
+    peers = lax.axis_size("ctx")
+    route = [(i, (i + 2) % peers) for i in range(peers)]
+    held = {(0, 0): [w_output]}
+    for step in range(1, min(RINGS_EARLY + 1, peers // 2)):
+        held[step, 0] = [lax.ppermute(held[step - 1, 0][0], "ctx", route)]
+    for step in range(SWAPS_EARLY + 1):
+        held[step, 1] = [swap(held[step, 0][0], "ctx", 1)]
+    return held
+
+
+def next_cuts(outer, rows):
+    return [ring_cut(RINGS_EARLY + 1, outer, rows), swap_cut(SWAPS_EARLY + 1, outer, rows)]
+
+
+def gather_late(held, following, middle, late):
+    peers = lax.axis_size("ctx")
+    outer = peers // 2
+    rows = held[0, 0][0].shape[0]
+    route = [(i, (i + 2) % peers) for i in range(peers)]
+    for step in range(RINGS_EARLY + 1, outer):
+        held[step, 0] = []
+        if step == RINGS_EARLY + 1:
+            source = following[0]
+        else:
+            source = recut(held[step - 1, 0], ring_cut(step, outer, rows))
+        for block in source:
+            held[step, 0].append(lax.ppermute(behind(block, late), "ctx", route))
+    for step in range(SWAPS_EARLY + 1, outer):
+        held[step, 1] = []
+        if step == SWAPS_EARLY + 1:
+            source = following[1]
+        else:
+            source = recut(held[step, 0], swap_cut(step, outer, rows))
+        for p, block in enumerate(source):
+            gate = middle if step == SWAPS_EARLY + 1 and p == 0 else late
+            held[step, 1].append(swap(behind(block, gate), "ctx", 1))
+    return [held[step, i] for step in range(outer) for i in range(2)]
 
 
 def layer(tokens, w_input, w_output, bias_update, bias_cand, recur_gain, start_state):
@@ -658,11 +688,13 @@
         )
         gates.append(out[0])
         maps.append(out[1])
-    peer_maps = lax.all_to_all(out[2], "ctx", 0, 0, tiled=True)
-    run, run_maps, totals = bend_all(place, gates, maps, peer_maps, gain, start)
+    held = gather_early(w_output)
+    following = [recut(held[RINGS_EARLY, 0], cut) for cut in next_cuts(peers // 2, w_output.shape[0])]
+    following, totals = lax.optimization_barrier((following, out[2]))
+    first_maps = lax.all_to_all(totals, "ctx", 0, 0, tiled=True)
+    run, run_maps, totals = bend_all(place, gates, maps, first_maps, gain, start)
     peer_maps = lax.all_to_all(totals, "ctx", 0, 0, tiled=True)
-    ring = Ring(w_output)
-    ring.run(peer_maps)
+    weights = gather_late(held, following, first_maps, peer_maps)
 
     blocks = []
     for c in range(chunks):
@@ -676,9 +708,9 @@
             lows.append(swap(own, "ch", d))
             highs.append(swap(across, "ch", d))
         blocks[c] = lows + highs
-    weights = ring.blocks()
-    late = max(1, ring.outer // 4)
-    slots = list(range(ring.outer))
+    outer = peers // 2
+    late = max(1, outer // 4)
+    slots = list(range(outer))
 
     def mix(part, used, prev, final, whole):
         return mix_rows(
@@ -691,7 +723,6 @@
             whole,
             firsts[part][0],
             total_rows,
-            ring.pieces,
         )
 
     early, late_slots = slots[:-late], slots[-late:]

time: 224 us -> 222 us (level)
  starting transfers between devices: 31.9 us -> 27.4 us
  waiting for transfers between devices: 98 us -> 102 us
  blocking collectives: 12.6 us -> 9.29 us
    ppermute x6 -> x4, waiting for transfers between devices: 0.02 us -> 5.84 us  [the longest x2 5.84 us: gather_early(): held[step, 0] = [lax.ppermute(held[step - 1, 0][0], 'ctx', route)]]
    ppermute x25 -> x23, waiting for transfers between devices: 96.5 us -> 91 us  [swap(): lax.ppermute(block, axis, [(i, i ^ bits) for i in range(lax.axis_size(axi...]
    ppermute x6 -> x4, starting transfers between devices: 9.14 us -> 5.52 us  [the longest x2 3.05 us: gather_early(): held[step, 0] = [lax.ppermute(held[step - 1, 0][0], 'ctx', route)]]
    all_to_all x1, waiting for transfers between devices: 1.49 us -> 4.99 us  [layer(): first_maps = lax.all_to_all(totals, 'ctx', 0, 0, tiled=True)]
    all_to_all x1, blocking collectives: 12.6 us -> 9.29 us  [layer(): peer_maps = lax.all_to_all(totals, 'ctx', 0, 0, tiled=True)]
    ppermute x25 -> x23, starting transfers between devices: 17.9 us -> 18 us  [swap(): lax.ppermute(block, axis, [(i, i ^ bits) for i in range(lax.axis_size(axi...]
  transfers between devices with their start and end apart: 32 -> 28, of which waited for: 11 -> 10; matrix products, arithmetic and copies ran while one was open for 1% -> 1% of each run, Pallas kernels for 28% -> 30%
where the time goes in v7:
time: 222 us; the launch traced here: 221 us
  waiting for transfers between devices  102 us (46%)
  Pallas kernels  71.7 us (32%)
  starting transfers between devices  27.4 us (12%)
  local copies, waits for them, and re-layouts  10.4 us (5%)
  blocking collectives  9.29 us (4%)
    ppermute x23, waiting for transfers between devices, swap(): lax.ppermute(block, axis, [(i, i ^ bits) for i in range(lax.axis_size(axi...  91 us
    pallas_call x3, Pallas kernels, gate_chunk(): pl.pallas_call(functools.partial(gate_kernel, half, first_row, rows, len(...  22.8 us
    pallas_call x4, Pallas kernels, mix_rows(): pl.pallas_call(functools.partial(mix_kernel, groups, group, cuts, peers,...  19.7 us
    ppermute x23, starting transfers between devices, swap(): lax.ppermute(block, axis, [(i, i ^ bits) for i in range(lax.axis_size(axi...  18 us
    pallas_call x1, Pallas kernels, near_product(): pl.pallas_call(functools.partial(near_kernel, half, tiles, heights), out_...  14.2 us
    all_to_all x1, blocking collectives, layer(): peer_maps = lax.all_to_all(totals, 'ctx', 0, 0, tiled=True)  9.29 us
    unnamed x32, local copies, waits for them, and re-layouts  7.6 us
    pallas_call x1, Pallas kernels, bend_all(): pl.pallas_call(functools.partial(bend_kernel, chunks, peers), out_shape=[...  6.88 us
  transfers between devices with their start and end apart: 28, of which 10 were waited for; matrix products, arithmetic and copies ran while one was open for 1% of the time, Pallas kernels for 30%

profile of v7, /device:TPU:0, one launch (start us, length us, event | category | flops | bytes accessed | tf_op | source)
XLA Modules:
  0.0 221.1 jit_solution(4530927346327663861)
XLA Ops:
  0.0 3.1 %collective-permute-start.8 = (bf16[512,1024]{1,0:T(8,128)(2,1)}, bf16[512,1024]{1,0:T(8,128)(2,1)S(1)}, u32[]{:S(2)}, u32[]{:S(2)}) collective-permute-start(bf16[512,1024]{1,0:T(8,128)(2,1)} %refs_4_.7), channel_id=1, source_target_pairs={{0,8},{4,12},{8,16},{12,20},{16,24},{20,28},{24,0},{28,4},{1,9},{5... | collective-permute-start | bytes 3145736 | tf_op jit(solution)/shard_map/ppermute | solution.py:611
  3.1 2.8 %shard_map.74 = (bf16[256,1024]{1,0:T(8,128)(2,1)}, bf16[256,1024]{1,0:T(8,128)(2,1)}, bf16[512,1024]{1,0:T(8,128)(2,1)}) custom-call(bf16[1024,1024]{1,0:T(8,128)(2,1)} %src.3), custom_call_target="tpu_custom_call" | custom-call | flops 268435456 | bytes 2097152 | tf_op jit(solution)/shard_map/pallas_call | solution.py:143
  5.9 1.6 collective-permute-start.4
  7.5 2.6 %shard_map.73.refs_0_ = bf16[512,1024]{1,0:T(8,128)(2,1)} custom-call(bf16[1024,1024]{1,0:T(8,128)(2,1)} %src.3), custom_call_target="tpu_custom_call" | custom-call | flops 268435456 | bytes 2097152 | tf_op jit(solution)/shard_map/pallas_call | solution.py:143
  11.2 9.9 %collective-permute-done.4.refs_0_ = bf16[256,1024]{1,0:T(8,128)(2,1)} collective-permute-done((bf16[256,1024]{1,0:T(8,128)(2,1)}, bf16[256,1024]{1,0:T(8,128)(2,1)}, u32[]{:S(2)}, u32[]{:S(2)}) %collective-permute-start.4) | collective-permute-done | bytes 524320 | tf_op jit(solution)/shard_map/ppermute | solution.py:21
  21.1 1.5 collective-permute-start.6
  22.6 5.8 %collective-permute-done.8.refs_6_ = bf16[512,1024]{1,0:T(8,128)(2,1)S(1)} collective-permute-done((bf16[512,1024]{1,0:T(8,128)(2,1)}, bf16[512,1024]{1,0:T(8,128)(2,1)S(1)}, u32[]{:S(2)}, u32[]{:S(2)}) %collective-permute-start.8) | collective-permute-done | bytes 1048608 | tf_op jit(solution)/shard_map/ppermute | solution.py:611
  28.5 24.9 %collective-permute-done.6.refs_0_ = bf16[256,1024]{1,0:T(8,128)(2,1)} collective-permute-done((bf16[256,1024]{1,0:T(8,128)(2,1)}, bf16[256,1024]{1,0:T(8,128)(2,1)}, u32[]{:S(2)}, u32[]{:S(2)}) %collective-permute-start.6) | collective-permute-done | bytes 524320 | tf_op jit(solution)/shard_map/ppermute | solution.py:21
  53.4 1.5 collective-permute-start.13
  55.5 1.2 copy-done.1
  56.7 14.2 %shard_map.75.refs_2_ = f32[2,1024,1024]{2,1,0:T(8,128)S(1)} custom-call(s32[2]{0:T(128)S(1)} %pad_add_fusion.place, bf16[512,1024]{1,0:T(8,128)(2,1)S(1)} %copy-done.1, bf16[512,1024]{1,0:T(8,128)(2,1)} %get-tuple-element.29.refs_1_, bf16[512,1024]{1,0:T(8,128)(2,1)} %collective-permute-done.2.refs_2_, bf16[512,1024]{1,0:T(8,128)(2,1)} %collective-permute-done.3.refs_3_, ...), custom_call_target="tpu_custom_call" | custom-call | flops 8589934592 | bytes 20971520 | tf_op jit(solution)/shard_map/pallas_call | solution.py:87
  71.0 6.3 %shard_map.77 = (bf16[2,256,1024]{2,1,0:T(8,128)(2,1)S(1)}, f32[2,8,1024]{2,1,0:T(8,128)S(1)}) custom-call(s32[2]{0:T(128)S(1)} %pad_add_fusion.place, bf16[256,1024]{1,0:T(8,128)(2,1)} %collective-permute-done.4.refs_0_, bf16[256,1024]{1,0:T(8,128)(2,1)S(1)} %collective-permute-done.5.refs_1_, f32[2,1024,1024]{2,1,0:T(8,128)S(1)} %shard_map.75.refs_2_, ...), custom_call_target="tpu_custom_call" | custom-call | flops 2147483648 | bytes 12582912 | tf_op jit(solution)/shard_map/pallas_call | solution.py:290
  77.3 1.1 fusion
  78.5 0.7 slice.18
  79.2 1.0 slice.19
  80.2 9.5 %shard_map.76 = (bf16[2,512,1024]{2,1,0:T(8,128)(2,1)S(1)}, f32[2,16,1024]{2,1,0:T(8,128)S(1)}) custom-call(s32[2]{0:T(128)S(1)} %pad_add_fusion.place, bf16[512,1024]{1,0:T(8,128)(2,1)} %collective-permute-done.refs_0_, bf16[512,1024]{1,0:T(8,128)(2,1)S(1)} %collective-permute-done.1.refs_1_, f32[2,1024,1024]{2,1,0:T(8,128)S(1)} %shard_map.75.refs_2_, ...), custom_call_target="tpu_custom_call" | custom-call | flops 4294967296 | bytes 16777216 | tf_op jit(solution)/shard_map/pallas_call | solution.py:290
  89.7 1.3 copy-done.4
  91.0 7.0 %shard_map.78 = (bf16[2,256,1024]{2,1,0:T(8,128)(2,1)S(1)}, f32[2,8,1024]{2,1,0:T(8,128)S(1)}, f32[8,2,1024]{2,1,0:T(2,128)}) custom-call(s32[2]{0:T(128)S(1)} %pad_add_fusion.place, bf16[256,1024]{1,0:T(8,128)(2,1)} %collective-permute-done.6.refs_0_, bf16[256,1024]{1,0:T(8,128)(2,1)S(1)} %collective-permute-done.7.refs_1_, ...), custom_call_target="tpu_custom_call" | custom-call | flops 2147483648 | bytes 12582912 | tf_op jit(solution)/shard_map/pallas_call | solution.py:290
  98.0 1.0 copy-done.8
  99.0 3.9 %all-to-all-start = ((f32[8,2,1024]{2,1,0:T(2,128)}), f32[8,2,1024]{2,1,0:T(2,128)S(1)}, u32[]{:S(2)}, u32[]{:S(2)}) async-start(f32[8,2,1024]{2,1,0:T(2,128)} %get-tuple-element.39), calls=%async_computation | async-start | bytes 131072 | tf_op jit(solution)/shard_map/all_to_all | solution.py:694
  102.9 2.0 collective-permute-start.14
  104.9 5.0 %all-to-all-done.refs_6_ = f32[8,2,1024]{2,1,0:T(2,128)S(1)} async-done(((f32[8,2,1024]{2,1,0:T(2,128)}), f32[8,2,1024]{2,1,0:T(2,128)S(1)}, u32[]{:S(2)}, u32[]{:S(2)}) %all-to-all-start) | async-done | bytes 65568 | tf_op jit(solution)/shard_map/all_to_all | solution.py:694
  109.9 1.6 copy-done.5
  111.5 1.2 copy-done.7
  112.7 1.2 copy-done.9
  113.9 6.9 %bend.1 = (f32[2,1024,1024]{2,1,0:T(8,128)S(1)}, f32[2,32,1024]{2,1,0:T(8,128)S(1)}, f32[8,2,1024]{2,1,0:T(2,128)S(1)}) custom-call(s32[2]{0:T(128)S(1)} %pad_add_fusion.place, bf16[2,512,1024]{2,1,0:T(8,128)(2,1)S(1)} %copy-done.5, bf16[2,256,1024]{2,1,0:T(8,128)(2,1)S(1)} %copy-done.7, bf16[2,256,1024]{2,1,0:T(8,128)(2,1)S(1)} %copy-done.9, ...), custom_call_target="tpu_custom_call" | custom-call | flops 41943040 | bytes 12582912 | tf_op jit(solution)/shard_map/bend/pallas_call | solution.py:396
  120.8 9.3 %all_to_all.10.peer_ref = f32[8,2,1024]{2,1,0:T(2,128)S(1)} all-to-all(f32[8,2,1024]{2,1,0:T(2,128)S(1)} %get-tuple-element.42), channel_id=1, replica_groups=mesh['ctx'=8,'ch'=4] {'ctx'}, dimensions={0} | all-to-all | bytes 131072 | tf_op jit(solution)/shard_map/all_to_all | solution.py:696
  130.1 1.0 shard_map.80.refs_0_
  131.1 1.6 collective-permute-start.22
  132.6 0.8 shard_map.79.refs_0_
  133.5 0.6 collective-permute-start.11
  134.1 1.1 collective-permute-start.17
  135.2 1.1 collective-permute-start.15
  136.3 1.4 collective-permute-start.18
  137.7 0.8 shard_map.81.refs_0_.refs_4_
  138.5 3.3 %collective-permute-done.15.refs_9_ = bf16[128,1024]{1,0:T(8,128)(2,1)S(1)} collective-permute-done((bf16[128,1024]{1,0:T(8,128)(2,1)S(1)}, bf16[128,1024]{1,0:T(8,128)(2,1)S(1)}, u32[]{:S(2)}, u32[]{:S(2)}) %collective-permute-start.15) | collective-permute-done | bytes 262176 | tf_op jit(solution)/shard_map/ppermute | solution.py:21
  141.8 24.5 %collective-permute-done.11.refs_2_ = bf16[256,1024]{1,0:T(8,128)(2,1)S(1)} collective-permute-done((bf16[256,1024]{1,0:T(8,128)(2,1)S(1)}, bf16[256,1024]{1,0:T(8,128)(2,1)S(1)}, u32[]{:S(2)}, u32[]{:S(2)}) %collective-permute-start.11) | collective-permute-done | bytes 524320 | tf_op jit(solution)/shard_map/ppermute | solution.py:21
  166.3 1.5 collective-permute-start.25
  167.8 1.3 collective-permute-start.16
  169.3 8.8 %collective-permute-done.25.refs_2_.refs_6_ = bf16[256,1024]{1,0:T(8,128)(2,1)S(1)} collective-permute-done((bf16[256,1024]{1,0:T(8,128)(2,1)S(1)}, bf16[256,1024]{1,0:T(8,128)(2,1)S(1)}, u32[]{:S(2)}, u32[]{:S(2)}) %collective-permute-start.25) | collective-permute-done | bytes 524320 | tf_op jit(solution)/shard_map/ppermute | solution.py:21
  178.1 1.7 collective-permute-start.19
  179.8 8.5 %collective-permute-done.16.refs_10_ = bf16[384,1024]{1,0:T(8,128)(2,1)S(1)} collective-permute-done((bf16[384,1024]{1,0:T(8,128)(2,1)S(1)}, bf16[384,1024]{1,0:T(8,128)(2,1)S(1)}, u32[]{:S(2)}, u32[]{:S(2)}) %collective-permute-start.16) | collective-permute-done | bytes 786464 | tf_op jit(solution)/shard_map/ppermute | solution.py:21
  188.3 1.3 collective-permute-start.20
  190.1 3.7 %shard_map.83.refs_13_ = f32[256,1024]{1,0:T(8,128)S(1)} custom-call(s32[2]{0:T(128)S(1)} %pad_add_fusion.place, bf16[256,1024]{1,0:T(8,128)(2,1)S(1)} %shard_map.81.refs_0_.refs_4_, bf16[256,1024]{1,0:T(8,128)(2,1)S(1)} %collective-permute-done.24.refs_1_.refs_5_, bf16[256,1024]{1,0:T(8,128)(2,1)S(1)} %collective-permute-done.25.refs_2_.refs_6_, ...), custom_call_target="tpu_custom_call" | custom-call | flops 1610612736 | bytes 8912896 | tf_op jit(solution)/shard_map/pallas_call | solution.py:550
  193.8 5.3 %shard_map.82.refs_12_ = f32[512,1024]{1,0:T(8,128)S(1)} custom-call(s32[2]{0:T(128)S(1)} %pad_add_fusion.place, bf16[512,1024]{1,0:T(8,128)(2,1)S(1)} %shard_map.80.refs_0_, bf16[512,1024]{1,0:T(8,128)(2,1)S(1)} %collective-permute-done.21.refs_1_, bf16[512,1024]{1,0:T(8,128)(2,1)S(1)} %collective-permute-done.22.refs_2_, ...), custom_call_target="tpu_custom_call" | custom-call | flops 3221225472 | bytes 11534336 | tf_op jit(solution)/shard_map/pallas_call | solution.py:550
  199.5 10.7 %collective-permute-done.20.refs_11_.refs_14_ = bf16[256,1024]{1,0:T(8,128)(2,1)S(1)} collective-permute-done((bf16[256,1024]{1,0:T(8,128)(2,1)S(1)}, bf16[256,1024]{1,0:T(8,128)(2,1)S(1)}, u32[]{:S(2)}, u32[]{:S(2)}) %collective-permute-start.20) | collective-permute-done | bytes 524320 | tf_op jit(solution)/shard_map/ppermute | solution.py:21
  210.2 5.3 %shard_map.84.refs_15_ = bf16[1024,1024]{1,0:T(8,128)(2,1)} custom-call(s32[2]{0:T(128)S(1)} %pad_add_fusion.place, bf16[512,1024]{1,0:T(8,128)(2,1)S(1)} %shard_map.80.refs_0_, bf16[512,1024]{1,0:T(8,128)(2,1)S(1)} %collective-permute-done.21.refs_1_, bf16[512,1024]{1,0:T(8,128)(2,1)S(1)} %collective-permute-done.22.refs_2_, ...), custom_call_target="tpu_custom_call" | custom-call | flops 1610612736 | bytes 6815744 | tf_op jit(solution)/shard_map/pallas_call | solution.py:550
  215.6 5.4 %shard_map.85 = bf16[1024,1024]{1,0:T(8,128)(2,1)} custom-call(s32[2]{0:T(128)S(1)} %pad_add_fusion.place, bf16[256,1024]{1,0:T(8,128)(2,1)S(1)} %shard_map.79.refs_0_, bf16[256,1024]{1,0:T(8,128)(2,1)S(1)} %collective-permute-done.10.refs_1_, bf16[256,1024]{1,0:T(8,128)(2,1)S(1)} %collective-permute-done.11.refs_2_, ...), custom_call_target="tpu_custom_call", output_to_operand_aliasing={{}: (16, {})} | custom-call | flops 2147483648 | bytes 11534336 | tf_op jit(solution)/shard_map/pallas_call | solution.py:550
  (60 shorter events, 3.0 us)
Async XLA Ops:
  0.0 28.4 %collective-permute-start.8 = (bf16[512,1024]{1,0:T(8,128)(2,1)}, bf16[512,1024]{1,0:T(8,128)(2,1)S(1)}, u32[]{:S(2)}, u32[]{:S(2)}) collective-permute-start(bf16[512,1024]{1,0:T(8,128)(2,1)} %refs_4_.7), channel_id=1, source_target_pairs={{0,8},{4,12},{8,16},{12,20},{16,24},{20,28},{24,0},{28,4},{1,9},{5... | collective-permute-start | bytes 3145736 | tf_op jit(solution)/shard_map/ppermute | solution.py:611
  5.9 16.7 %copy-start.14 = (f32[1024]{0:T(1024)S(1)}, f32[1024]{0:T(1024)}, u32[]{:S(2)}) copy-start(f32[1024]{0:T(1024)} %param.11) | copy-start | bytes 12292
  5.9 16.7 %copy-start.15 = (f32[1024]{0:T(1024)S(1)}, f32[1024]{0:T(1024)}, u32[]{:S(2)}) copy-start(f32[1024]{0:T(1024)} %param.10) | copy-start | bytes 12292
  5.9 47.5 %copy-start = (bf16[512,1024]{1,0:T(8,128)(2,1)S(1)}, bf16[512,1024]{1,0:T(8,128)(2,1)}, u32[]{:S(2)}) copy-start(bf16[512,1024]{1,0:T(8,128)(2,1)} %refs_4_.7) | copy-start | bytes 3145732
  5.9 15.2 %collective-permute-start.4 = (bf16[256,1024]{1,0:T(8,128)(2,1)}, bf16[256,1024]{1,0:T(8,128)(2,1)}, u32[]{:S(2)}, u32[]{:S(2)}) collective-permute-start(bf16[256,1024]{1,0:T(8,128)(2,1)} %get-tuple-element.31), channel_id=1, source_target_pairs={{0,2},{1,3},{2,0},{3,1},{4,6},{5,7},{6,4},{7,5},{8,10},{9,11},{10,... | collective-permute-start | bytes 1572872 | tf_op jit(solution)/shard_map/ppermute | solution.py:21
  10.1 44.8 %collective-permute-start = (bf16[512,1024]{1,0:T(8,128)(2,1)}, bf16[512,1024]{1,0:T(8,128)(2,1)}, u32[]{:S(2)}, u32[]{:S(2)}) collective-permute-start(bf16[512,1024]{1,0:T(8,128)(2,1)} %shard_map.73.refs_0_), channel_id=1, source_target_pairs={{0,2},{1,3},{2,0},{3,1},{4,6},{5,7},{6,4},{7,5},{8,10},{9,11},{10,... | collective-permute-start | bytes 3145736 | tf_op jit(solution)/shard_map/ppermute | solution.py:21
  10.7 44.2 %collective-permute-start.2 = (bf16[512,1024]{1,0:T(8,128)(2,1)}, bf16[512,1024]{1,0:T(8,128)(2,1)}, u32[]{:S(2)}, u32[]{:S(2)}) collective-permute-start(bf16[512,1024]{1,0:T(8,128)(2,1)} %shard_map.73.refs_0_), channel_id=1, source_target_pairs={{0,1},{1,0},{2,3},{3,2},{4,5},{5,4},{6,7},{7,6},{8,9},{9,8},{10,11... | collective-permute-start | bytes 3145736 | tf_op jit(solution)/shard_map/ppermute | solution.py:21
  10.7 44.7 %collective-permute-start.3 = (bf16[512,1024]{1,0:T(8,128)(2,1)}, bf16[512,1024]{1,0:T(8,128)(2,1)}, u32[]{:S(2)}, u32[]{:S(2)}) collective-permute-start(bf16[512,1024]{1,0:T(8,128)(2,1)} %get-tuple-element.29.refs_1_), channel_id=1, source_target_pairs={{0,1},{1,0},{2,3},{3,2},{4,5},{5,4},{6,7},{7,6},{8,9},{9,8},{10,11... | collective-permute-start | bytes 3145736 | tf_op jit(solution)/shard_map/ppermute | solution.py:21
  21.1 32.3 %collective-permute-start.6 = (bf16[256,1024]{1,0:T(8,128)(2,1)}, bf16[256,1024]{1,0:T(8,128)(2,1)}, u32[]{:S(2)}, u32[]{:S(2)}) collective-permute-start(bf16[256,1024]{1,0:T(8,128)(2,1)} %get-tuple-element.33), channel_id=1, source_target_pairs={{0,2},{1,3},{2,0},{3,1},{4,6},{5,7},{6,4},{7,5},{8,10},{9,11},{10,... | collective-permute-start | bytes 1572872 | tf_op jit(solution)/shard_map/ppermute | solution.py:21
  22.6 48.4 %copy-start.3 = (f32[1024]{0:T(1024)S(1)}, f32[1024]{0:T(1024)}, u32[]{:S(2)}) copy-start(f32[1024]{0:T(1024)} %param.12) | copy-start | bytes 12292
  28.4 48.9 %collective-permute-start.9 = (bf16[512,1024]{1,0:T(8,128)(2,1)S(1)}, bf16[512,1024]{1,0:T(8,128)(2,1)S(1)}, u32[]{:S(2)}, u32[]{:S(2)}) collective-permute-start(bf16[512,1024]{1,0:T(8,128)(2,1)S(1)} %collective-permute-done.8.refs_6_), channel_id=1, source_target_pairs={{0,8},{4,12},{8,16},{12,20},{16,24},{20,28},{24,0},{28,4},{1,9},{5... | collective-permute-start | bytes 3145736 | tf_op jit(solution)/shard_map/ppermute | solution.py:611
  28.4 42.6 %copy-start.2 = (f32[1024]{0:T(1024)S(1)}, f32[1024]{0:T(1024)}, u32[]{:S(2)}) copy-start(f32[1024]{0:T(1024)} %param.13) | copy-start | bytes 12292
  53.4 81.8 %collective-permute-start.13 = (bf16[512,1024]{1,0:T(8,128)(2,1)S(1)}, bf16[512,1024]{1,0:T(8,128)(2,1)}, u32[]{:S(2)}, u32[]{:S(2)}) collective-permute-start(bf16[512,1024]{1,0:T(8,128)(2,1)S(1)} %copy-done), channel_id=1, source_target_pairs={{0,4},{4,0},{8,12},{12,8},{16,20},{20,16},{24,28},{28,24},{1,5},{5... | collective-permute-start | bytes 3145736 | tf_op jit(solution)/shard_map/ppermute | solution.py:21
  54.9 16.1 %collective-permute-start.5 = (bf16[256,1024]{1,0:T(8,128)(2,1)}, bf16[256,1024]{1,0:T(8,128)(2,1)S(1)}, u32[]{:S(2)}, u32[]{:S(2)}) collective-permute-start(bf16[256,1024]{1,0:T(8,128)(2,1)} %collective-permute-done.4.refs_0_), channel_id=1, source_target_pairs={{0,1},{1,0},{2,3},{3,2},{4,5},{5,4},{6,7},{7,6},{8,9},{9,8},{10,11... | collective-permute-start | bytes 1572872 | tf_op jit(solution)/shard_map/ppermute | solution.py:21
  54.9 36.1 %collective-permute-start.7 = (bf16[256,1024]{1,0:T(8,128)(2,1)}, bf16[256,1024]{1,0:T(8,128)(2,1)S(1)}, u32[]{:S(2)}, u32[]{:S(2)}) collective-permute-start(bf16[256,1024]{1,0:T(8,128)(2,1)} %collective-permute-done.6.refs_0_), channel_id=1, source_target_pairs={{0,1},{1,0},{2,3},{3,2},{4,5},{5,4},{6,7},{7,6},{8,9},{9,8},{10,11... | collective-permute-start | bytes 1572872 | tf_op jit(solution)/shard_map/ppermute | solution.py:21
  55.4 24.7 %collective-permute-start.1 = (bf16[512,1024]{1,0:T(8,128)(2,1)}, bf16[512,1024]{1,0:T(8,128)(2,1)S(1)}, u32[]{:S(2)}, u32[]{:S(2)}) collective-permute-start(bf16[512,1024]{1,0:T(8,128)(2,1)} %collective-permute-done.refs_0_), channel_id=1, source_target_pairs={{0,1},{1,0},{2,3},{3,2},{4,5},{5,4},{6,7},{7,6},{8,9},{9,8},{10,11... | collective-permute-start | bytes 3145736 | tf_op jit(solution)/shard_map/ppermute | solution.py:21
  55.5 1.2 copy-start.1
  77.3 2.9 %copy-start.6 = (bf16[2,256,1024]{2,1,0:T(8,128)(2,1)}, bf16[2,256,1024]{2,1,0:T(8,128)(2,1)S(1)}, u32[]{:S(2)}) copy-start(bf16[2,256,1024]{2,1,0:T(8,128)(2,1)S(1)} %get-tuple-element.32.refs_1_) | copy-start | bytes 3145732
  89.7 1.3 copy-start.4
  98.0 1.0 copy-start.8
  99.0 10.9 %all-to-all-start = ((f32[8,2,1024]{2,1,0:T(2,128)}), f32[8,2,1024]{2,1,0:T(2,128)S(1)}, u32[]{:S(2)}, u32[]{:S(2)}) async-start(f32[8,2,1024]{2,1,0:T(2,128)} %get-tuple-element.39), calls=%async_computation | async-start | bytes 131072 | tf_op jit(solution)/shard_map/all_to_all | solution.py:694
  102.9 33.4 %collective-permute-start.14 = (bf16[512,1024]{1,0:T(8,128)(2,1)S(1)}, bf16[512,1024]{1,0:T(8,128)(2,1)}, u32[]{:S(2)}, u32[]{:S(2)}) collective-permute-start(bf16[512,1024]{1,0:T(8,128)(2,1)S(1)} %collective-permute-done.8.refs_6_), channel_id=1, source_target_pairs={{0,4},{4,0},{8,12},{12,8},{16,20},{20,16},{24,28},{28,24},{1,5},{5... | collective-permute-start | bytes 3145736 | tf_op jit(solution)/shard_map/ppermute | solution.py:21
  109.9 1.6 copy-start.5
  111.5 1.2 copy-start.7
  112.7 1.2 copy-start.9
  131.1 3.0 %copy-start.12 = (bf16[256,1024]{1,0:T(8,128)(2,1)S(1)}, bf16[256,1024]{1,0:T(8,128)(2,1)}, u32[]{:S(2)}) copy-start(bf16[256,1024]{1,0:T(8,128)(2,1)} %get-tuple-element.48) | copy-start | bytes 1572868
  131.1 4.1 %copy-start.13 = (bf16[128,1024]{1,0:T(8,128)(2,1)S(1)}, bf16[128,1024]{1,0:T(8,128)(2,1)}, u32[]{:S(2)}) copy-start(bf16[128,1024]{1,0:T(8,128)(2,1)} %slice.18) | copy-start | bytes 786436
  131.1 5.2 %copy-start.11 = (bf16[256,1024]{1,0:T(8,128)(2,1)S(1)}, bf16[256,1024]{1,0:T(8,128)(2,1)}, u32[]{:S(2)}) copy-start(bf16[256,1024]{1,0:T(8,128)(2,1)} %get-tuple-element.50) | copy-start | bytes 1572868
  131.1 36.7 %collective-permute-start.22 = (bf16[512,1024]{1,0:T(8,128)(2,1)S(1)}, bf16[512,1024]{1,0:T(8,128)(2,1)S(1)}, u32[]{:S(2)}, u32[]{:S(2)}) collective-permute-start(bf16[512,1024]{1,0:T(8,128)(2,1)S(1)} %shard_map.80.refs_0_), channel_id=1, source_target_pairs={{0,2},{1,3},{2,0},{3,1},{4,6},{5,7},{6,4},{7,5},{8,10},{9,11},{10,... | collective-permute-start | bytes 3145736 | tf_op jit(solution)/shard_map/ppermute | solution.py:21
  133.5 34.3 %copy-start.10 = (bf16[384,1024]{1,0:T(8,128)(2,1)S(1)}, bf16[384,1024]{1,0:T(8,128)(2,1)}, u32[]{:S(2)}) copy-start(bf16[384,1024]{1,0:T(8,128)(2,1)} %slice.19) | copy-start | bytes 2359300
  133.5 32.8 %collective-permute-start.11 = (bf16[256,1024]{1,0:T(8,128)(2,1)S(1)}, bf16[256,1024]{1,0:T(8,128)(2,1)S(1)}, u32[]{:S(2)}, u32[]{:S(2)}) collective-permute-start(bf16[256,1024]{1,0:T(8,128)(2,1)S(1)} %shard_map.79.refs_0_), channel_id=1, source_target_pairs={{0,2},{1,3},{2,0},{3,1},{4,6},{5,7},{6,4},{7,5},{8,10},{9,11},{10,... | collective-permute-start | bytes 1572872 | tf_op jit(solution)/shard_map/ppermute | solution.py:21
  134.1 33.7 %collective-permute-start.17 = (bf16[256,1024]{1,0:T(8,128)(2,1)S(1)}, bf16[256,1024]{1,0:T(8,128)(2,1)S(1)}, u32[]{:S(2)}, u32[]{:S(2)}) collective-permute-start(bf16[256,1024]{1,0:T(8,128)(2,1)S(1)} %copy-done.12), channel_id=1, source_target_pairs={{0,8},{4,12},{8,16},{12,20},{16,24},{20,28},{24,0},{28,4},{1,9},{5... | collective-permute-start | bytes 1572872 | tf_op jit(solution)/shard_map/ppermute | solution.py:633
  135.2 6.6 %collective-permute-start.15 = (bf16[128,1024]{1,0:T(8,128)(2,1)S(1)}, bf16[128,1024]{1,0:T(8,128)(2,1)S(1)}, u32[]{:S(2)}, u32[]{:S(2)}) collective-permute-start(bf16[128,1024]{1,0:T(8,128)(2,1)S(1)} %copy-done.13), channel_id=1, source_target_pairs={{0,4},{4,0},{8,12},{12,8},{16,20},{20,16},{24,28},{28,24},{1,5},{5... | collective-permute-start | bytes 786440 | tf_op jit(solution)/shard_map/ppermute | solution.py:21
  136.3 32.9 %collective-permute-start.18 = (bf16[256,1024]{1,0:T(8,128)(2,1)S(1)}, bf16[256,1024]{1,0:T(8,128)(2,1)S(1)}, u32[]{:S(2)}, u32[]{:S(2)}) collective-permute-start(bf16[256,1024]{1,0:T(8,128)(2,1)S(1)} %copy-done.11), channel_id=1, source_target_pairs={{0,8},{4,12},{8,16},{12,20},{16,24},{20,28},{24,0},{28,4},{1,9},{5... | collective-permute-start | bytes 1572872 | tf_op jit(solution)/shard_map/ppermute | solution.py:633
  141.8 47.8 %collective-permute-start.21 = (bf16[512,1024]{1,0:T(8,128)(2,1)S(1)}, bf16[512,1024]{1,0:T(8,128)(2,1)S(1)}, u32[]{:S(2)}, u32[]{:S(2)}) collective-permute-start(bf16[512,1024]{1,0:T(8,128)(2,1)S(1)} %shard_map.80.refs_0_), channel_id=1, source_target_pairs={{0,1},{1,0},{2,3},{3,2},{4,5},{5,4},{6,7},{7,6},{8,9},{9,8},{10,11... | collective-permute-start | bytes 3145736 | tf_op jit(solution)/shard_map/ppermute | solution.py:21
  166.3 11.8 %collective-permute-start.25 = (bf16[256,1024]{1,0:T(8,128)(2,1)S(1)}, bf16[256,1024]{1,0:T(8,128)(2,1)S(1)}, u32[]{:S(2)}, u32[]{:S(2)}) collective-permute-start(bf16[256,1024]{1,0:T(8,128)(2,1)S(1)} %shard_map.81.refs_0_.refs_4_), channel_id=1, source_target_pairs={{0,2},{1,3},{2,0},{3,1},{4,6},{5,7},{6,4},{7,5},{8,10},{9,11},{10,... | collective-permute-start | bytes 1572872 | tf_op jit(solution)/shard_map/ppermute | solution.py:21
  167.8 26.0 %collective-permute-start.23 = (bf16[512,1024]{1,0:T(8,128)(2,1)S(1)}, bf16[512,1024]{1,0:T(8,128)(2,1)S(1)}, u32[]{:S(2)}, u32[]{:S(2)}) collective-permute-start(bf16[512,1024]{1,0:T(8,128)(2,1)S(1)} %collective-permute-done.22.refs_2_), channel_id=1, source_target_pairs={{0,1},{1,0},{2,3},{3,2},{4,5},{5,4},{6,7},{7,6},{8,9},{9,8},{10,11... | collective-permute-start | bytes 3145736 | tf_op jit(solution)/shard_map/ppermute | solution.py:21
  167.8 20.5 %collective-permute-start.16 = (bf16[384,1024]{1,0:T(8,128)(2,1)S(1)}, bf16[384,1024]{1,0:T(8,128)(2,1)S(1)}, u32[]{:S(2)}, u32[]{:S(2)}) collective-permute-start(bf16[384,1024]{1,0:T(8,128)(2,1)S(1)} %copy-done.10), channel_id=1, source_target_pairs={{0,4},{4,0},{8,12},{12,8},{16,20},{20,16},{24,28},{28,24},{1,5},{5... | collective-permute-start | bytes 2359304 | tf_op jit(solution)/shard_map/ppermute | solution.py:21
  169.2 9.0 %collective-permute-start.24 = (bf16[256,1024]{1,0:T(8,128)(2,1)S(1)}, bf16[256,1024]{1,0:T(8,128)(2,1)S(1)}, u32[]{:S(2)}, u32[]{:S(2)}) collective-permute-start(bf16[256,1024]{1,0:T(8,128)(2,1)S(1)} %shard_map.81.refs_0_.refs_4_), channel_id=1, source_target_pairs={{0,1},{1,0},{2,3},{3,2},{4,5},{5,4},{6,7},{7,6},{8,9},{9,8},{10,11... | collective-permute-start | bytes 1572872 | tf_op jit(solution)/shard_map/ppermute | solution.py:21
  178.1 11.5 %collective-permute-start.26 = (bf16[256,1024]{1,0:T(8,128)(2,1)S(1)}, bf16[256,1024]{1,0:T(8,128)(2,1)S(1)}, u32[]{:S(2)}, u32[]{:S(2)}) collective-permute-start(bf16[256,1024]{1,0:T(8,128)(2,1)S(1)} %collective-permute-done.25.refs_2_.refs_6_), channel_id=1, source_target_pairs={{0,1},{1,0},{2,3},{3,2},{4,5},{5,4},{6,7},{7,6},{8,9},{9,8},{10,11... | collective-permute-start | bytes 1572872 | tf_op jit(solution)/shard_map/ppermute | solution.py:21
  178.1 21.4 %collective-permute-start.19 = (bf16[256,1024]{1,0:T(8,128)(2,1)S(1)}, bf16[256,1024]{1,0:T(8,128)(2,1)S(1)}, u32[]{:S(2)}, u32[]{:S(2)}) collective-permute-start(bf16[256,1024]{1,0:T(8,128)(2,1)S(1)} %collective-permute-done.17.refs_8_.refs_11_), channel_id=1, source_target_pairs={{0,4},{4,0},{8,12},{12,8},{16,20},{20,16},{24,28},{28,24},{1,5},{5... | collective-permute-start | bytes 1572872 | tf_op jit(solution)/shard_map/ppermute | solution.py:21
  188.3 21.9 %collective-permute-start.20 = (bf16[256,1024]{1,0:T(8,128)(2,1)S(1)}, bf16[256,1024]{1,0:T(8,128)(2,1)S(1)}, u32[]{:S(2)}, u32[]{:S(2)}) collective-permute-start(bf16[256,1024]{1,0:T(8,128)(2,1)S(1)} %collective-permute-done.18.refs_9_.refs_12_), channel_id=1, source_target_pairs={{0,4},{4,0},{8,12},{12,8},{16,20},{20,16},{24,28},{28,24},{1,5},{5... | collective-permute-start | bytes 1572872 | tf_op jit(solution)/shard_map/ppermute | solution.py:21
  189.6 26.0 %collective-permute-start.10 = (bf16[256,1024]{1,0:T(8,128)(2,1)S(1)}, bf16[256,1024]{1,0:T(8,128)(2,1)S(1)}, u32[]{:S(2)}, u32[]{:S(2)}) collective-permute-start(bf16[256,1024]{1,0:T(8,128)(2,1)S(1)} %shard_map.79.refs_0_), channel_id=1, source_target_pairs={{0,1},{1,0},{2,3},{3,2},{4,5},{5,4},{6,7},{7,6},{8,9},{9,8},{10,11... | collective-permute-start | bytes 1572872 | tf_op jit(solution)/shard_map/ppermute | solution.py:21
  189.6 26.0 %collective-permute-start.12 = (bf16[256,1024]{1,0:T(8,128)(2,1)S(1)}, bf16[256,1024]{1,0:T(8,128)(2,1)S(1)}, u32[]{:S(2)}, u32[]{:S(2)}) collective-permute-start(bf16[256,1024]{1,0:T(8,128)(2,1)S(1)} %collective-permute-done.11.refs_2_), channel_id=1, source_target_pairs={{0,1},{1,0},{2,3},{3,2},{4,5},{5,4},{6,7},{7,6},{8,9},{9,8},{10,11... | collective-permute-start | bytes 1572872 | tf_op jit(solution)/shard_map/ppermute | solution.py:21

commit v8 on v7

--- a/solution.py
+++ b/solution.py
@@ -656,15 +656,13 @@
     gain = recur_gain[None, :]
     start = start_state[None, :]
 
-    (head,) = split_rows(tokens, 0, sizes[:1], False)
-    *others, tail = split_rows(tokens, sizes[0], sizes[1:], True)
+    *ordered, whole = split_rows(tokens, 0, sizes, True)
     far = []
-    for piece in [head, *others]:
+    for piece in ordered:
         far.append([swap(piece, "ch", half)])
-    near = [[head, tail]]
+    near = [[whole]]
     for d in range(1, half):
-        near.append([swap(head, "ch", d)])
-        near[d].append(swap(tail, "ch", d))
+        near.append([swap(whole, "ch", d)])
     for c in range(chunks):
         for d in range(1, half):
             far[c].append(swap(far[c][0], "ch", d))

time: 222 us -> 224 us (level)
    ppermute x2, waiting for transfers between devices: 5.84 us -> 22.3 us  [gather_early(): held[step, 0] = [lax.ppermute(held[step - 1, 0][0], 'ctx', route)]]
    ppermute x23 -> x22, waiting for transfers between devices: 91 us -> 76.7 us  [swap(): lax.ppermute(block, axis, [(i, i ^ bits) for i in range(lax.axis_size(axi...]
    pallas_call x2 -> x1, Pallas kernels: 5.46 us -> 4.09 us  [split_rows(): pl.pallas_call(functools.partial(split_kernel, first, tuple(sizes), joine...]
    ppermute x23 -> x22, starting transfers between devices: 18 us -> 17.9 us  [swap(): lax.ppermute(block, axis, [(i, i ^ bits) for i in range(lax.axis_size(axi...]
  transfers between devices with their start and end apart: 28 -> 27, of which waited for: 10 -> 10; matrix products, arithmetic and copies ran while one was open for 1% -> 1% of each run, Pallas kernels for 30% -> 27%
where the time goes in v8:
time: 224 us
  waiting for transfers between devices  104 us (46%)
  Pallas kernels  70.5 us (31%)
  starting transfers between devices  27.9 us (12%)
  local copies, waits for them, and re-layouts  11.7 us (5%)
  blocking collectives  9.29 us (4%)
    ppermute x22, waiting for transfers between devices, swap(): lax.ppermute(block, axis, [(i, i ^ bits) for i in range(lax.axis_size(axi...  76.7 us
    pallas_call x3, Pallas kernels, gate_chunk(): pl.pallas_call(functools.partial(gate_kernel, half, first_row, rows, len(...  22.7 us
    ppermute x2, waiting for transfers between devices, gather_early(): held[step, 0] = [lax.ppermute(held[step - 1, 0][0], 'ctx', route)]  22.3 us
    pallas_call x4, Pallas kernels, mix_rows(): pl.pallas_call(functools.partial(mix_kernel, groups, group, cuts, peers,...  20.1 us
    ppermute x22, starting transfers between devices, swap(): lax.ppermute(block, axis, [(i, i ^ bits) for i in range(lax.axis_size(axi...  17.9 us
    pallas_call x1, Pallas kernels, near_product(): pl.pallas_call(functools.partial(near_kernel, half, tiles, heights), out_...  14.1 us
    all_to_all x1, blocking collectives, layer(): peer_maps = lax.all_to_all(totals, 'ctx', 0, 0, tiled=True)  9.29 us
    unnamed x32, local copies, waits for them, and re-layouts  8.94 us
  transfers between devices with their start and end apart: 27, of which 10 were waited for; matrix products, arithmetic and copies ran while one was open for 1% of the time, Pallas kernels for 27%

profile of v8, /device:TPU:0, one launch (start us, length us, event | category | flops | bytes accessed | tf_op | source)
XLA Modules:
  0.0 223.7 jit_solution(172683233539499437)
XLA Ops:
  0.0 4.1 %shard_map.73 = (bf16[512,1024]{1,0:T(8,128)(2,1)}, bf16[256,1024]{1,0:T(8,128)(2,1)}, bf16[256,1024]{1,0:T(8,128)(2,1)}, bf16[1024,1024]{1,0:T(8,128)(2,1)}) custom-call(bf16[1024,1024]{1,0:T(8,128)(2,1)} %src.1), custom_call_target="tpu_custom_call" | custom-call | flops 536870912 | bytes 4194304 | tf_op jit(solution)/shard_map/pallas_call | solution.py:143
  4.7 2.6 %collective-permute-start.7 = (bf16[512,1024]{1,0:T(8,128)(2,1)S(1)}, bf16[512,1024]{1,0:T(8,128)(2,1)S(1)}, u32[]{:S(2)}, u32[]{:S(2)}) collective-permute-start(bf16[512,1024]{1,0:T(8,128)(2,1)S(1)} %copy-done), channel_id=1, source_target_pairs={{0,8},{4,12},{8,16},{12,20},{16,24},{20,28},{24,0},{28,4},{1,9},{5... | collective-permute-start | bytes 3145736 | tf_op jit(solution)/shard_map/ppermute | solution.py:611
  7.3 1.5 collective-permute-start
  9.3 1.5 collective-permute-start.5
  10.8 22.3 %collective-permute-done.7.refs_6_ = bf16[512,1024]{1,0:T(8,128)(2,1)S(1)} collective-permute-done((bf16[512,1024]{1,0:T(8,128)(2,1)S(1)}, bf16[512,1024]{1,0:T(8,128)(2,1)S(1)}, u32[]{:S(2)}, u32[]{:S(2)}) %collective-permute-start.7) | collective-permute-done | bytes 1048608 | tf_op jit(solution)/shard_map/ppermute | solution.py:611
  33.2 11.7 %collective-permute-done.3.refs_0_ = bf16[256,1024]{1,0:T(8,128)(2,1)} collective-permute-done((bf16[256,1024]{1,0:T(8,128)(2,1)}, bf16[256,1024]{1,0:T(8,128)(2,1)}, u32[]{:S(2)}, u32[]{:S(2)}) %collective-permute-start.3) | collective-permute-done | bytes 524320 | tf_op jit(solution)/shard_map/ppermute | solution.py:21
  44.9 1.5 collective-permute-start.12
  46.4 8.9 %collective-permute-done.5.refs_0_ = bf16[256,1024]{1,0:T(8,128)(2,1)} collective-permute-done((bf16[256,1024]{1,0:T(8,128)(2,1)}, bf16[256,1024]{1,0:T(8,128)(2,1)}, u32[]{:S(2)}, u32[]{:S(2)}) %collective-permute-start.5) | collective-permute-done | bytes 524320 | tf_op jit(solution)/shard_map/ppermute | solution.py:21
  55.9 1.6 copy-done.3
  57.5 14.1 %shard_map.74.refs_2_ = f32[2,1024,1024]{2,1,0:T(8,128)S(1)} custom-call(s32[2]{0:T(128)S(1)} %pad_add_fusion.place, bf16[1024,1024]{1,0:T(8,128)(2,1)S(1)} %copy-done.3, bf16[1024,1024]{1,0:T(8,128)(2,1)} %collective-permute-done.2.refs_1_, bf16[2,4096,1024]{2,1,0:T(8,128)(2,1)} %refs_3_.5), custom_call_target="tpu_custom_call" | custom-call | flops 8589934592 | bytes 20971520 | tf_op jit(solution)/shard_map/pallas_call | solution.py:87
  71.7 0.7 slice.18
  72.4 1.0 slice.19
  73.3 1.0 fusion
  74.4 6.3 %shard_map.76 = (bf16[2,256,1024]{2,1,0:T(8,128)(2,1)S(1)}, f32[2,8,1024]{2,1,0:T(8,128)S(1)}) custom-call(s32[2]{0:T(128)S(1)} %pad_add_fusion.place, bf16[256,1024]{1,0:T(8,128)(2,1)} %collective-permute-done.3.refs_0_, bf16[256,1024]{1,0:T(8,128)(2,1)S(1)} %collective-permute-done.4.refs_1_, f32[2,1024,1024]{2,1,0:T(8,128)S(1)} %shard_map.74.refs_2_, ...), custom_call_target="tpu_custom_call" | custom-call | flops 2147483648 | bytes 12582912 | tf_op jit(solution)/shard_map/pallas_call | solution.py:290
  80.7 1.0 copy-done.6
  81.7 9.5 %shard_map.75 = (bf16[2,512,1024]{2,1,0:T(8,128)(2,1)S(1)}, f32[2,16,1024]{2,1,0:T(8,128)S(1)}) custom-call(s32[2]{0:T(128)S(1)} %pad_add_fusion.place, bf16[512,1024]{1,0:T(8,128)(2,1)} %collective-permute-done.refs_0_, bf16[512,1024]{1,0:T(8,128)(2,1)S(1)} %collective-permute-done.1.refs_1_, f32[2,1024,1024]{2,1,0:T(8,128)S(1)} %shard_map.74.refs_2_, ...), custom_call_target="tpu_custom_call" | custom-call | flops 4294967296 | bytes 16777216 | tf_op jit(solution)/shard_map/pallas_call | solution.py:290
  91.2 1.3 copy-done.4
  92.5 7.0 %shard_map.77 = (bf16[2,256,1024]{2,1,0:T(8,128)(2,1)S(1)}, f32[2,8,1024]{2,1,0:T(8,128)S(1)}, f32[8,2,1024]{2,1,0:T(2,128)}) custom-call(s32[2]{0:T(128)S(1)} %pad_add_fusion.place, bf16[256,1024]{1,0:T(8,128)(2,1)} %collective-permute-done.5.refs_0_, bf16[256,1024]{1,0:T(8,128)(2,1)S(1)} %collective-permute-done.6.refs_1_, ...), custom_call_target="tpu_custom_call" | custom-call | flops 2147483648 | bytes 12582912 | tf_op jit(solution)/shard_map/pallas_call | solution.py:290
  99.5 1.0 copy-done.8
  100.4 4.8 %all-to-all-start = ((f32[8,2,1024]{2,1,0:T(2,128)}), f32[8,2,1024]{2,1,0:T(2,128)S(1)}, u32[]{:S(2)}, u32[]{:S(2)}) async-start(f32[8,2,1024]{2,1,0:T(2,128)} %get-tuple-element.41), calls=%async_computation | async-start | bytes 131072 | tf_op jit(solution)/shard_map/all_to_all | solution.py:692
  105.3 2.0 collective-permute-start.13
  107.3 5.0 %all-to-all-done.refs_6_ = f32[8,2,1024]{2,1,0:T(2,128)S(1)} async-done(((f32[8,2,1024]{2,1,0:T(2,128)}), f32[8,2,1024]{2,1,0:T(2,128)S(1)}, u32[]{:S(2)}, u32[]{:S(2)}) %all-to-all-start) | async-done | bytes 65568 | tf_op jit(solution)/shard_map/all_to_all | solution.py:692
  112.3 1.6 copy-done.5
  113.9 1.2 copy-done.7
  115.1 1.2 copy-done.9
  116.3 6.9 %bend.1 = (f32[2,1024,1024]{2,1,0:T(8,128)S(1)}, f32[2,32,1024]{2,1,0:T(8,128)S(1)}, f32[8,2,1024]{2,1,0:T(2,128)S(1)}) custom-call(s32[2]{0:T(128)S(1)} %pad_add_fusion.place, bf16[2,512,1024]{2,1,0:T(8,128)(2,1)S(1)} %copy-done.5, bf16[2,256,1024]{2,1,0:T(8,128)(2,1)S(1)} %copy-done.7, bf16[2,256,1024]{2,1,0:T(8,128)(2,1)S(1)} %copy-done.9, ...), custom_call_target="tpu_custom_call" | custom-call | flops 41943040 | bytes 12582912 | tf_op jit(solution)/shard_map/bend/pallas_call | solution.py:396
  123.2 9.3 %all_to_all.10.peer_ref = f32[8,2,1024]{2,1,0:T(2,128)S(1)} all-to-all(f32[8,2,1024]{2,1,0:T(2,128)S(1)} %get-tuple-element.44), channel_id=1, replica_groups=mesh['ctx'=8,'ch'=4] {'ctx'}, dimensions={0} | all-to-all | bytes 131072 | tf_op jit(solution)/shard_map/all_to_all | solution.py:694
  132.5 1.0 shard_map.79.refs_0_
  133.5 1.6 collective-permute-start.21
  135.0 0.8 shard_map.78.refs_0_
  135.9 0.6 collective-permute-start.10
  136.5 1.1 collective-permute-start.16
  137.6 1.1 collective-permute-start.14
  138.7 1.4 collective-permute-start.17
  140.1 0.8 shard_map.80.refs_0_.refs_4_
  140.9 3.3 %collective-permute-done.14.refs_9_ = bf16[128,1024]{1,0:T(8,128)(2,1)S(1)} collective-permute-done((bf16[128,1024]{1,0:T(8,128)(2,1)S(1)}, bf16[128,1024]{1,0:T(8,128)(2,1)S(1)}, u32[]{:S(2)}, u32[]{:S(2)}) %collective-permute-start.14) | collective-permute-done | bytes 262176 | tf_op jit(solution)/shard_map/ppermute | solution.py:21
  144.1 24.5 %collective-permute-done.10.refs_2_ = bf16[256,1024]{1,0:T(8,128)(2,1)S(1)} collective-permute-done((bf16[256,1024]{1,0:T(8,128)(2,1)S(1)}, bf16[256,1024]{1,0:T(8,128)(2,1)S(1)}, u32[]{:S(2)}, u32[]{:S(2)}) %collective-permute-start.10) | collective-permute-done | bytes 524320 | tf_op jit(solution)/shard_map/ppermute | solution.py:21
  168.7 1.5 collective-permute-start.24
  170.2 1.3 collective-permute-start.15
  171.7 8.8 %collective-permute-done.24.refs_2_.refs_6_ = bf16[256,1024]{1,0:T(8,128)(2,1)S(1)} collective-permute-done((bf16[256,1024]{1,0:T(8,128)(2,1)S(1)}, bf16[256,1024]{1,0:T(8,128)(2,1)S(1)}, u32[]{:S(2)}, u32[]{:S(2)}) %collective-permute-start.24) | collective-permute-done | bytes 524320 | tf_op jit(solution)/shard_map/ppermute | solution.py:21
  180.5 1.7 collective-permute-start.18
  182.1 8.5 %collective-permute-done.15.refs_10_ = bf16[384,1024]{1,0:T(8,128)(2,1)S(1)} collective-permute-done((bf16[384,1024]{1,0:T(8,128)(2,1)S(1)}, bf16[384,1024]{1,0:T(8,128)(2,1)S(1)}, u32[]{:S(2)}, u32[]{:S(2)}) %collective-permute-start.15) | collective-permute-done | bytes 786464 | tf_op jit(solution)/shard_map/ppermute | solution.py:21
  190.7 1.3 collective-permute-start.19
  192.5 3.7 %shard_map.82.refs_13_ = f32[256,1024]{1,0:T(8,128)S(1)} custom-call(s32[2]{0:T(128)S(1)} %pad_add_fusion.place, bf16[256,1024]{1,0:T(8,128)(2,1)S(1)} %shard_map.80.refs_0_.refs_4_, bf16[256,1024]{1,0:T(8,128)(2,1)S(1)} %collective-permute-done.23.refs_1_.refs_5_, bf16[256,1024]{1,0:T(8,128)(2,1)S(1)} %collective-permute-done.24.refs_2_.refs_6_, ...), custom_call_target="tpu_custom_call" | custom-call | flops 1610612736 | bytes 8912896 | tf_op jit(solution)/shard_map/pallas_call | solution.py:550
  196.2 5.5 %shard_map.81.refs_12_ = f32[512,1024]{1,0:T(8,128)S(1)} custom-call(s32[2]{0:T(128)S(1)} %pad_add_fusion.place, bf16[512,1024]{1,0:T(8,128)(2,1)S(1)} %shard_map.79.refs_0_, bf16[512,1024]{1,0:T(8,128)(2,1)S(1)} %collective-permute-done.20.refs_1_, bf16[512,1024]{1,0:T(8,128)(2,1)S(1)} %collective-permute-done.21.refs_2_, ...), custom_call_target="tpu_custom_call" | custom-call | flops 3221225472 | bytes 11534336 | tf_op jit(solution)/shard_map/pallas_call | solution.py:550
  201.9 10.7 %collective-permute-done.19.refs_11_.refs_14_ = bf16[256,1024]{1,0:T(8,128)(2,1)S(1)} collective-permute-done((bf16[256,1024]{1,0:T(8,128)(2,1)S(1)}, bf16[256,1024]{1,0:T(8,128)(2,1)S(1)}, u32[]{:S(2)}, u32[]{:S(2)}) %collective-permute-start.19) | collective-permute-done | bytes 524320 | tf_op jit(solution)/shard_map/ppermute | solution.py:21
  212.6 5.5 %shard_map.83.refs_15_ = bf16[1024,1024]{1,0:T(8,128)(2,1)} custom-call(s32[2]{0:T(128)S(1)} %pad_add_fusion.place, bf16[512,1024]{1,0:T(8,128)(2,1)S(1)} %shard_map.79.refs_0_, bf16[512,1024]{1,0:T(8,128)(2,1)S(1)} %collective-permute-done.20.refs_1_, bf16[512,1024]{1,0:T(8,128)(2,1)S(1)} %collective-permute-done.21.refs_2_, ...), custom_call_target="tpu_custom_call" | custom-call | flops 1610612736 | bytes 6815744 | tf_op jit(solution)/shard_map/pallas_call | solution.py:550
  218.1 5.4 %shard_map.84 = bf16[1024,1024]{1,0:T(8,128)(2,1)} custom-call(s32[2]{0:T(128)S(1)} %pad_add_fusion.place, bf16[256,1024]{1,0:T(8,128)(2,1)S(1)} %shard_map.78.refs_0_, bf16[256,1024]{1,0:T(8,128)(2,1)S(1)} %collective-permute-done.9.refs_1_, bf16[256,1024]{1,0:T(8,128)(2,1)S(1)} %collective-permute-done.10.refs_2_, ...), custom_call_target="tpu_custom_call", output_to_operand_aliasing={{}: (16, {})} | custom-call | flops 2147483648 | bytes 11534336 | tf_op jit(solution)/shard_map/pallas_call | solution.py:550
  (57 shorter events, 2.7 us)
Async XLA Ops:
  0.0 4.7 %copy-start = (bf16[512,1024]{1,0:T(8,128)(2,1)S(1)}, bf16[512,1024]{1,0:T(8,128)(2,1)}, u32[]{:S(2)}) copy-start(bf16[512,1024]{1,0:T(8,128)(2,1)} %refs_4_.5) | copy-start | bytes 3145732
  0.0 33.2 %copy-start.14 = (f32[1024]{0:T(1024)S(1)}, f32[1024]{0:T(1024)}, u32[]{:S(2)}) copy-start(f32[1024]{0:T(1024)} %param.11) | copy-start | bytes 12292
  0.0 33.2 %copy-start.15 = (f32[1024]{0:T(1024)S(1)}, f32[1024]{0:T(1024)}, u32[]{:S(2)}) copy-start(f32[1024]{0:T(1024)} %param.10) | copy-start | bytes 12292
  4.1 51.7 %collective-permute-start.2 = (bf16[1024,1024]{1,0:T(8,128)(2,1)}, bf16[1024,1024]{1,0:T(8,128)(2,1)}, u32[]{:S(2)}, u32[]{:S(2)}) collective-permute-start(bf16[1024,1024]{1,0:T(8,128)(2,1)} %get-tuple-element.31.refs_0_), channel_id=1, source_target_pairs={{0,1},{1,0},{2,3},{3,2},{4,5},{5,4},{6,7},{7,6},{8,9},{9,8},{10,11... | collective-permute-start | bytes 6291464 | tf_op jit(solution)/shard_map/ppermute | solution.py:21
  4.7 28.4 %collective-permute-start.7 = (bf16[512,1024]{1,0:T(8,128)(2,1)S(1)}, bf16[512,1024]{1,0:T(8,128)(2,1)S(1)}, u32[]{:S(2)}, u32[]{:S(2)}) collective-permute-start(bf16[512,1024]{1,0:T(8,128)(2,1)S(1)} %copy-done), channel_id=1, source_target_pairs={{0,8},{4,12},{8,16},{12,20},{16,24},{20,28},{24,0},{28,4},{1,9},{5... | collective-permute-start | bytes 3145736 | tf_op jit(solution)/shard_map/ppermute | solution.py:611
  7.3 48.0 %collective-permute-start = (bf16[512,1024]{1,0:T(8,128)(2,1)}, bf16[512,1024]{1,0:T(8,128)(2,1)}, u32[]{:S(2)}, u32[]{:S(2)}) collective-permute-start(bf16[512,1024]{1,0:T(8,128)(2,1)} %get-tuple-element.30), channel_id=1, source_target_pairs={{0,2},{1,3},{2,0},{3,1},{4,6},{5,7},{6,4},{7,5},{8,10},{9,11},{10,... | collective-permute-start | bytes 3145736 | tf_op jit(solution)/shard_map/ppermute | solution.py:21
  8.8 36.1 %collective-permute-start.3 = (bf16[256,1024]{1,0:T(8,128)(2,1)}, bf16[256,1024]{1,0:T(8,128)(2,1)}, u32[]{:S(2)}, u32[]{:S(2)}) collective-permute-start(bf16[256,1024]{1,0:T(8,128)(2,1)} %get-tuple-element.33), channel_id=1, source_target_pairs={{0,2},{1,3},{2,0},{3,1},{4,6},{5,7},{6,4},{7,5},{8,10},{9,11},{10,... | collective-permute-start | bytes 1572872 | tf_op jit(solution)/shard_map/ppermute | solution.py:21
  9.3 46.0 %collective-permute-start.5 = (bf16[256,1024]{1,0:T(8,128)(2,1)}, bf16[256,1024]{1,0:T(8,128)(2,1)}, u32[]{:S(2)}, u32[]{:S(2)}) collective-permute-start(bf16[256,1024]{1,0:T(8,128)(2,1)} %get-tuple-element.35), channel_id=1, source_target_pairs={{0,2},{1,3},{2,0},{3,1},{4,6},{5,7},{6,4},{7,5},{8,10},{9,11},{10,... | collective-permute-start | bytes 1572872 | tf_op jit(solution)/shard_map/ppermute | solution.py:21
  33.1 38.6 %collective-permute-start.8 = (bf16[512,1024]{1,0:T(8,128)(2,1)S(1)}, bf16[512,1024]{1,0:T(8,128)(2,1)S(1)}, u32[]{:S(2)}, u32[]{:S(2)}) collective-permute-start(bf16[512,1024]{1,0:T(8,128)(2,1)S(1)} %collective-permute-done.7.refs_6_), channel_id=1, source_target_pairs={{0,8},{4,12},{8,16},{12,20},{16,24},{20,28},{24,0},{28,4},{1,9},{5... | collective-permute-start | bytes 3145736 | tf_op jit(solution)/shard_map/ppermute | solution.py:611
  44.9 92.7 %collective-permute-start.12 = (bf16[512,1024]{1,0:T(8,128)(2,1)S(1)}, bf16[512,1024]{1,0:T(8,128)(2,1)}, u32[]{:S(2)}, u32[]{:S(2)}) collective-permute-start(bf16[512,1024]{1,0:T(8,128)(2,1)S(1)} %copy-done), channel_id=1, source_target_pairs={{0,4},{4,0},{8,12},{12,8},{16,20},{20,16},{24,28},{28,24},{1,5},{5... | collective-permute-start | bytes 3145736 | tf_op jit(solution)/shard_map/ppermute | solution.py:21
  55.3 19.1 %collective-permute-start.4 = (bf16[256,1024]{1,0:T(8,128)(2,1)}, bf16[256,1024]{1,0:T(8,128)(2,1)S(1)}, u32[]{:S(2)}, u32[]{:S(2)}) collective-permute-start(bf16[256,1024]{1,0:T(8,128)(2,1)} %collective-permute-done.3.refs_0_), channel_id=1, source_target_pairs={{0,1},{1,0},{2,3},{3,2},{4,5},{5,4},{6,7},{7,6},{8,9},{9,8},{10,11... | collective-permute-start | bytes 1572872 | tf_op jit(solution)/shard_map/ppermute | solution.py:21
  55.3 37.2 %collective-permute-start.6 = (bf16[256,1024]{1,0:T(8,128)(2,1)}, bf16[256,1024]{1,0:T(8,128)(2,1)S(1)}, u32[]{:S(2)}, u32[]{:S(2)}) collective-permute-start(bf16[256,1024]{1,0:T(8,128)(2,1)} %collective-permute-done.5.refs_0_), channel_id=1, source_target_pairs={{0,1},{1,0},{2,3},{3,2},{4,5},{5,4},{6,7},{7,6},{8,9},{9,8},{10,11... | collective-permute-start | bytes 1572872 | tf_op jit(solution)/shard_map/ppermute | solution.py:21
  55.8 25.9 %collective-permute-start.1 = (bf16[512,1024]{1,0:T(8,128)(2,1)}, bf16[512,1024]{1,0:T(8,128)(2,1)S(1)}, u32[]{:S(2)}, u32[]{:S(2)}) collective-permute-start(bf16[512,1024]{1,0:T(8,128)(2,1)} %collective-permute-done.refs_0_), channel_id=1, source_target_pairs={{0,1},{1,0},{2,3},{3,2},{4,5},{5,4},{6,7},{7,6},{8,9},{9,8},{10,11... | collective-permute-start | bytes 3145736 | tf_op jit(solution)/shard_map/ppermute | solution.py:21
  55.9 1.6 copy-start.3
  71.6 2.8 %copy-start.1 = (f32[1024]{0:T(1024)S(1)}, f32[1024]{0:T(1024)}, u32[]{:S(2)}) copy-start(f32[1024]{0:T(1024)} %param.13) | copy-start | bytes 12292
  71.6 2.8 %copy-start.2 = (f32[1024]{0:T(1024)S(1)}, f32[1024]{0:T(1024)}, u32[]{:S(2)}) copy-start(f32[1024]{0:T(1024)} %param.12) | copy-start | bytes 12292
  80.7 1.0 copy-start.6
  91.2 1.3 copy-start.4
  99.5 1.0 copy-start.8
  100.4 11.8 %all-to-all-start = ((f32[8,2,1024]{2,1,0:T(2,128)}), f32[8,2,1024]{2,1,0:T(2,128)S(1)}, u32[]{:S(2)}, u32[]{:S(2)}) async-start(f32[8,2,1024]{2,1,0:T(2,128)} %get-tuple-element.41), calls=%async_computation | async-start | bytes 131072 | tf_op jit(solution)/shard_map/all_to_all | solution.py:692
  105.3 33.4 %collective-permute-start.13 = (bf16[512,1024]{1,0:T(8,128)(2,1)S(1)}, bf16[512,1024]{1,0:T(8,128)(2,1)}, u32[]{:S(2)}, u32[]{:S(2)}) collective-permute-start(bf16[512,1024]{1,0:T(8,128)(2,1)S(1)} %collective-permute-done.7.refs_6_), channel_id=1, source_target_pairs={{0,4},{4,0},{8,12},{12,8},{16,20},{20,16},{24,28},{28,24},{1,5},{5... | collective-permute-start | bytes 3145736 | tf_op jit(solution)/shard_map/ppermute | solution.py:21
  112.3 1.6 copy-start.5
  113.9 1.2 copy-start.7
  115.1 1.2 copy-start.9
  133.4 3.0 %copy-start.12 = (bf16[256,1024]{1,0:T(8,128)(2,1)S(1)}, bf16[256,1024]{1,0:T(8,128)(2,1)}, u32[]{:S(2)}) copy-start(bf16[256,1024]{1,0:T(8,128)(2,1)} %get-tuple-element.50) | copy-start | bytes 1572868
  133.4 4.1 %copy-start.13 = (bf16[128,1024]{1,0:T(8,128)(2,1)S(1)}, bf16[128,1024]{1,0:T(8,128)(2,1)}, u32[]{:S(2)}) copy-start(bf16[128,1024]{1,0:T(8,128)(2,1)} %slice.18) | copy-start | bytes 786436
  133.5 5.2 %copy-start.11 = (bf16[256,1024]{1,0:T(8,128)(2,1)S(1)}, bf16[256,1024]{1,0:T(8,128)(2,1)}, u32[]{:S(2)}) copy-start(bf16[256,1024]{1,0:T(8,128)(2,1)} %get-tuple-element.52) | copy-start | bytes 1572868
  133.5 36.7 %collective-permute-start.21 = (bf16[512,1024]{1,0:T(8,128)(2,1)S(1)}, bf16[512,1024]{1,0:T(8,128)(2,1)S(1)}, u32[]{:S(2)}, u32[]{:S(2)}) collective-permute-start(bf16[512,1024]{1,0:T(8,128)(2,1)S(1)} %shard_map.79.refs_0_), channel_id=1, source_target_pairs={{0,2},{1,3},{2,0},{3,1},{4,6},{5,7},{6,4},{7,5},{8,10},{9,11},{10,... | collective-permute-start | bytes 3145736 | tf_op jit(solution)/shard_map/ppermute | solution.py:21
  135.8 34.3 %copy-start.10 = (bf16[384,1024]{1,0:T(8,128)(2,1)S(1)}, bf16[384,1024]{1,0:T(8,128)(2,1)}, u32[]{:S(2)}) copy-start(bf16[384,1024]{1,0:T(8,128)(2,1)} %slice.19) | copy-start | bytes 2359300
  135.9 32.8 %collective-permute-start.10 = (bf16[256,1024]{1,0:T(8,128)(2,1)S(1)}, bf16[256,1024]{1,0:T(8,128)(2,1)S(1)}, u32[]{:S(2)}, u32[]{:S(2)}) collective-permute-start(bf16[256,1024]{1,0:T(8,128)(2,1)S(1)} %shard_map.78.refs_0_), channel_id=1, source_target_pairs={{0,2},{1,3},{2,0},{3,1},{4,6},{5,7},{6,4},{7,5},{8,10},{9,11},{10,... | collective-permute-start | bytes 1572872 | tf_op jit(solution)/shard_map/ppermute | solution.py:21
  136.5 33.7 %collective-permute-start.16 = (bf16[256,1024]{1,0:T(8,128)(2,1)S(1)}, bf16[256,1024]{1,0:T(8,128)(2,1)S(1)}, u32[]{:S(2)}, u32[]{:S(2)}) collective-permute-start(bf16[256,1024]{1,0:T(8,128)(2,1)S(1)} %copy-done.12), channel_id=1, source_target_pairs={{0,8},{4,12},{8,16},{12,20},{16,24},{20,28},{24,0},{28,4},{1,9},{5... | collective-permute-start | bytes 1572872 | tf_op jit(solution)/shard_map/ppermute | solution.py:633
  137.6 6.6 %collective-permute-start.14 = (bf16[128,1024]{1,0:T(8,128)(2,1)S(1)}, bf16[128,1024]{1,0:T(8,128)(2,1)S(1)}, u32[]{:S(2)}, u32[]{:S(2)}) collective-permute-start(bf16[128,1024]{1,0:T(8,128)(2,1)S(1)} %copy-done.13), channel_id=1, source_target_pairs={{0,4},{4,0},{8,12},{12,8},{16,20},{20,16},{24,28},{28,24},{1,5},{5... | collective-permute-start | bytes 786440 | tf_op jit(solution)/shard_map/ppermute | solution.py:21
  138.7 32.9 %collective-permute-start.17 = (bf16[256,1024]{1,0:T(8,128)(2,1)S(1)}, bf16[256,1024]{1,0:T(8,128)(2,1)S(1)}, u32[]{:S(2)}, u32[]{:S(2)}) collective-permute-start(bf16[256,1024]{1,0:T(8,128)(2,1)S(1)} %copy-done.11), channel_id=1, source_target_pairs={{0,8},{4,12},{8,16},{12,20},{16,24},{20,28},{24,0},{28,4},{1,9},{5... | collective-permute-start | bytes 1572872 | tf_op jit(solution)/shard_map/ppermute | solution.py:633
  144.1 47.8 %collective-permute-start.20 = (bf16[512,1024]{1,0:T(8,128)(2,1)S(1)}, bf16[512,1024]{1,0:T(8,128)(2,1)S(1)}, u32[]{:S(2)}, u32[]{:S(2)}) collective-permute-start(bf16[512,1024]{1,0:T(8,128)(2,1)S(1)} %shard_map.79.refs_0_), channel_id=1, source_target_pairs={{0,1},{1,0},{2,3},{3,2},{4,5},{5,4},{6,7},{7,6},{8,9},{9,8},{10,11... | collective-permute-start | bytes 3145736 | tf_op jit(solution)/shard_map/ppermute | solution.py:21
  168.7 11.8 %collective-permute-start.24 = (bf16[256,1024]{1,0:T(8,128)(2,1)S(1)}, bf16[256,1024]{1,0:T(8,128)(2,1)S(1)}, u32[]{:S(2)}, u32[]{:S(2)}) collective-permute-start(bf16[256,1024]{1,0:T(8,128)(2,1)S(1)} %shard_map.80.refs_0_.refs_4_), channel_id=1, source_target_pairs={{0,2},{1,3},{2,0},{3,1},{4,6},{5,7},{6,4},{7,5},{8,10},{9,11},{10,... | collective-permute-start | bytes 1572872 | tf_op jit(solution)/shard_map/ppermute | solution.py:21
  170.2 26.0 %collective-permute-start.22 = (bf16[512,1024]{1,0:T(8,128)(2,1)S(1)}, bf16[512,1024]{1,0:T(8,128)(2,1)S(1)}, u32[]{:S(2)}, u32[]{:S(2)}) collective-permute-start(bf16[512,1024]{1,0:T(8,128)(2,1)S(1)} %collective-permute-done.21.refs_2_), channel_id=1, source_target_pairs={{0,1},{1,0},{2,3},{3,2},{4,5},{5,4},{6,7},{7,6},{8,9},{9,8},{10,11... | collective-permute-start | bytes 3145736 | tf_op jit(solution)/shard_map/ppermute | solution.py:21
  170.2 20.5 %collective-permute-start.15 = (bf16[384,1024]{1,0:T(8,128)(2,1)S(1)}, bf16[384,1024]{1,0:T(8,128)(2,1)S(1)}, u32[]{:S(2)}, u32[]{:S(2)}) collective-permute-start(bf16[384,1024]{1,0:T(8,128)(2,1)S(1)} %copy-done.10), channel_id=1, source_target_pairs={{0,4},{4,0},{8,12},{12,8},{16,20},{20,16},{24,28},{28,24},{1,5},{5... | collective-permute-start | bytes 2359304 | tf_op jit(solution)/shard_map/ppermute | solution.py:21
  171.5 8.9 %collective-permute-start.23 = (bf16[256,1024]{1,0:T(8,128)(2,1)S(1)}, bf16[256,1024]{1,0:T(8,128)(2,1)S(1)}, u32[]{:S(2)}, u32[]{:S(2)}) collective-permute-start(bf16[256,1024]{1,0:T(8,128)(2,1)S(1)} %shard_map.80.refs_0_.refs_4_), channel_id=1, source_target_pairs={{0,1},{1,0},{2,3},{3,2},{4,5},{5,4},{6,7},{7,6},{8,9},{9,8},{10,11... | collective-permute-start | bytes 1572872 | tf_op jit(solution)/shard_map/ppermute | solution.py:21
  180.5 11.5 %collective-permute-start.25 = (bf16[256,1024]{1,0:T(8,128)(2,1)S(1)}, bf16[256,1024]{1,0:T(8,128)(2,1)S(1)}, u32[]{:S(2)}, u32[]{:S(2)}) collective-permute-start(bf16[256,1024]{1,0:T(8,128)(2,1)S(1)} %collective-permute-done.24.refs_2_.refs_6_), channel_id=1, source_target_pairs={{0,1},{1,0},{2,3},{3,2},{4,5},{5,4},{6,7},{7,6},{8,9},{9,8},{10,11... | collective-permute-start | bytes 1572872 | tf_op jit(solution)/shard_map/ppermute | solution.py:21
  180.5 21.4 %collective-permute-start.18 = (bf16[256,1024]{1,0:T(8,128)(2,1)S(1)}, bf16[256,1024]{1,0:T(8,128)(2,1)S(1)}, u32[]{:S(2)}, u32[]{:S(2)}) collective-permute-start(bf16[256,1024]{1,0:T(8,128)(2,1)S(1)} %collective-permute-done.16.refs_8_.refs_11_), channel_id=1, source_target_pairs={{0,4},{4,0},{8,12},{12,8},{16,20},{20,16},{24,28},{28,24},{1,5},{5... | collective-permute-start | bytes 1572872 | tf_op jit(solution)/shard_map/ppermute | solution.py:21
  190.7 21.9 %collective-permute-start.19 = (bf16[256,1024]{1,0:T(8,128)(2,1)S(1)}, bf16[256,1024]{1,0:T(8,128)(2,1)S(1)}, u32[]{:S(2)}, u32[]{:S(2)}) collective-permute-start(bf16[256,1024]{1,0:T(8,128)(2,1)S(1)} %collective-permute-done.17.refs_9_.refs_12_), channel_id=1, source_target_pairs={{0,4},{4,0},{8,12},{12,8},{16,20},{20,16},{24,28},{28,24},{1,5},{5... | collective-permute-start | bytes 1572872 | tf_op jit(solution)/shard_map/ppermute | solution.py:21
  192.0 26.2 %collective-permute-start.9 = (bf16[256,1024]{1,0:T(8,128)(2,1)S(1)}, bf16[256,1024]{1,0:T(8,128)(2,1)S(1)}, u32[]{:S(2)}, u32[]{:S(2)}) collective-permute-start(bf16[256,1024]{1,0:T(8,128)(2,1)S(1)} %shard_map.78.refs_0_), channel_id=1, source_target_pairs={{0,1},{1,0},{2,3},{3,2},{4,5},{5,4},{6,7},{7,6},{8,9},{9,8},{10,11... | collective-permute-start | bytes 1572872 | tf_op jit(solution)/shard_map/ppermute | solution.py:21
  192.0 26.2 %collective-permute-start.11 = (bf16[256,1024]{1,0:T(8,128)(2,1)S(1)}, bf16[256,1024]{1,0:T(8,128)(2,1)S(1)}, u32[]{:S(2)}, u32[]{:S(2)}) collective-permute-start(bf16[256,1024]{1,0:T(8,128)(2,1)S(1)} %collective-permute-done.10.refs_2_), channel_id=1, source_target_pairs={{0,1},{1,0},{2,3},{3,2},{4,5},{5,4},{6,7},{7,6},{8,9},{9,8},{10,11... | collective-permute-start | bytes 1572872 | tf_op jit(solution)/shard_map/ppermute | solution.py:21

commit v9 on v8

--- a/solution.py
+++ b/solution.py
@@ -115,8 +115,10 @@
 
 def split_kernel(first, sizes, joined, src, *refs):
     count = len(sizes)
+    if joined:
+        head, refs = refs[0], refs[1:]
     outs = refs[:count]
-    buf, sem = refs[-2:]
+    buf, sem, head_sem = refs[-3:]
     blocks = sum(sizes) // BLOCK
     copies = []
     for k in range(blocks):
@@ -124,6 +126,9 @@
         copies.append(pltpu.make_async_copy(src.at[lines, :], buf.at[k], sem.at[k]))
     for copy in copies:
         copy.start()
+    if joined:
+        join = pltpu.make_async_copy(head, refs[count].at[0:first, :], head_sem)
+        join.start()
     order = row_order(False)
     k = 0
     for c in range(count):
@@ -132,26 +137,31 @@
             moved = jnp.dot(order, buf[k], preferred_element_type=F32).astype(BF16)
             outs[c][r * BLOCK : (r + 1) * BLOCK, :] = moved
             if joined:
-                refs[count][k * BLOCK : (k + 1) * BLOCK, :] = moved
+                refs[count][first + k * BLOCK : first + (k + 1) * BLOCK, :] = moved
             k += 1
-
-
-def split_rows(array, first, sizes, joined):
+    if joined:
+        join.wait()
+
+
+def split_rows(array, first, sizes, head):
     vmem = pl.BlockSpec(memory_space=pltpu.VMEM)
     rows, width = sum(sizes), array.shape[1]
-    shapes = list(sizes) + ([rows] if joined else [])
+    joined = head is not None
+    shapes = list(sizes) + ([first + rows] if joined else [])
+    args = [array] + ([head] if joined else [])
     return pl.pallas_call(
         functools.partial(split_kernel, first, tuple(sizes), joined),
         out_shape=[jax.ShapeDtypeStruct((r, width), array.dtype) for r in shapes],
-        in_specs=[pl.BlockSpec(memory_space=pltpu.HBM)],
+        in_specs=[pl.BlockSpec(memory_space=pl.ANY)] * len(args),
         out_specs=[vmem] * len(shapes),
         scratch_shapes=[
             pltpu.VMEM((rows // BLOCK, BLOCK, width), BF16),
             pltpu.SemaphoreType.DMA((rows // BLOCK,)),
+            pltpu.SemaphoreType.DMA,
         ],
         compiler_params=params(60),
         cost_estimate=cost(2 * rows * BLOCK * width, 4 * rows * width),
-    )(array)
+    )(*args)
 
 
 def compose_rows(maps, count, a, b):
@@ -534,7 +544,7 @@
     in_specs = [pl.BlockSpec(memory_space=pl.ANY)] * (groups * group)
     in_specs += [pl.BlockSpec(memory_space=pltpu.HBM)] * len(used)
     args += prev
-    in_specs += [pl.BlockSpec((q.shape[0], width), lambda n, p: (0, 0)) for q in prev]
+    in_specs += [pl.BlockSpec(memory_space=pltpu.VMEM)] * len(prev)
     aliases = {}
     if whole is not None:
         aliases = {len(args): 0}
@@ -546,7 +556,7 @@
         out_spec = pl.BlockSpec((rows, width), lambda n, p: (first // rows, 0))
     else:
         out_shape = jax.ShapeDtypeStruct((rows, width), F32)
-        out_spec = pl.BlockSpec((rows, width), lambda n, p: (0, 0))
+        out_spec = pl.BlockSpec(memory_space=pltpu.VMEM)
     return pl.pallas_call(
         functools.partial(
             mix_kernel, groups, group, cuts, peers, tuple(slots), final, len(prev)
@@ -581,14 +591,12 @@
     return parts if min(parts) >= LANES else [rows]
 
 
-def ring_cut(step, outer, rows):
-    return cut_of(rows, (1, 1) if step == outer - 1 else (1,))
-
-
-def swap_cut(step, outer, rows):
-    if step == SWAPS_EARLY + 1 and step < outer - 1:
-        return cut_of(rows, (1, 3))
-    return ring_cut(step, outer, rows)
+def ring_cut(rows):
+    return cut_of(rows, (1, 1))
+
+
+def swap_cut(step, rows):
+    return cut_of(rows, (1,) if step == 0 else (1, 1))
 
 
 def recut(blocks, parts):
@@ -605,20 +613,25 @@
 
 def gather_early(w_output):
     peers = lax.axis_size("ctx")
+    rows = w_output.shape[0]
     route = [(i, (i + 2) % peers) for i in range(peers)]
     held = {(0, 0): [w_output]}
-    for step in range(1, min(RINGS_EARLY + 1, peers // 2)):
-        held[step, 0] = [lax.ppermute(held[step - 1, 0][0], "ctx", route)]
+    for step in range(1, RINGS_EARLY + 1):
+        held[step, 0] = []
+        for block in recut(held[step - 1, 0], ring_cut(rows)):
+            held[step, 0].append(lax.ppermute(block, "ctx", route))
     for step in range(SWAPS_EARLY + 1):
-        held[step, 1] = [swap(held[step, 0][0], "ctx", 1)]
+        held[step, 1] = []
+        for block in recut(held[step, 0], swap_cut(step, rows)):
+            held[step, 1].append(swap(block, "ctx", 1))
     return held
 
 
-def next_cuts(outer, rows):
-    return [ring_cut(RINGS_EARLY + 1, outer, rows), swap_cut(SWAPS_EARLY + 1, outer, rows)]
-
-
-def gather_late(held, following, middle, late):
+def next_cuts(rows):
+    return [ring_cut(rows), swap_cut(SWAPS_EARLY + 1, rows)]
+
+
+def gather_late(held, following, late):
     peers = lax.axis_size("ctx")
     outer = peers // 2
     rows = held[0, 0][0].shape[0]
@@ -628,17 +641,20 @@
         if step == RINGS_EARLY + 1:
             source = following[0]
         else:
-            source = recut(held[step - 1, 0], ring_cut(step, outer, rows))
-        for block in source:
-            held[step, 0].append(lax.ppermute(behind(block, late), "ctx", route))
+            source = recut(held[step - 1, 0], ring_cut(rows))
+        for p, block in enumerate(source):
+            ahead = step == RINGS_EARLY + 1 and p < len(source) - 1
+            gate = None if ahead else late
+            held[step, 0].append(lax.ppermute(behind(block, gate), "ctx", route))
     for step in range(SWAPS_EARLY + 1, outer):
         held[step, 1] = []
         if step == SWAPS_EARLY + 1:
             source = following[1]
         else:
-            source = recut(held[step, 0], swap_cut(step, outer, rows))
+            source = recut(held[step, 0], swap_cut(step, rows))
         for p, block in enumerate(source):
-            gate = middle if step == SWAPS_EARLY + 1 and p == 0 else late
+            ahead = step == SWAPS_EARLY + 1 and p < len(source) - 1
+            gate = None if ahead else late
             held[step, 1].append(swap(behind(block, gate), "ctx", 1))
     return [held[step, i] for step in range(outer) for i in range(2)]
 
@@ -656,7 +672,9 @@
     gain = recur_gain[None, :]
     start = start_state[None, :]
 
-    *ordered, whole = split_rows(tokens, 0, sizes, True)
+    ordered = split_rows(tokens, 0, sizes[:1], None)
+    *others, whole = split_rows(tokens, sizes[0], sizes[1:], ordered[0])
+    ordered = [*ordered, *others]
     far = []
     for piece in ordered:
         far.append([swap(piece, "ch", half)])
@@ -687,12 +705,15 @@
         gates.append(out[0])
         maps.append(out[1])
     held = gather_early(w_output)
-    following = [recut(held[RINGS_EARLY, 0], cut) for cut in next_cuts(peers // 2, w_output.shape[0])]
-    following, totals = lax.optimization_barrier((following, out[2]))
+    following = [recut(held[RINGS_EARLY, 0], cut) for cut in next_cuts(w_output.shape[0])]
+    ready = [len(pieces) - 1 for pieces in following]
+    waiting = [pieces[n:] for pieces, n in zip(following, ready)]
+    waiting, totals = lax.optimization_barrier((waiting, out[2]))
+    following = [pieces[:n] + rest for pieces, n, rest in zip(following, ready, waiting)]
     first_maps = lax.all_to_all(totals, "ctx", 0, 0, tiled=True)
     run, run_maps, totals = bend_all(place, gates, maps, first_maps, gain, start)
     peer_maps = lax.all_to_all(totals, "ctx", 0, 0, tiled=True)
-    weights = gather_late(held, following, first_maps, peer_maps)
+    weights = gather_late(held, following, peer_maps)
 
     blocks = []
     for c in range(chunks):

time: 224 us -> 235 us (1.049)
  blocking collectives: 9.29 us -> 19.3 us
  starting transfers between devices: 27.9 us -> 34 us
  waiting for transfers between devices: 104 us -> 99.2 us
    ppermute x4 -> x6, waiting for transfers between devices: 22.3 us -> 0.02 us  [the longest x4 0.01 us: gather_early(): held[step, 0].append(lax.ppermute(block, 'ctx', route))]
    ppermute x22 -> x23, waiting for transfers between devices: 76.7 us -> 95.8 us  [swap(): lax.ppermute(block, axis, [(i, i ^ bits) for i in range(lax.axis_size(axi...]
    all_to_all x1, blocking collectives: 9.29 us -> 19.3 us  [layer(): peer_maps = lax.all_to_all(totals, 'ctx', 0, 0, tiled=True)]
    ppermute x4 -> x6, starting transfers between devices: 5.1 us -> 10.1 us  [the longest x4 7.3 us: gather_early(): held[step, 0].append(lax.ppermute(block, 'ctx', route))]
    pallas_call x1 -> x2, Pallas kernels: 4.09 us -> 6.09 us  [split_rows(): pl.pallas_call(functools.partial(split_kernel, first, tuple(sizes), joine...]
    unnamed x32 -> x28, local copies, waits for them, and re-layouts: 8.94 us -> 9.75 us
    ppermute x22 -> x23, starting transfers between devices: 17.9 us -> 17.7 us  [swap(): lax.ppermute(block, axis, [(i, i ^ bits) for i in range(lax.axis_size(axi...]
  transfers between devices with their start and end apart: 27 -> 30, of which waited for: 10 -> 12; matrix products, arithmetic and copies ran while one was open for 1% -> 0% of each run, Pallas kernels for 27% -> 26%
where the time goes in v9:
time: 235 us
  waiting for transfers between devices  99.2 us (42%)
  Pallas kernels  71.2 us (30%)
  starting transfers between devices  34 us (14%)
  blocking collectives  19.3 us (8%)
  local copies, waits for them, and re-layouts  10.6 us (5%)
    ppermute x23, waiting for transfers between devices, swap(): lax.ppermute(block, axis, [(i, i ^ bits) for i in range(lax.axis_size(axi...  95.8 us
    pallas_call x3, Pallas kernels, gate_chunk(): pl.pallas_call(functools.partial(gate_kernel, half, first_row, rows, len(...  22.5 us
    all_to_all x1, blocking collectives, layer(): peer_maps = lax.all_to_all(totals, 'ctx', 0, 0, tiled=True)  19.3 us
    pallas_call x4, Pallas kernels, mix_rows(): pl.pallas_call(functools.partial(mix_kernel, groups, group, cuts, peers,...  19.1 us
    ppermute x23, starting transfers between devices, swap(): lax.ppermute(block, axis, [(i, i ^ bits) for i in range(lax.axis_size(axi...  17.7 us
    pallas_call x1, Pallas kernels, near_product(): pl.pallas_call(functools.partial(near_kernel, half, tiles, heights), out_...  14.1 us
    unnamed x28, local copies, waits for them, and re-layouts  9.75 us
    ppermute x4, starting transfers between devices, gather_early(): held[step, 0].append(lax.ppermute(block, 'ctx', route))  7.3 us
  transfers between devices with their start and end apart: 30, of which 12 were waited for; matrix products, arithmetic and copies ran while one was open for 0% of the time, Pallas kernels for 26%

profile of v9, /device:TPU:0, one launch (start us, length us, event | category | flops | bytes accessed | tf_op | source)
XLA Modules:
  0.0 234.9 jit_solution(176967703164465248)
XLA Ops:
  0.0 2.7 %shard_map.73.refs_0_ = bf16[512,1024]{1,0:T(8,128)(2,1)} custom-call(bf16[1024,1024]{1,0:T(8,128)(2,1)} %src.3), custom_call_target="tpu_custom_call" | custom-call | flops 268435456 | bytes 2097152 | tf_op jit(solution)/shard_map/pallas_call | solution.py:152
  2.7 3.4 %shard_map.74 = (bf16[256,1024]{1,0:T(8,128)(2,1)}, bf16[256,1024]{1,0:T(8,128)(2,1)}, bf16[1024,1024]{1,0:T(8,128)(2,1)}) custom-call(bf16[1024,1024]{1,0:T(8,128)(2,1)} %src.3, bf16[512,1024]{1,0:T(8,128)(2,1)} %shard_map.73.refs_0_), custom_call_target="tpu_custom_call" | custom-call | flops 268435456 | bytes 2097152 | tf_op jit(solution)/shard_map/pallas_call | solution.py:152
  6.7 2.6 %collective-permute-start = (bf16[512,1024]{1,0:T(8,128)(2,1)}, bf16[512,1024]{1,0:T(8,128)(2,1)}, u32[]{:S(2)}, u32[]{:S(2)}) collective-permute-start(bf16[512,1024]{1,0:T(8,128)(2,1)} %shard_map.73.refs_0_), channel_id=1, source_target_pairs={{0,2},{1,3},{2,0},{3,1},{4,6},{5,7},{6,4},{7,5},{8,10},{9,11},{10,... | collective-permute-start | bytes 3145736 | tf_op jit(solution)/shard_map/ppermute | solution.py:21
  9.3 0.9 fusion
  10.1 1.6 collective-permute-start.7
  12.2 1.5 collective-permute-start.5
  13.7 19.8 %collective-permute-done.refs_0_ = bf16[512,1024]{1,0:T(8,128)(2,1)} collective-permute-done((bf16[512,1024]{1,0:T(8,128)(2,1)}, bf16[512,1024]{1,0:T(8,128)(2,1)}, u32[]{:S(2)}, u32[]{:S(2)}) %collective-permute-start) | collective-permute-done | bytes 1048608 | tf_op jit(solution)/shard_map/ppermute | solution.py:21
  33.7 2.2 collective-permute-start.13
  35.9 8.9 %collective-permute-done.3.refs_0_ = bf16[256,1024]{1,0:T(8,128)(2,1)} collective-permute-done((bf16[256,1024]{1,0:T(8,128)(2,1)}, bf16[256,1024]{1,0:T(8,128)(2,1)}, u32[]{:S(2)}, u32[]{:S(2)}) %collective-permute-start.3) | collective-permute-done | bytes 524320 | tf_op jit(solution)/shard_map/ppermute | solution.py:21
  44.8 2.1 collective-permute-start.8
  46.9 8.8 %collective-permute-done.5.refs_0_ = bf16[256,1024]{1,0:T(8,128)(2,1)S(1)} collective-permute-done((bf16[256,1024]{1,0:T(8,128)(2,1)}, bf16[256,1024]{1,0:T(8,128)(2,1)S(1)}, u32[]{:S(2)}, u32[]{:S(2)}) %collective-permute-start.5) | collective-permute-done | bytes 524320 | tf_op jit(solution)/shard_map/ppermute | solution.py:21
  56.2 1.6 copy-done.5
  57.8 14.1 %shard_map.75.refs_2_ = f32[2,1024,1024]{2,1,0:T(8,128)S(1)} custom-call(s32[2]{0:T(128)S(1)} %pad_add_fusion.place, bf16[1024,1024]{1,0:T(8,128)(2,1)S(1)} %copy-done.5, bf16[1024,1024]{1,0:T(8,128)(2,1)} %collective-permute-done.2.refs_1_, bf16[2,4096,1024]{2,1,0:T(8,128)(2,1)} %refs_3_.5), custom_call_target="tpu_custom_call" | custom-call | flops 8589934592 | bytes 20971520 | tf_op jit(solution)/shard_map/pallas_call | solution.py:87
  71.9 9.8 %shard_map.76 = (bf16[2,512,1024]{2,1,0:T(8,128)(2,1)S(1)}, f32[2,16,1024]{2,1,0:T(8,128)S(1)}) custom-call(s32[2]{0:T(128)S(1)} %pad_add_fusion.place, bf16[512,1024]{1,0:T(8,128)(2,1)} %collective-permute-done.refs_0_, bf16[512,1024]{1,0:T(8,128)(2,1)} %collective-permute-done.1.refs_1_, f32[2,1024,1024]{2,1,0:T(8,128)S(1)} %shard_map.75.refs_2_, ...), custom_call_target="tpu_custom_call" | custom-call | flops 4294967296 | bytes 16777216 | tf_op jit(solution)/shard_map/pallas_call | solution.py:300
  81.7 1.3 copy-done.6
  83.0 6.3 %shard_map.77 = (bf16[2,256,1024]{2,1,0:T(8,128)(2,1)S(1)}, f32[2,8,1024]{2,1,0:T(8,128)S(1)}) custom-call(s32[2]{0:T(128)S(1)} %pad_add_fusion.place, bf16[256,1024]{1,0:T(8,128)(2,1)} %collective-permute-done.3.refs_0_, bf16[256,1024]{1,0:T(8,128)(2,1)S(1)} %collective-permute-done.4.refs_1_, f32[2,1024,1024]{2,1,0:T(8,128)S(1)} %shard_map.75.refs_2_, ...), custom_call_target="tpu_custom_call" | custom-call | flops 2147483648 | bytes 12582912 | tf_op jit(solution)/shard_map/pallas_call | solution.py:300
  89.3 1.0 copy-done.8
  90.3 6.4 %shard_map.78 = (bf16[2,256,1024]{2,1,0:T(8,128)(2,1)S(1)}, f32[2,8,1024]{2,1,0:T(8,128)S(1)}, f32[8,2,1024]{2,1,0:T(2,128)}) custom-call(s32[2]{0:T(128)S(1)} %pad_add_fusion.place, bf16[256,1024]{1,0:T(8,128)(2,1)S(1)} %collective-permute-done.5.refs_0_, bf16[256,1024]{1,0:T(8,128)(2,1)S(1)} %collective-permute-done.6.refs_1_, ...), custom_call_target="tpu_custom_call" | custom-call | flops 2147483648 | bytes 12582912 | tf_op jit(solution)/shard_map/pallas_call | solution.py:300
  96.8 1.0 copy-done.10
  98.6 6.1 %all-to-all-start = ((f32[8,2,1024]{2,1,0:T(2,128)}), f32[8,2,1024]{2,1,0:T(2,128)S(1)}, u32[]{:S(2)}, u32[]{:S(2)}) async-start(f32[8,2,1024]{2,1,0:T(2,128)} %get-tuple-element.35), calls=%async_computation | async-start | bytes 131072 | tf_op jit(solution)/shard_map/all_to_all | solution.py:713
  104.7 2.0 collective-permute-start.12
  106.7 1.5 collective-permute-start.16
  108.7 3.3 %all-to-all-done.refs_6_ = f32[8,2,1024]{2,1,0:T(2,128)S(1)} async-done(((f32[8,2,1024]{2,1,0:T(2,128)}), f32[8,2,1024]{2,1,0:T(2,128)S(1)}, u32[]{:S(2)}, u32[]{:S(2)}) %all-to-all-start) | async-done | bytes 65568 | tf_op jit(solution)/shard_map/all_to_all | solution.py:713
  112.0 1.6 copy-done.7
  113.6 1.2 copy-done.9
  114.9 1.2 copy-done.11
  116.1 6.9 %bend.1 = (f32[2,1024,1024]{2,1,0:T(8,128)S(1)}, f32[2,32,1024]{2,1,0:T(8,128)S(1)}, f32[8,2,1024]{2,1,0:T(2,128)S(1)}) custom-call(s32[2]{0:T(128)S(1)} %pad_add_fusion.place, bf16[2,512,1024]{2,1,0:T(8,128)(2,1)S(1)} %copy-done.7, bf16[2,256,1024]{2,1,0:T(8,128)(2,1)S(1)} %copy-done.9, bf16[2,256,1024]{2,1,0:T(8,128)(2,1)S(1)} %copy-done.11, ...), custom_call_target="tpu_custom_call" | custom-call | flops 41943040 | bytes 12582912 | tf_op jit(solution)/shard_map/bend/pallas_call | solution.py:406
  123.0 19.3 %all_to_all.10.peer_ref = f32[8,2,1024]{2,1,0:T(2,128)S(1)} all-to-all(f32[8,2,1024]{2,1,0:T(2,128)S(1)} %get-tuple-element.38), channel_id=1, replica_groups=mesh['ctx'=8,'ch'=4] {'ctx'}, dimensions={0} | all-to-all | bytes 131072 | tf_op jit(solution)/shard_map/all_to_all | solution.py:715
  142.3 1.0 shard_map.80.refs_0_
  143.3 1.6 collective-permute-start.24
  144.8 1.3 collective-permute-start.15
  146.1 1.4 collective-permute-start.19
  150.0 9.7 %collective-permute-done.15.refs_9_ = bf16[256,1024]{1,0:T(8,128)(2,1)S(1)} collective-permute-done((bf16[256,1024]{1,0:T(8,128)(2,1)S(1)}, bf16[256,1024]{1,0:T(8,128)(2,1)S(1)}, u32[]{:S(2)}, u32[]{:S(2)}) %collective-permute-start.15) | collective-permute-done | bytes 524320 | tf_op jit(solution)/shard_map/ppermute | solution.py:21
  160.2 1.5 collective-permute-start.27
  161.6 1.5 collective-permute-start.20
  163.1 5.4 %collective-permute-done.17.refs_12_ = bf16[256,1024]{1,0:T(8,128)(2,1)S(1)} collective-permute-done((bf16[256,1024]{1,0:T(8,128)(2,1)}, bf16[256,1024]{1,0:T(8,128)(2,1)S(1)}, u32[]{:S(2)}, u32[]{:S(2)}) %collective-permute-start.17) | collective-permute-done | bytes 524320 | tf_op jit(solution)/shard_map/ppermute | solution.py:21
  169.4 11.2 %collective-permute-done.10.refs_2_ = bf16[256,1024]{1,0:T(8,128)(2,1)S(1)} collective-permute-done((bf16[256,1024]{1,0:T(8,128)(2,1)S(1)}, bf16[256,1024]{1,0:T(8,128)(2,1)S(1)}, u32[]{:S(2)}, u32[]{:S(2)}) %collective-permute-start.10) | collective-permute-done | bytes 524320 | tf_op jit(solution)/shard_map/ppermute | solution.py:21
  180.6 9.2 %collective-permute-done.27.refs_2_.refs_6_ = bf16[256,1024]{1,0:T(8,128)(2,1)S(1)} collective-permute-done((bf16[256,1024]{1,0:T(8,128)(2,1)S(1)}, bf16[256,1024]{1,0:T(8,128)(2,1)S(1)}, u32[]{:S(2)}, u32[]{:S(2)}) %collective-permute-start.27) | collective-permute-done | bytes 524320 | tf_op jit(solution)/shard_map/ppermute | solution.py:21
  189.8 1.2 collective-permute-start.18
  191.0 0.9 collective-permute-start.21
  191.9 12.7 %collective-permute-done.18.refs_13_ = bf16[256,1024]{1,0:T(8,128)(2,1)S(1)} collective-permute-done((bf16[256,1024]{1,0:T(8,128)(2,1)S(1)}, bf16[256,1024]{1,0:T(8,128)(2,1)S(1)}, u32[]{:S(2)}, u32[]{:S(2)}) %collective-permute-start.18) | collective-permute-done | bytes 524320 | tf_op jit(solution)/shard_map/ppermute | solution.py:21
  204.6 1.2 collective-permute-start.22
  206.3 3.3 %shard_map.83.refs_13_ = f32[256,1024]{1,0:T(8,128)S(1)} custom-call(s32[2]{0:T(128)S(1)} %pad_add_fusion.place, bf16[256,1024]{1,0:T(8,128)(2,1)S(1)} %shard_map.81.refs_0_.refs_4_, bf16[256,1024]{1,0:T(8,128)(2,1)S(1)} %collective-permute-done.26.refs_1_.refs_5_, bf16[256,1024]{1,0:T(8,128)(2,1)S(1)} %collective-permute-done.27.refs_2_.refs_6_, ...), custom_call_target="tpu_custom_call" | custom-call | flops 1610612736 | bytes 8912896 | tf_op jit(solution)/shard_map/pallas_call | solution.py:560
  209.7 5.3 %shard_map.82.refs_12_ = f32[512,1024]{1,0:T(8,128)S(1)} custom-call(s32[2]{0:T(128)S(1)} %pad_add_fusion.place, bf16[512,1024]{1,0:T(8,128)(2,1)S(1)} %shard_map.80.refs_0_, bf16[512,1024]{1,0:T(8,128)(2,1)S(1)} %collective-permute-done.23.refs_1_, bf16[512,1024]{1,0:T(8,128)(2,1)S(1)} %collective-permute-done.24.refs_2_, ...), custom_call_target="tpu_custom_call" | custom-call | flops 3221225472 | bytes 11534336 | tf_op jit(solution)/shard_map/pallas_call | solution.py:560
  215.0 0.8 collective-permute-done.21.refs_10_.refs_16_
  215.9 8.4 %collective-permute-done.22.refs_11_.refs_17_ = bf16[256,1024]{1,0:T(8,128)(2,1)S(1)} collective-permute-done((bf16[256,1024]{1,0:T(8,128)(2,1)S(1)}, bf16[256,1024]{1,0:T(8,128)(2,1)S(1)}, u32[]{:S(2)}, u32[]{:S(2)}) %collective-permute-start.22) | collective-permute-done | bytes 524320 | tf_op jit(solution)/shard_map/ppermute | solution.py:21
  224.2 5.3 %shard_map.84.refs_18_ = bf16[1024,1024]{1,0:T(8,128)(2,1)} custom-call(s32[2]{0:T(128)S(1)} %pad_add_fusion.place, bf16[512,1024]{1,0:T(8,128)(2,1)S(1)} %shard_map.80.refs_0_, bf16[512,1024]{1,0:T(8,128)(2,1)S(1)} %collective-permute-done.23.refs_1_, bf16[512,1024]{1,0:T(8,128)(2,1)S(1)} %collective-permute-done.24.refs_2_, ...), custom_call_target="tpu_custom_call" | custom-call | flops 1610612736 | bytes 6815744 | tf_op jit(solution)/shard_map/pallas_call | solution.py:560
  229.6 5.2 %shard_map.85 = bf16[1024,1024]{1,0:T(8,128)(2,1)} custom-call(s32[2]{0:T(128)S(1)} %pad_add_fusion.place, bf16[256,1024]{1,0:T(8,128)(2,1)S(1)} %shard_map.79.refs_0_, bf16[256,1024]{1,0:T(8,128)(2,1)S(1)} %collective-permute-done.9.refs_1_, bf16[256,1024]{1,0:T(8,128)(2,1)S(1)} %collective-permute-done.10.refs_2_, ...), custom_call_target="tpu_custom_call", output_to_operand_aliasing={{}: (19, {})} | custom-call | flops 2147483648 | bytes 11534336 | tf_op jit(solution)/shard_map/pallas_call | solution.py:560
  (58 shorter events, 7.5 us)
Async XLA Ops:
  2.7 6.6 %copy-start = (bf16[512,1024]{1,0:T(8,128)(2,1)S(1)}, bf16[512,1024]{1,0:T(8,128)(2,1)}, u32[]{:S(2)}) copy-start(bf16[512,1024]{1,0:T(8,128)(2,1)} %refs_4_.5) | copy-start | bytes 3145732
  2.7 31.0 %copy-start.12 = (f32[1024]{0:T(1024)S(1)}, f32[1024]{0:T(1024)}, u32[]{:S(2)}) copy-start(f32[1024]{0:T(1024)} %param.11) | copy-start | bytes 12292
  2.7 31.0 %copy-start.13 = (f32[1024]{0:T(1024)S(1)}, f32[1024]{0:T(1024)}, u32[]{:S(2)}) copy-start(f32[1024]{0:T(1024)} %param.10) | copy-start | bytes 12292
  6.1 49.5 %collective-permute-start.2 = (bf16[1024,1024]{1,0:T(8,128)(2,1)}, bf16[1024,1024]{1,0:T(8,128)(2,1)}, u32[]{:S(2)}, u32[]{:S(2)}) collective-permute-start(bf16[1024,1024]{1,0:T(8,128)(2,1)} %get-tuple-element.25.refs_0_), channel_id=1, source_target_pairs={{0,1},{1,0},{2,3},{3,2},{4,5},{5,4},{6,7},{7,6},{8,9},{9,8},{10,11... | collective-permute-start | bytes 6291464 | tf_op jit(solution)/shard_map/ppermute | solution.py:21
  6.7 26.9 %collective-permute-start = (bf16[512,1024]{1,0:T(8,128)(2,1)}, bf16[512,1024]{1,0:T(8,128)(2,1)}, u32[]{:S(2)}, u32[]{:S(2)}) collective-permute-start(bf16[512,1024]{1,0:T(8,128)(2,1)} %shard_map.73.refs_0_), channel_id=1, source_target_pairs={{0,2},{1,3},{2,0},{3,1},{4,6},{5,7},{6,4},{7,5},{8,10},{9,11},{10,... | collective-permute-start | bytes 3145736 | tf_op jit(solution)/shard_map/ppermute | solution.py:21
  10.1 23.6 %collective-permute-start.7 = (bf16[256,1024]{1,0:T(8,128)(2,1)S(1)}, bf16[256,1024]{1,0:T(8,128)(2,1)S(1)}, u32[]{:S(2)}, u32[]{:S(2)}) collective-permute-start(bf16[256,1024]{1,0:T(8,128)(2,1)S(1)} %get-tuple-element.46), channel_id=1, source_target_pairs={{0,8},{4,12},{8,16},{12,20},{16,24},{20,28},{24,0},{28,4},{1,9},{5... | collective-permute-start | bytes 1572872 | tf_op jit(solution)/shard_map/ppermute | solution.py:622
  11.7 33.1 %collective-permute-start.3 = (bf16[256,1024]{1,0:T(8,128)(2,1)}, bf16[256,1024]{1,0:T(8,128)(2,1)}, u32[]{:S(2)}, u32[]{:S(2)}) collective-permute-start(bf16[256,1024]{1,0:T(8,128)(2,1)} %get-tuple-element.27), channel_id=1, source_target_pairs={{0,2},{1,3},{2,0},{3,1},{4,6},{5,7},{6,4},{7,5},{8,10},{9,11},{10,... | collective-permute-start | bytes 1572872 | tf_op jit(solution)/shard_map/ppermute | solution.py:21
  12.2 43.4 %collective-permute-start.5 = (bf16[256,1024]{1,0:T(8,128)(2,1)}, bf16[256,1024]{1,0:T(8,128)(2,1)S(1)}, u32[]{:S(2)}, u32[]{:S(2)}) collective-permute-start(bf16[256,1024]{1,0:T(8,128)(2,1)} %get-tuple-element.29), channel_id=1, source_target_pairs={{0,2},{1,3},{2,0},{3,1},{4,6},{5,7},{6,4},{7,5},{8,10},{9,11},{10,... | collective-permute-start | bytes 1572872 | tf_op jit(solution)/shard_map/ppermute | solution.py:21
  33.6 38.3 %collective-permute-start.1 = (bf16[512,1024]{1,0:T(8,128)(2,1)}, bf16[512,1024]{1,0:T(8,128)(2,1)}, u32[]{:S(2)}, u32[]{:S(2)}) collective-permute-start(bf16[512,1024]{1,0:T(8,128)(2,1)} %collective-permute-done.refs_0_), channel_id=1, source_target_pairs={{0,1},{1,0},{2,3},{3,2},{4,5},{5,4},{6,7},{7,6},{8,9},{9,8},{10,11... | collective-permute-start | bytes 3145736 | tf_op jit(solution)/shard_map/ppermute | solution.py:21
  33.7 38.2 %copy-start.3 = (f32[1024]{0:T(1024)S(1)}, f32[1024]{0:T(1024)}, u32[]{:S(2)}) copy-start(f32[1024]{0:T(1024)} %param.13) | copy-start | bytes 12292
  33.7 38.2 %copy-start.4 = (f32[1024]{0:T(1024)S(1)}, f32[1024]{0:T(1024)}, u32[]{:S(2)}) copy-start(f32[1024]{0:T(1024)} %param.12) | copy-start | bytes 12292
  33.7 73.0 %collective-permute-start.13 = (bf16[256,1024]{1,0:T(8,128)(2,1)}, bf16[256,1024]{1,0:T(8,128)(2,1)S(1)}, u32[]{:S(2)}, u32[]{:S(2)}) collective-permute-start(bf16[256,1024]{1,0:T(8,128)(2,1)} %get-tuple-element.45), channel_id=1, source_target_pairs={{0,8},{4,12},{8,16},{12,20},{16,24},{20,28},{24,0},{28,4},{1,9},{5... | collective-permute-start | bytes 1572872 | tf_op jit(solution)/shard_map/ppermute | solution.py:622
  44.8 52.9 %collective-permute-start.8 = (bf16[256,1024]{1,0:T(8,128)(2,1)S(1)}, bf16[256,1024]{1,0:T(8,128)(2,1)S(1)}, u32[]{:S(2)}, u32[]{:S(2)}) collective-permute-start(bf16[256,1024]{1,0:T(8,128)(2,1)S(1)} %collective-permute-done.7.refs_7_), channel_id=1, source_target_pairs={{0,8},{4,12},{8,16},{12,20},{16,24},{20,28},{24,0},{28,4},{1,9},{5... | collective-permute-start | bytes 1572872 | tf_op jit(solution)/shard_map/ppermute | solution.py:622
  55.7 27.3 %collective-permute-start.4 = (bf16[256,1024]{1,0:T(8,128)(2,1)}, bf16[256,1024]{1,0:T(8,128)(2,1)S(1)}, u32[]{:S(2)}, u32[]{:S(2)}) collective-permute-start(bf16[256,1024]{1,0:T(8,128)(2,1)} %collective-permute-done.3.refs_0_), channel_id=1, source_target_pairs={{0,1},{1,0},{2,3},{3,2},{4,5},{5,4},{6,7},{7,6},{8,9},{9,8},{10,11... | collective-permute-start | bytes 1572872 | tf_op jit(solution)/shard_map/ppermute | solution.py:21
  55.7 34.6 %collective-permute-start.6 = (bf16[256,1024]{1,0:T(8,128)(2,1)S(1)}, bf16[256,1024]{1,0:T(8,128)(2,1)S(1)}, u32[]{:S(2)}, u32[]{:S(2)}) collective-permute-start(bf16[256,1024]{1,0:T(8,128)(2,1)S(1)} %collective-permute-done.5.refs_0_), channel_id=1, source_target_pairs={{0,1},{1,0},{2,3},{3,2},{4,5},{5,4},{6,7},{7,6},{8,9},{9,8},{10,11... | collective-permute-start | bytes 1572872 | tf_op jit(solution)/shard_map/ppermute | solution.py:21
  56.2 1.6 copy-start.5
  81.7 1.3 copy-start.6
  89.3 1.0 copy-start.8
  96.8 1.0 copy-start.10
  97.8 0.8 copy-start.1
  98.6 13.5 %all-to-all-start = ((f32[8,2,1024]{2,1,0:T(2,128)}), f32[8,2,1024]{2,1,0:T(2,128)S(1)}, u32[]{:S(2)}, u32[]{:S(2)}) async-start(f32[8,2,1024]{2,1,0:T(2,128)} %get-tuple-element.35), calls=%async_computation | async-start | bytes 131072 | tf_op jit(solution)/shard_map/all_to_all | solution.py:713
  104.7 55.5 %collective-permute-start.12 = (bf16[512,1024]{1,0:T(8,128)(2,1)S(1)}, bf16[512,1024]{1,0:T(8,128)(2,1)S(1)}, u32[]{:S(2)}, u32[]{:S(2)}) collective-permute-start(bf16[512,1024]{1,0:T(8,128)(2,1)S(1)} %copy-done), channel_id=1, source_target_pairs={{0,4},{4,0},{8,12},{12,8},{16,20},{20,16},{24,28},{28,24},{1,5},{5... | collective-permute-start | bytes 3145736 | tf_op jit(solution)/shard_map/ppermute | solution.py:21
  106.7 39.4 %collective-permute-start.16 = (bf16[256,1024]{1,0:T(8,128)(2,1)S(1)}, bf16[256,1024]{1,0:T(8,128)(2,1)}, u32[]{:S(2)}, u32[]{:S(2)}) collective-permute-start(bf16[256,1024]{1,0:T(8,128)(2,1)S(1)} %collective-permute-done.13.refs_6_), channel_id=1, source_target_pairs={{0,8},{4,12},{8,16},{12,20},{16,24},{20,28},{24,0},{28,4},{1,9},{5... | collective-permute-start | bytes 1572872 | tf_op jit(solution)/shard_map/ppermute | solution.py:622
  108.1 39.3 %collective-permute-start.14 = (bf16[256,1024]{1,0:T(8,128)(2,1)S(1)}, bf16[256,1024]{1,0:T(8,128)(2,1)}, u32[]{:S(2)}, u32[]{:S(2)}) collective-permute-start(bf16[256,1024]{1,0:T(8,128)(2,1)S(1)} %collective-permute-done.13.refs_6_), channel_id=1, source_target_pairs={{0,4},{4,0},{8,12},{12,8},{16,20},{20,16},{24,28},{28,24},{1,5},{5... | collective-permute-start | bytes 1572872 | tf_op jit(solution)/shard_map/ppermute | solution.py:21
  112.0 1.6 copy-start.7
  113.6 1.2 copy-start.9
  114.9 1.2 copy-start.11
  143.3 26.1 %collective-permute-start.24 = (bf16[512,1024]{1,0:T(8,128)(2,1)S(1)}, bf16[512,1024]{1,0:T(8,128)(2,1)S(1)}, u32[]{:S(2)}, u32[]{:S(2)}) collective-permute-start(bf16[512,1024]{1,0:T(8,128)(2,1)S(1)} %shard_map.80.refs_0_), channel_id=1, source_target_pairs={{0,2},{1,3},{2,0},{3,1},{4,6},{5,7},{6,4},{7,5},{8,10},{9,11},{10,... | collective-permute-start | bytes 3145736 | tf_op jit(solution)/shard_map/ppermute | solution.py:21
  144.8 14.8 %collective-permute-start.15 = (bf16[256,1024]{1,0:T(8,128)(2,1)S(1)}, bf16[256,1024]{1,0:T(8,128)(2,1)S(1)}, u32[]{:S(2)}, u32[]{:S(2)}) collective-permute-start(bf16[256,1024]{1,0:T(8,128)(2,1)S(1)} %collective-permute-done.7.refs_7_), channel_id=1, source_target_pairs={{0,4},{4,0},{8,12},{12,8},{16,20},{20,16},{24,28},{28,24},{1,5},{5... | collective-permute-start | bytes 1572872 | tf_op jit(solution)/shard_map/ppermute | solution.py:21
  146.1 15.5 %collective-permute-start.19 = (bf16[256,1024]{1,0:T(8,128)(2,1)}, bf16[256,1024]{1,0:T(8,128)(2,1)S(1)}, u32[]{:S(2)}, u32[]{:S(2)}) collective-permute-start(bf16[256,1024]{1,0:T(8,128)(2,1)} %collective-permute-done.16.refs_10_), channel_id=1, source_target_pairs={{0,8},{4,12},{8,16},{12,20},{16,24},{20,28},{24,0},{28,4},{1,9},{5... | collective-permute-start | bytes 1572872 | tf_op jit(solution)/shard_map/ppermute | solution.py:648
  147.5 21.1 %collective-permute-start.17 = (bf16[256,1024]{1,0:T(8,128)(2,1)}, bf16[256,1024]{1,0:T(8,128)(2,1)S(1)}, u32[]{:S(2)}, u32[]{:S(2)}) collective-permute-start(bf16[256,1024]{1,0:T(8,128)(2,1)} %collective-permute-done.16.refs_10_), channel_id=1, source_target_pairs={{0,4},{4,0},{8,12},{12,8},{16,20},{20,16},{24,28},{28,24},{1,5},{5... | collective-permute-start | bytes 1572872 | tf_op jit(solution)/shard_map/ppermute | solution.py:21
  149.1 12.5 %copy-start.2 = (bf16[256,1024]{1,0:T(8,128)(2,1)S(1)}, bf16[256,1024]{1,0:T(8,128)(2,1)}, u32[]{:S(2)}) copy-start(bf16[256,1024]{1,0:T(8,128)(2,1)} %copy-done.1) | copy-start | bytes 1572868
  159.6 21.0 %collective-permute-start.10 = (bf16[256,1024]{1,0:T(8,128)(2,1)S(1)}, bf16[256,1024]{1,0:T(8,128)(2,1)S(1)}, u32[]{:S(2)}, u32[]{:S(2)}) collective-permute-start(bf16[256,1024]{1,0:T(8,128)(2,1)S(1)} %shard_map.79.refs_0_), channel_id=1, source_target_pairs={{0,2},{1,3},{2,0},{3,1},{4,6},{5,7},{6,4},{7,5},{8,10},{9,11},{10,... | collective-permute-start | bytes 1572872 | tf_op jit(solution)/shard_map/ppermute | solution.py:21
  160.2 29.7 %collective-permute-start.27 = (bf16[256,1024]{1,0:T(8,128)(2,1)S(1)}, bf16[256,1024]{1,0:T(8,128)(2,1)S(1)}, u32[]{:S(2)}, u32[]{:S(2)}) collective-permute-start(bf16[256,1024]{1,0:T(8,128)(2,1)S(1)} %shard_map.81.refs_0_.refs_4_), channel_id=1, source_target_pairs={{0,2},{1,3},{2,0},{3,1},{4,6},{5,7},{6,4},{7,5},{8,10},{9,11},{10,... | collective-permute-start | bytes 1572872 | tf_op jit(solution)/shard_map/ppermute | solution.py:21
  161.6 29.4 %collective-permute-start.20 = (bf16[256,1024]{1,0:T(8,128)(2,1)S(1)}, bf16[256,1024]{1,0:T(8,128)(2,1)S(1)}, u32[]{:S(2)}, u32[]{:S(2)}) collective-permute-start(bf16[256,1024]{1,0:T(8,128)(2,1)S(1)} %copy-done.2), channel_id=1, source_target_pairs={{0,8},{4,12},{8,16},{12,20},{16,24},{20,28},{24,0},{28,4},{1,9},{5... | collective-permute-start | bytes 1572872 | tf_op jit(solution)/shard_map/ppermute | solution.py:648
  168.6 37.3 %collective-permute-start.23 = (bf16[512,1024]{1,0:T(8,128)(2,1)S(1)}, bf16[512,1024]{1,0:T(8,128)(2,1)S(1)}, u32[]{:S(2)}, u32[]{:S(2)}) collective-permute-start(bf16[512,1024]{1,0:T(8,128)(2,1)S(1)} %shard_map.80.refs_0_), channel_id=1, source_target_pairs={{0,1},{1,0},{2,3},{3,2},{4,5},{5,4},{6,7},{7,6},{8,9},{9,8},{10,11... | collective-permute-start | bytes 3145736 | tf_op jit(solution)/shard_map/ppermute | solution.py:21
  169.4 40.3 %collective-permute-start.25 = (bf16[512,1024]{1,0:T(8,128)(2,1)S(1)}, bf16[512,1024]{1,0:T(8,128)(2,1)S(1)}, u32[]{:S(2)}, u32[]{:S(2)}) collective-permute-start(bf16[512,1024]{1,0:T(8,128)(2,1)S(1)} %collective-permute-done.24.refs_2_), channel_id=1, source_target_pairs={{0,1},{1,0},{2,3},{3,2},{4,5},{5,4},{6,7},{7,6},{8,9},{9,8},{10,11... | collective-permute-start | bytes 3145736 | tf_op jit(solution)/shard_map/ppermute | solution.py:21
  180.6 10.4 %collective-permute-start.26 = (bf16[256,1024]{1,0:T(8,128)(2,1)S(1)}, bf16[256,1024]{1,0:T(8,128)(2,1)S(1)}, u32[]{:S(2)}, u32[]{:S(2)}) collective-permute-start(bf16[256,1024]{1,0:T(8,128)(2,1)S(1)} %shard_map.81.refs_0_.refs_4_), channel_id=1, source_target_pairs={{0,1},{1,0},{2,3},{3,2},{4,5},{5,4},{6,7},{7,6},{8,9},{9,8},{10,11... | collective-permute-start | bytes 1572872 | tf_op jit(solution)/shard_map/ppermute | solution.py:21
  189.8 14.8 %collective-permute-start.18 = (bf16[256,1024]{1,0:T(8,128)(2,1)S(1)}, bf16[256,1024]{1,0:T(8,128)(2,1)S(1)}, u32[]{:S(2)}, u32[]{:S(2)}) collective-permute-start(bf16[256,1024]{1,0:T(8,128)(2,1)S(1)} %copy-done.2), channel_id=1, source_target_pairs={{0,4},{4,0},{8,12},{12,8},{16,20},{20,16},{24,28},{28,24},{1,5},{5... | collective-permute-start | bytes 1572872 | tf_op jit(solution)/shard_map/ppermute | solution.py:21
  191.0 14.8 %collective-permute-start.28 = (bf16[256,1024]{1,0:T(8,128)(2,1)S(1)}, bf16[256,1024]{1,0:T(8,128)(2,1)S(1)}, u32[]{:S(2)}, u32[]{:S(2)}) collective-permute-start(bf16[256,1024]{1,0:T(8,128)(2,1)S(1)} %collective-permute-done.27.refs_2_.refs_6_), channel_id=1, source_target_pairs={{0,1},{1,0},{2,3},{3,2},{4,5},{5,4},{6,7},{7,6},{8,9},{9,8},{10,11... | collective-permute-start | bytes 1572872 | tf_op jit(solution)/shard_map/ppermute | solution.py:21
  191.0 24.8 %collective-permute-start.21 = (bf16[256,1024]{1,0:T(8,128)(2,1)S(1)}, bf16[256,1024]{1,0:T(8,128)(2,1)S(1)}, u32[]{:S(2)}, u32[]{:S(2)}) collective-permute-start(bf16[256,1024]{1,0:T(8,128)(2,1)S(1)} %collective-permute-done.19.refs_8_.refs_14_), channel_id=1, source_target_pairs={{0,4},{4,0},{8,12},{12,8},{16,20},{20,16},{24,28},{28,24},{1,5},{5... | collective-permute-start | bytes 1572872 | tf_op jit(solution)/shard_map/ppermute | solution.py:21
  204.6 19.6 %collective-permute-start.22 = (bf16[256,1024]{1,0:T(8,128)(2,1)S(1)}, bf16[256,1024]{1,0:T(8,128)(2,1)S(1)}, u32[]{:S(2)}, u32[]{:S(2)}) collective-permute-start(bf16[256,1024]{1,0:T(8,128)(2,1)S(1)} %collective-permute-done.20.refs_9_.refs_15_), channel_id=1, source_target_pairs={{0,4},{4,0},{8,12},{12,8},{16,20},{20,16},{24,28},{28,24},{1,5},{5... | collective-permute-start | bytes 1572872 | tf_op jit(solution)/shard_map/ppermute | solution.py:21
  205.8 23.7 %collective-permute-start.9 = (bf16[256,1024]{1,0:T(8,128)(2,1)S(1)}, bf16[256,1024]{1,0:T(8,128)(2,1)S(1)}, u32[]{:S(2)}, u32[]{:S(2)}) collective-permute-start(bf16[256,1024]{1,0:T(8,128)(2,1)S(1)} %shard_map.79.refs_0_), channel_id=1, source_target_pairs={{0,1},{1,0},{2,3},{3,2},{4,5},{5,4},{6,7},{7,6},{8,9},{9,8},{10,11... | collective-permute-start | bytes 1572872 | tf_op jit(solution)/shard_map/ppermute | solution.py:21
  205.8 23.7 %collective-permute-start.11 = (bf16[256,1024]{1,0:T(8,128)(2,1)S(1)}, bf16[256,1024]{1,0:T(8,128)(2,1)S(1)}, u32[]{:S(2)}, u32[]{:S(2)}) collective-permute-start(bf16[256,1024]{1,0:T(8,128)(2,1)S(1)} %collective-permute-done.10.refs_2_), channel_id=1, source_target_pairs={{0,1},{1,0},{2,3},{3,2},{4,5},{5,4},{6,7},{7,6},{8,9},{9,8},{10,11... | collective-permute-start | bytes 1572872 | tf_op jit(solution)/shard_map/ppermute | solution.py:21

commit v10 on v9

--- a/solution.py
+++ b/solution.py
@@ -631,7 +631,7 @@
     return [ring_cut(rows), swap_cut(SWAPS_EARLY + 1, rows)]
 
 
-def gather_late(held, following, late):
+def gather_late(held, following, middle, late):
     peers = lax.axis_size("ctx")
     outer = peers // 2
     rows = held[0, 0][0].shape[0]
@@ -642,10 +642,8 @@
             source = following[0]
         else:
             source = recut(held[step - 1, 0], ring_cut(rows))
-        for p, block in enumerate(source):
-            ahead = step == RINGS_EARLY + 1 and p < len(source) - 1
-            gate = None if ahead else late
-            held[step, 0].append(lax.ppermute(behind(block, gate), "ctx", route))
+        for block in source:
+            held[step, 0].append(lax.ppermute(behind(block, late), "ctx", route))
     for step in range(SWAPS_EARLY + 1, outer):
         held[step, 1] = []
         if step == SWAPS_EARLY + 1:
@@ -654,7 +652,7 @@
             source = recut(held[step, 0], swap_cut(step, rows))
         for p, block in enumerate(source):
             ahead = step == SWAPS_EARLY + 1 and p < len(source) - 1
-            gate = None if ahead else late
+            gate = middle if ahead else late
             held[step, 1].append(swap(behind(block, gate), "ctx", 1))
     return [held[step, i] for step in range(outer) for i in range(2)]
 
@@ -706,14 +704,11 @@
         maps.append(out[1])
     held = gather_early(w_output)
     following = [recut(held[RINGS_EARLY, 0], cut) for cut in next_cuts(w_output.shape[0])]
-    ready = [len(pieces) - 1 for pieces in following]
-    waiting = [pieces[n:] for pieces, n in zip(following, ready)]
-    waiting, totals = lax.optimization_barrier((waiting, out[2]))
-    following = [pieces[:n] + rest for pieces, n, rest in zip(following, ready, waiting)]
+    following, totals = lax.optimization_barrier((following, out[2]))
     first_maps = lax.all_to_all(totals, "ctx", 0, 0, tiled=True)
     run, run_maps, totals = bend_all(place, gates, maps, first_maps, gain, start)
     peer_maps = lax.all_to_all(totals, "ctx", 0, 0, tiled=True)
-    weights = gather_late(held, following, peer_maps)
+    weights = gather_late(held, following, first_maps, peer_maps)
 
     blocks = []
     for c in range(chunks):

time: 235 us -> 238 us (1.013)
  waiting for transfers between devices: 99.2 us -> 105 us
  starting transfers between devices: 34 us -> 30 us
    ppermute x4, waiting for transfers between devices: 0.01 us -> 16.7 us  [gather_early(): held[step, 0].append(lax.ppermute(block, 'ctx', route))]
    ppermute x23, waiting for transfers between devices: 95.8 us -> 83.5 us  [swap(): lax.ppermute(block, axis, [(i, i ^ bits) for i in range(lax.axis_size(axi...]
    unnamed x28 -> x34, local copies, waits for them, and re-layouts: 9.75 us -> 9.9 us
  transfers between devices with their start and end apart: 30 -> 30, of which waited for: 12 -> 14; matrix products, arithmetic and copies ran while one was open for 0% -> 0% of each run, Pallas kernels for 26% -> 25%
where the time goes in v10:
time: 238 us
  waiting for transfers between devices  105 us (44%)
  Pallas kernels  71.6 us (30%)
  starting transfers between devices  30 us (13%)
  blocking collectives  19.7 us (8%)
  local copies, waits for them, and re-layouts  10.8 us (5%)
    ppermute x23, waiting for transfers between devices, swap(): lax.ppermute(block, axis, [(i, i ^ bits) for i in range(lax.axis_size(axi...  83.5 us
    pallas_call x3, Pallas kernels, gate_chunk(): pl.pallas_call(functools.partial(gate_kernel, half, first_row, rows, len(...  22.8 us
    all_to_all x1, blocking collectives, layer(): peer_maps = lax.all_to_all(totals, 'ctx', 0, 0, tiled=True)  19.7 us
    pallas_call x4, Pallas kernels, mix_rows(): pl.pallas_call(functools.partial(mix_kernel, groups, group, cuts, peers,...  19.2 us
    ppermute x4, waiting for transfers between devices, gather_early(): held[step, 0].append(lax.ppermute(block, 'ctx', route))  16.7 us
    ppermute x23, starting transfers between devices, swap(): lax.ppermute(block, axis, [(i, i ^ bits) for i in range(lax.axis_size(axi...  15.8 us
    pallas_call x1, Pallas kernels, near_product(): pl.pallas_call(functools.partial(near_kernel, half, tiles, heights), out_...  14.1 us
    unnamed x34, local copies, waits for them, and re-layouts  9.9 us
  transfers between devices with their start and end apart: 30, of which 14 were waited for; matrix products, arithmetic and copies ran while one was open for 0% of the time, Pallas kernels for 25%

profile of v10, /device:TPU:0, one launch (start us, length us, event | category | flops | bytes accessed | tf_op | source)
XLA Modules:
  0.0 237.8 jit_solution(5267944316543343438)
XLA Ops:
  0.0 2.6 %shard_map.73.refs_0_ = bf16[512,1024]{1,0:T(8,128)(2,1)} custom-call(bf16[1024,1024]{1,0:T(8,128)(2,1)} %src.3), custom_call_target="tpu_custom_call" | custom-call | flops 268435456 | bytes 2097152 | tf_op jit(solution)/shard_map/pallas_call | solution.py:152
  2.7 3.5 %shard_map.74 = (bf16[256,1024]{1,0:T(8,128)(2,1)}, bf16[256,1024]{1,0:T(8,128)(2,1)}, bf16[1024,1024]{1,0:T(8,128)(2,1)}) custom-call(bf16[1024,1024]{1,0:T(8,128)(2,1)} %src.3, bf16[512,1024]{1,0:T(8,128)(2,1)} %shard_map.73.refs_0_), custom_call_target="tpu_custom_call" | custom-call | flops 268435456 | bytes 2097152 | tf_op jit(solution)/shard_map/pallas_call | solution.py:152
  6.8 2.6 %collective-permute-start = (bf16[512,1024]{1,0:T(8,128)(2,1)S(1)}, bf16[512,1024]{1,0:T(8,128)(2,1)}, u32[]{:S(2)}, u32[]{:S(2)}) collective-permute-start(bf16[512,1024]{1,0:T(8,128)(2,1)S(1)} %copy-done.14), channel_id=1, source_target_pairs={{0,2},{1,3},{2,0},{3,1},{4,6},{5,7},{6,4},{7,5},{8,10},{9,11},{10,... | collective-permute-start | bytes 3145736 | tf_op jit(solution)/shard_map/ppermute | solution.py:21
  9.3 0.9 fusion
  10.2 1.6 collective-permute-start.9
  11.8 1.6 collective-permute-start.7
  13.9 12.9 %collective-permute-done.9.refs_7_ = bf16[256,1024]{1,0:T(8,128)(2,1)S(1)} collective-permute-done((bf16[256,1024]{1,0:T(8,128)(2,1)S(1)}, bf16[256,1024]{1,0:T(8,128)(2,1)S(1)}, u32[]{:S(2)}, u32[]{:S(2)}) %collective-permute-start.9) | collective-permute-done | bytes 524320 | tf_op jit(solution)/shard_map/ppermute | solution.py:622
  27.1 6.3 %collective-permute-done.refs_0_ = bf16[512,1024]{1,0:T(8,128)(2,1)} collective-permute-done((bf16[512,1024]{1,0:T(8,128)(2,1)S(1)}, bf16[512,1024]{1,0:T(8,128)(2,1)}, u32[]{:S(2)}, u32[]{:S(2)}) %collective-permute-start) | collective-permute-done | bytes 1048608 | tf_op jit(solution)/shard_map/ppermute | solution.py:21
  33.5 3.7 %collective-permute-done.7.refs_6_ = bf16[256,1024]{1,0:T(8,128)(2,1)S(1)} collective-permute-done((bf16[256,1024]{1,0:T(8,128)(2,1)}, bf16[256,1024]{1,0:T(8,128)(2,1)S(1)}, u32[]{:S(2)}, u32[]{:S(2)}) %collective-permute-start.7) | collective-permute-done | bytes 524320 | tf_op jit(solution)/shard_map/ppermute | solution.py:622
  37.3 7.4 %collective-permute-done.3.refs_0_ = bf16[256,1024]{1,0:T(8,128)(2,1)} collective-permute-done((bf16[256,1024]{1,0:T(8,128)(2,1)}, bf16[256,1024]{1,0:T(8,128)(2,1)}, u32[]{:S(2)}, u32[]{:S(2)}) %collective-permute-start.3) | collective-permute-done | bytes 524320 | tf_op jit(solution)/shard_map/ppermute | solution.py:21
  44.7 2.1 collective-permute-start.8
  46.8 8.9 %collective-permute-done.5.refs_0_ = bf16[256,1024]{1,0:T(8,128)(2,1)} collective-permute-done((bf16[256,1024]{1,0:T(8,128)(2,1)}, bf16[256,1024]{1,0:T(8,128)(2,1)}, u32[]{:S(2)}, u32[]{:S(2)}) %collective-permute-start.5) | collective-permute-done | bytes 524320 | tf_op jit(solution)/shard_map/ppermute | solution.py:21
  56.2 1.6 copy-done.7
  57.7 14.1 %shard_map.75.refs_2_ = f32[2,1024,1024]{2,1,0:T(8,128)S(1)} custom-call(s32[2]{0:T(128)S(1)} %pad_add_fusion.place, bf16[1024,1024]{1,0:T(8,128)(2,1)S(1)} %copy-done.7, bf16[1024,1024]{1,0:T(8,128)(2,1)} %collective-permute-done.2.refs_1_, bf16[2,4096,1024]{2,1,0:T(8,128)(2,1)} %refs_3_.5), custom_call_target="tpu_custom_call" | custom-call | flops 8589934592 | bytes 20971520 | tf_op jit(solution)/shard_map/pallas_call | solution.py:87
  71.8 6.3 %shard_map.77 = (bf16[2,256,1024]{2,1,0:T(8,128)(2,1)S(1)}, f32[2,8,1024]{2,1,0:T(8,128)S(1)}) custom-call(s32[2]{0:T(128)S(1)} %pad_add_fusion.place, bf16[256,1024]{1,0:T(8,128)(2,1)} %collective-permute-done.3.refs_0_, bf16[256,1024]{1,0:T(8,128)(2,1)S(1)} %collective-permute-done.4.refs_1_, f32[2,1024,1024]{2,1,0:T(8,128)S(1)} %shard_map.75.refs_2_, ...), custom_call_target="tpu_custom_call" | custom-call | flops 2147483648 | bytes 12582912 | tf_op jit(solution)/shard_map/pallas_call | solution.py:300
  78.1 1.0 copy-done.10
  79.1 9.5 %shard_map.76 = (bf16[2,512,1024]{2,1,0:T(8,128)(2,1)S(1)}, f32[2,16,1024]{2,1,0:T(8,128)S(1)}) custom-call(s32[2]{0:T(128)S(1)} %pad_add_fusion.place, bf16[512,1024]{1,0:T(8,128)(2,1)} %collective-permute-done.refs_0_, bf16[512,1024]{1,0:T(8,128)(2,1)S(1)} %collective-permute-done.1.refs_1_, f32[2,1024,1024]{2,1,0:T(8,128)S(1)} %shard_map.75.refs_2_, ...), custom_call_target="tpu_custom_call" | custom-call | flops 4294967296 | bytes 16777216 | tf_op jit(solution)/shard_map/pallas_call | solution.py:300
  88.7 1.3 copy-done.8
  90.0 7.0 %shard_map.78 = (bf16[2,256,1024]{2,1,0:T(8,128)(2,1)S(1)}, f32[2,8,1024]{2,1,0:T(8,128)S(1)}, f32[8,2,1024]{2,1,0:T(2,128)}) custom-call(s32[2]{0:T(128)S(1)} %pad_add_fusion.place, bf16[256,1024]{1,0:T(8,128)(2,1)} %collective-permute-done.5.refs_0_, bf16[256,1024]{1,0:T(8,128)(2,1)S(1)} %collective-permute-done.6.refs_1_, ...), custom_call_target="tpu_custom_call" | custom-call | flops 2147483648 | bytes 12582912 | tf_op jit(solution)/shard_map/pallas_call | solution.py:300
  97.0 1.0 copy-done.12
  98.9 6.1 %all-to-all-start = ((f32[8,2,1024]{2,1,0:T(2,128)}), f32[8,2,1024]{2,1,0:T(2,128)S(1)}, u32[]{:S(2)}, u32[]{:S(2)}) async-start(f32[8,2,1024]{2,1,0:T(2,128)} %get-tuple-element.39), calls=%async_computation | async-start | bytes 131072 | tf_op jit(solution)/shard_map/all_to_all | solution.py:708
  105.0 2.0 collective-permute-start.14
  107.0 5.0 %all-to-all-done.refs_6_ = f32[8,2,1024]{2,1,0:T(2,128)S(1)} async-done(((f32[8,2,1024]{2,1,0:T(2,128)}), f32[8,2,1024]{2,1,0:T(2,128)S(1)}, u32[]{:S(2)}, u32[]{:S(2)}) %all-to-all-start) | async-done | bytes 65568 | tf_op jit(solution)/shard_map/all_to_all | solution.py:708
  112.0 1.6 copy-done.9
  113.6 1.2 copy-done.11
  114.8 1.2 copy-done.13
  116.0 6.9 %bend.1 = (f32[2,1024,1024]{2,1,0:T(8,128)S(1)}, f32[2,32,1024]{2,1,0:T(8,128)S(1)}, f32[8,2,1024]{2,1,0:T(2,128)S(1)}) custom-call(s32[2]{0:T(128)S(1)} %pad_add_fusion.place, bf16[2,512,1024]{2,1,0:T(8,128)(2,1)S(1)} %copy-done.9, bf16[2,256,1024]{2,1,0:T(8,128)(2,1)S(1)} %copy-done.11, bf16[2,256,1024]{2,1,0:T(8,128)(2,1)S(1)} %copy-done.13, ...), custom_call_target="tpu_custom_call" | custom-call | flops 41943040 | bytes 12582912 | tf_op jit(solution)/shard_map/bend/pallas_call | solution.py:406
  122.9 19.7 %all_to_all.10.peer_ref = f32[8,2,1024]{2,1,0:T(2,128)S(1)} all-to-all(f32[8,2,1024]{2,1,0:T(2,128)S(1)} %get-tuple-element.42), channel_id=1, replica_groups=mesh['ctx'=8,'ch'=4] {'ctx'}, dimensions={0} | all-to-all | bytes 131072 | tf_op jit(solution)/shard_map/all_to_all | solution.py:710
  142.6 1.0 shard_map.80.refs_0_
  143.6 1.6 collective-permute-start.24
  145.2 1.3 collective-permute-start.15
  147.2 0.8 shard_map.79.refs_0_
  149.4 10.5 %collective-permute-done.15.refs_8_ = bf16[256,1024]{1,0:T(8,128)(2,1)S(1)} collective-permute-done((bf16[256,1024]{1,0:T(8,128)(2,1)S(1)}, bf16[256,1024]{1,0:T(8,128)(2,1)S(1)}, u32[]{:S(2)}, u32[]{:S(2)}) %collective-permute-start.15) | collective-permute-done | bytes 524320 | tf_op jit(solution)/shard_map/ppermute | solution.py:21
  160.5 1.5 collective-permute-start.19
  162.0 7.0 %collective-permute-done.17.refs_12_ = bf16[256,1024]{1,0:T(8,128)(2,1)S(1)} collective-permute-done((bf16[256,1024]{1,0:T(8,128)(2,1)S(1)}, bf16[256,1024]{1,0:T(8,128)(2,1)S(1)}, u32[]{:S(2)}, u32[]{:S(2)}) %collective-permute-start.17) | collective-permute-done | bytes 524320 | tf_op jit(solution)/shard_map/ppermute | solution.py:21
  169.0 1.4 collective-permute-start.20
  170.4 10.6 %collective-permute-done.12.refs_2_ = bf16[256,1024]{1,0:T(8,128)(2,1)S(1)} collective-permute-done((bf16[256,1024]{1,0:T(8,128)(2,1)S(1)}, bf16[256,1024]{1,0:T(8,128)(2,1)S(1)}, u32[]{:S(2)}, u32[]{:S(2)}) %collective-permute-start.12) | collective-permute-done | bytes 524320 | tf_op jit(solution)/shard_map/ppermute | solution.py:21
  181.5 8.8 %collective-permute-done.27.refs_2_.refs_6_ = bf16[256,1024]{1,0:T(8,128)(2,1)S(1)} collective-permute-done((bf16[256,1024]{1,0:T(8,128)(2,1)S(1)}, bf16[256,1024]{1,0:T(8,128)(2,1)S(1)}, u32[]{:S(2)}, u32[]{:S(2)}) %collective-permute-start.27) | collective-permute-done | bytes 524320 | tf_op jit(solution)/shard_map/ppermute | solution.py:21
  190.3 1.1 collective-permute-start.18
  192.2 1.1 collective-permute-start.21
  193.3 11.8 %collective-permute-done.18.refs_13_ = bf16[256,1024]{1,0:T(8,128)(2,1)S(1)} collective-permute-done((bf16[256,1024]{1,0:T(8,128)(2,1)S(1)}, bf16[256,1024]{1,0:T(8,128)(2,1)S(1)}, u32[]{:S(2)}, u32[]{:S(2)}) %collective-permute-start.18) | collective-permute-done | bytes 524320 | tf_op jit(solution)/shard_map/ppermute | solution.py:21
  205.1 1.1 collective-permute-start.22
  206.7 3.3 %shard_map.83.refs_13_ = f32[256,1024]{1,0:T(8,128)S(1)} custom-call(s32[2]{0:T(128)S(1)} %pad_add_fusion.place, bf16[256,1024]{1,0:T(8,128)(2,1)S(1)} %shard_map.81.refs_0_.refs_4_, bf16[256,1024]{1,0:T(8,128)(2,1)S(1)} %collective-permute-done.26.refs_1_.refs_5_, bf16[256,1024]{1,0:T(8,128)(2,1)S(1)} %collective-permute-done.27.refs_2_.refs_6_, ...), custom_call_target="tpu_custom_call" | custom-call | flops 1610612736 | bytes 8912896 | tf_op jit(solution)/shard_map/pallas_call | solution.py:560
  210.1 5.4 %shard_map.82.refs_12_ = f32[512,1024]{1,0:T(8,128)S(1)} custom-call(s32[2]{0:T(128)S(1)} %pad_add_fusion.place, bf16[512,1024]{1,0:T(8,128)(2,1)S(1)} %shard_map.80.refs_0_, bf16[512,1024]{1,0:T(8,128)(2,1)S(1)} %collective-permute-done.23.refs_1_, bf16[512,1024]{1,0:T(8,128)(2,1)S(1)} %collective-permute-done.24.refs_2_, ...), custom_call_target="tpu_custom_call" | custom-call | flops 3221225472 | bytes 11534336 | tf_op jit(solution)/shard_map/pallas_call | solution.py:560
  215.4 0.9 collective-permute-done.21.refs_10_.refs_16_
  216.3 10.8 %collective-permute-done.22.refs_11_.refs_17_ = bf16[256,1024]{1,0:T(8,128)(2,1)S(1)} collective-permute-done((bf16[256,1024]{1,0:T(8,128)(2,1)S(1)}, bf16[256,1024]{1,0:T(8,128)(2,1)S(1)}, u32[]{:S(2)}, u32[]{:S(2)}) %collective-permute-start.22) | collective-permute-done | bytes 524320 | tf_op jit(solution)/shard_map/ppermute | solution.py:21
  227.1 5.3 %shard_map.84.refs_18_ = bf16[1024,1024]{1,0:T(8,128)(2,1)} custom-call(s32[2]{0:T(128)S(1)} %pad_add_fusion.place, bf16[512,1024]{1,0:T(8,128)(2,1)S(1)} %shard_map.80.refs_0_, bf16[512,1024]{1,0:T(8,128)(2,1)S(1)} %collective-permute-done.23.refs_1_, bf16[512,1024]{1,0:T(8,128)(2,1)S(1)} %collective-permute-done.24.refs_2_, ...), custom_call_target="tpu_custom_call" | custom-call | flops 1610612736 | bytes 6815744 | tf_op jit(solution)/shard_map/pallas_call | solution.py:560
  232.4 5.2 %shard_map.85 = bf16[1024,1024]{1,0:T(8,128)(2,1)} custom-call(s32[2]{0:T(128)S(1)} %pad_add_fusion.place, bf16[256,1024]{1,0:T(8,128)(2,1)S(1)} %shard_map.79.refs_0_, bf16[256,1024]{1,0:T(8,128)(2,1)S(1)} %collective-permute-done.11.refs_1_, bf16[256,1024]{1,0:T(8,128)(2,1)S(1)} %collective-permute-done.12.refs_2_, ...), custom_call_target="tpu_custom_call", output_to_operand_aliasing={{}: (19, {})} | custom-call | flops 2147483648 | bytes 11534336 | tf_op jit(solution)/shard_map/pallas_call | solution.py:560
  (64 shorter events, 7.6 us)
Async XLA Ops:
  2.7 4.1 %copy-start.14 = (bf16[512,1024]{1,0:T(8,128)(2,1)S(1)}, bf16[512,1024]{1,0:T(8,128)(2,1)}, u32[]{:S(2)}) copy-start(bf16[512,1024]{1,0:T(8,128)(2,1)} %shard_map.73.refs_0_) | copy-start | bytes 3145732
  2.7 6.7 %copy-start = (bf16[512,1024]{1,0:T(8,128)(2,1)S(1)}, bf16[512,1024]{1,0:T(8,128)(2,1)}, u32[]{:S(2)}) copy-start(bf16[512,1024]{1,0:T(8,128)(2,1)} %refs_4_.5) | copy-start | bytes 3145732
  2.7 24.4 %copy-start.15 = (f32[1024]{0:T(1024)S(1)}, f32[1024]{0:T(1024)}, u32[]{:S(2)}) copy-start(f32[1024]{0:T(1024)} %param.11) | copy-start | bytes 12292
  2.7 24.4 %copy-start.16 = (f32[1024]{0:T(1024)S(1)}, f32[1024]{0:T(1024)}, u32[]{:S(2)}) copy-start(f32[1024]{0:T(1024)} %param.10) | copy-start | bytes 12292
  6.2 49.4 %collective-permute-start.2 = (bf16[1024,1024]{1,0:T(8,128)(2,1)}, bf16[1024,1024]{1,0:T(8,128)(2,1)}, u32[]{:S(2)}, u32[]{:S(2)}) collective-permute-start(bf16[1024,1024]{1,0:T(8,128)(2,1)} %get-tuple-element.29.refs_0_), channel_id=1, source_target_pairs={{0,1},{1,0},{2,3},{3,2},{4,5},{5,4},{6,7},{7,6},{8,9},{9,8},{10,11... | collective-permute-start | bytes 6291464 | tf_op jit(solution)/shard_map/ppermute | solution.py:21
  6.8 26.7 %collective-permute-start = (bf16[512,1024]{1,0:T(8,128)(2,1)S(1)}, bf16[512,1024]{1,0:T(8,128)(2,1)}, u32[]{:S(2)}, u32[]{:S(2)}) collective-permute-start(bf16[512,1024]{1,0:T(8,128)(2,1)S(1)} %copy-done.14), channel_id=1, source_target_pairs={{0,2},{1,3},{2,0},{3,1},{4,6},{5,7},{6,4},{7,5},{8,10},{9,11},{10,... | collective-permute-start | bytes 3145736 | tf_op jit(solution)/shard_map/ppermute | solution.py:21
  10.2 16.6 %collective-permute-start.9 = (bf16[256,1024]{1,0:T(8,128)(2,1)S(1)}, bf16[256,1024]{1,0:T(8,128)(2,1)S(1)}, u32[]{:S(2)}, u32[]{:S(2)}) collective-permute-start(bf16[256,1024]{1,0:T(8,128)(2,1)S(1)} %get-tuple-element.53), channel_id=1, source_target_pairs={{0,8},{4,12},{8,16},{12,20},{16,24},{20,28},{24,0},{28,4},{1,9},{5... | collective-permute-start | bytes 1572872 | tf_op jit(solution)/shard_map/ppermute | solution.py:622
  11.8 25.5 %collective-permute-start.7 = (bf16[256,1024]{1,0:T(8,128)(2,1)}, bf16[256,1024]{1,0:T(8,128)(2,1)S(1)}, u32[]{:S(2)}, u32[]{:S(2)}) collective-permute-start(bf16[256,1024]{1,0:T(8,128)(2,1)} %get-tuple-element.54), channel_id=1, source_target_pairs={{0,8},{4,12},{8,16},{12,20},{16,24},{20,28},{24,0},{28,4},{1,9},{5... | collective-permute-start | bytes 1572872 | tf_op jit(solution)/shard_map/ppermute | solution.py:622
  13.4 31.3 %collective-permute-start.3 = (bf16[256,1024]{1,0:T(8,128)(2,1)}, bf16[256,1024]{1,0:T(8,128)(2,1)}, u32[]{:S(2)}, u32[]{:S(2)}) collective-permute-start(bf16[256,1024]{1,0:T(8,128)(2,1)} %get-tuple-element.31), channel_id=1, source_target_pairs={{0,2},{1,3},{2,0},{3,1},{4,6},{5,7},{6,4},{7,5},{8,10},{9,11},{10,... | collective-permute-start | bytes 1572872 | tf_op jit(solution)/shard_map/ppermute | solution.py:21
  26.8 28.8 %collective-permute-start.5 = (bf16[256,1024]{1,0:T(8,128)(2,1)}, bf16[256,1024]{1,0:T(8,128)(2,1)}, u32[]{:S(2)}, u32[]{:S(2)}) collective-permute-start(bf16[256,1024]{1,0:T(8,128)(2,1)} %get-tuple-element.33), channel_id=1, source_target_pairs={{0,2},{1,3},{2,0},{3,1},{4,6},{5,7},{6,4},{7,5},{8,10},{9,11},{10,... | collective-permute-start | bytes 1572872 | tf_op jit(solution)/shard_map/ppermute | solution.py:21
  33.4 45.7 %collective-permute-start.1 = (bf16[512,1024]{1,0:T(8,128)(2,1)}, bf16[512,1024]{1,0:T(8,128)(2,1)S(1)}, u32[]{:S(2)}, u32[]{:S(2)}) collective-permute-start(bf16[512,1024]{1,0:T(8,128)(2,1)} %collective-permute-done.refs_0_), channel_id=1, source_target_pairs={{0,1},{1,0},{2,3},{3,2},{4,5},{5,4},{6,7},{7,6},{8,9},{9,8},{10,11... | collective-permute-start | bytes 3145736 | tf_op jit(solution)/shard_map/ppermute | solution.py:21
  33.5 38.3 %copy-start.5 = (f32[1024]{0:T(1024)S(1)}, f32[1024]{0:T(1024)}, u32[]{:S(2)}) copy-start(f32[1024]{0:T(1024)} %param.13) | copy-start | bytes 12292
  33.5 38.3 %copy-start.6 = (f32[1024]{0:T(1024)S(1)}, f32[1024]{0:T(1024)}, u32[]{:S(2)}) copy-start(f32[1024]{0:T(1024)} %param.12) | copy-start | bytes 12292
  37.3 60.7 %collective-permute-start.10 = (bf16[256,1024]{1,0:T(8,128)(2,1)S(1)}, bf16[256,1024]{1,0:T(8,128)(2,1)S(1)}, u32[]{:S(2)}, u32[]{:S(2)}) collective-permute-start(bf16[256,1024]{1,0:T(8,128)(2,1)S(1)} %collective-permute-done.9.refs_7_), channel_id=1, source_target_pairs={{0,8},{4,12},{8,16},{12,20},{16,24},{20,28},{24,0},{28,4},{1,9},{5... | collective-permute-start | bytes 1572872 | tf_op jit(solution)/shard_map/ppermute | solution.py:622
  44.7 53.3 %collective-permute-start.8 = (bf16[256,1024]{1,0:T(8,128)(2,1)S(1)}, bf16[256,1024]{1,0:T(8,128)(2,1)S(1)}, u32[]{:S(2)}, u32[]{:S(2)}) collective-permute-start(bf16[256,1024]{1,0:T(8,128)(2,1)S(1)} %collective-permute-done.7.refs_6_), channel_id=1, source_target_pairs={{0,8},{4,12},{8,16},{12,20},{16,24},{20,28},{24,0},{28,4},{1,9},{5... | collective-permute-start | bytes 1572872 | tf_op jit(solution)/shard_map/ppermute | solution.py:622
  55.6 16.2 %collective-permute-start.4 = (bf16[256,1024]{1,0:T(8,128)(2,1)}, bf16[256,1024]{1,0:T(8,128)(2,1)S(1)}, u32[]{:S(2)}, u32[]{:S(2)}) collective-permute-start(bf16[256,1024]{1,0:T(8,128)(2,1)} %collective-permute-done.3.refs_0_), channel_id=1, source_target_pairs={{0,1},{1,0},{2,3},{3,2},{4,5},{5,4},{6,7},{7,6},{8,9},{9,8},{10,11... | collective-permute-start | bytes 1572872 | tf_op jit(solution)/shard_map/ppermute | solution.py:21
  55.6 34.3 %collective-permute-start.6 = (bf16[256,1024]{1,0:T(8,128)(2,1)}, bf16[256,1024]{1,0:T(8,128)(2,1)S(1)}, u32[]{:S(2)}, u32[]{:S(2)}) collective-permute-start(bf16[256,1024]{1,0:T(8,128)(2,1)} %collective-permute-done.5.refs_0_), channel_id=1, source_target_pairs={{0,1},{1,0},{2,3},{3,2},{4,5},{5,4},{6,7},{7,6},{8,9},{9,8},{10,11... | collective-permute-start | bytes 1572872 | tf_op jit(solution)/shard_map/ppermute | solution.py:21
  56.2 1.6 copy-start.7
  78.1 1.0 copy-start.10
  88.7 1.3 copy-start.8
  97.0 1.0 copy-start.12
  97.9 0.8 copy-start.1
  98.0 1.0 copy-start.3
  98.9 13.1 %all-to-all-start = ((f32[8,2,1024]{2,1,0:T(2,128)}), f32[8,2,1024]{2,1,0:T(2,128)S(1)}, u32[]{:S(2)}, u32[]{:S(2)}) async-start(f32[8,2,1024]{2,1,0:T(2,128)} %get-tuple-element.39), calls=%async_computation | async-start | bytes 131072 | tf_op jit(solution)/shard_map/all_to_all | solution.py:708
  105.0 55.5 %collective-permute-start.14 = (bf16[512,1024]{1,0:T(8,128)(2,1)S(1)}, bf16[512,1024]{1,0:T(8,128)(2,1)S(1)}, u32[]{:S(2)}, u32[]{:S(2)}) collective-permute-start(bf16[512,1024]{1,0:T(8,128)(2,1)S(1)} %copy-done), channel_id=1, source_target_pairs={{0,4},{4,0},{8,12},{12,8},{16,20},{20,16},{24,28},{28,24},{1,5},{5... | collective-permute-start | bytes 3145736 | tf_op jit(solution)/shard_map/ppermute | solution.py:21
  107.0 41.0 %collective-permute-start.16 = (bf16[256,1024]{1,0:T(8,128)(2,1)S(1)}, bf16[256,1024]{1,0:T(8,128)(2,1)}, u32[]{:S(2)}, u32[]{:S(2)}) collective-permute-start(bf16[256,1024]{1,0:T(8,128)(2,1)S(1)} %collective-permute-done.9.refs_7_), channel_id=1, source_target_pairs={{0,4},{4,0},{8,12},{12,8},{16,20},{20,16},{24,28},{28,24},{1,5},{5... | collective-permute-start | bytes 1572872 | tf_op jit(solution)/shard_map/ppermute | solution.py:21
  112.0 1.6 copy-start.9
  113.6 1.2 copy-start.11
  114.8 1.2 copy-start.13
  142.6 3.8 %copy-start.4 = (bf16[256,1024]{1,0:T(8,128)(2,1)S(1)}, bf16[256,1024]{1,0:T(8,128)(2,1)}, u32[]{:S(2)}) copy-start(bf16[256,1024]{1,0:T(8,128)(2,1)} %copy-done.3) | copy-start | bytes 1572868
  143.6 37.3 %collective-permute-start.24 = (bf16[512,1024]{1,0:T(8,128)(2,1)S(1)}, bf16[512,1024]{1,0:T(8,128)(2,1)S(1)}, u32[]{:S(2)}, u32[]{:S(2)}) collective-permute-start(bf16[512,1024]{1,0:T(8,128)(2,1)S(1)} %shard_map.80.refs_0_), channel_id=1, source_target_pairs={{0,2},{1,3},{2,0},{3,1},{4,6},{5,7},{6,4},{7,5},{8,10},{9,11},{10,... | collective-permute-start | bytes 3145736 | tf_op jit(solution)/shard_map/ppermute | solution.py:21
  145.2 14.8 %collective-permute-start.15 = (bf16[256,1024]{1,0:T(8,128)(2,1)S(1)}, bf16[256,1024]{1,0:T(8,128)(2,1)S(1)}, u32[]{:S(2)}, u32[]{:S(2)}) collective-permute-start(bf16[256,1024]{1,0:T(8,128)(2,1)S(1)} %collective-permute-done.7.refs_6_), channel_id=1, source_target_pairs={{0,4},{4,0},{8,12},{12,8},{16,20},{20,16},{24,28},{28,24},{1,5},{5... | collective-permute-start | bytes 1572872 | tf_op jit(solution)/shard_map/ppermute | solution.py:21
  146.5 22.5 %collective-permute-start.17 = (bf16[256,1024]{1,0:T(8,128)(2,1)S(1)}, bf16[256,1024]{1,0:T(8,128)(2,1)S(1)}, u32[]{:S(2)}, u32[]{:S(2)}) collective-permute-start(bf16[256,1024]{1,0:T(8,128)(2,1)S(1)} %copy-done.4), channel_id=1, source_target_pairs={{0,4},{4,0},{8,12},{12,8},{16,20},{20,16},{24,28},{28,24},{1,5},{5... | collective-permute-start | bytes 1572872 | tf_op jit(solution)/shard_map/ppermute | solution.py:21
  148.0 21.0 %copy-start.2 = (bf16[256,1024]{1,0:T(8,128)(2,1)S(1)}, bf16[256,1024]{1,0:T(8,128)(2,1)}, u32[]{:S(2)}) copy-start(bf16[256,1024]{1,0:T(8,128)(2,1)} %copy-done.1) | copy-start | bytes 1572868
  148.0 32.9 %collective-permute-start.12 = (bf16[256,1024]{1,0:T(8,128)(2,1)S(1)}, bf16[256,1024]{1,0:T(8,128)(2,1)S(1)}, u32[]{:S(2)}, u32[]{:S(2)}) collective-permute-start(bf16[256,1024]{1,0:T(8,128)(2,1)S(1)} %shard_map.79.refs_0_), channel_id=1, source_target_pairs={{0,2},{1,3},{2,0},{3,1},{4,6},{5,7},{6,4},{7,5},{8,10},{9,11},{10,... | collective-permute-start | bytes 1572872 | tf_op jit(solution)/shard_map/ppermute | solution.py:21
  160.0 30.3 %collective-permute-start.27 = (bf16[256,1024]{1,0:T(8,128)(2,1)S(1)}, bf16[256,1024]{1,0:T(8,128)(2,1)S(1)}, u32[]{:S(2)}, u32[]{:S(2)}) collective-permute-start(bf16[256,1024]{1,0:T(8,128)(2,1)S(1)} %shard_map.81.refs_0_.refs_4_), channel_id=1, source_target_pairs={{0,2},{1,3},{2,0},{3,1},{4,6},{5,7},{6,4},{7,5},{8,10},{9,11},{10,... | collective-permute-start | bytes 1572872 | tf_op jit(solution)/shard_map/ppermute | solution.py:21
  160.5 29.8 %collective-permute-start.19 = (bf16[256,1024]{1,0:T(8,128)(2,1)S(1)}, bf16[256,1024]{1,0:T(8,128)(2,1)S(1)}, u32[]{:S(2)}, u32[]{:S(2)}) collective-permute-start(bf16[256,1024]{1,0:T(8,128)(2,1)S(1)} %copy-done.4), channel_id=1, source_target_pairs={{0,8},{4,12},{8,16},{12,20},{16,24},{20,28},{24,0},{28,4},{1,9},{5... | collective-permute-start | bytes 1572872 | tf_op jit(solution)/shard_map/ppermute | solution.py:646
  169.0 22.4 %collective-permute-start.20 = (bf16[256,1024]{1,0:T(8,128)(2,1)S(1)}, bf16[256,1024]{1,0:T(8,128)(2,1)S(1)}, u32[]{:S(2)}, u32[]{:S(2)}) collective-permute-start(bf16[256,1024]{1,0:T(8,128)(2,1)S(1)} %copy-done.2), channel_id=1, source_target_pairs={{0,8},{4,12},{8,16},{12,20},{16,24},{20,28},{24,0},{28,4},{1,9},{5... | collective-permute-start | bytes 1572872 | tf_op jit(solution)/shard_map/ppermute | solution.py:646
  180.9 25.2 %collective-permute-start.23 = (bf16[512,1024]{1,0:T(8,128)(2,1)S(1)}, bf16[512,1024]{1,0:T(8,128)(2,1)S(1)}, u32[]{:S(2)}, u32[]{:S(2)}) collective-permute-start(bf16[512,1024]{1,0:T(8,128)(2,1)S(1)} %shard_map.80.refs_0_), channel_id=1, source_target_pairs={{0,1},{1,0},{2,3},{3,2},{4,5},{5,4},{6,7},{7,6},{8,9},{9,8},{10,11... | collective-permute-start | bytes 3145736 | tf_op jit(solution)/shard_map/ppermute | solution.py:21
  180.9 29.1 %collective-permute-start.25 = (bf16[512,1024]{1,0:T(8,128)(2,1)S(1)}, bf16[512,1024]{1,0:T(8,128)(2,1)S(1)}, u32[]{:S(2)}, u32[]{:S(2)}) collective-permute-start(bf16[512,1024]{1,0:T(8,128)(2,1)S(1)} %collective-permute-done.24.refs_2_), channel_id=1, source_target_pairs={{0,1},{1,0},{2,3},{3,2},{4,5},{5,4},{6,7},{7,6},{8,9},{9,8},{10,11... | collective-permute-start | bytes 3145736 | tf_op jit(solution)/shard_map/ppermute | solution.py:21
  190.3 1.9 collective-permute-start.26
  190.3 14.8 %collective-permute-start.18 = (bf16[256,1024]{1,0:T(8,128)(2,1)S(1)}, bf16[256,1024]{1,0:T(8,128)(2,1)S(1)}, u32[]{:S(2)}, u32[]{:S(2)}) collective-permute-start(bf16[256,1024]{1,0:T(8,128)(2,1)S(1)} %copy-done.2), channel_id=1, source_target_pairs={{0,4},{4,0},{8,12},{12,8},{16,20},{20,16},{24,28},{28,24},{1,5},{5... | collective-permute-start | bytes 1572872 | tf_op jit(solution)/shard_map/ppermute | solution.py:21
  191.4 14.8 %collective-permute-start.28 = (bf16[256,1024]{1,0:T(8,128)(2,1)S(1)}, bf16[256,1024]{1,0:T(8,128)(2,1)S(1)}, u32[]{:S(2)}, u32[]{:S(2)}) collective-permute-start(bf16[256,1024]{1,0:T(8,128)(2,1)S(1)} %collective-permute-done.27.refs_2_.refs_6_), channel_id=1, source_target_pairs={{0,1},{1,0},{2,3},{3,2},{4,5},{5,4},{6,7},{7,6},{8,9},{9,8},{10,11... | collective-permute-start | bytes 1572872 | tf_op jit(solution)/shard_map/ppermute | solution.py:21
  192.2 24.1 %collective-permute-start.21 = (bf16[256,1024]{1,0:T(8,128)(2,1)S(1)}, bf16[256,1024]{1,0:T(8,128)(2,1)S(1)}, u32[]{:S(2)}, u32[]{:S(2)}) collective-permute-start(bf16[256,1024]{1,0:T(8,128)(2,1)S(1)} %collective-permute-done.19.refs_8_.refs_14_), channel_id=1, source_target_pairs={{0,4},{4,0},{8,12},{12,8},{16,20},{20,16},{24,28},{28,24},{1,5},{5... | collective-permute-start | bytes 1572872 | tf_op jit(solution)/shard_map/ppermute | solution.py:21
  205.1 22.0 %collective-permute-start.22 = (bf16[256,1024]{1,0:T(8,128)(2,1)S(1)}, bf16[256,1024]{1,0:T(8,128)(2,1)S(1)}, u32[]{:S(2)}, u32[]{:S(2)}) collective-permute-start(bf16[256,1024]{1,0:T(8,128)(2,1)S(1)} %collective-permute-done.20.refs_9_.refs_15_), channel_id=1, source_target_pairs={{0,4},{4,0},{8,12},{12,8},{16,20},{20,16},{24,28},{28,24},{1,5},{5... | collective-permute-start | bytes 1572872 | tf_op jit(solution)/shard_map/ppermute | solution.py:21
  206.2 26.2 %collective-permute-start.11 = (bf16[256,1024]{1,0:T(8,128)(2,1)S(1)}, bf16[256,1024]{1,0:T(8,128)(2,1)S(1)}, u32[]{:S(2)}, u32[]{:S(2)}) collective-permute-start(bf16[256,1024]{1,0:T(8,128)(2,1)S(1)} %shard_map.79.refs_0_), channel_id=1, source_target_pairs={{0,1},{1,0},{2,3},{3,2},{4,5},{5,4},{6,7},{7,6},{8,9},{9,8},{10,11... | collective-permute-start | bytes 1572872 | tf_op jit(solution)/shard_map/ppermute | solution.py:21
  206.2 26.2 %collective-permute-start.13 = (bf16[256,1024]{1,0:T(8,128)(2,1)S(1)}, bf16[256,1024]{1,0:T(8,128)(2,1)S(1)}, u32[]{:S(2)}, u32[]{:S(2)}) collective-permute-start(bf16[256,1024]{1,0:T(8,128)(2,1)S(1)} %collective-permute-done.12.refs_2_), channel_id=1, source_target_pairs={{0,1},{1,0},{2,3},{3,2},{4,5},{5,4},{6,7},{7,6},{8,9},{9,8},{10,11... | collective-permute-start | bytes 1572872 | tf_op jit(solution)/shard_map/ppermute | solution.py:21

commit v11 on v10

--- a/solution.py
+++ b/solution.py
@@ -495,12 +495,26 @@
     for n in range(here):
         for p in range(len(cuts[n])):
             w_copy(n, p).start()
-    for c in range(groups):
-        for d in range(group):
-            l_copy(c, d).start()
-    for c in range(groups):
-        for d in range(group):
-            l_copy(c, d).wait()
+    pairs_of = max(1, depth // (2 * wbuf.shape[1]))
+
+    def used(d):
+        found = None
+        for r in range(pairs_of):
+            source = (place[0] ^ d) * pairs_of + r
+            slot = lax.rem(place[1] // 2 + outer - source, outer)
+            inside = (slot >= slots[0]) & (slot <= slots[-1])
+            found = inside if found is None else found | inside
+        return found
+
+    for d in range(group):
+
+        @pl.when(used(d))
+        def _():
+            for c in range(groups):
+                l_copy(c, d).start()
+            for c in range(groups):
+                l_copy(c, d).wait()
+
     top = 0
     for prev in prev_refs:
         acc[top : top + prev.shape[0], :] = prev[...]

time: 238 us -> 238 us (level)
  no operation moved by 1% of the time
where the time goes in v11:
time: 238 us; the launch traced here: 237 us
  waiting for transfers between devices  105 us (44%)
  Pallas kernels  71.1 us (30%)
  starting transfers between devices  30 us (13%)
  blocking collectives  19.7 us (8%)
  local copies, waits for them, and re-layouts  10.8 us (5%)
    ppermute x23, waiting for transfers between devices, swap(): lax.ppermute(block, axis, [(i, i ^ bits) for i in range(lax.axis_size(axi...  83.6 us
    pallas_call x3, Pallas kernels, gate_chunk(): pl.pallas_call(functools.partial(gate_kernel, half, first_row, rows, len(...  22.8 us
    all_to_all x1, blocking collectives, layer(): peer_maps = lax.all_to_all(totals, 'ctx', 0, 0, tiled=True)  19.7 us
    pallas_call x4, Pallas kernels, mix_rows(): pl.pallas_call(functools.partial(mix_kernel, groups, group, cuts, peers,...  18.7 us
    ppermute x4, waiting for transfers between devices, gather_early(): held[step, 0].append(lax.ppermute(block, 'ctx', route))  16.7 us
    ppermute x23, starting transfers between devices, swap(): lax.ppermute(block, axis, [(i, i ^ bits) for i in range(lax.axis_size(axi...  15.8 us
    pallas_call x1, Pallas kernels, near_product(): pl.pallas_call(functools.partial(near_kernel, half, tiles, heights), out_...  14.1 us
    unnamed x34, local copies, waits for them, and re-layouts  9.9 us
  transfers between devices with their start and end apart: 30, of which 14 were waited for; matrix products, arithmetic and copies ran while one was open for 0% of the time, Pallas kernels for 25%

profile of v11, /device:TPU:0, one launch (start us, length us, event | category | flops | bytes accessed | tf_op | source)
XLA Modules:
  0.0 237.3 jit_solution(6703686436310278488)
XLA Ops:
  0.0 2.6 %shard_map.73.refs_0_ = bf16[512,1024]{1,0:T(8,128)(2,1)} custom-call(bf16[1024,1024]{1,0:T(8,128)(2,1)} %src.3), custom_call_target="tpu_custom_call" | custom-call | flops 268435456 | bytes 2097152 | tf_op jit(solution)/shard_map/pallas_call | solution.py:152
  2.7 3.5 %shard_map.74 = (bf16[256,1024]{1,0:T(8,128)(2,1)}, bf16[256,1024]{1,0:T(8,128)(2,1)}, bf16[1024,1024]{1,0:T(8,128)(2,1)}) custom-call(bf16[1024,1024]{1,0:T(8,128)(2,1)} %src.3, bf16[512,1024]{1,0:T(8,128)(2,1)} %shard_map.73.refs_0_), custom_call_target="tpu_custom_call" | custom-call | flops 268435456 | bytes 2097152 | tf_op jit(solution)/shard_map/pallas_call | solution.py:152
  6.8 2.6 %collective-permute-start = (bf16[512,1024]{1,0:T(8,128)(2,1)S(1)}, bf16[512,1024]{1,0:T(8,128)(2,1)}, u32[]{:S(2)}, u32[]{:S(2)}) collective-permute-start(bf16[512,1024]{1,0:T(8,128)(2,1)S(1)} %copy-done.14), channel_id=1, source_target_pairs={{0,2},{1,3},{2,0},{3,1},{4,6},{5,7},{6,4},{7,5},{8,10},{9,11},{10,... | collective-permute-start | bytes 3145736 | tf_op jit(solution)/shard_map/ppermute | solution.py:21
  9.3 0.9 fusion
  10.2 1.6 collective-permute-start.9
  11.8 1.6 collective-permute-start.7
  13.9 12.9 %collective-permute-done.9.refs_7_ = bf16[256,1024]{1,0:T(8,128)(2,1)S(1)} collective-permute-done((bf16[256,1024]{1,0:T(8,128)(2,1)S(1)}, bf16[256,1024]{1,0:T(8,128)(2,1)S(1)}, u32[]{:S(2)}, u32[]{:S(2)}) %collective-permute-start.9) | collective-permute-done | bytes 524320 | tf_op jit(solution)/shard_map/ppermute | solution.py:636
  27.1 6.3 %collective-permute-done.refs_0_ = bf16[512,1024]{1,0:T(8,128)(2,1)} collective-permute-done((bf16[512,1024]{1,0:T(8,128)(2,1)S(1)}, bf16[512,1024]{1,0:T(8,128)(2,1)}, u32[]{:S(2)}, u32[]{:S(2)}) %collective-permute-start) | collective-permute-done | bytes 1048608 | tf_op jit(solution)/shard_map/ppermute | solution.py:21
  33.5 3.7 %collective-permute-done.7.refs_6_ = bf16[256,1024]{1,0:T(8,128)(2,1)S(1)} collective-permute-done((bf16[256,1024]{1,0:T(8,128)(2,1)}, bf16[256,1024]{1,0:T(8,128)(2,1)S(1)}, u32[]{:S(2)}, u32[]{:S(2)}) %collective-permute-start.7) | collective-permute-done | bytes 524320 | tf_op jit(solution)/shard_map/ppermute | solution.py:636
  37.3 7.4 %collective-permute-done.3.refs_0_ = bf16[256,1024]{1,0:T(8,128)(2,1)} collective-permute-done((bf16[256,1024]{1,0:T(8,128)(2,1)}, bf16[256,1024]{1,0:T(8,128)(2,1)}, u32[]{:S(2)}, u32[]{:S(2)}) %collective-permute-start.3) | collective-permute-done | bytes 524320 | tf_op jit(solution)/shard_map/ppermute | solution.py:21
  44.7 2.1 collective-permute-start.8
  46.8 8.9 %collective-permute-done.5.refs_0_ = bf16[256,1024]{1,0:T(8,128)(2,1)} collective-permute-done((bf16[256,1024]{1,0:T(8,128)(2,1)}, bf16[256,1024]{1,0:T(8,128)(2,1)}, u32[]{:S(2)}, u32[]{:S(2)}) %collective-permute-start.5) | collective-permute-done | bytes 524320 | tf_op jit(solution)/shard_map/ppermute | solution.py:21
  56.2 1.6 copy-done.7
  57.7 14.1 %shard_map.75.refs_2_ = f32[2,1024,1024]{2,1,0:T(8,128)S(1)} custom-call(s32[2]{0:T(128)S(1)} %pad_add_fusion.place, bf16[1024,1024]{1,0:T(8,128)(2,1)S(1)} %copy-done.7, bf16[1024,1024]{1,0:T(8,128)(2,1)} %collective-permute-done.2.refs_1_, bf16[2,4096,1024]{2,1,0:T(8,128)(2,1)} %refs_3_.5), custom_call_target="tpu_custom_call" | custom-call | flops 8589934592 | bytes 20971520 | tf_op jit(solution)/shard_map/pallas_call | solution.py:87
  71.8 6.3 %shard_map.77 = (bf16[2,256,1024]{2,1,0:T(8,128)(2,1)S(1)}, f32[2,8,1024]{2,1,0:T(8,128)S(1)}) custom-call(s32[2]{0:T(128)S(1)} %pad_add_fusion.place, bf16[256,1024]{1,0:T(8,128)(2,1)} %collective-permute-done.3.refs_0_, bf16[256,1024]{1,0:T(8,128)(2,1)S(1)} %collective-permute-done.4.refs_1_, f32[2,1024,1024]{2,1,0:T(8,128)S(1)} %shard_map.75.refs_2_, ...), custom_call_target="tpu_custom_call" | custom-call | flops 2147483648 | bytes 12582912 | tf_op jit(solution)/shard_map/pallas_call | solution.py:300
  78.1 1.0 copy-done.10
  79.1 9.5 %shard_map.76 = (bf16[2,512,1024]{2,1,0:T(8,128)(2,1)S(1)}, f32[2,16,1024]{2,1,0:T(8,128)S(1)}) custom-call(s32[2]{0:T(128)S(1)} %pad_add_fusion.place, bf16[512,1024]{1,0:T(8,128)(2,1)} %collective-permute-done.refs_0_, bf16[512,1024]{1,0:T(8,128)(2,1)S(1)} %collective-permute-done.1.refs_1_, f32[2,1024,1024]{2,1,0:T(8,128)S(1)} %shard_map.75.refs_2_, ...), custom_call_target="tpu_custom_call" | custom-call | flops 4294967296 | bytes 16777216 | tf_op jit(solution)/shard_map/pallas_call | solution.py:300
  88.7 1.3 copy-done.8
  90.0 7.0 %shard_map.78 = (bf16[2,256,1024]{2,1,0:T(8,128)(2,1)S(1)}, f32[2,8,1024]{2,1,0:T(8,128)S(1)}, f32[8,2,1024]{2,1,0:T(2,128)}) custom-call(s32[2]{0:T(128)S(1)} %pad_add_fusion.place, bf16[256,1024]{1,0:T(8,128)(2,1)} %collective-permute-done.5.refs_0_, bf16[256,1024]{1,0:T(8,128)(2,1)S(1)} %collective-permute-done.6.refs_1_, ...), custom_call_target="tpu_custom_call" | custom-call | flops 2147483648 | bytes 12582912 | tf_op jit(solution)/shard_map/pallas_call | solution.py:300
  97.0 1.0 copy-done.12
  98.9 6.1 %all-to-all-start = ((f32[8,2,1024]{2,1,0:T(2,128)}), f32[8,2,1024]{2,1,0:T(2,128)S(1)}, u32[]{:S(2)}, u32[]{:S(2)}) async-start(f32[8,2,1024]{2,1,0:T(2,128)} %get-tuple-element.39), calls=%async_computation | async-start | bytes 131072 | tf_op jit(solution)/shard_map/all_to_all | solution.py:722
  105.0 2.0 collective-permute-start.14
  107.0 5.0 %all-to-all-done.refs_6_ = f32[8,2,1024]{2,1,0:T(2,128)S(1)} async-done(((f32[8,2,1024]{2,1,0:T(2,128)}), f32[8,2,1024]{2,1,0:T(2,128)S(1)}, u32[]{:S(2)}, u32[]{:S(2)}) %all-to-all-start) | async-done | bytes 65568 | tf_op jit(solution)/shard_map/all_to_all | solution.py:722
  112.0 1.6 copy-done.9
  113.6 1.2 copy-done.11
  114.8 1.2 copy-done.13
  116.0 6.9 %bend.1 = (f32[2,1024,1024]{2,1,0:T(8,128)S(1)}, f32[2,32,1024]{2,1,0:T(8,128)S(1)}, f32[8,2,1024]{2,1,0:T(2,128)S(1)}) custom-call(s32[2]{0:T(128)S(1)} %pad_add_fusion.place, bf16[2,512,1024]{2,1,0:T(8,128)(2,1)S(1)} %copy-done.9, bf16[2,256,1024]{2,1,0:T(8,128)(2,1)S(1)} %copy-done.11, bf16[2,256,1024]{2,1,0:T(8,128)(2,1)S(1)} %copy-done.13, ...), custom_call_target="tpu_custom_call" | custom-call | flops 41943040 | bytes 12582912 | tf_op jit(solution)/shard_map/bend/pallas_call | solution.py:406
  122.9 19.7 %all_to_all.10.peer_ref = f32[8,2,1024]{2,1,0:T(2,128)S(1)} all-to-all(f32[8,2,1024]{2,1,0:T(2,128)S(1)} %get-tuple-element.42), channel_id=1, replica_groups=mesh['ctx'=8,'ch'=4] {'ctx'}, dimensions={0} | all-to-all | bytes 131072 | tf_op jit(solution)/shard_map/all_to_all | solution.py:724
  142.6 1.0 shard_map.80.refs_0_
  143.6 1.6 collective-permute-start.24
  145.2 1.3 collective-permute-start.15
  147.2 0.8 shard_map.79.refs_0_
  149.4 10.5 %collective-permute-done.15.refs_8_ = bf16[256,1024]{1,0:T(8,128)(2,1)S(1)} collective-permute-done((bf16[256,1024]{1,0:T(8,128)(2,1)S(1)}, bf16[256,1024]{1,0:T(8,128)(2,1)S(1)}, u32[]{:S(2)}, u32[]{:S(2)}) %collective-permute-start.15) | collective-permute-done | bytes 524320 | tf_op jit(solution)/shard_map/ppermute | solution.py:21
  160.5 1.5 collective-permute-start.19
  162.0 7.0 %collective-permute-done.17.refs_12_ = bf16[256,1024]{1,0:T(8,128)(2,1)S(1)} collective-permute-done((bf16[256,1024]{1,0:T(8,128)(2,1)S(1)}, bf16[256,1024]{1,0:T(8,128)(2,1)S(1)}, u32[]{:S(2)}, u32[]{:S(2)}) %collective-permute-start.17) | collective-permute-done | bytes 524320 | tf_op jit(solution)/shard_map/ppermute | solution.py:21
  169.0 1.4 collective-permute-start.20
  170.4 10.6 %collective-permute-done.12.refs_2_ = bf16[256,1024]{1,0:T(8,128)(2,1)S(1)} collective-permute-done((bf16[256,1024]{1,0:T(8,128)(2,1)S(1)}, bf16[256,1024]{1,0:T(8,128)(2,1)S(1)}, u32[]{:S(2)}, u32[]{:S(2)}) %collective-permute-start.12) | collective-permute-done | bytes 524320 | tf_op jit(solution)/shard_map/ppermute | solution.py:21
  181.5 8.8 %collective-permute-done.27.refs_2_.refs_6_ = bf16[256,1024]{1,0:T(8,128)(2,1)S(1)} collective-permute-done((bf16[256,1024]{1,0:T(8,128)(2,1)S(1)}, bf16[256,1024]{1,0:T(8,128)(2,1)S(1)}, u32[]{:S(2)}, u32[]{:S(2)}) %collective-permute-start.27) | collective-permute-done | bytes 524320 | tf_op jit(solution)/shard_map/ppermute | solution.py:21
  190.3 1.1 collective-permute-start.18
  192.2 1.1 collective-permute-start.21
  193.3 11.8 %collective-permute-done.18.refs_13_ = bf16[256,1024]{1,0:T(8,128)(2,1)S(1)} collective-permute-done((bf16[256,1024]{1,0:T(8,128)(2,1)S(1)}, bf16[256,1024]{1,0:T(8,128)(2,1)S(1)}, u32[]{:S(2)}, u32[]{:S(2)}) %collective-permute-start.18) | collective-permute-done | bytes 524320 | tf_op jit(solution)/shard_map/ppermute | solution.py:21
  205.1 1.1 collective-permute-start.22
  206.7 3.4 %shard_map.83.refs_13_ = f32[256,1024]{1,0:T(8,128)S(1)} custom-call(s32[2]{0:T(128)S(1)} %pad_add_fusion.place, bf16[256,1024]{1,0:T(8,128)(2,1)S(1)} %shard_map.81.refs_0_.refs_4_, bf16[256,1024]{1,0:T(8,128)(2,1)S(1)} %collective-permute-done.26.refs_1_.refs_5_, bf16[256,1024]{1,0:T(8,128)(2,1)S(1)} %collective-permute-done.27.refs_2_.refs_6_, ...), custom_call_target="tpu_custom_call" | custom-call | flops 1610612736 | bytes 8912896 | tf_op jit(solution)/shard_map/pallas_call | solution.py:574
  210.1 5.3 %shard_map.82.refs_12_ = f32[512,1024]{1,0:T(8,128)S(1)} custom-call(s32[2]{0:T(128)S(1)} %pad_add_fusion.place, bf16[512,1024]{1,0:T(8,128)(2,1)S(1)} %shard_map.80.refs_0_, bf16[512,1024]{1,0:T(8,128)(2,1)S(1)} %collective-permute-done.23.refs_1_, bf16[512,1024]{1,0:T(8,128)(2,1)S(1)} %collective-permute-done.24.refs_2_, ...), custom_call_target="tpu_custom_call" | custom-call | flops 3221225472 | bytes 11534336 | tf_op jit(solution)/shard_map/pallas_call | solution.py:574
  215.4 0.9 collective-permute-done.21.refs_10_.refs_16_
  216.3 10.8 %collective-permute-done.22.refs_11_.refs_17_ = bf16[256,1024]{1,0:T(8,128)(2,1)S(1)} collective-permute-done((bf16[256,1024]{1,0:T(8,128)(2,1)S(1)}, bf16[256,1024]{1,0:T(8,128)(2,1)S(1)}, u32[]{:S(2)}, u32[]{:S(2)}) %collective-permute-start.22) | collective-permute-done | bytes 524320 | tf_op jit(solution)/shard_map/ppermute | solution.py:21
  227.1 4.8 %shard_map.84.refs_18_ = bf16[1024,1024]{1,0:T(8,128)(2,1)} custom-call(s32[2]{0:T(128)S(1)} %pad_add_fusion.place, bf16[512,1024]{1,0:T(8,128)(2,1)S(1)} %shard_map.80.refs_0_, bf16[512,1024]{1,0:T(8,128)(2,1)S(1)} %collective-permute-done.23.refs_1_, bf16[512,1024]{1,0:T(8,128)(2,1)S(1)} %collective-permute-done.24.refs_2_, ...), custom_call_target="tpu_custom_call" | custom-call | flops 1610612736 | bytes 6815744 | tf_op jit(solution)/shard_map/pallas_call | solution.py:574
  231.9 5.2 %shard_map.85 = bf16[1024,1024]{1,0:T(8,128)(2,1)} custom-call(s32[2]{0:T(128)S(1)} %pad_add_fusion.place, bf16[256,1024]{1,0:T(8,128)(2,1)S(1)} %shard_map.79.refs_0_, bf16[256,1024]{1,0:T(8,128)(2,1)S(1)} %collective-permute-done.11.refs_1_, bf16[256,1024]{1,0:T(8,128)(2,1)S(1)} %collective-permute-done.12.refs_2_, ...), custom_call_target="tpu_custom_call", output_to_operand_aliasing={{}: (19, {})} | custom-call | flops 2147483648 | bytes 11534336 | tf_op jit(solution)/shard_map/pallas_call | solution.py:574
  (64 shorter events, 7.6 us)
Async XLA Ops:
  2.7 4.1 %copy-start.14 = (bf16[512,1024]{1,0:T(8,128)(2,1)S(1)}, bf16[512,1024]{1,0:T(8,128)(2,1)}, u32[]{:S(2)}) copy-start(bf16[512,1024]{1,0:T(8,128)(2,1)} %shard_map.73.refs_0_) | copy-start | bytes 3145732
  2.7 6.7 %copy-start = (bf16[512,1024]{1,0:T(8,128)(2,1)S(1)}, bf16[512,1024]{1,0:T(8,128)(2,1)}, u32[]{:S(2)}) copy-start(bf16[512,1024]{1,0:T(8,128)(2,1)} %refs_4_.5) | copy-start | bytes 3145732
  2.7 24.4 %copy-start.15 = (f32[1024]{0:T(1024)S(1)}, f32[1024]{0:T(1024)}, u32[]{:S(2)}) copy-start(f32[1024]{0:T(1024)} %param.11) | copy-start | bytes 12292
  2.7 24.4 %copy-start.16 = (f32[1024]{0:T(1024)S(1)}, f32[1024]{0:T(1024)}, u32[]{:S(2)}) copy-start(f32[1024]{0:T(1024)} %param.10) | copy-start | bytes 12292
  6.2 49.4 %collective-permute-start.2 = (bf16[1024,1024]{1,0:T(8,128)(2,1)}, bf16[1024,1024]{1,0:T(8,128)(2,1)}, u32[]{:S(2)}, u32[]{:S(2)}) collective-permute-start(bf16[1024,1024]{1,0:T(8,128)(2,1)} %get-tuple-element.29.refs_0_), channel_id=1, source_target_pairs={{0,1},{1,0},{2,3},{3,2},{4,5},{5,4},{6,7},{7,6},{8,9},{9,8},{10,11... | collective-permute-start | bytes 6291464 | tf_op jit(solution)/shard_map/ppermute | solution.py:21
  6.8 26.7 %collective-permute-start = (bf16[512,1024]{1,0:T(8,128)(2,1)S(1)}, bf16[512,1024]{1,0:T(8,128)(2,1)}, u32[]{:S(2)}, u32[]{:S(2)}) collective-permute-start(bf16[512,1024]{1,0:T(8,128)(2,1)S(1)} %copy-done.14), channel_id=1, source_target_pairs={{0,2},{1,3},{2,0},{3,1},{4,6},{5,7},{6,4},{7,5},{8,10},{9,11},{10,... | collective-permute-start | bytes 3145736 | tf_op jit(solution)/shard_map/ppermute | solution.py:21
  10.2 16.6 %collective-permute-start.9 = (bf16[256,1024]{1,0:T(8,128)(2,1)S(1)}, bf16[256,1024]{1,0:T(8,128)(2,1)S(1)}, u32[]{:S(2)}, u32[]{:S(2)}) collective-permute-start(bf16[256,1024]{1,0:T(8,128)(2,1)S(1)} %get-tuple-element.53), channel_id=1, source_target_pairs={{0,8},{4,12},{8,16},{12,20},{16,24},{20,28},{24,0},{28,4},{1,9},{5... | collective-permute-start | bytes 1572872 | tf_op jit(solution)/shard_map/ppermute | solution.py:636
  11.8 25.5 %collective-permute-start.7 = (bf16[256,1024]{1,0:T(8,128)(2,1)}, bf16[256,1024]{1,0:T(8,128)(2,1)S(1)}, u32[]{:S(2)}, u32[]{:S(2)}) collective-permute-start(bf16[256,1024]{1,0:T(8,128)(2,1)} %get-tuple-element.54), channel_id=1, source_target_pairs={{0,8},{4,12},{8,16},{12,20},{16,24},{20,28},{24,0},{28,4},{1,9},{5... | collective-permute-start | bytes 1572872 | tf_op jit(solution)/shard_map/ppermute | solution.py:636
  13.4 31.3 %collective-permute-start.3 = (bf16[256,1024]{1,0:T(8,128)(2,1)}, bf16[256,1024]{1,0:T(8,128)(2,1)}, u32[]{:S(2)}, u32[]{:S(2)}) collective-permute-start(bf16[256,1024]{1,0:T(8,128)(2,1)} %get-tuple-element.31), channel_id=1, source_target_pairs={{0,2},{1,3},{2,0},{3,1},{4,6},{5,7},{6,4},{7,5},{8,10},{9,11},{10,... | collective-permute-start | bytes 1572872 | tf_op jit(solution)/shard_map/ppermute | solution.py:21
  26.8 28.8 %collective-permute-start.5 = (bf16[256,1024]{1,0:T(8,128)(2,1)}, bf16[256,1024]{1,0:T(8,128)(2,1)}, u32[]{:S(2)}, u32[]{:S(2)}) collective-permute-start(bf16[256,1024]{1,0:T(8,128)(2,1)} %get-tuple-element.33), channel_id=1, source_target_pairs={{0,2},{1,3},{2,0},{3,1},{4,6},{5,7},{6,4},{7,5},{8,10},{9,11},{10,... | collective-permute-start | bytes 1572872 | tf_op jit(solution)/shard_map/ppermute | solution.py:21
  33.4 45.7 %collective-permute-start.1 = (bf16[512,1024]{1,0:T(8,128)(2,1)}, bf16[512,1024]{1,0:T(8,128)(2,1)S(1)}, u32[]{:S(2)}, u32[]{:S(2)}) collective-permute-start(bf16[512,1024]{1,0:T(8,128)(2,1)} %collective-permute-done.refs_0_), channel_id=1, source_target_pairs={{0,1},{1,0},{2,3},{3,2},{4,5},{5,4},{6,7},{7,6},{8,9},{9,8},{10,11... | collective-permute-start | bytes 3145736 | tf_op jit(solution)/shard_map/ppermute | solution.py:21
  33.5 38.3 %copy-start.5 = (f32[1024]{0:T(1024)S(1)}, f32[1024]{0:T(1024)}, u32[]{:S(2)}) copy-start(f32[1024]{0:T(1024)} %param.13) | copy-start | bytes 12292
  33.5 38.3 %copy-start.6 = (f32[1024]{0:T(1024)S(1)}, f32[1024]{0:T(1024)}, u32[]{:S(2)}) copy-start(f32[1024]{0:T(1024)} %param.12) | copy-start | bytes 12292
  37.3 60.7 %collective-permute-start.10 = (bf16[256,1024]{1,0:T(8,128)(2,1)S(1)}, bf16[256,1024]{1,0:T(8,128)(2,1)S(1)}, u32[]{:S(2)}, u32[]{:S(2)}) collective-permute-start(bf16[256,1024]{1,0:T(8,128)(2,1)S(1)} %collective-permute-done.9.refs_7_), channel_id=1, source_target_pairs={{0,8},{4,12},{8,16},{12,20},{16,24},{20,28},{24,0},{28,4},{1,9},{5... | collective-permute-start | bytes 1572872 | tf_op jit(solution)/shard_map/ppermute | solution.py:636
  44.7 53.3 %collective-permute-start.8 = (bf16[256,1024]{1,0:T(8,128)(2,1)S(1)}, bf16[256,1024]{1,0:T(8,128)(2,1)S(1)}, u32[]{:S(2)}, u32[]{:S(2)}) collective-permute-start(bf16[256,1024]{1,0:T(8,128)(2,1)S(1)} %collective-permute-done.7.refs_6_), channel_id=1, source_target_pairs={{0,8},{4,12},{8,16},{12,20},{16,24},{20,28},{24,0},{28,4},{1,9},{5... | collective-permute-start | bytes 1572872 | tf_op jit(solution)/shard_map/ppermute | solution.py:636
  55.6 16.2 %collective-permute-start.4 = (bf16[256,1024]{1,0:T(8,128)(2,1)}, bf16[256,1024]{1,0:T(8,128)(2,1)S(1)}, u32[]{:S(2)}, u32[]{:S(2)}) collective-permute-start(bf16[256,1024]{1,0:T(8,128)(2,1)} %collective-permute-done.3.refs_0_), channel_id=1, source_target_pairs={{0,1},{1,0},{2,3},{3,2},{4,5},{5,4},{6,7},{7,6},{8,9},{9,8},{10,11... | collective-permute-start | bytes 1572872 | tf_op jit(solution)/shard_map/ppermute | solution.py:21
  55.6 34.3 %collective-permute-start.6 = (bf16[256,1024]{1,0:T(8,128)(2,1)}, bf16[256,1024]{1,0:T(8,128)(2,1)S(1)}, u32[]{:S(2)}, u32[]{:S(2)}) collective-permute-start(bf16[256,1024]{1,0:T(8,128)(2,1)} %collective-permute-done.5.refs_0_), channel_id=1, source_target_pairs={{0,1},{1,0},{2,3},{3,2},{4,5},{5,4},{6,7},{7,6},{8,9},{9,8},{10,11... | collective-permute-start | bytes 1572872 | tf_op jit(solution)/shard_map/ppermute | solution.py:21
  56.2 1.6 copy-start.7
  78.1 1.0 copy-start.10
  88.7 1.3 copy-start.8
  97.0 1.0 copy-start.12
  97.9 0.8 copy-start.1
  98.0 1.0 copy-start.3
  98.9 13.1 %all-to-all-start = ((f32[8,2,1024]{2,1,0:T(2,128)}), f32[8,2,1024]{2,1,0:T(2,128)S(1)}, u32[]{:S(2)}, u32[]{:S(2)}) async-start(f32[8,2,1024]{2,1,0:T(2,128)} %get-tuple-element.39), calls=%async_computation | async-start | bytes 131072 | tf_op jit(solution)/shard_map/all_to_all | solution.py:722
  105.0 55.5 %collective-permute-start.14 = (bf16[512,1024]{1,0:T(8,128)(2,1)S(1)}, bf16[512,1024]{1,0:T(8,128)(2,1)S(1)}, u32[]{:S(2)}, u32[]{:S(2)}) collective-permute-start(bf16[512,1024]{1,0:T(8,128)(2,1)S(1)} %copy-done), channel_id=1, source_target_pairs={{0,4},{4,0},{8,12},{12,8},{16,20},{20,16},{24,28},{28,24},{1,5},{5... | collective-permute-start | bytes 3145736 | tf_op jit(solution)/shard_map/ppermute | solution.py:21
  107.0 41.0 %collective-permute-start.16 = (bf16[256,1024]{1,0:T(8,128)(2,1)S(1)}, bf16[256,1024]{1,0:T(8,128)(2,1)}, u32[]{:S(2)}, u32[]{:S(2)}) collective-permute-start(bf16[256,1024]{1,0:T(8,128)(2,1)S(1)} %collective-permute-done.9.refs_7_), channel_id=1, source_target_pairs={{0,4},{4,0},{8,12},{12,8},{16,20},{20,16},{24,28},{28,24},{1,5},{5... | collective-permute-start | bytes 1572872 | tf_op jit(solution)/shard_map/ppermute | solution.py:21
  112.0 1.6 copy-start.9
  113.6 1.2 copy-start.11
  114.8 1.2 copy-start.13
  142.6 3.8 %copy-start.4 = (bf16[256,1024]{1,0:T(8,128)(2,1)S(1)}, bf16[256,1024]{1,0:T(8,128)(2,1)}, u32[]{:S(2)}) copy-start(bf16[256,1024]{1,0:T(8,128)(2,1)} %copy-done.3) | copy-start | bytes 1572868
  143.6 37.3 %collective-permute-start.24 = (bf16[512,1024]{1,0:T(8,128)(2,1)S(1)}, bf16[512,1024]{1,0:T(8,128)(2,1)S(1)}, u32[]{:S(2)}, u32[]{:S(2)}) collective-permute-start(bf16[512,1024]{1,0:T(8,128)(2,1)S(1)} %shard_map.80.refs_0_), channel_id=1, source_target_pairs={{0,2},{1,3},{2,0},{3,1},{4,6},{5,7},{6,4},{7,5},{8,10},{9,11},{10,... | collective-permute-start | bytes 3145736 | tf_op jit(solution)/shard_map/ppermute | solution.py:21
  145.2 14.8 %collective-permute-start.15 = (bf16[256,1024]{1,0:T(8,128)(2,1)S(1)}, bf16[256,1024]{1,0:T(8,128)(2,1)S(1)}, u32[]{:S(2)}, u32[]{:S(2)}) collective-permute-start(bf16[256,1024]{1,0:T(8,128)(2,1)S(1)} %collective-permute-done.7.refs_6_), channel_id=1, source_target_pairs={{0,4},{4,0},{8,12},{12,8},{16,20},{20,16},{24,28},{28,24},{1,5},{5... | collective-permute-start | bytes 1572872 | tf_op jit(solution)/shard_map/ppermute | solution.py:21
  146.5 22.5 %collective-permute-start.17 = (bf16[256,1024]{1,0:T(8,128)(2,1)S(1)}, bf16[256,1024]{1,0:T(8,128)(2,1)S(1)}, u32[]{:S(2)}, u32[]{:S(2)}) collective-permute-start(bf16[256,1024]{1,0:T(8,128)(2,1)S(1)} %copy-done.4), channel_id=1, source_target_pairs={{0,4},{4,0},{8,12},{12,8},{16,20},{20,16},{24,28},{28,24},{1,5},{5... | collective-permute-start | bytes 1572872 | tf_op jit(solution)/shard_map/ppermute | solution.py:21
  148.0 21.0 %copy-start.2 = (bf16[256,1024]{1,0:T(8,128)(2,1)S(1)}, bf16[256,1024]{1,0:T(8,128)(2,1)}, u32[]{:S(2)}) copy-start(bf16[256,1024]{1,0:T(8,128)(2,1)} %copy-done.1) | copy-start | bytes 1572868
  148.0 32.9 %collective-permute-start.12 = (bf16[256,1024]{1,0:T(8,128)(2,1)S(1)}, bf16[256,1024]{1,0:T(8,128)(2,1)S(1)}, u32[]{:S(2)}, u32[]{:S(2)}) collective-permute-start(bf16[256,1024]{1,0:T(8,128)(2,1)S(1)} %shard_map.79.refs_0_), channel_id=1, source_target_pairs={{0,2},{1,3},{2,0},{3,1},{4,6},{5,7},{6,4},{7,5},{8,10},{9,11},{10,... | collective-permute-start | bytes 1572872 | tf_op jit(solution)/shard_map/ppermute | solution.py:21
  160.0 30.3 %collective-permute-start.27 = (bf16[256,1024]{1,0:T(8,128)(2,1)S(1)}, bf16[256,1024]{1,0:T(8,128)(2,1)S(1)}, u32[]{:S(2)}, u32[]{:S(2)}) collective-permute-start(bf16[256,1024]{1,0:T(8,128)(2,1)S(1)} %shard_map.81.refs_0_.refs_4_), channel_id=1, source_target_pairs={{0,2},{1,3},{2,0},{3,1},{4,6},{5,7},{6,4},{7,5},{8,10},{9,11},{10,... | collective-permute-start | bytes 1572872 | tf_op jit(solution)/shard_map/ppermute | solution.py:21
  160.5 29.8 %collective-permute-start.19 = (bf16[256,1024]{1,0:T(8,128)(2,1)S(1)}, bf16[256,1024]{1,0:T(8,128)(2,1)S(1)}, u32[]{:S(2)}, u32[]{:S(2)}) collective-permute-start(bf16[256,1024]{1,0:T(8,128)(2,1)S(1)} %copy-done.4), channel_id=1, source_target_pairs={{0,8},{4,12},{8,16},{12,20},{16,24},{20,28},{24,0},{28,4},{1,9},{5... | collective-permute-start | bytes 1572872 | tf_op jit(solution)/shard_map/ppermute | solution.py:660
  169.0 22.4 %collective-permute-start.20 = (bf16[256,1024]{1,0:T(8,128)(2,1)S(1)}, bf16[256,1024]{1,0:T(8,128)(2,1)S(1)}, u32[]{:S(2)}, u32[]{:S(2)}) collective-permute-start(bf16[256,1024]{1,0:T(8,128)(2,1)S(1)} %copy-done.2), channel_id=1, source_target_pairs={{0,8},{4,12},{8,16},{12,20},{16,24},{20,28},{24,0},{28,4},{1,9},{5... | collective-permute-start | bytes 1572872 | tf_op jit(solution)/shard_map/ppermute | solution.py:660
  180.9 25.2 %collective-permute-start.23 = (bf16[512,1024]{1,0:T(8,128)(2,1)S(1)}, bf16[512,1024]{1,0:T(8,128)(2,1)S(1)}, u32[]{:S(2)}, u32[]{:S(2)}) collective-permute-start(bf16[512,1024]{1,0:T(8,128)(2,1)S(1)} %shard_map.80.refs_0_), channel_id=1, source_target_pairs={{0,1},{1,0},{2,3},{3,2},{4,5},{5,4},{6,7},{7,6},{8,9},{9,8},{10,11... | collective-permute-start | bytes 3145736 | tf_op jit(solution)/shard_map/ppermute | solution.py:21
  180.9 29.1 %collective-permute-start.25 = (bf16[512,1024]{1,0:T(8,128)(2,1)S(1)}, bf16[512,1024]{1,0:T(8,128)(2,1)S(1)}, u32[]{:S(2)}, u32[]{:S(2)}) collective-permute-start(bf16[512,1024]{1,0:T(8,128)(2,1)S(1)} %collective-permute-done.24.refs_2_), channel_id=1, source_target_pairs={{0,1},{1,0},{2,3},{3,2},{4,5},{5,4},{6,7},{7,6},{8,9},{9,8},{10,11... | collective-permute-start | bytes 3145736 | tf_op jit(solution)/shard_map/ppermute | solution.py:21
  190.3 1.9 collective-permute-start.26
  190.3 14.8 %collective-permute-start.18 = (bf16[256,1024]{1,0:T(8,128)(2,1)S(1)}, bf16[256,1024]{1,0:T(8,128)(2,1)S(1)}, u32[]{:S(2)}, u32[]{:S(2)}) collective-permute-start(bf16[256,1024]{1,0:T(8,128)(2,1)S(1)} %copy-done.2), channel_id=1, source_target_pairs={{0,4},{4,0},{8,12},{12,8},{16,20},{20,16},{24,28},{28,24},{1,5},{5... | collective-permute-start | bytes 1572872 | tf_op jit(solution)/shard_map/ppermute | solution.py:21
  191.4 14.8 %collective-permute-start.28 = (bf16[256,1024]{1,0:T(8,128)(2,1)S(1)}, bf16[256,1024]{1,0:T(8,128)(2,1)S(1)}, u32[]{:S(2)}, u32[]{:S(2)}) collective-permute-start(bf16[256,1024]{1,0:T(8,128)(2,1)S(1)} %collective-permute-done.27.refs_2_.refs_6_), channel_id=1, source_target_pairs={{0,1},{1,0},{2,3},{3,2},{4,5},{5,4},{6,7},{7,6},{8,9},{9,8},{10,11... | collective-permute-start | bytes 1572872 | tf_op jit(solution)/shard_map/ppermute | solution.py:21
  192.2 24.1 %collective-permute-start.21 = (bf16[256,1024]{1,0:T(8,128)(2,1)S(1)}, bf16[256,1024]{1,0:T(8,128)(2,1)S(1)}, u32[]{:S(2)}, u32[]{:S(2)}) collective-permute-start(bf16[256,1024]{1,0:T(8,128)(2,1)S(1)} %collective-permute-done.19.refs_8_.refs_14_), channel_id=1, source_target_pairs={{0,4},{4,0},{8,12},{12,8},{16,20},{20,16},{24,28},{28,24},{1,5},{5... | collective-permute-start | bytes 1572872 | tf_op jit(solution)/shard_map/ppermute | solution.py:21
  205.1 22.0 %collective-permute-start.22 = (bf16[256,1024]{1,0:T(8,128)(2,1)S(1)}, bf16[256,1024]{1,0:T(8,128)(2,1)S(1)}, u32[]{:S(2)}, u32[]{:S(2)}) collective-permute-start(bf16[256,1024]{1,0:T(8,128)(2,1)S(1)} %collective-permute-done.20.refs_9_.refs_15_), channel_id=1, source_target_pairs={{0,4},{4,0},{8,12},{12,8},{16,20},{20,16},{24,28},{28,24},{1,5},{5... | collective-permute-start | bytes 1572872 | tf_op jit(solution)/shard_map/ppermute | solution.py:21
  206.2 25.7 %collective-permute-start.11 = (bf16[256,1024]{1,0:T(8,128)(2,1)S(1)}, bf16[256,1024]{1,0:T(8,128)(2,1)S(1)}, u32[]{:S(2)}, u32[]{:S(2)}) collective-permute-start(bf16[256,1024]{1,0:T(8,128)(2,1)S(1)} %shard_map.79.refs_0_), channel_id=1, source_target_pairs={{0,1},{1,0},{2,3},{3,2},{4,5},{5,4},{6,7},{7,6},{8,9},{9,8},{10,11... | collective-permute-start | bytes 1572872 | tf_op jit(solution)/shard_map/ppermute | solution.py:21
  206.2 25.7 %collective-permute-start.13 = (bf16[256,1024]{1,0:T(8,128)(2,1)S(1)}, bf16[256,1024]{1,0:T(8,128)(2,1)S(1)}, u32[]{:S(2)}, u32[]{:S(2)}) collective-permute-start(bf16[256,1024]{1,0:T(8,128)(2,1)S(1)} %collective-permute-done.12.refs_2_), channel_id=1, source_target_pairs={{0,1},{1,0},{2,3},{3,2},{4,5},{5,4},{6,7},{7,6},{8,9},{9,8},{10,11... | collective-permute-start | bytes 1572872 | tf_op jit(solution)/shard_map/ppermute | solution.py:21
